TPU v7x, 32 devices: a whole 2x2x4 slice. The times are simulated.
32 devices in a mesh: dp: 4 (over z), head: 2 (over y), hid: 4 (over x, core).
Axes of the slice: x: 2, y: 2, z: 4, core: 2. Of those that a mesh axis runs over, the one named last changes fastest.
Arguments:
- inputs: bfloat16 [8, 1024, 1472], P('dp', ('head', 'hid')), may hold values from -6 to 6
- lengths: int32 [8], P('dp'), may hold values from 512 to 1024, as said below
- delete_mask: float32 [8, 1024], P('dp'), may hold values from -3 to 0
- buckets: int32 [2047], replicated, may hold values from 0 to 31
- gain_attn: float32 [1472], replicated, may hold values from 0.1 to 1.9
- w_query: bfloat16 [1472, 384], P(None, 'head'), may hold values from -0.078125 to 0.078125
- w_key: bfloat16 [1472, 384], P(None, 'head'), may hold values from -0.078125 to 0.078125
- w_value: bfloat16 [1472, 384], P(None, 'head'), may hold values from -0.15625 to 0.15625
- w_out: bfloat16 [384, 1472], P('head'), may hold values from -1.25 to 1.25
- rel_bias: float32 [32, 6], replicated, may hold values from -4 to 4
- gain_ffn: float32 [1472], replicated, may hold values from 0.1 to 1.9
- gate_weight: bfloat16 [1472, 3584], P(None, ('head', 'hid')), may hold values from -0.15625 to 0.15625
- up_weight: bfloat16 [1472, 3584], P(None, ('head', 'hid')), may hold values from -0.15625 to 0.15625
- down_weight: bfloat16 [3584, 1472], P(('head', 'hid')), may hold values from -0.125 to 0.125
- cotangent: bfloat16 [8, 1024, 1472], P('dp', ('head', 'hid')), may hold values from -6 to 6
Outputs:
- output: bfloat16 [8, 1024, 1472], P('dp', ('head', 'hid'))
- grad_inputs: float32 [8, 1024, 1472], P('dp', ('head', 'hid'))
- grad_mask: float32 [8, 1024], P('dp', ('head', 'hid'))
- grad_gain_attn: float32 [1472], replicated
- grad_w_query: float32 [1472, 384], P(None, 'head')
- grad_w_key: float32 [1472, 384], P(None, 'head')
- grad_w_value: float32 [1472, 384], P(None, 'head')
- grad_w_out: float32 [384, 1472], P('head')
- grad_rel_bias: float32 [32, 6], replicated
- grad_gain_ffn: float32 [1472], replicated
- gate_weight_gradient: float32 [1472, 3584], P(None, ('head', 'hid'))
- up_weight_gradient: float32 [1472, 3584], P(None, ('head', 'hid'))
- grad_w_down: float32 [3584, 1472], P(('head', 'hid'))
Inputs may be any that keep to these rules, and one draw needn't show every extreme that they name: `lengths`: keys at or after a sequence's length are padding; the first sequence has length 1024.
All inputs are finite; a program needn't handle non-finite values.
Results may differ from a plain program's by a relative error of at most 0.017.
The roundings to bfloat16 on the way count: a program that leaves them out, or rounds other values in their place, can miss the bound.
Values may be sent and summed in bfloat16 or wider, within the bound.
No kernel may reach another device: no remote copies, remote signals or barrier semaphores. Data moves between devices by JAX's collectives and lax.ppermute only.
A program may use at most 192 MiB of HBM per device.

v0:
```python
import jax
import jax.numpy as jnp
from jax import lax
from jax.sharding import PartitionSpec as P

DH = 64


epsilon = 1e-06
neg_fill = -1e30


def rms_scale(rows_in, gain_vec):
    inverse = lax.rsqrt(jnp.mean(rows_in * rows_in, axis=-1, keepdims=True) + epsilon)
    return rows_in * inverse * gain_vec


def gated_unit(gate_in, up_in):
    return jax.nn.gelu(gate_in, approximate=True) * up_in


def per_device(
    inputs,
    lengths,
    delete_mask,
    buckets,
    gain_attn,
    w_query,
    w_key,
    w_value,
    w_out,
    rel_bias,
    gain_ffn,
    gate_weight,
    up_weight,
    down_weight,
    cotangent,
):
    highest = lax.Precision.HIGHEST
    seq_count, row_count, model_width = inputs.shape
    head_count = lax.axis_size("head")
    hid_count = lax.axis_size("hid")
    head_index = lax.axis_index("head")
    hid_index = lax.axis_index("hid")
    seq_length = row_count * head_count * hid_count
    query_rows = row_count * head_count
    key_count = seq_length // hid_count
    inner_width = w_query.shape[1]
    local_heads = inner_width // DH
    bucket_count = rel_bias.shape[0]
    total_heads = rel_bias.shape[1]
    x_full = inputs.astype(jnp.float32)
    normed_one = rms_scale(x_full, gain_attn).astype(jnp.bfloat16)
    gathered_one = lax.all_gather(normed_one, ("head", "hid"), axis=1, tiled=True)
    blocks_all = gathered_one.reshape(seq_count, head_count, hid_count, row_count, model_width)
    query_in = lax.dynamic_index_in_dim(blocks_all, hid_index, 2, keepdims=False).reshape(
        seq_count, query_rows, model_width
    )
    key_start = hid_index * key_count
    key_in = lax.dynamic_slice_in_dim(gathered_one, key_start, key_count, 1)
    queries = jnp.dot(query_in, w_query, preferred_element_type=jnp.float32).astype(jnp.bfloat16)
    key_rows = jnp.dot(gathered_one, w_key, preferred_element_type=jnp.float32).astype(jnp.bfloat16)
    value_rows = jnp.dot(gathered_one, w_value, preferred_element_type=jnp.float32).astype(
        jnp.bfloat16
    )
    query_four = queries.reshape(seq_count, query_rows, local_heads, DH)
    key_four = key_rows.reshape(seq_count, seq_length, local_heads, DH)
    value_four = value_rows.reshape(seq_count, seq_length, local_heads, DH)
    key_pos = jnp.arange(seq_length, dtype=jnp.int32)
    block_of = jnp.arange(head_count, dtype=jnp.int32)[:, None] * hid_count + hid_index
    query_pos = (block_of * row_count + jnp.arange(row_count, dtype=jnp.int32)[None, :]).reshape(
        query_rows
    )
    bucket_of = buckets[key_pos[None, :] - query_pos[:, None] + seq_length - 1]
    bucket_table = (
        bucket_of[:, :, None] == jnp.arange(bucket_count, dtype=jnp.int32)[None, None, :]
    ).astype(jnp.float32)
    local_bias = lax.dynamic_slice_in_dim(rel_bias, head_index * local_heads, local_heads, 1)
    bias_rows = jnp.einsum("qkb,bh->hqk", bucket_table, local_bias, precision=highest)
    key_valid = key_pos[None, :] < lengths[:, None]
    mask_term = delete_mask[:, None, None, :]

    def scores_of():
        product = jnp.einsum(
            "sqhd,skhd->shqk", query_four, key_four, preferred_element_type=jnp.float32
        )
        summed = product + bias_rows[None] + mask_term
        return jnp.where(key_valid[:, None, None, :], summed, neg_fill)

    scores = scores_of()
    row_max = jnp.max(scores, axis=-1, keepdims=True)
    shifted = jnp.exp(scores - row_max)
    row_total = jnp.sum(shifted, axis=-1, keepdims=True)
    weights_soft = shifted / row_total
    log_total = row_max + jnp.log(row_total)
    mixed_heads = (
        jnp.einsum(
            "shqk,skhd->sqhd",
            weights_soft.astype(jnp.bfloat16),
            value_four,
            preferred_element_type=jnp.float32,
        )
        .astype(jnp.bfloat16)
        .reshape(seq_count, query_rows, inner_width)
    )
    head_part = jnp.dot(mixed_heads, w_out, preferred_element_type=jnp.float32).reshape(
        seq_count, head_count, row_count, model_width
    )
    attended = lax.psum_scatter(head_part, "head", scatter_dimension=1, tiled=True).reshape(
        seq_count, row_count, model_width
    )
    residual = x_full + attended
    normed_two = rms_scale(residual, gain_ffn).astype(jnp.bfloat16)
    gathered_two = lax.all_gather(normed_two, ("head", "hid"), axis=1, tiled=True)
    gate_proj = jnp.dot(gathered_two, gate_weight, preferred_element_type=jnp.float32)
    up_proj = jnp.dot(gathered_two, up_weight, preferred_element_type=jnp.float32)
    hidden_activation = gated_unit(gate_proj, up_proj).astype(jnp.bfloat16)
    ffn_part = jnp.dot(hidden_activation, down_weight, preferred_element_type=jnp.float32)
    ffn_out = lax.psum_scatter(
        ffn_part.astype(jnp.bfloat16), ("head", "hid"), scatter_dimension=1, tiled=True
    ).astype(jnp.float32)
    output = (residual + ffn_out).astype(jnp.bfloat16)
    row_gradient = lax.all_gather(cotangent, ("head", "hid"), axis=1, tiled=True)
    activation_gradient = jnp.einsum(
        "qky,ry->qkr", row_gradient, down_weight, preferred_element_type=jnp.float32
    )
    grad_w_down = jnp.einsum(
        "gzj,gzi->ji", hidden_activation, row_gradient, preferred_element_type=jnp.float32
    )
    unused_value, gated_pullback = jax.vjp(gated_unit, gate_proj, up_proj)
    gate_gradient, up_gradient = gated_pullback(activation_gradient)
    gate_gradient = gate_gradient.astype(jnp.bfloat16)
    up_gradient = up_gradient.astype(jnp.bfloat16)
    feedforward_rows = lax.all_gather(normed_two, ("head", "hid"), axis=1, tiled=True)
    gate_weight_gradient = jnp.einsum(
        "wkr,wki->ri", feedforward_rows, gate_gradient, preferred_element_type=jnp.float32
    )
    up_weight_gradient = jnp.einsum(
        "wkr,wki->ri", feedforward_rows, up_gradient, preferred_element_type=jnp.float32
    )
    second_backward = jnp.einsum(
        "bjk,zk->bjz", gate_gradient, gate_weight, preferred_element_type=jnp.float32
    )
    second_backward = second_backward + jnp.einsum(
        "bjk,zk->bjz", up_gradient, up_weight, preferred_element_type=jnp.float32
    )
    ffn_grads = (
        lax.psum(gate_weight_gradient.astype(jnp.bfloat16), "dp").astype(jnp.float32),
        lax.psum(up_weight_gradient.astype(jnp.bfloat16), "dp").astype(jnp.float32),
        lax.psum(grad_w_down.astype(jnp.bfloat16), "dp").astype(jnp.float32),
    )
    grad_normed_two = lax.psum_scatter(
        second_backward, ("head", "hid"), scatter_dimension=1, tiled=True
    )
    unused_norm, norm_two_pullback = jax.vjp(rms_scale, residual, gain_ffn)
    grad_resid_norm, grad_gain_ffn = norm_two_pullback(grad_normed_two)
    grad_residual = cotangent.astype(jnp.float32) + grad_resid_norm
    grad_branch = grad_residual.astype(jnp.bfloat16)[:, None]
    grad_heads = lax.all_gather(grad_branch, "head", axis=1, tiled=True).reshape(
        seq_count, query_rows, model_width
    )
    grad_w_out = jnp.einsum(
        "sqi,sqd->id", mixed_heads, grad_heads, preferred_element_type=jnp.float32
    )
    grad_mixed = jnp.einsum(
        "sqd,id->sqi", grad_heads, w_out, preferred_element_type=jnp.float32
    ).astype(jnp.bfloat16)
    grad_mixed_four = grad_mixed.reshape(seq_count, query_rows, local_heads, DH)
    attn_probs = jnp.exp(scores_of() - log_total)
    grad_probs = jnp.einsum(
        "sqhd,skhd->shqk", grad_mixed_four, value_four, preferred_element_type=jnp.float32
    )
    inner_sum = jnp.sum(attn_probs * grad_probs, axis=-1, keepdims=True)
    grad_scores = attn_probs * (grad_probs - inner_sum)
    grad_mask_part = jnp.sum(grad_scores, axis=(1, 2))
    grad_bias = jnp.sum(grad_scores, axis=0)
    grad_rel_local = jnp.einsum("qkb,hqk->bh", bucket_table, grad_bias, precision=highest)
    grad_rel = lax.dynamic_update_slice_in_dim(
        jnp.zeros((bucket_count, total_heads), jnp.float32),
        grad_rel_local,
        head_index * local_heads,
        1,
    )
    grad_low = grad_scores.astype(jnp.bfloat16)
    grad_query = (
        jnp.einsum("shqk,skhd->sqhd", grad_low, key_four, preferred_element_type=jnp.float32)
        .astype(jnp.bfloat16)
        .reshape(seq_count, query_rows, inner_width)
    )
    grad_key_part = jnp.einsum(
        "shqk,sqhd->skhd", grad_low, query_four, preferred_element_type=jnp.float32
    ).reshape(seq_count, seq_length, inner_width)
    grad_value_part = jnp.einsum(
        "shqk,sqhd->skhd",
        attn_probs.astype(jnp.bfloat16),
        grad_mixed_four,
        preferred_element_type=jnp.float32,
    ).reshape(seq_count, seq_length, inner_width)
    grad_w_query = jnp.einsum(
        "sqd,sqi->di", query_in, grad_query, preferred_element_type=jnp.float32
    )
    query_back = jnp.einsum("sqi,di->sqd", grad_query, w_query, preferred_element_type=jnp.float32)
    grad_key, grad_value = (
        lax.psum_scatter(grad_key_part, "hid", scatter_dimension=1, tiled=True),
        lax.psum_scatter(grad_value_part, "hid", scatter_dimension=1, tiled=True),
    )
    grad_key = grad_key.astype(jnp.bfloat16)
    grad_value = grad_value.astype(jnp.bfloat16)
    grad_w_key = jnp.einsum("skd,ski->di", key_in, grad_key, preferred_element_type=jnp.float32)
    grad_w_value = jnp.einsum("skd,ski->di", key_in, grad_value, preferred_element_type=jnp.float32)
    key_back = jnp.einsum("ski,di->skd", grad_key, w_key, preferred_element_type=jnp.float32)
    key_back = key_back + jnp.einsum(
        "ski,di->skd", grad_value, w_value, preferred_element_type=jnp.float32
    )
    key_spread = lax.dynamic_update_slice_in_dim(
        jnp.zeros((seq_count, seq_length, model_width), jnp.float32), key_back, key_start, 1
    )
    spread_blocks = key_spread.reshape(seq_count, head_count, hid_count, row_count, model_width)
    own_blocks = lax.dynamic_index_in_dim(spread_blocks, hid_index, 2, keepdims=False)
    own_blocks = own_blocks + query_back.reshape(seq_count, head_count, row_count, model_width)
    back_one = lax.dynamic_update_index_in_dim(spread_blocks, own_blocks, hid_index, 2).reshape(
        seq_count, seq_length, model_width
    )
    grad_normed_one, grad_mask = (
        lax.psum_scatter(
            back_one.astype(jnp.bfloat16), ("head", "hid"), scatter_dimension=1, tiled=True
        ).astype(jnp.float32),
        lax.psum_scatter(
            grad_mask_part.astype(jnp.bfloat16), ("head", "hid"), scatter_dimension=1, tiled=True
        ).astype(jnp.float32),
    )
    unused_first, norm_one_pullback = jax.vjp(rms_scale, x_full, gain_attn)
    grad_x_norm, grad_gain_attn = norm_one_pullback(grad_normed_one)
    grad_inputs = grad_residual + grad_x_norm
    attn_grads = lax.psum(
        (
            grad_w_query,
            grad_w_key,
            grad_w_value,
            grad_w_out,
            grad_gain_attn,
            grad_gain_ffn,
            grad_rel,
        ),
        ("dp", "hid"),
    )
    gain_attn_sum, gain_ffn_sum, rel_sum = lax.psum(
        (attn_grads[4], attn_grads[5], attn_grads[6]), "head"
    )
    return (
        output,
        grad_inputs,
        grad_mask,
        gain_attn_sum,
        attn_grads[0],
        attn_grads[1],
        attn_grads[2],
        attn_grads[3],
        rel_sum,
        gain_ffn_sum,
        ffn_grads[0],
        ffn_grads[1],
        ffn_grads[2],
    )


def solution(mesh):
    return jax.shard_map(
        per_device,
        mesh=mesh,
        in_specs=(
            P("dp", ("head", "hid"), None),
            P("dp"),
            P("dp", None),
            P(),
            P(),
            P(None, "head"),
            P(None, "head"),
            P(None, "head"),
            P("head", None),
            P(),
            P(),
            P(None, ("head", "hid")),
            P(None, ("head", "hid")),
            P(("head", "hid"), None),
            P("dp", ("head", "hid"), None),
        ),
        out_specs=(
            P("dp", ("head", "hid"), None),
            P("dp", ("head", "hid"), None),
            P("dp", ("head", "hid")),
            P(),
            P(None, "head"),
            P(None, "head"),
            P(None, "head"),
            P("head", None),
            P(),
            P(),
            P(None, ("head", "hid")),
            P(None, ("head", "hid")),
            P(("head", "hid"), None),
        ),
        check_vma=False,
    )
```

profile of v0, /device:TPU:0, one launch (start us, length us, event | category | flops | bytes accessed | tf_op | source)
XLA Modules:
  0.0 3512.7 jit_solution(8366894833644946990)
XLA Ops:
  12.8 2561.6 %gather_fusion = s32[262144]{0:T(1024)} fusion(s32[2047]{0:T(1024)S(1)} %copy-done.1, s32[262144]{0:T(1024)S(1)} %broadcast_clamp_fusion), kind=kCustom, calls=%fused_computation | custom fusion | bytes 3145728 | tf_op jit(solution)/shard_map/gather | solution.py:74
  2578.4 7.9 iota_compare_fusion
  2586.3 46.0 %copy.61 = pred[256,1024,32]{1,2,0:T(32,128)(4,1)} copy(pred[256,1024,32]{0,2,1:T(32,128)(4,1)} %iota_compare_fusion) | data formatting | bytes 16777216 | tf_op jit(solution)/shard_map/eq | solution.py:76
  2632.4 10.6 fusion.62
  2643.0 3.6 copy.62
  2646.7 11.8 reshape.211
  2658.5 7.1 constant_dynamic-slice_fusion.1
  2665.7 8.3 copy.85
  2676.2 4.3 convolution_convert_fusion.1
  2684.8 13.9 fusion.44
  2701.3 44.7 %reduce-scatter.14.cloned.1.call-done = f32[2,1,128,1472]{2,3,0,1:T(8,128)} async-done(((f32[2,2,128,1472]{2,3,0,1:T(8,128)}), f32[2,1,128,1472]{2,3,0,1:T(8,128)}) %reduce-scatter.14.cloned.1.call-update) | async-done | bytes 1507344 | tf_op jit(solution)/shard_map/reduce_scatter | solution.py:109
  2749.6 45.0 %all-gather.8.cloned.1.call-done = bf16[2,1024,1472]{1,2,0:T(8,128)(2,1)} async-done(((bf16[2,128,1472]{1,2,0:T(8,128)(2,1)}), bf16[2,1024,1472]{1,2,0:T(8,128)(2,1)}) %all-gather.8.cloned.1.call-update) | async-done | bytes 6029328 | tf_op jit(solution)/shard_map/all_gather | solution.py:114
  2794.6 8.2 fusion.37
  2802.8 4.8 fusion.33
  2807.6 34.4 all-gather.10.cloned.1.call-done
  2842.1 10.4 multiply_convert_fusion
  2855.9 6.3 convolution_add_fusion
  2862.3 89.7 %reduce-scatter.16.cloned.1.call-done = f32[2,128,1472]{1,2,0:T(8,128)} async-done(((f32[2,1024,1472]{1,2,0:T(8,128)}), f32[2,128,1472]{1,2,0:T(8,128)}) %reduce-scatter.16.cloned.1.call-update) | async-done | bytes 1507344 | tf_op jit(solution)/shard_map/reduce_scatter | solution.py:152
  2955.6 26.5 all-gather.12.cloned.1.call-done
  2984.0 4.2 multiply_reduce_fusion
  2989.0 3.9 fusion.71
  2997.0 5.1 fusion.10
  3002.2 8.0 fusion.15
  3010.2 7.8 fusion.14
  3018.0 4.2 fusion.16
  3022.2 6.8 convolution_convert_fusion
  3029.0 16.6 copy.78
  3045.6 15.0 reshape.252
  3068.7 4.4 convolution_add_fusion.2
  3073.1 3.5 copy.65
  3078.9 4.4 copy-done.3
  3085.3 3.6 copy.66
  3088.9 4.3 fusion.9
  3093.2 3.7 copy.68
  3096.9 3.8 constant_dynamic-update-slice_fusion
  3100.6 8.2 convert_element_type.130
  3108.8 12.7 copy.92
  3121.5 15.0 reshape.254
  3147.9 65.2 %all-reduce.9.cloned.1.call-done = (bf16[1472,448]{0,1:T(8,128)(2,1)}, bf16[1472,448]{0,1:T(8,128)(2,1)}, bf16[448,1472]{1,0:T(8,128)(2,1)}) async-done(((bf16[1472,448]{0,1:T(8,128)(2,1)}, bf16[1472,448]{0,1:T(8,128)(2,1)}, bf16[448,1472]{1,0:T(8,128)(2,1)}), (bf16[1472,448]{0,1:T(8,128)(2,1)}, bf16[1472,448]{0,1:T(8,128)(2,1)}, bf16[448,1472]{1,0:T(8,128)(2,1)})) %all-reduce.9.cloned.1.call-update) | async-done | bytes 3956752 | tf_op jit(solution)/shard_map/psum | solution.py:148
  3220.2 55.6 %reduce-scatter.22.cloned.1.call-done = bf16[128,2944]{1,0:T(8,128)(2,1)} async-done(((bf16[1024,2944]{1,0:T(8,128)(2,1)}), bf16[128,2944]{1,0:T(8,128)(2,1)}) %reduce-scatter.22.cloned.1.call-update) | async-done | bytes 753680
  3282.4 5.0 copy.71
  3287.3 17.5 convolution_bitcast_fusion.7
  3305.0 8.3 reduce-scatter.26.cloned.1.call-done
  3314.7 62.3 %reduce-scatter.24.cloned.1.call-done = bf16[128,2944]{1,0:T(8,128)(2,1)} async-done(((bf16[1024,2944]{1,0:T(8,128)(2,1)}), bf16[128,2944]{1,0:T(8,128)(2,1)}) %reduce-scatter.24.cloned.1.call-update) | async-done | bytes 753680
  3385.7 62.8 %all-reduce = (f32[1472]{0:T(1024)S(1)}, f32[32,6]{0,1:T(8,128)S(1)}, f32[1472]{0:T(1024)S(1)}) all-reduce(f32[1472]{0:T(1024)S(1)} %get-tuple-element.17, f32[32,6]{0,1:T(8,128)S(1)} %dynamic_update_slice.12, f32[1472]{0:T(1024)S(1)} %get-tuple-element.15), channel_id=1, replica_groups=mesh['dp'=4,'head'=2,'hid'=4] {'dp','hid'}, use_global_device_ids=true, to_apply=%region_16.17 | all-reduce | flops 3136 | bytes 25088 | tf_op jit(solution)/shard_map/psum | solution.py:235
  3448.5 8.0 all-reduce.2
  3456.5 3.9 fusion.26
  3460.4 40.0 %all-reduce.7.cloned.1.call-done = (f32[1472,192]{0,1:T(8,128)}, f32[1472,192]{0,1:T(8,128)}, f32[1472,192]{0,1:T(8,128)}, f32[192,1472]{1,0:T(8,128)}) async-done(((f32[1472,192]{0,1:T(8,128)}, f32[1472,192]{0,1:T(8,128)}, f32[1472,192]{0,1:T(8,128)}, f32[192,1472]{1,0:T(8,128)}), (f32[1472,192]{0,1:T(8,128)}, f32[1472,192]{0,1:T(8,128)}, f32[1472,192]{0,1:T(8,128)}, ...) | async-done | bytes 4522000 | tf_op jit(solution)/shard_map/psum | solution.py:235
  (190 shorter events, 88.9 us)
Async XLA Ops:
  7.2 2834.9 %copy-start = (bf16[448,1472]{1,0:T(8,128)(2,1)S(1)}, bf16[448,1472]{1,0:T(8,128)(2,1)}, u32[]{:S(2)}) copy-start(bf16[448,1472]{1,0:T(8,128)(2,1)} %param.28) | copy-start | bytes 3956740
  7.2 2639.5 %all-gather.6.cloned.1.call-start = ((), (), s32[]{:S(2)}) async-start(), calls=%async_computation.7 | async-start | bytes 6782976 | tf_op jit(solution)/shard_map/all_gather | solution.py:54
  12.1 2733.9 %reduce-scatter.14.cloned.1.call-start = ((), (), s32[]{:S(2)}) async-start(), calls=%async_computation.8 | async-start | bytes 4521984 | tf_op jit(solution)/shard_map/reduce_scatter | solution.py:109
  2578.4 8.0 copy-start.13
  2586.3 46.0 %copy-start.41 = (f32[32,6]{0,1:T(8,128)S(1)}, f32[32,6]{0,1:T(8,128)}, u32[]{:S(2)}) copy-start(f32[32,6]{0,1:T(8,128)} %param.24) | copy-start | bytes 2308
  2643.0 3.6 copy-start.42
  2665.7 8.4 copy-start.33
  2665.7 10.4 copy-start.31
  2676.1 4.3 copy-start.28
  2676.1 4.3 copy-start.5
  2676.1 4.3 copy-start.36
  2676.1 7.1 slice-start.2
  2684.8 14.0 copy-start.27
  2684.8 14.0 copy-start.15
  2701.2 46.6 %copy-start.34 = (f32[1472]{0:T(1024)S(1)}, f32[1472]{0:T(1024)}, u32[]{:S(2)}) copy-start(f32[1472]{0:T(1024)} %param.25) | copy-start | bytes 17668
  2701.2 93.4 %all-gather.8.cloned.1.call-start = ((), (), s32[]{:S(2)}) async-start(), calls=%async_computation.9 | async-start | bytes 6782976 | tf_op jit(solution)/shard_map/all_gather | solution.py:114
  2749.0 93.1 %all-gather.10.cloned.1.call-start = ((), (), s32[]{:S(2)}) async-start(), calls=%async_computation.10 | async-start | bytes 6782976 | tf_op jit(solution)/shard_map/all_gather | solution.py:123
  2749.5 202.4 %reduce-scatter.16.cloned.1.call-start = ((), (), s32[]{:S(2)}) async-start(), calls=%async_computation.11 | async-start | bytes 13565952 | tf_op jit(solution)/shard_map/reduce_scatter | solution.py:152
  2794.6 8.2 copy-start.4
  2794.6 8.2 copy-start.10
  2842.1 10.4 copy-start.16
  2852.4 3.4 copy-start.43
  2852.4 3.5 copy-start.17
  2852.4 3.5 copy-start.11
  2862.2 119.8 %all-gather.12.cloned.1.call-start = ((), (), s32[]{:S(2)}) async-start(), calls=%async_computation.14 | async-start | bytes 2260992 | tf_op jit(solution)/shard_map/all_gather | solution.py:159
  2955.5 109.7 %reduce-scatter.18.cloned.1.call-start = ((), (), s32[]{:S(2)}) async-start(), calls=%async_computation.12 | async-start | bytes 1966080 | tf_op jit(solution)/shard_map/reduce_scatter | solution.py:204
  2983.9 4.2 copy-start.18
  2984.0 4.3 slice-start
  2984.0 5.0 slice-start.1
  2989.0 5.6 copy-start.29
  2996.5 72.2 %reduce-scatter.20.cloned.1.call-start = ((), (), s32[]{:S(2)}) async-start(), calls=%async_computation.13 | async-start | bytes 1966080 | tf_op jit(solution)/shard_map/reduce_scatter | solution.py:205
  3002.1 211.0 %all-reduce.9.cloned.1.call-start = ((), (), s32[]{:S(2)}) async-start(), calls=%async_computation.19 | async-start | bytes 8257536 | tf_op jit(solution)/shard_map/psum | solution.py:148
  3002.1 8.0 copy-start.44
  3002.1 15.8 slice-start.4
  3010.2 7.8 slice-start.5
  3010.2 7.8 copy-start.45
  3022.2 253.7 %reduce-scatter.22.cloned.1.call-start = ((), (), s32[]{:S(2)}) async-start(), calls=%async_computation.15 | async-start | bytes 6782976
  3060.7 252.6 %reduce-scatter.26.cloned.1.call-start = ((), (), s32[]{:S(2)}) async-start(), calls=%async_computation.17 | async-start | bytes 294912
  3064.9 312.1 %reduce-scatter.24.cloned.1.call-start = ((), (), s32[]{:S(2)}) async-start(), calls=%async_computation.16 | async-start | bytes 6782976
  3078.9 4.5 copy-start.3
  3136.6 5.0 copy-start.21
  3136.6 363.8 %all-reduce.7.cloned.1.call-start = ((), (), s32[]{:S(2)}) async-start(), calls=%async_computation.18 | async-start | bytes 9437184 | tf_op jit(solution)/shard_map/psum | solution.py:235
  3140.1 4.7 copy-start.20
  3304.9 78.7 %copy-start.35 = (f32[1472]{0:T(1024)S(1)}, f32[1472]{0:T(1024)}, u32[]{:S(2)}) copy-start(f32[1472]{0:T(1024)} %param.19) | copy-start | bytes 17668
  3304.9 78.7 %copy-start.38 = (f32[2,128]{1,0:T(2,128)S(1)}, f32[2,128]{1,0:T(2,128)}, u32[]{:S(2)}) copy-start(f32[2,128]{1,0:T(2,128)} %copy-done.37) | copy-start | bytes 3076
  3304.9 151.6 %copy-start.40 = (f32[2,128]{1,0:T(2,128)S(1)}, f32[2,128]{1,0:T(2,128)}, u32[]{:S(2)}) copy-start(f32[2,128]{1,0:T(2,128)} %copy-done.39) | copy-start | bytes 3076
  3500.4 3.5 copy-start.25
  3500.4 4.5 copy-start.24
  (17 other events, 34.3 us)
Sparse Core Ops, SparseCore 0:
  12.2 48.2 all-gather.5
  2701.3 44.5 reduce-scatter.13
  2749.1 45.4 all-gather.7
  2796.5 45.4 all-gather.9
  2862.3 89.5 reduce-scatter.15
  2955.6 26.4 all-gather.11
  2996.6 28.1 reduce-scatter.17
  3027.4 28.1 reduce-scatter.19
  3059.5 153.5 all-reduce.8
  3216.5 59.3 reduce-scatter.21
  3279.7 33.5 reduce-scatter.25
  3316.7 60.2 reduce-scatter.23
  3382.1 118.2 all-reduce.6
where the time goes:
time: 3520 us; the launch traced here: 3510 us
  local copies, waits for them, and re-layouts  2750 us (78%)
  waiting for transfers between devices  473 us (13%)
  matrix products  153 us (4%)
  blocking collectives  70.8 us (2%)
  other arithmetic  45.8 us (1%)
    gather x3, local copies, waits for them, and re-layouts, per_device(): bucket_of = buckets[key_pos[None, :] - query_pos[:, None] + seq_length - 1]  2570 us
    unnamed x16, waiting for transfers between devices  127 us
    unnamed x120, local copies, waits for them, and re-layouts  96.8 us
    reduce_scatter x1, waiting for transfers between devices, per_device(): lax.psum_scatter(second_backward, ('head', 'hid'), scatter_dimension=1, t...  89.7 us
  transfers between devices with their start and end apart: 13, of which 10 were waited for; matrix products, arithmetic and copies ran while one was open for 81% of the time, Pallas kernels for 0%

commit v1 on v0

v1 whole, which is shorter than its diff:
```python
import functools

import jax
import jax.numpy as jnp
from jax import lax
from jax.experimental import pallas as pl
from jax.experimental.pallas import tpu as pltpu
from jax.sharding import PartitionSpec as P

DH = 64
EPS = 1e-06
NEG = -1e30
BF = jnp.bfloat16
F32 = jnp.float32
GELU_C = 0.7978845608028654
GELU_K = 0.044715

NT = (((1,), (1,)), ((), ()))
TN = (((0,), (0,)), ((), ()))


def dot(a, b):
    return jnp.dot(a, b, preferred_element_type=F32)


def dot_nt(a, b):
    return lax.dot_general(a, b, NT, preferred_element_type=F32)


def dot_tn(a, b):
    return lax.dot_general(a, b, TN, preferred_element_type=F32)


def bias_kernel(start_ref, table_ref, mask_ref, out_ref, *, heads, block, q_blocks):
    kb = pl.program_id(0)
    qb = pl.program_id(1)
    start = pl.multiple_of(start_ref[kb * q_blocks + qb], block)
    k_at = pl.multiple_of(kb * block, block)
    mask = mask_ref[:, pl.ds(k_at, block)]
    mask = jnp.broadcast_to(mask, (block, block)).T
    for h in range(heads):
        window = table_ref[h : h + 1, pl.ds(start, 2 * block)]
        window = jnp.broadcast_to(window, (block, 2 * block))
        rolled = pltpu.roll(window, block, 1, stride=1, stride_axis=0)
        out_ref[h] = rolled[:, :block] + mask


def make_bias(starts, table, mask_row, heads, block, k_blocks, q_blocks):
    length = k_blocks * block
    return pl.pallas_call(
        functools.partial(bias_kernel, heads=heads, block=block, q_blocks=q_blocks),
        out_shape=jax.ShapeDtypeStruct((heads, length, q_blocks * block), F32),
        grid_spec=pltpu.PrefetchScalarGridSpec(
            num_scalar_prefetch=1,
            grid=(k_blocks, q_blocks),
            in_specs=[
                pl.BlockSpec(table.shape, lambda k, q, s: (0, 0)),
                pl.BlockSpec((1, length), lambda k, q, s: (0, 0)),
            ],
            out_specs=pl.BlockSpec((heads, block, block), lambda k, q, s: (0, k, q)),
        ),
        name="bias",
    )(starts, table, mask_row)


def head_mask(h, rows, width):
    lane = lax.broadcasted_iota(jnp.int32, (rows, width), 1)
    return (lane >= h * DH) & (lane < (h + 1) * DH)


def attn_fwd_kernel(q_ref, kv0_ref, kv1_ref, bias_ref, p_ref, o_ref, *, heads):
    inner = heads * DH
    q = q_ref[...]
    rows = q.shape[0]
    outs = []
    for h in range(heads):
        qm = jnp.where(head_mask(h, rows, inner), q, jnp.zeros_like(q))
        s0 = dot_nt(kv0_ref[:, :inner], qm)
        s1 = dot_nt(kv1_ref[:, :inner], qm)
        s = jnp.concatenate([s0, s1], axis=0) + bias_ref[h]
        top = jnp.max(s, axis=0, keepdims=True)
        e = jnp.exp(s - top)
        total = jnp.sum(e, axis=0, keepdims=True)
        p = e * (1.0 / total)
        p_ref[h] = p
        pb = p.astype(BF)
        half = s0.shape[0]
        o_t = dot_tn(kv0_ref[:, inner:], pb[:half]) + dot_tn(kv1_ref[:, inner:], pb[half:])
        outs.append(o_t[h * DH : (h + 1) * DH])
    o_ref[...] = jnp.concatenate(outs, axis=0).T.astype(BF)


def attn_fwd(q, kv0, kv1, bias, heads, block):
    rows, inner = q.shape
    length = bias.shape[1]
    full = lambda i: (0, 0)
    return pl.pallas_call(
        functools.partial(attn_fwd_kernel, heads=heads),
        out_shape=(
            jax.ShapeDtypeStruct((heads, length, rows), F32),
            jax.ShapeDtypeStruct((rows, inner), BF),
        ),
        grid=(rows // block,),
        in_specs=[
            pl.BlockSpec((block, inner), lambda i: (i, 0)),
            pl.BlockSpec(kv0.shape, full),
            pl.BlockSpec(kv1.shape, full),
            pl.BlockSpec((heads, length, block), lambda i: (0, 0, i)),
        ],
        out_specs=(
            pl.BlockSpec((heads, length, block), lambda i: (0, 0, i)),
            pl.BlockSpec((block, inner), lambda i: (i, 0)),
        ),
        compiler_params=pltpu.CompilerParams(vmem_limit_bytes=48 << 20),
        name="attn_fwd",
    )(q, kv0, kv1, bias)


def diagonals(piece, block):
    lanes = 128
    total = None
    for shift in range(0, lanes, 8):
        wide = None
        for part in range(block // lanes):
            rows = piece[part * lanes + shift : part * lanes + shift + 8]
            pieces = [jnp.zeros((8, block - part * lanes), F32), rows]
            if part:
                pieces.append(jnp.zeros((8, part * lanes), F32))
            rows = jnp.concatenate(pieces, axis=1)
            wide = rows if wide is None else wide + rows
        if shift:
            wide = pltpu.roll(wide, 2 * block - shift, 1)
        total = wide if total is None else total + wide
    return total


def attn_bwd_kernel(
    start_ref,
    p_ref,
    q_ref,
    do_ref,
    kv0_ref,
    kv1_ref,
    dq_ref,
    dkv0_ref,
    dkv1_ref,
    col_ref,
    table_ref,
    acc0,
    acc1,
    *,
    heads,
    block,
    q_blocks,
):
    qb = pl.program_id(0)
    inner = heads * DH
    rows = q_ref.shape[0]
    half = kv0_ref.shape[0]

    @pl.when(qb == 0)
    def _():
        acc0[...] = jnp.zeros_like(acc0)
        acc1[...] = jnp.zeros_like(acc1)
        col_ref[...] = jnp.zeros_like(col_ref)
        table_ref[...] = jnp.zeros_like(table_ref)

    q = q_ref[...]
    do = do_ref[...]
    zero = jnp.zeros_like(q)
    outs = []
    col = None
    for h in range(heads):
        pick = head_mask(h, rows, inner)
        qm = jnp.where(pick, q, zero)
        dom = jnp.where(pick, do, zero)
        dp = jnp.concatenate(
            [dot_nt(kv0_ref[:, inner:], dom), dot_nt(kv1_ref[:, inner:], dom)], axis=0
        )
        p = p_ref[h]
        inside = jnp.sum(p * dp, axis=0, keepdims=True)
        ds = p * (dp - inside)
        col = ds if col is None else col + ds
        for kb in range(2 * half // block):
            start = pl.multiple_of(start_ref[kb * q_blocks + qb], block)
            piece = ds[kb * block : (kb + 1) * block]
            table_ref[h, :, pl.ds(start, 2 * block)] += diagonals(piece, block)
        dsb = ds.astype(BF)
        pb = p.astype(BF)
        acc0[:, :inner] += dot(dsb[:half], qm)
        acc1[:, :inner] += dot(dsb[half:], qm)
        acc0[:, inner:] += dot(pb[:half], dom)
        acc1[:, inner:] += dot(pb[half:], dom)
        dq_t = dot_tn(kv0_ref[:, :inner], dsb[:half]) + dot_tn(kv1_ref[:, :inner], dsb[half:])
        outs.append(dq_t[h * DH : (h + 1) * DH])
    dq_ref[...] = jnp.concatenate(outs, axis=0).T.astype(BF)
    col_ref[...] += jnp.sum(col.T, axis=0, keepdims=True)

    @pl.when(qb == q_blocks - 1)
    def _():
        dkv0_ref[...] = acc0[...]
        dkv1_ref[...] = acc1[...].astype(BF)


def attn_bwd(starts, p, q, do, kv0, kv1, heads, block):
    rows, inner = q.shape
    length = p.shape[1]
    q_blocks = rows // block
    full = lambda i, s: (0, 0)
    row = lambda i, s: (i, 0)
    return pl.pallas_call(
        functools.partial(attn_bwd_kernel, heads=heads, block=block, q_blocks=q_blocks),
        out_shape=(
            jax.ShapeDtypeStruct((rows, inner), BF),
            jax.ShapeDtypeStruct(kv0.shape, F32),
            jax.ShapeDtypeStruct(kv1.shape, BF),
            jax.ShapeDtypeStruct((1, length), F32),
            jax.ShapeDtypeStruct((heads, 8, 2 * length), F32),
        ),
        grid_spec=pltpu.PrefetchScalarGridSpec(
            num_scalar_prefetch=1,
            grid=(q_blocks,),
            in_specs=[
                pl.BlockSpec((heads, length, block), lambda i, s: (0, 0, i)),
                pl.BlockSpec((block, inner), row),
                pl.BlockSpec((block, inner), row),
                pl.BlockSpec(kv0.shape, full),
                pl.BlockSpec(kv1.shape, full),
            ],
            out_specs=(
                pl.BlockSpec((block, inner), row),
                pl.BlockSpec(kv0.shape, full),
                pl.BlockSpec(kv1.shape, full),
                pl.BlockSpec((1, length), full),
                pl.BlockSpec((heads, 8, 2 * length), lambda i, s: (0, 0, 0)),
            ),
            scratch_shapes=[pltpu.VMEM(kv0.shape, F32), pltpu.VMEM(kv1.shape, F32)],
        ),
        compiler_params=pltpu.CompilerParams(vmem_limit_bytes=48 << 20),
        name="attn_bwd",
    )(starts, p, q, do, kv0, kv1)


def ffn_kernel(n_ref, dy_ref, g0, g1, u0, u1, d0, d1, a_ref, dg_ref, du_ref, dn_ref):
    n = n_ref[...]
    dy = dy_ref[...]
    total = None
    for part, (g_w, u_w, d_w) in enumerate(((g0, u0, d0), (g1, u1, d1))):
        gate = dot(n, g_w[...])
        up = dot(n, u_w[...])
        d_act = dot_nt(dy, d_w[...])
        square = gate * gate
        t = jnp.tanh(GELU_C * gate * (1.0 + GELU_K * square))
        half = 0.5 * (1.0 + t)
        gelu = gate * half
        slope = half + 0.5 * gate * (1.0 - t * t) * (GELU_C * (1.0 + 3.0 * GELU_K * square))
        a_ref[part] = (gelu * up).astype(BF)
        d_gate = (d_act * up * slope).astype(BF)
        d_up = (d_act * gelu).astype(BF)
        dg_ref[part] = d_gate
        du_ref[part] = d_up
        more = dot_nt(d_gate, g_w[...]) + dot_nt(d_up, u_w[...])
        total = more if total is None else total + more
    dn_ref[...] = total.astype(dn_ref.dtype)


def ffn_chunk(n, dy, weights, tile, out_dtype):
    rows, width = n.shape
    hidden = weights[0].shape[1]
    row = lambda i: (i, 0)
    full = lambda i: (0, 0)
    mid = pl.BlockSpec((2, tile, hidden), lambda i: (0, i, 0))
    mid_shape = jax.ShapeDtypeStruct((2, rows, hidden), BF)
    return pl.pallas_call(
        ffn_kernel,
        out_shape=(mid_shape, mid_shape, mid_shape, jax.ShapeDtypeStruct((rows, width), out_dtype)),
        grid=(rows // tile,),
        in_specs=[pl.BlockSpec((tile, width), row)] * 2
        + [pl.BlockSpec(w.shape, full, pipeline_mode=pl.Buffered(1)) for w in weights],
        out_specs=(mid, mid, mid, pl.BlockSpec((tile, width), row)),
        compiler_params=pltpu.CompilerParams(vmem_limit_bytes=56 << 20),
        name="ffn",
    )(n, dy, *weights)


def rms_parts(rows):
    return lax.rsqrt(jnp.mean(rows * rows, axis=-1, keepdims=True) + EPS)


def rms_back(rows, inverse, gain, grad):
    scaled = grad * gain
    inside = jnp.mean(rows * scaled, axis=-1, keepdims=True)
    return inverse * scaled - rows * (inverse * inverse * inverse * inside)


def per_device(
    inputs,
    lengths,
    delete_mask,
    buckets,
    gain_attn,
    w_query,
    w_key,
    w_value,
    w_out,
    rel_bias,
    gain_ffn,
    gate_weight,
    up_weight,
    down_weight,
    cotangent,
):
    seqs, row_count, width = inputs.shape
    heads_axis = lax.axis_size("head")
    hid_axis = lax.axis_size("hid")
    assert seqs == 2 and heads_axis == 2 and hid_axis == 4
    h_at = lax.axis_index("head")
    hid_at = lax.axis_index("hid")
    c_at = hid_at % 2
    x_at = hid_at // 2
    length = row_count * heads_axis * hid_axis
    block = 2 * row_count
    inner = w_query.shape[1]
    heads = inner // DH
    bucket_count, total_heads = rel_bias.shape

    def core_swap(v):
        return lax.ppermute(v, "hid", [(i, i ^ 1) for i in range(hid_axis)])

    def x_swap(v):
        return lax.ppermute(v, "hid", [(i, i ^ 2) for i in range(hid_axis)])

    def y_swap(v):
        return lax.ppermute(v, "head", [(0, 1), (1, 0)])

    def grid_swap(v, first):
        pairs = []
        for h in range(heads_axis):
            for i in range(hid_axis):
                along_x = (i % 2 == 0) == first
                to = (h * hid_axis + (i ^ 2)) if along_x else ((1 - h) * hid_axis + i)
                pairs.append((h * hid_axis + i, to))
        return lax.ppermute(v, ("head", "hid"), pairs)

    def pair_rows(own, other):
        return jnp.where(
            c_at == 0,
            jnp.concatenate([own, other], axis=0),
            jnp.concatenate([other, own], axis=0),
        )

    def mine(v):
        return lax.dynamic_index_in_dim(v, c_at, 0, keepdims=False)

    def others(v):
        return lax.dynamic_index_in_dim(v, 1 - c_at, 0, keepdims=False)

    x_rows = pair_rows(mine(inputs), core_swap(others(inputs))).astype(F32)
    inv_one = rms_parts(x_rows)
    normed_one = (x_rows * inv_one * gain_attn).astype(BF)
    normed_far = y_swap(normed_one)

    dy_own = pair_rows(mine(cotangent), core_swap(others(cotangent)))
    dy_a = grid_swap(dy_own, True)
    dy_b = grid_swap(jnp.concatenate([dy_own, dy_a], axis=0), False)

    gate_other = core_swap(gate_weight)
    up_other = core_swap(up_weight)
    down_other = core_swap(down_weight)
    ffn_weights = (gate_weight, gate_other, up_weight, up_other, down_weight, down_other)
    w_out_far = y_swap(w_out)

    base = jnp.stack(
        [
            (h * 2 + x) * block
            for x in (x_at, 1 - x_at)
            for h in (h_at, 1 - h_at)
        ]
    ).astype(jnp.int32)
    starts = (length - block - (base[:, None] - base[None, :2])).reshape(-1).astype(jnp.int32)
    bucket_rev = jnp.concatenate([jnp.full((1,), -1, jnp.int32), buckets[::-1]])
    hot = bucket_rev[None, :] == jnp.arange(bucket_count, dtype=jnp.int32)[:, None]
    local_bias = lax.dynamic_slice_in_dim(rel_bias, h_at * heads, heads, 1)
    table = jnp.sum(jnp.where(hot[None], local_bias.T[:, :, None], 0.0), axis=1)
    table = jnp.concatenate([table, jnp.zeros((8 - heads, 2 * length), F32)], axis=0)
    seq_mask = lax.dynamic_index_in_dim(delete_mask, c_at, 0, keepdims=False)
    seq_len = lax.dynamic_index_in_dim(lengths, c_at, 0, keepdims=False)
    seq_mask = jnp.where(jnp.arange(length, dtype=jnp.int32) < seq_len, seq_mask, NEG)

    def own_order(v):
        v = v.reshape(2, 2, block)
        v = jnp.where(h_at == 0, v, v[::-1])
        v = jnp.where(x_at == 0, v, v[:, ::-1])
        return jnp.swapaxes(v, 0, 1).reshape(1, length)

    bias = make_bias(starts, table, own_order(seq_mask), heads, block, 4, 2)

    w_qkv = jnp.concatenate([w_query, w_key, w_value], axis=1)
    qkv_own = dot(normed_one, w_qkv).astype(BF)
    qkv_far = dot(normed_far, w_qkv).astype(BF)
    qkv = jnp.concatenate([qkv_own, qkv_far], axis=0)
    queries = qkv[:, :inner]
    kv0 = qkv[:, inner:]
    kv1 = x_swap(kv0)

    probs, mixed = attn_fwd(queries, kv0, kv1, bias, heads, block)
    mixed_far = y_swap(mixed[block:])
    mixed_own = mixed[:block]
    attended = dot(mixed_own, w_out) + dot(mixed_far, w_out_far)
    residual = x_rows + attended
    inv_two = rms_parts(residual)
    normed_two = (residual * inv_two * gain_ffn).astype(BF)

    n_a = grid_swap(normed_two, True)
    n_b = grid_swap(jnp.concatenate([normed_two, n_a], axis=0), False)

    act_o, dg_o, du_o, dn_o = ffn_chunk(normed_two, dy_own, ffn_weights, block, F32)
    act_a, dg_a, du_a, dn_a = ffn_chunk(n_a, dy_a, ffn_weights, block, BF)
    act_b, dg_b, du_b, dn_b = ffn_chunk(n_b, dy_b, ffn_weights, block, BF)

    def scatter(own, part_a, part_b):
        got_a = grid_swap(part_a, True)
        got_d = grid_swap(part_b[block:], True)
        relay = (part_b[:block].astype(F32) + got_d.astype(F32)).astype(BF)
        got_b = grid_swap(relay, False)
        return own + got_a.astype(F32) + got_b.astype(F32)

    d_normed_two = scatter(dn_o, dn_a, dn_b)

    n_all = jnp.concatenate([normed_two, n_a, n_b], axis=0)
    dy_all = jnp.concatenate([dy_own, dy_a, dy_b], axis=0)
    act_all = jnp.concatenate([act_o, act_a, act_b], axis=1)
    dg_all = jnp.concatenate([dg_o, dg_a, dg_b], axis=1)
    du_all = jnp.concatenate([du_o, du_a, du_b], axis=1)

    def pair_sum(own, other):
        return (own + core_swap(other.astype(BF)).astype(F32)).astype(BF)

    grad_down = pair_sum(dot_tn(act_all[0], dy_all), dot_tn(act_all[1], dy_all))
    grad_gate = pair_sum(dot_tn(n_all, dg_all[0]), dot_tn(n_all, dg_all[1]))
    grad_up = pair_sum(dot_tn(n_all, du_all[0]), dot_tn(n_all, du_all[1]))
    grad_gate, grad_up, grad_down = [
        v.astype(F32) for v in lax.psum((grad_gate, grad_up, grad_down), "dp")
    ]

    def down(act):
        return dot(act[0], down_weight) + dot(act[1], down_other)

    ffn_out = scatter(down(act_o), down(act_a).astype(BF), down(act_b).astype(BF))
    out_rows = (residual + ffn_out).astype(BF)

    grad_gain_ffn = jnp.sum(d_normed_two * (residual * inv_two), axis=0)
    d_residual = dy_own.astype(F32) + rms_back(residual, inv_two, gain_ffn, d_normed_two)
    d_branch = d_residual.astype(BF)
    d_mixed_own = dot_nt(d_branch, w_out).astype(BF)
    d_mixed_far = y_swap(dot_nt(d_branch, w_out_far).astype(BF))
    d_mixed = jnp.concatenate([d_mixed_own, d_mixed_far], axis=0)
    grad_out_own = dot_tn(d_branch, mixed_own)
    grad_out_far = y_swap(dot_tn(d_branch, mixed_far).astype(BF))
    grad_out = grad_out_own + grad_out_far.astype(F32)

    dq, dkv0, dkv1, col, table_grad = attn_bwd(
        starts, probs, queries, d_mixed, kv0, kv1, heads, block
    )
    d_kv = (dkv0 + x_swap(dkv1).astype(F32)).astype(BF)
    d_qkv = jnp.concatenate([dq, d_kv], axis=1)

    col = col.reshape(2, 2, block)
    col = col[0] + x_swap(col[1])
    col = col[0] + y_swap(col[1])
    col = col.reshape(2, row_count)
    grad_mask_own = mine(col)
    grad_mask_far = core_swap(others(col))

    def by_seq(own, far):
        return jnp.where(c_at == 0, jnp.stack([own, far]), jnp.stack([far, own]))

    grad_mask = by_seq(grad_mask_own, grad_mask_far)

    d_normed_one = dot_nt(d_qkv, w_qkv)
    d_normed_one = d_normed_one[:block] + y_swap(d_normed_one[block:].astype(BF)).astype(F32)
    grad_gain_attn = jnp.sum(d_normed_one * (x_rows * inv_one), axis=0)
    grad_rows = d_residual + rms_back(x_rows, inv_one, gain_attn, d_normed_one)

    def to_owner(rows):
        rows = rows.reshape(2, row_count, width)
        return by_seq(mine(rows), core_swap(others(rows)))

    output = to_owner(out_rows)
    grad_inputs = to_owner(grad_rows)

    normed_both = jnp.concatenate([normed_one, normed_far], axis=0)
    grads = jnp.concatenate([dot_tn(normed_both, d_qkv), grad_out], axis=1)

    def half_sum(v, at, swap):
        v = v.reshape(2, v.shape[0] // 2, v.shape[1])
        keep = lax.dynamic_index_in_dim(v, at, 0, keepdims=False)
        give = lax.dynamic_index_in_dim(v, 1 - at, 0, keepdims=False)
        return keep + swap(give.astype(BF)).astype(F32)

    def half_join(v, at, swap):
        far = swap(v)
        return jnp.where(
            at == 0, jnp.concatenate([v, far], axis=0), jnp.concatenate([far, v], axis=0)
        )

    grads = half_sum(grads, c_at, core_swap)
    grads = half_sum(grads, x_at, x_swap)
    grads = lax.psum(grads.astype(BF), "dp")
    grads = half_join(grads, x_at, x_swap)
    grads = half_join(grads, c_at, core_swap).astype(F32)
    grad_w_query = grads[:, :inner]
    grad_w_key = grads[:, inner : 2 * inner]
    grad_w_value = grads[:, 2 * inner : 3 * inner]
    grad_w_out = grads[:, 3 * inner :].T

    table_grad = sum(jnp.roll(table_grad[:, i], -i, axis=1) for i in range(8))
    grad_rel = jnp.sum(jnp.where(hot[None], table_grad[:, None, :], 0.0), axis=2).T
    grad_rel = lax.dynamic_update_slice_in_dim(
        jnp.zeros((bucket_count, total_heads), F32), grad_rel, h_at * heads, 1
    )
    small = jnp.concatenate([grad_gain_attn, grad_gain_ffn, grad_rel.reshape(-1)])
    small = lax.psum(small, ("dp", "head", "hid"))
    grad_gain_attn = small[:width]
    grad_gain_ffn = small[width : 2 * width]
    grad_rel = small[2 * width :].reshape(bucket_count, total_heads)
    return (
        output,
        grad_inputs,
        grad_mask,
        grad_gain_attn,
        grad_w_query,
        grad_w_key,
        grad_w_value,
        grad_w_out,
        grad_rel,
        grad_gain_ffn,
        grad_gate,
        grad_up,
        grad_down,
    )


def solution(mesh):
    rows = P("dp", ("head", "hid"), None)
    return jax.shard_map(
        per_device,
        mesh=mesh,
        in_specs=(
            rows,
            P("dp"),
            P("dp", None),
            P(),
            P(),
            P(None, "head"),
            P(None, "head"),
            P(None, "head"),
            P("head", None),
            P(),
            P(),
            P(None, ("head", "hid")),
            P(None, ("head", "hid")),
            P(("head", "hid"), None),
            rows,
        ),
        out_specs=(
            rows,
            rows,
            P("dp", ("head", "hid")),
            P(),
            P(None, "head"),
            P(None, "head"),
            P(None, "head"),
            P("head", None),
            P(),
            P(),
            P(None, ("head", "hid")),
            P(None, ("head", "hid")),
            P(("head", "hid"), None),
        ),
        check_vma=False,
    )
```

time: 3520 us -> 578 us (0.16)
  local copies, waits for them, and re-layouts: 2750 us -> 100 us
  waiting for transfers between devices: 473 us -> 217 us
  matrix products: 153 us -> 58 us
  Pallas kernels: 0 us -> 67.8 us
    gather x3 -> x0, local copies, waits for them, and re-layouts: 2570 us -> none  [per_device(): bucket_of = buckets[key_pos[None, :] - query_pos[:, None] + seq_length - 1]]
    reduce_scatter x4 -> x0, waiting for transfers between devices: 134 us -> none  [the longest x1 89.7 us: per_device(): lax.psum_scatter(second_backward, ('head', 'hid'), scatter_dimension=1, t...]
    unnamed x16 -> x1, waiting for transfers between devices: 127 us -> 0.02 us
    all_gather x4 -> x0, waiting for transfers between devices: 106 us -> none  [the longest x1 45 us: per_device(): lax.all_gather(normed_two, ('head', 'hid'), axis=1, tiled=True)]
    dot_general x29 -> x22, matrix products: 153 us -> 58 us  [the longest x9 35.5 us: dot_tn(): return lax.dot_general(a, b, TN, preferred_element_type=F32)]
    ppermute x0 -> x35, waiting for transfers between devices: none -> 71.1 us  [the longest x7 34.1 us: y_swap(): return lax.ppermute(v, 'head', [(0, 1), (1, 0)])]
    unnamed x120 -> x178, local copies, waits for them, and re-layouts: 96.8 us -> 28.7 us
    pallas_call x0 -> x6, Pallas kernels: none -> 67.8 us  [the longest x3 41.9 us: ffn_chunk(): pl.pallas_call(ffn_kernel, out_shape=(mid_shape, mid_shape, mid_shape, ja...]
  transfers between devices with their start and end apart: 13 -> 36, of which waited for: 10 -> 10; matrix products, arithmetic and copies ran while one was open for 81% -> 32% of each run, Pallas kernels for 0% -> 8%
where the time goes in v1:
time: 578 us; the launch traced here: 568 us
  waiting for transfers between devices  217 us (38%)
  local copies, waits for them, and re-layouts  100 us (17%)
  Pallas kernels  67.8 us (12%)
  matrix products  58 us (10%)
  other arithmetic  41.9 us (7%)
  blocking collectives  39.2 us (7%)
  starting transfers between devices  28.6 us (5%)
  between operations  15.7 us (3%)
    psum x1, waiting for transfers between devices, per_device(): grads = lax.psum(grads.astype(BF), 'dp')  146 us
    pallas_call x3, Pallas kernels, ffn_chunk(): pl.pallas_call(ffn_kernel, out_shape=(mid_shape, mid_shape, mid_shape, ja...  41.9 us
    psum x1, blocking collectives, per_device(): small = lax.psum(small, ('dp', 'head', 'hid'))  39.2 us
    dot_general x9, matrix products, dot_tn(): return lax.dot_general(a, b, TN, preferred_element_type=F32)  35.5 us
    ppermute x7, waiting for transfers between devices, y_swap(): return lax.ppermute(v, 'head', [(0, 1), (1, 0)])  34.1 us
    ppermute x5, waiting for transfers between devices, x_swap(): return lax.ppermute(v, 'hid', [(i, i ^ 2) for i in range(hid_axis)])  29 us
    unnamed x178, local copies, waits for them, and re-layouts  28.7 us
    ppermute x9, local copies, waits for them, and re-layouts, grid_swap(): return lax.ppermute(v, ('head', 'hid'), pairs)  19.3 us
  transfers between devices with their start and end apart: 36, of which 10 were waited for; matrix products, arithmetic and copies ran while one was open for 32% of the time, Pallas kernels for 8%

profile of v1, /device:TPU:0, one launch (start us, length us, event | category | flops | bytes accessed | tf_op | source)
XLA Modules:
  0.0 568.2 jit_solution(4379507822054704791)
XLA Ops:
  7.3 3.0 collective-permute-start.4
  23.8 16.5 %collective-permute-done.1 = bf16[256,1472]{0,1:T(8,128)(2,1)} collective-permute-done((bf16[256,1472]{0,1:T(8,128)(2,1)}, bf16[256,1472]{0,1:T(8,128)(2,1)}, u32[]{:S(2)}, u32[]{:S(2)}) %collective-permute-start.1) | collective-permute-done | bytes 753696 | tf_op jit(solution)/shard_map/ppermute | solution.py:334
  47.6 7.1 %bias.1.bias_ref = f32[3,1024,512]{2,1,0:T(8,128)} custom-call(s32[8]{0:T(128)} %sub.56.start_ref, f32[8,2048]{1,0:T(8,128)} %concatenate.141.table_ref, f32[1,1024]{1,0:T(1,128)} %reshape.146.mask_ref), custom_call_target="tpu_custom_call" | custom-call | tf_op jit(solution)/shard_map/bias/pallas_call | solution.py:50
  54.9 7.3 %attn_fwd.1 = (f32[3,1024,512]{2,1,0:T(8,128)}, bf16[512,192]{1,0:T(8,128)(2,1)S(1)}) custom-call(bf16[512,192]{1,0:T(8,128)(2,1)S(1)} %pad_maximum_fusion.11.q_ref, bf16[512,384]{1,0:T(8,128)(2,1)S(1)} %pad_maximum_fusion.10.kv0_ref, bf16[512,384]{1,0:T(8,128)(2,1)S(1)} %collective-permute-done.2.kv1_ref, f32[3,1024,512]{2,1,0:T(8,128)} %bias.1.bias_ref), custom_call_target="tpu_custom_call" | custom-call | tf_op jit(solution)/shard_map/attn_fwd/pallas_call | solution.py:97
  76.2 2.5 copy.264.g0
  78.8 2.6 copy.266.u0
  83.7 2.4 pad_maximum_fusion.4
  86.1 2.6 copy.282
  90.2 2.3 copy.315
  92.5 2.6 copy.265.g1
  95.1 2.8 copy.267.u1
  97.9 9.6 %ffn.3 = (bf16[2,256,448]{2,1,0:T(8,128)(2,1)}, bf16[2,256,448]{2,1,0:T(8,128)(2,1)}, bf16[2,256,448]{2,1,0:T(8,128)(2,1)}, f32[256,1472]{1,0:T(8,128)}) custom-call(bf16[256,1472]{1,0:T(8,128)(2,1)} %multiply_convert_fusion.n_ref, bf16[256,1472]{1,0:T(8,128)(2,1)} %copy-done.10, bf16[1472,448]{1,0:T(8,128)(2,1)} %copy.264.g0, bf16[1472,448]{1,0:T(8,128)(2,1)} %copy.265.g1, ...), custom_call_target="tpu_custom_call" | custom-call | tf_op jit(solution)/shard_map/ffn/pallas_call | solution.py:274
  110.5 2.7 copy.280
  115.7 9.4 %ffn.4 = (bf16[2,256,448]{2,1,0:T(8,128)(2,1)}, bf16[2,256,448]{2,1,0:T(8,128)(2,1)}, bf16[2,256,448]{2,1,0:T(8,128)(2,1)}, bf16[256,1472]{1,0:T(8,128)(2,1)}) custom-call(bf16[256,1472]{1,0:T(8,128)(2,1)} %copy-done.19, bf16[256,1472]{1,0:T(8,128)(2,1)} %copy.273.dy_ref, bf16[1472,448]{1,0:T(8,128)(2,1)} %copy.264.g0, bf16[1472,448]{1,0:T(8,128)(2,1)} %copy.265.g1, ...), custom_call_target="tpu_custom_call" | custom-call | tf_op jit(solution)/shard_map/ffn/pallas_call | solution.py:274
  125.1 2.3 copy.292
  133.3 3.1 fusion.34
  138.6 2.6 copy.284.dy_ref
  143.5 4.0 collective-permute-done.11
  147.5 2.3 copy.278
  151.4 22.9 %ffn.5 = (bf16[2,512,448]{2,1,0:T(8,128)(2,1)}, bf16[2,512,448]{2,1,0:T(8,128)(2,1)}, bf16[2,512,448]{2,1,0:T(8,128)(2,1)}, bf16[512,1472]{1,0:T(8,128)(2,1)}) custom-call(bf16[512,1472]{1,0:T(8,128)(2,1)} %copy.283.n_ref, bf16[512,1472]{1,0:T(8,128)(2,1)} %copy.284.dy_ref, bf16[1472,448]{1,0:T(8,128)(2,1)} %copy.264.g0, bf16[1472,448]{1,0:T(8,128)(2,1)} %copy.265.g1, ...), custom_call_target="tpu_custom_call" | custom-call | tf_op jit(solution)/shard_map/ffn/pallas_call | solution.py:274
  178.3 2.5 fusion.25
  183.4 5.5 convolution_convert_fusion
  190.3 4.5 convolution_convert_fusion.2
  196.0 4.4 convolution_convert_fusion.1
  202.7 2.4 add_convert_fusion
  211.6 4.7 fusion.1
  216.3 4.5 fusion.2
  220.8 5.4 fusion.3
  228.6 2.7 multiply_reduce_fusion
  236.9 2.3 convolution_convert_fusion.3
  243.3 11.4 %attn_bwd.1 = (bf16[512,192]{1,0:T(8,128)(2,1)S(1)}, f32[512,384]{1,0:T(8,128)S(1)}, bf16[512,384]{1,0:T(8,128)(2,1)S(1)}, f32[1,1024]{1,0:T(1,128)S(1)}, f32[3,8,2048]{2,1,0:T(8,128)S(1)}) custom-call(s32[8]{0:T(128)S(1)} %copy-done.2, f32[3,1024,512]{2,1,0:T(8,128)} %get-tuple-element.39.p_ref, bf16[512,192]{1,0:T(8,128)(2,1)S(1)} %pad_maximum_fusion.11.q_ref, ...), custom_call_target="tpu_custom_call" | custom-call | tf_op jit(solution)/shard_map/attn_bwd/pallas_call | solution.py:211
  261.4 4.2 collective-permute-done.21
  266.7 2.8 fusion.18
  270.9 2.5 pad_maximum_fusion
  273.4 6.3 %copy.316 = f32[1472,768]{1,0:T(8,128)} copy(f32[1472,768]{0,1:T(8,128)} %pad_maximum_fusion) | data formatting | bytes 9043968 | tf_op jit(solution)/shard_map/concatenate | solution.py:493
  281.7 2.6 collective-permute-done.28
  287.5 13.6 %collective-permute-done.29 = bf16[368,768]{1,0:T(8,128)(2,1)S(1)} collective-permute-done((bf16[368,768]{1,0:T(8,128)(2,1)S(1)}, bf16[368,768]{1,0:T(8,128)(2,1)S(1)}, u32[]{:S(2)}, u32[]{:S(2)}) %collective-permute-start.29) | collective-permute-done | bytes 565280 | tf_op jit(solution)/shard_map/ppermute | solution.py:331
  302.5 2.9 fusion.30
  307.8 16.1 %collective-permute-done.25 = f32[256]{0:T(256)S(1)} collective-permute-done((f32[256]{0:T(256)S(1)}, f32[256]{0:T(256)S(1)}, u32[]{:S(2)}, u32[]{:S(2)}) %collective-permute-start.25) | collective-permute-done | bytes 1056 | tf_op jit(solution)/shard_map/ppermute | solution.py:334
  329.3 145.6 %all-reduce.4.cloned.1.call-done = (bf16[368,768]{1,0:T(8,128)(2,1)}, bf16[1472,448]{0,1:T(8,128)(2,1)}, bf16[1472,448]{0,1:T(8,128)(2,1)}, bf16[448,1472]{1,0:T(8,128)(2,1)}) async-done(((bf16[368,768]{1,0:T(8,128)(2,1)}, bf16[1472,448]{0,1:T(8,128)(2,1)}, bf16[1472,448]{0,1:T(8,128)(2,1)}, bf16[448,1472]{1,0:T(8,128)(2,1)}), (bf16[368,768]{1,0:T(8,128)(2,1)}, bf16[1472,448]{0,1:T(8,128)(2,1)}, ...) | async-done | bytes 4522000 | tf_op jit(solution)/shard_map/psum | solution.py:509
  478.4 11.3 %collective-permute-done.30 = bf16[368,768]{1,0:T(8,128)(2,1)S(1)} collective-permute-done((bf16[368,768]{1,0:T(8,128)(2,1)}, bf16[368,768]{1,0:T(8,128)(2,1)S(1)}, u32[]{:S(2)}, u32[]{:S(2)}) %collective-permute-start.30) | collective-permute-done | bytes 565280 | tf_op jit(solution)/shard_map/ppermute | solution.py:331
  497.0 39.2 %psum.35 = f32[3136]{0:T(1024)S(1)} all-reduce(f32[3136]{0:T(1024)S(1)} %concatenate.169), channel_id=1, replica_groups=mesh['dp'=4,'head'=2,'hid'=4] {'dp','head','hid'}, use_global_device_ids=true, to_apply=%region_8.9 | all-reduce | flops 3136 | bytes 25088 | tf_op jit(solution)/shard_map/psum | solution.py:523
  537.7 2.6 maximum_select_fusion.1
  540.3 3.3 convert_element_type.180
  547.4 2.3 fusion.9
  549.7 2.6 slice_bitcast_fusion
  552.2 2.9 copy.322
  555.1 2.9 copy.321
  (363 shorter events, 128.1 us)
Async XLA Ops:
  7.2 7.2 %copy-start = (f32[2,1024]{1,0:T(2,128)S(1)}, f32[2,1024]{1,0:T(2,128)}, u32[]{:S(2)}) copy-start(f32[2,1024]{1,0:T(2,128)} %param.17) | copy-start | bytes 24580
  7.2 467.7 %all-reduce.4.cloned.1.call-start = ((), (), s32[]{:S(2)}) async-start(), calls=%async_computation | async-start | bytes 9388032 | tf_op jit(solution)/shard_map/psum | solution.py:509
  7.3 59.7 %collective-permute-start.4 = (bf16[192,1472]{1,0:T(8,128)(2,1)}, bf16[192,1472]{1,0:T(8,128)(2,1)}, u32[]{:S(2)}, u32[]{:S(2)}) collective-permute-start(bf16[192,1472]{1,0:T(8,128)(2,1)} %param.23), channel_id=1, source_target_pairs={{0,4},{4,0},{1,5},{5,1},{2,6},{6,2},{3,7},{7,3},{8,12},{12,8},{9,1... | collective-permute-start | bytes 1695752 | tf_op jit(solution)/shard_map/ppermute | solution.py:334
  11.7 7.7 %collective-permute-start = (bf16[128,1472]{1,0:T(8,128)(2,1)S(1)}, bf16[128,1472]{1,0:T(8,128)(2,1)S(1)}, u32[]{:S(2)}, u32[]{:S(2)}) collective-permute-start(bf16[128,1472]{1,0:T(8,128)(2,1)S(1)} %bitcast.157), channel_id=1, source_target_pairs={{0,1},{1,0},{2,3},{3,2},{4,5},{5,4},{6,7},{7,6},{8,9},{9,8},{10,11... | collective-permute-start | bytes 1130504 | tf_op jit(solution)/shard_map/ppermute | solution.py:328
  12.8 50.1 %collective-permute-start.5 = (bf16[128,1472]{1,0:T(8,128)(2,1)}, bf16[128,1472]{1,0:T(8,128)(2,1)}, u32[]{:S(2)}, u32[]{:S(2)}) collective-permute-start(bf16[128,1472]{1,0:T(8,128)(2,1)} %bitcast.10), channel_id=1, source_target_pairs={{0,1},{1,0},{2,3},{3,2},{4,5},{5,4},{6,7},{7,6},{8,9},{9,8},{10,11... | collective-permute-start | bytes 1130504 | tf_op jit(solution)/shard_map/ppermute | solution.py:328
  13.2 79.3 %collective-permute-start.6 = (bf16[1472,448]{0,1:T(8,128)(2,1)}, bf16[1472,448]{0,1:T(8,128)(2,1)}, u32[]{:S(2)}, u32[]{:S(2)}) collective-permute-start(bf16[1472,448]{0,1:T(8,128)(2,1)} %param.26), channel_id=1, source_target_pairs={{0,1},{1,0},{2,3},{3,2},{4,5},{5,4},{6,7},{7,6},{8,9},{9,8},{10,11... | collective-permute-start | bytes 3956744 | tf_op jit(solution)/shard_map/ppermute | solution.py:328
  13.3 81.8 %collective-permute-start.7 = (bf16[1472,448]{0,1:T(8,128)(2,1)}, bf16[1472,448]{0,1:T(8,128)(2,1)}, u32[]{:S(2)}, u32[]{:S(2)}) collective-permute-start(bf16[1472,448]{0,1:T(8,128)(2,1)} %param.27), channel_id=1, source_target_pairs={{0,1},{1,0},{2,3},{3,2},{4,5},{5,4},{6,7},{7,6},{8,9},{9,8},{10,11... | collective-permute-start | bytes 3956744 | tf_op jit(solution)/shard_map/ppermute | solution.py:328
  21.2 19.1 %collective-permute-start.1 = (bf16[256,1472]{0,1:T(8,128)(2,1)}, bf16[256,1472]{0,1:T(8,128)(2,1)}, u32[]{:S(2)}, u32[]{:S(2)}) collective-permute-start(bf16[256,1472]{0,1:T(8,128)(2,1)} %copy.256), channel_id=1, source_target_pairs={{0,4},{4,0},{1,5},{5,1},{2,6},{6,2},{3,7},{7,3},{8,12},{12,8},{9,1... | collective-permute-start | bytes 2261000 | tf_op jit(solution)/shard_map/ppermute | solution.py:334
  43.0 11.8 %collective-permute-start.2 = (bf16[512,384]{1,0:T(8,128)(2,1)S(1)}, bf16[512,384]{1,0:T(8,128)(2,1)S(1)}, u32[]{:S(2)}, u32[]{:S(2)}) collective-permute-start(bf16[512,384]{1,0:T(8,128)(2,1)S(1)} %pad_maximum_fusion.10.kv0_ref), channel_id=1, source_target_pairs={{0,2},{1,3},{2,0},{3,1},{4,6},{5,7},{6,4},{7,5},{8,10},{9,11},{10,... | collective-permute-start | bytes 1179656 | tf_op jit(solution)/shard_map/ppermute | solution.py:331
  54.8 9.6 %copy-start.35 = (bf16[1,128,1472]{2,1,0:T(8,128)(2,1)S(1)}, bf16[1,128,1472]{2,1,0:T(8,128)(2,1)}, u32[]{:S(2)}) copy-start(bf16[1,128,1472]{2,1,0:T(8,128)(2,1)} %copy.262) | copy-start | bytes 1130500
  54.8 43.1 %collective-permute-start.8 = (bf16[448,1472]{1,0:T(8,128)(2,1)S(1)}, bf16[448,1472]{1,0:T(8,128)(2,1)}, u32[]{:S(2)}, u32[]{:S(2)}) collective-permute-start(bf16[448,1472]{1,0:T(8,128)(2,1)S(1)} %copy-done.3), channel_id=1, source_target_pairs={{0,1},{1,0},{2,3},{3,2},{4,5},{5,4},{6,7},{7,6},{8,9},{9,8},{10,11... | collective-permute-start | bytes 3956744 | tf_op jit(solution)/shard_map/ppermute | solution.py:328
  62.9 6.2 %collective-permute-start.3 = (bf16[256,192]{1,0:T(8,128)(2,1)}, bf16[256,192]{1,0:T(8,128)(2,1)}, u32[]{:S(2)}, u32[]{:S(2)}) collective-permute-start(bf16[256,192]{1,0:T(8,128)(2,1)} %slice.187), channel_id=1, source_target_pairs={{0,4},{4,0},{1,5},{5,1},{2,6},{6,2},{3,7},{7,3},{8,12},{12,8},{9,1... | collective-permute-start | bytes 294920 | tf_op jit(solution)/shard_map/ppermute | solution.py:334
  65.8 17.9 %copy-start.10 = (bf16[256,1472]{1,0:T(8,128)(2,1)}, bf16[256,1472]{1,0:T(8,128)(2,1)S(1)}, u32[]{:S(2)}) copy-start(bf16[256,1472]{1,0:T(8,128)(2,1)S(1)} %maximum_select_fusion.4.dy_ref) | copy-start | bytes 2260996
  67.0 14.4 %collective-permute-start.10 = (bf16[256,1472]{0,1:T(8,128)(2,1)}, bf16[256,1472]{0,1:T(8,128)(2,1)}, u32[]{:S(2)}, u32[]{:S(2)}) collective-permute-start(bf16[256,1472]{0,1:T(8,128)(2,1)} %copy.271), channel_id=1, source_target_pairs={{0,2},{1,5},{2,0},{3,7},{4,6},{5,1},{6,4},{7,3},{8,10},{9,13},{10,... | collective-permute-start | bytes 2261000 | tf_op jit(solution)/shard_map/ppermute | solution.py:343
  75.7 31.8 %collective-permute-start.9 = (bf16[256,1472]{0,1:T(8,128)(2,1)}, bf16[256,1472]{0,1:T(8,128)(2,1)}, u32[]{:S(2)}, u32[]{:S(2)}) collective-permute-start(bf16[256,1472]{0,1:T(8,128)(2,1)} %copy.270), channel_id=1, source_target_pairs={{0,2},{1,5},{2,0},{3,7},{4,6},{5,1},{6,4},{7,3},{8,10},{9,13},{10,... | collective-permute-start | bytes 2261000 | tf_op jit(solution)/shard_map/ppermute | solution.py:343
  88.6 50.0 %collective-permute-start.13 = (bf16[512,1472]{0,1:T(8,128)(2,1)}, bf16[512,1472]{0,1:T(8,128)(2,1)}, u32[]{:S(2)}, u32[]{:S(2)}) collective-permute-start(bf16[512,1472]{0,1:T(8,128)(2,1)} %copy.282), channel_id=1, source_target_pairs={{0,4},{1,3},{2,6},{3,1},{4,0},{5,7},{6,2},{7,5},{8,12},{9,11},{10,... | collective-permute-start | bytes 4521992 | tf_op jit(solution)/shard_map/ppermute | solution.py:343
  113.1 36.7 %collective-permute-start.12 = (bf16[512,1472]{0,1:T(8,128)(2,1)}, bf16[512,1472]{0,1:T(8,128)(2,1)S(1)}, u32[]{:S(2)}, u32[]{:S(2)}) collective-permute-start(bf16[512,1472]{0,1:T(8,128)(2,1)} %copy.280), channel_id=1, source_target_pairs={{0,4},{1,3},{2,6},{3,1},{4,0},{5,7},{6,2},{7,5},{8,12},{9,11},{10,... | collective-permute-start | bytes 4521992 | tf_op jit(solution)/shard_map/ppermute | solution.py:343
  127.4 13.8 %collective-permute-start.17 = (bf16[256,1472]{0,1:T(8,128)(2,1)}, bf16[256,1472]{0,1:T(8,128)(2,1)}, u32[]{:S(2)}, u32[]{:S(2)}) collective-permute-start(bf16[256,1472]{0,1:T(8,128)(2,1)} %copy.292), channel_id=1, source_target_pairs={{0,2},{1,5},{2,0},{3,7},{4,6},{5,1},{6,4},{7,3},{8,10},{9,13},{10,... | collective-permute-start | bytes 2261000 | tf_op jit(solution)/shard_map/ppermute | solution.py:343
  132.8 14.7 %collective-permute-start.11 = (bf16[256,1472]{0,1:T(8,128)(2,1)}, bf16[256,1472]{0,1:T(8,128)(2,1)}, u32[]{:S(2)}, u32[]{:S(2)}) collective-permute-start(bf16[256,1472]{0,1:T(8,128)(2,1)} %fusion.7), channel_id=1, source_target_pairs={{0,2},{1,5},{2,0},{3,7},{4,6},{5,1},{6,4},{7,3},{8,10},{9,13},{10,... | collective-permute-start | bytes 2261000 | tf_op jit(solution)/shard_map/ppermute | solution.py:343
  176.8 23.6 %collective-permute-start.18 = (bf16[256,1472]{0,1:T(8,128)(2,1)}, bf16[256,1472]{0,1:T(8,128)(2,1)}, u32[]{:S(2)}, u32[]{:S(2)}) collective-permute-start(bf16[256,1472]{0,1:T(8,128)(2,1)} %copy.294), channel_id=1, source_target_pairs={{0,2},{1,5},{2,0},{3,7},{4,6},{5,1},{6,4},{7,3},{8,10},{9,13},{10,... | collective-permute-start | bytes 2261000 | tf_op jit(solution)/shard_map/ppermute | solution.py:343
  182.8 25.6 %collective-permute-start.14 = (bf16[256,1472]{0,1:T(8,128)(2,1)}, bf16[256,1472]{0,1:T(8,128)(2,1)}, u32[]{:S(2)}, u32[]{:S(2)}) collective-permute-start(bf16[256,1472]{0,1:T(8,128)(2,1)} %slice.240), channel_id=1, source_target_pairs={{0,2},{1,5},{2,0},{3,7},{4,6},{5,1},{6,4},{7,3},{8,10},{9,13},{10,... | collective-permute-start | bytes 2261000 | tf_op jit(solution)/shard_map/ppermute | solution.py:343
  188.9 31.9 %collective-permute-start.34 = (bf16[448,1472]{1,0:T(8,128)(2,1)}, bf16[448,1472]{1,0:T(8,128)(2,1)}, u32[]{:S(2)}, u32[]{:S(2)}) collective-permute-start(bf16[448,1472]{1,0:T(8,128)(2,1)} %convolution_convert_fusion), channel_id=1, source_target_pairs={{0,1},{1,0},{2,3},{3,2},{4,5},{5,4},{6,7},{7,6},{8,9},{9,8},{10,11... | collective-permute-start | bytes 3956744 | tf_op jit(solution)/shard_map/ppermute | solution.py:328
  194.9 16.8 %collective-permute-start.32 = (bf16[1472,448]{0,1:T(8,128)(2,1)}, bf16[1472,448]{0,1:T(8,128)(2,1)}, u32[]{:S(2)}, u32[]{:S(2)}) collective-permute-start(bf16[1472,448]{0,1:T(8,128)(2,1)} %convolution_convert_fusion.2), channel_id=1, source_target_pairs={{0,1},{1,0},{2,3},{3,2},{4,5},{5,4},{6,7},{7,6},{8,9},{9,8},{10,11... | collective-permute-start | bytes 3956744 | tf_op jit(solution)/shard_map/ppermute | solution.py:328
  200.4 15.9 %collective-permute-start.33 = (bf16[1472,448]{0,1:T(8,128)(2,1)}, bf16[1472,448]{0,1:T(8,128)(2,1)}, u32[]{:S(2)}, u32[]{:S(2)}) collective-permute-start(bf16[1472,448]{0,1:T(8,128)(2,1)} %convolution_convert_fusion.1), channel_id=1, source_target_pairs={{0,1},{1,0},{2,3},{3,2},{4,5},{5,4},{6,7},{7,6},{8,9},{9,8},{10,11... | collective-permute-start | bytes 3956744 | tf_op jit(solution)/shard_map/ppermute | solution.py:328
  207.4 18.8 %collective-permute-start.19 = (bf16[256,1472]{0,1:T(8,128)(2,1)}, bf16[256,1472]{0,1:T(8,128)(2,1)}, u32[]{:S(2)}, u32[]{:S(2)}) collective-permute-start(bf16[256,1472]{0,1:T(8,128)(2,1)} %copy.296), channel_id=1, source_target_pairs={{0,4},{1,3},{2,6},{3,1},{4,0},{5,7},{6,2},{7,5},{8,12},{9,11},{10,... | collective-permute-start | bytes 2261000 | tf_op jit(solution)/shard_map/ppermute | solution.py:343
  210.5 30.3 %collective-permute-start.15 = (bf16[256,1472]{0,1:T(8,128)(2,1)}, bf16[256,1472]{0,1:T(8,128)(2,1)}, u32[]{:S(2)}, u32[]{:S(2)}) collective-permute-start(bf16[256,1472]{0,1:T(8,128)(2,1)} %add_convert_fusion.1), channel_id=1, source_target_pairs={{0,4},{1,3},{2,6},{3,1},{4,0},{5,7},{6,2},{7,5},{8,12},{9,11},{10,... | collective-permute-start | bytes 2261000 | tf_op jit(solution)/shard_map/ppermute | solution.py:343
  220.8 7.8 %copy-start.71 = (f32[256]{0:T(256)S(1)}, f32[256]{0:T(256)}, u32[]{:S(2)}) copy-start(f32[256]{0:T(256)} %copy-done.70) | copy-start | bytes 3076
  220.8 7.7 %copy-start.8 = (f32[256,1472]{1,0:T(8,128)S(1)}, f32[256,1472]{1,0:T(8,128)}, u32[]{:S(2)}) copy-start(f32[256,1472]{1,0:T(8,128)} %copy-done.7) | copy-start | bytes 4521988
  235.9 7.3 %collective-permute-start.20 = (bf16[256,192]{1,0:T(8,128)(2,1)S(1)}, bf16[256,192]{1,0:T(8,128)(2,1)S(1)}, u32[]{:S(2)}, u32[]{:S(2)}) collective-permute-start(bf16[256,192]{1,0:T(8,128)(2,1)S(1)} %copy.298), channel_id=1, source_target_pairs={{0,4},{4,0},{1,5},{5,1},{2,6},{6,2},{3,7},{7,3},{8,12},{12,8},{9,1... | collective-permute-start | bytes 294920 | tf_op jit(solution)/shard_map/ppermute | solution.py:334
  239.7 29.7 %collective-permute-start.27 = (bf16[1472,192]{0,1:T(8,128)(2,1)}, bf16[1472,192]{0,1:T(8,128)(2,1)}, u32[]{:S(2)}, u32[]{:S(2)}) collective-permute-start(bf16[1472,192]{0,1:T(8,128)(2,1)} %convolution_convert_fusion.3), channel_id=1, source_target_pairs={{0,4},{4,0},{1,5},{5,1},{2,6},{6,2},{3,7},{7,3},{8,12},{12,8},{9,1... | collective-permute-start | bytes 1695752 | tf_op jit(solution)/shard_map/ppermute | solution.py:334
  243.2 13.1 %copy-start.6 = (bf16[448,1472]{1,0:T(8,128)(2,1)S(1)}, bf16[448,1472]{1,0:T(8,128)(2,1)}, u32[]{:S(2)}) copy-start(bf16[448,1472]{1,0:T(8,128)(2,1)} %d0.5) | copy-start | bytes 3956740
  243.2 13.0 %copy-start.9 = (f32[256,1472]{1,0:T(8,128)S(1)}, f32[256,1472]{1,0:T(8,128)}, u32[]{:S(2)}) copy-start(f32[256,1472]{1,0:T(8,128)} %copy-done.7) | copy-start | bytes 4521988
  243.2 13.0 %copy-start.22 = (f32[256,1472]{1,0:T(8,128)S(1)}, f32[256,1472]{1,0:T(8,128)}, u32[]{:S(2)}) copy-start(f32[256,1472]{1,0:T(8,128)} %fusion.34) | copy-start | bytes 4521988
  243.2 13.0 %copy-start.29 = (bf16[256,1472]{1,0:T(8,128)(2,1)S(1)}, bf16[256,1472]{1,0:T(8,128)(2,1)}, u32[]{:S(2)}) copy-start(bf16[256,1472]{1,0:T(8,128)(2,1)} %copy.278) | copy-start | bytes 2260996
  243.2 13.0 %copy-start.30 = (bf16[256,1472]{1,0:T(8,128)(2,1)S(1)}, bf16[256,1472]{1,0:T(8,128)(2,1)}, u32[]{:S(2)}) copy-start(bf16[256,1472]{1,0:T(8,128)(2,1)} %copy.289) | copy-start | bytes 2260996
  243.3 13.0 %copy-start.33 = (bf16[2,256,448]{2,1,0:T(8,128)(2,1)S(1)}, bf16[2,256,448]{2,1,0:T(8,128)(2,1)}, u32[]{:S(2)}) copy-start(bf16[2,256,448]{2,1,0:T(8,128)(2,1)} %get-tuple-element.33) | copy-start | bytes 1376260
  254.7 10.9 %collective-permute-start.21 = (bf16[512,384]{1,0:T(8,128)(2,1)S(1)}, bf16[512,384]{1,0:T(8,128)(2,1)}, u32[]{:S(2)}, u32[]{:S(2)}) collective-permute-start(bf16[512,384]{1,0:T(8,128)(2,1)S(1)} %get-tuple-element.42), channel_id=1, source_target_pairs={{0,2},{1,3},{2,0},{3,1},{4,6},{5,7},{6,4},{7,5},{8,10},{9,11},{10,... | collective-permute-start | bytes 1179656 | tf_op jit(solution)/shard_map/ppermute | solution.py:331
  260.6 233.9 %collective-permute-start.16 = (bf16[128,1472]{0,1:T(8,128)(2,1)}, bf16[128,1472]{0,1:T(8,128)(2,1)}, u32[]{:S(2)}, u32[]{:S(2)}) collective-permute-start(bf16[128,1472]{0,1:T(8,128)(2,1)} %bitcast.18), channel_id=1, source_target_pairs={{0,1},{1,0},{2,3},{3,2},{4,5},{5,4},{6,7},{7,6},{8,9},{9,8},{10,11... | collective-permute-start | bytes 1130504 | tf_op jit(solution)/shard_map/ppermute | solution.py:328
  260.7 41.8 %collective-permute-start.24 = (f32[2,256]{1,0:T(2,128)S(1)}, f32[2,256]{1,0:T(2,128)S(1)}, u32[]{:S(2)}, u32[]{:S(2)}) collective-permute-start(f32[2,256]{1,0:T(2,128)S(1)} %squeeze.130), channel_id=1, source_target_pairs={{0,2},{1,3},{2,0},{3,1},{4,6},{5,7},{6,4},{7,5},{8,10},{9,11},{10,... | collective-permute-start | bytes 6152 | tf_op jit(solution)/shard_map/ppermute | solution.py:331
  281.4 2.8 collective-permute-start.28
  286.2 14.9 %collective-permute-start.29 = (bf16[368,768]{1,0:T(8,128)(2,1)S(1)}, bf16[368,768]{1,0:T(8,128)(2,1)S(1)}, u32[]{:S(2)}, u32[]{:S(2)}) collective-permute-start(bf16[368,768]{1,0:T(8,128)(2,1)S(1)} %fusion.24), channel_id=1, source_target_pairs={{0,2},{1,3},{2,0},{3,1},{4,6},{5,7},{6,4},{7,5},{8,10},{9,11},{10,... | collective-permute-start | bytes 1695752 | tf_op jit(solution)/shard_map/ppermute | solution.py:331
  305.6 21.5 %collective-permute-start.22 = (bf16[256,1472]{0,1:T(8,128)(2,1)S(1)}, bf16[256,1472]{0,1:T(8,128)(2,1)}, u32[]{:S(2)}, u32[]{:S(2)}) collective-permute-start(bf16[256,1472]{0,1:T(8,128)(2,1)S(1)} %slice.361), channel_id=1, source_target_pairs={{0,4},{4,0},{1,5},{5,1},{2,6},{6,2},{3,7},{7,3},{8,12},{12,8},{9,1... | collective-permute-start | bytes 2261000 | tf_op jit(solution)/shard_map/ppermute | solution.py:334
  306.5 17.4 %collective-permute-start.25 = (f32[256]{0:T(256)S(1)}, f32[256]{0:T(256)S(1)}, u32[]{:S(2)}, u32[]{:S(2)}) collective-permute-start(f32[256]{0:T(256)S(1)} %bitcast.163), channel_id=1, source_target_pairs={{0,4},{4,0},{1,5},{5,1},{2,6},{6,2},{3,7},{7,3},{8,12},{12,8},{9,1... | collective-permute-start | bytes 3080 | tf_op jit(solution)/shard_map/ppermute | solution.py:334
  474.9 14.8 %collective-permute-start.30 = (bf16[368,768]{1,0:T(8,128)(2,1)}, bf16[368,768]{1,0:T(8,128)(2,1)S(1)}, u32[]{:S(2)}, u32[]{:S(2)}) collective-permute-start(bf16[368,768]{1,0:T(8,128)(2,1)} %get-tuple-element.109), channel_id=1, source_target_pairs={{0,2},{1,3},{2,0},{3,1},{4,6},{5,7},{6,4},{7,5},{8,10},{9,11},{10,... | collective-permute-start | bytes 1695752 | tf_op jit(solution)/shard_map/ppermute | solution.py:331
  476.3 13.3 %copy-start.53 = (bf16[368,768]{1,0:T(8,128)(2,1)S(1)}, bf16[368,768]{1,0:T(8,128)(2,1)}, u32[]{:S(2)}) copy-start(bf16[368,768]{1,0:T(8,128)(2,1)} %get-tuple-element.109) | copy-start | bytes 1695748
  490.1 57.3 %collective-permute-start.31 = (bf16[736,768]{1,0:T(8,128)(2,1)S(1)}, bf16[736,768]{1,0:T(8,128)(2,1)}, u32[]{:S(2)}, u32[]{:S(2)}) collective-permute-start(bf16[736,768]{1,0:T(8,128)(2,1)S(1)} %maximum_select_fusion.2), channel_id=1, source_target_pairs={{0,1},{1,0},{2,3},{3,2},{4,5},{5,4},{6,7},{7,6},{8,9},{9,8},{10,11... | collective-permute-start | bytes 3391496 | tf_op jit(solution)/shard_map/ppermute | solution.py:328
  491.4 46.2 %collective-permute-start.23 = (f32[128,1472]{0,1:T(8,128)}, f32[128,1472]{0,1:T(8,128)}, u32[]{:S(2)}, u32[]{:S(2)}) collective-permute-start(f32[128,1472]{0,1:T(8,128)} %bitcast.156), channel_id=1, source_target_pairs={{0,1},{1,0},{2,3},{3,2},{4,5},{5,4},{6,7},{7,6},{8,9},{9,8},{10,11... | collective-permute-start | bytes 2261000 | tf_op jit(solution)/shard_map/ppermute | solution.py:328
  491.9 2.0 collective-permute-start.26
  (67 other events, 217.6 us)
Sparse Core Ops, SparseCore 0:
  302.2 172.6 all-reduce.3

commit v2 on v1

v2 whole, which is shorter than its diff:
```python
import functools

import jax
import jax.numpy as jnp
from jax import lax
from jax.experimental import pallas as pl
from jax.experimental.pallas import tpu as pltpu
from jax.sharding import PartitionSpec as P


DH = 64
EPS = 1e-06
NEG = -1e30
BF = jnp.bfloat16
F32 = jnp.float32
GELU_C = 0.7978845608028654
GELU_K = 0.044715
LANES = 128
EXTRA = 16


def cost(us):
    return pl.CostEstimate(flops=0, bytes_accessed=int(us * 3.0e6), transcendentals=0)


NT = (((1,), (1,)), ((), ()))
TN = (((0,), (0,)), ((), ()))


def dot(a, b):
    return jnp.dot(a, b, preferred_element_type=F32)


def dot_nt(a, b):
    return lax.dot_general(a, b, NT, preferred_element_type=F32)


def dot_tn(a, b):
    return lax.dot_general(a, b, TN, preferred_element_type=F32)


def sds(shape, dtype):
    return jax.ShapeDtypeStruct(shape, dtype)


class Order:
    last = None

    @classmethod
    def follow(cls, v):
        return v if cls.last is None else lax.optimization_barrier((v, cls.last))[0]

    @classmethod
    def done(cls, outs):
        cls.last = min(jax.tree.leaves(outs), key=lambda v: v.size)
        return outs


def call(kernel, out_shape, args, name, scalars=(), vmem=12, us=0.01, **kw):
    args = (Order.follow(args[0]), *args[1:])
    in_specs = [pl.BlockSpec(memory_space=pltpu.SMEM)] * len(scalars)
    in_specs += [pl.BlockSpec(memory_space=pltpu.VMEM)] * len(args)
    outs = pl.pallas_call(
        kernel,
        out_shape=out_shape,
        in_specs=in_specs,
        out_specs=jax.tree.map(lambda _: pl.BlockSpec(memory_space=pltpu.VMEM), out_shape),
        compiler_params=pltpu.CompilerParams(vmem_limit_bytes=vmem << 20),
        cost_estimate=cost(us),
        name=name,
        **kw,
    )(*scalars, *args)
    return Order.done(outs)


def in_hbm(v):
    return pltpu.with_memory_space_constraint(v, pltpu.HBM)


def move(v, axes, pairs, name):
    with jax.named_scope(name):
        return lax.ppermute(v, axes, pairs)


def lane_sum(v):
    total = v[:, :LANES]
    for at in range(LANES, v.shape[1], LANES):
        total = total + v[:, at : at + LANES]
    return jnp.sum(total.T, axis=0, keepdims=True)


def column(row, width):
    wide = jnp.broadcast_to(row, (LANES, row.shape[1])).T
    return jnp.concatenate([wide] * (width // LANES), axis=1)


def pair_rows(c, own_ref, far_ref):
    own = own_ref[c]
    far = far_ref[c]
    first = c == 0
    return jnp.concatenate([jnp.where(first, own, far), jnp.where(first, far, own)], axis=1)


def pick_kernel(c_ref, first_ref, second_ref, out_ref):
    out_ref[...] = jnp.where(c_ref[0] == 0, first_ref[...], second_ref[...])


def pair_kernel(c_ref, own_ref, far_ref, out_ref):
    out_ref[...] = pair_rows(c_ref[0], own_ref, far_ref)


def prep_kernel(c_ref, own_ref, far_ref, gain_ref, x_ref, n_ref, inv_ref):
    rows = pair_rows(c_ref[0], own_ref, far_ref)
    x_ref[...] = rows
    x = rows.astype(F32)
    inverse = lax.rsqrt(jnp.mean(x * x, axis=0, keepdims=True) + EPS)
    inv_ref[...] = inverse
    n_ref[...] = (x * inverse * column(gain_ref[...], x.shape[1])).astype(BF)


def qkv_kernel(n_ref, wq_ref, wk_ref, wv_ref, q_ref, kv_ref):
    n = n_ref[...]
    inner = wq_ref.shape[0]
    q_ref[...] = dot(wq_ref[...], n).astype(BF)
    kv_ref[:inner] = dot(wk_ref[...], n).astype(BF)
    kv_ref[inner:] = dot(wv_ref[...], n).astype(BF)


def bias_kernel(start_ref, table_ref, mask_ref, out_ref, *, heads, block, q_blocks):
    kb = pl.program_id(0)
    qb = pl.program_id(1)
    start = pl.multiple_of(start_ref[kb * q_blocks + qb], block)
    k_at = pl.multiple_of(kb * block, block)
    mask = column(mask_ref[:, pl.ds(k_at, block)], block)
    for h in range(heads):
        window = table_ref[h : h + 1, pl.ds(start, 2 * block)]
        window = jnp.broadcast_to(window, (block, 2 * block))
        rolled = pltpu.roll(window, block, 1, stride=1, stride_axis=0)
        out_ref[h] = rolled[:, :block] + mask


def make_bias(starts, table, mask_row, heads, block, k_blocks, q_blocks):
    length = k_blocks * block
    outs = pl.pallas_call(
        functools.partial(bias_kernel, heads=heads, block=block, q_blocks=q_blocks),
        out_shape=pltpu.HBM((heads, length, q_blocks * block), F32),
        grid_spec=pltpu.PrefetchScalarGridSpec(
            num_scalar_prefetch=1,
            grid=(k_blocks, q_blocks),
            in_specs=[
                pl.BlockSpec(table.shape, lambda k, q, s: (0, 0)),
                pl.BlockSpec((1, length), lambda k, q, s: (0, 0)),
            ],
            out_specs=pl.BlockSpec((heads, block, block), lambda k, q, s: (0, k, q)),
        ),
        compiler_params=pltpu.CompilerParams(vmem_limit_bytes=16 << 20),
        cost_estimate=cost(0.01),
        name="bias",
    )(starts, table, Order.follow(mask_row))
    return Order.done(outs)


def attn_fwd_kernel(q_ref, k0, k1, k2, k3, bias_ref, p_ref, o_ref, *, inner):
    h = pl.program_id(1)
    at_k = pl.ds(pl.multiple_of(h * DH, DH), DH)
    at_v = pl.ds(pl.multiple_of(inner + h * DH, DH), DH)
    q = q_ref[...]
    parts = [dot_tn(ref[at_k, :], q) for ref in (k0, k1, k2, k3)]
    s = jnp.concatenate(parts, axis=0) + bias_ref[0]
    top = jnp.max(s, axis=0, keepdims=True)
    e = jnp.exp(s - top)
    total = jnp.sum(e, axis=0, keepdims=True)
    p = e * (1.0 / total)
    p_ref[0] = p
    pb = p.astype(BF)
    values = jnp.concatenate([ref[at_v, :] for ref in (k0, k1, k2, k3)], axis=1)
    o_ref[...] = dot(values, pb).astype(BF)


def attn_fwd(q, kvs, bias, heads, block):
    inner, rows = q.shape
    length = bias.shape[1]
    full = lambda i, h: (0, 0)
    slab = pl.BlockSpec((1, length, block), lambda i, h: (h, 0, i))
    head = pl.BlockSpec((DH, block), lambda i, h: (h, i))
    outs = pl.pallas_call(
        functools.partial(attn_fwd_kernel, inner=inner),
        out_shape=(pltpu.HBM((heads, length, rows), F32), sds((inner, rows), BF)),
        grid=(rows // block, heads),
        in_specs=[head] + [pl.BlockSpec(kv.shape, full) for kv in kvs] + [slab],
        out_specs=(slab, head),
        compiler_params=pltpu.CompilerParams(vmem_limit_bytes=14 << 20),
        cost_estimate=cost(0.01),
        name="attn_fwd",
    )(Order.follow(q), *kvs, in_hbm(bias))
    return Order.done(outs)


def diagonals(piece, block):
    total = None
    for shift in range(0, LANES, 8):
        wide = None
        for part in range(block // LANES):
            rows = piece[part * LANES + shift : part * LANES + shift + 8]
            pieces = [jnp.zeros((8, block - part * LANES), F32), rows]
            if part:
                pieces.append(jnp.zeros((8, part * LANES), F32))
            rows = jnp.concatenate(pieces, axis=1)
            wide = rows if wide is None else wide + rows
        if shift:
            wide = pltpu.roll(wide, 2 * block - shift, 1)
        total = wide if total is None else total + wide
    return total


def attn_bwd_kernel(
    start_ref, p_ref, q_ref, do_ref, k0, k1, k2, k3, dq_ref, own_ref, give_ref, col_ref, table_ref,
    acc, col_acc, *, inner, heads, block, q_blocks,
):
    qb = pl.program_id(0)
    h = pl.program_id(1)
    kvs = (k0, k1, k2, k3)
    at_k = pl.ds(pl.multiple_of(h * DH, DH), DH)
    at_v = pl.ds(pl.multiple_of(inner + h * DH, DH), DH)
    half = len(kvs) * block // 2

    @pl.when((qb == 0) & (h == 0))
    def _():
        acc[...] = jnp.zeros_like(acc)
        col_acc[...] = jnp.zeros_like(col_acc)
        table_ref[...] = jnp.zeros_like(table_ref)

    q = q_ref[...]
    do = do_ref[...]
    dp = jnp.concatenate([dot_tn(ref[at_v, :], do) for ref in kvs], axis=0)
    p = p_ref[0]
    inside = jnp.sum(p * dp, axis=0, keepdims=True)
    ds = p * (dp - inside)
    col_acc[...] += ds
    for kb in range(len(kvs)):
        start = pl.multiple_of(start_ref[kb * q_blocks + qb], block)
        piece = ds[kb * block : (kb + 1) * block]
        table_ref[h, :, pl.ds(start, 2 * block)] += diagonals(piece, block)
    dsb = ds.astype(BF)
    pb = p.astype(BF)
    acc[at_k, :] += dot_nt(q, dsb)
    acc[at_v, :] += dot_nt(do, pb)
    keys = jnp.concatenate([ref[at_k, :] for ref in kvs], axis=1)
    dq_ref[...] = dot(keys, dsb).astype(BF)

    @pl.when((qb == q_blocks - 1) & (h == heads - 1))
    def _():
        own_ref[...] = acc[:, :half]
        col = lane_sum(col_acc[...])
        col_ref[...] = col[:, :half]
        give_ref[: 2 * inner] = acc[:, half:].astype(BF)
        give_ref[2 * inner :] = split_rows(col[:, half:])


def split(v):
    high = v.astype(BF)
    return high, (v - high.astype(F32)).astype(BF)


def merge(high, low):
    return high.astype(F32) + low.astype(F32)


def split_rows(row):
    high = row.astype(BF)
    low = (row - high.astype(F32)).astype(BF)
    at = lax.broadcasted_iota(jnp.int32, (EXTRA, row.shape[1]), 0)
    wide = jnp.where(at == 0, high.astype(F32), jnp.where(at == 1, low.astype(F32), 0.0))
    return wide.astype(BF)


def attn_bwd(starts, p, q, do, kvs, heads, block):
    inner, rows = q.shape
    length = p.shape[1]
    half = length // 2
    q_blocks = rows // block
    full = lambda i, h, s: (0, 0)
    head = pl.BlockSpec((DH, block), lambda i, h, s: (h, i))
    outs = pl.pallas_call(
        functools.partial(
            attn_bwd_kernel, inner=inner, heads=heads, block=block, q_blocks=q_blocks
        ),
        out_shape=(
            sds((inner, rows), BF),
            sds((2 * inner, half), F32),
            sds((2 * inner + EXTRA, half), BF),
            sds((1, half), F32),
            sds((heads, 8, 2 * length), F32),
        ),
        grid_spec=pltpu.PrefetchScalarGridSpec(
            num_scalar_prefetch=1,
            grid=(q_blocks, heads),
            in_specs=[pl.BlockSpec((1, length, block), lambda i, h, s: (h, 0, i)), head, head]
            + [pl.BlockSpec(kv.shape, full) for kv in kvs],
            out_specs=(
                head,
                pl.BlockSpec((2 * inner, half), full),
                pl.BlockSpec((2 * inner + EXTRA, half), full),
                pl.BlockSpec((1, half), full),
                pl.BlockSpec((heads, 8, 2 * length), lambda i, h, s: (0, 0, 0)),
            ),
            scratch_shapes=[
                pltpu.VMEM((2 * inner, length), F32),
                pltpu.VMEM((length, block), F32),
            ],
        ),
        compiler_params=pltpu.CompilerParams(vmem_limit_bytes=28 << 20),
        cost_estimate=cost(500),
        name="attn_bwd",
    )(starts, in_hbm(p), Order.follow(q), do, *kvs)
    return Order.done(outs)


def halves(c_ref, half):
    return [pl.ds(pl.multiple_of(at * half, half), half) for at in (c_ref[0], 1 - c_ref[0])]


def mid_kernel(
    c_ref, x_ref, m0_ref, m1_ref, w0_ref, w1_ref, w2_ref, gain_ref, res_ref, n_ref, inv_ref
):
    attended = dot_tn(w0_ref[...], m0_ref[...])
    for at, w_ref in zip(halves(c_ref, w1_ref.shape[0]), (w1_ref, w2_ref)):
        attended = attended + dot_tn(w_ref[...], m1_ref[at, :])
    res = x_ref[...].astype(F32) + attended
    res_ref[...] = res
    inverse = lax.rsqrt(jnp.mean(res * res, axis=0, keepdims=True) + EPS)
    inv_ref[...] = inverse
    n_ref[...] = (res * inverse * column(gain_ref[...], res.shape[1])).astype(BF)


def rms_back(rows, inverse, gain, grad):
    scaled = grad * gain
    inside = jnp.mean(rows * scaled, axis=0, keepdims=True)
    return inverse * scaled - rows * (inverse * inverse * inverse * inside)


def mid_back_kernel(
    c_ref, own_ref, ga_ref, gb_ref, gd_ref, dy_ref, res_ref, inv_ref, gain_ref, w0_ref, w1_ref, w2_ref,
    dres_ref, branch_ref, gain_grad_ref, dm0_ref, dm1_ref,
):
    grad = own_ref[...] + ga_ref[...].astype(F32) + gb_ref[...].astype(F32)
    grad = grad + gd_ref[...].astype(F32)
    res = res_ref[...]
    inverse = inv_ref[...]
    gain_grad_ref[...] = lane_sum(grad * (res * inverse))
    gain = column(gain_ref[...], res.shape[1])
    d_res = dy_ref[...].astype(F32) + rms_back(res, inverse, gain, grad)
    dres_ref[...] = d_res
    branch = d_res.astype(BF)
    branch_ref[...] = branch
    dm0_ref[...] = dot(w0_ref[...], branch).astype(BF)
    for at, w_ref in zip(halves(c_ref, w1_ref.shape[0]), (w1_ref, w2_ref)):
        dm1_ref[at, :] = dot(w_ref[...], branch).astype(BF)


def out_grad_kernel(m0_ref, m1_ref, branch_ref, own_ref, far_ref):
    branch = branch_ref[...]
    own_ref[...] = dot_nt(m0_ref[...], branch)
    far_ref[...] = dot_nt(m1_ref[...], branch).astype(BF)


def ffn_kernel(n_ref, dy_ref, g0, g1, u0, u1, d0, d1, a_ref, dg_ref, du_ref, dn_ref):
    n = n_ref[...]
    dy = dy_ref[...]
    total = None
    for part, (g_w, u_w, d_w) in enumerate(((g0, u0, d0), (g1, u1, d1))):
        gate = dot(g_w[...], n)
        up = dot(u_w[...], n)
        d_act = dot(d_w[...], dy)
        square = gate * gate
        t = jnp.tanh(gate * (GELU_C + (GELU_C * GELU_K) * square))
        half = 0.5 + 0.5 * t
        gelu = gate * half
        slope = half + gelu * (1.0 - t) * (GELU_C + (3.0 * GELU_C * GELU_K) * square)
        a_ref[part] = (gelu * up).astype(BF)
        d_gate = (d_act * up * slope).astype(BF)
        d_up = (d_act * gelu).astype(BF)
        dg_ref[part] = d_gate
        du_ref[part] = d_up
        more = dot_tn(g_w[...], d_gate) + dot_tn(u_w[...], d_up)
        total = more if total is None else total + more
    dn_ref[...] = total.astype(dn_ref.dtype)


def ffn_chunk(n, dy, weights, out_dtype):
    width, rows = n.shape
    hidden = weights[0].shape[0]
    mid = sds((2, hidden, rows), BF)
    return call(
        ffn_kernel,
        (mid, mid, mid, sds((width, rows), out_dtype)),
        (n, dy, *weights),
        "ffn",
        vmem=16,
    )


def ffn_out_kernel(a_ref, d0, d1, o_ref):
    total = dot_tn(d0[...], a_ref[0]) + dot_tn(d1[...], a_ref[1])
    o_ref[...] = total.astype(o_ref.dtype)


def ffn_out(act, d0, d1, dtype):
    _, hidden, rows = act.shape
    width = d0.shape[1]
    return call(
        ffn_out_kernel, sds((width, rows), dtype), (act, d0, d1), "ffn_out",
    )


def wgrad_sum_kernel(*refs):
    out_ref = refs[-1]
    n, pieces, rows, _ = out_ref.shape
    got = refs[-2]
    for at in range(pieces):
        mids, blocks = refs[8 * at : 8 * at + 4], refs[8 * at + 4 : 8 * at + 8]
        total = None
        for mid, block in zip(mids, blocks):
            more = dot_nt(mid[0], block[...])
            total = more if total is None else total + more
        total = (total + got[at].astype(F32)).astype(BF)
        for q in range(n):
            out_ref[q, at] = total[q * rows : (q + 1) * rows]


def wgrad_stack_kernel(part, *refs):
    out_ref = refs[-1]
    for at in range(out_ref.shape[0]):
        mids, rows = refs[8 * at : 8 * at + 4], refs[8 * at + 4 : 8 * at + 8]
        total = None
        for mid, row in zip(mids, rows):
            more = dot_nt(mid[part], row[...])
            total = more if total is None else total + more
        out_ref[at] = total.astype(BF)


def wgrad_give(pieces):
    mids, rows = pieces[0]
    shape = (len(pieces), mids[0].shape[1], rows[0].shape[0])
    args = [v for mids, rows in pieces for v in (*mids, *rows)]
    return call(
        functools.partial(wgrad_stack_kernel, 1), sds(shape, BF), args, "wgrad_give",
        vmem=20,
    )


def wgrad_sum(pieces, got, shares):
    mids, rows = pieces[0]
    shape = (shares, len(pieces), mids[0].shape[1] // shares, rows[0].shape[0])
    args = [v for mids, rows in pieces for v in (*mids, *rows)]
    return call(
        wgrad_sum_kernel, sds(shape, BF), (*args, got), "wgrad_sum", vmem=20,
    )


def q_back_kernel(dq_ref, n0_ref, n1_ref, w_ref, gw_ref, own_ref, far_ref):
    block = n0_ref.shape[1]
    dq0 = dq_ref[:, :block]
    dq1 = dq_ref[:, block:]
    gw_ref[...] = (dot_nt(dq0, n0_ref[...]) + dot_nt(dq1, n1_ref[...])).astype(gw_ref.dtype)
    own_ref[...] = dot_tn(w_ref[...], dq0)
    far_ref[...] = dot_tn(w_ref[...], dq1)


def kv_sum_kernel(
    own_ref, got_ref, col_ref, back_own_ref, back_far_ref, n0_ref, n1_ref, wk_ref, wv_ref,
    gain_ref, gain_ffn_ref, rel_ref, dkv_ref, total_ref, give_ref, small_ref,
):
    inner = wk_ref.shape[0]
    width, block = back_far_ref.shape
    d_kv = (own_ref[...] + got_ref[: 2 * inner].astype(F32)).astype(BF)
    dkv_ref[...] = d_kv
    col = col_ref[...] + merge(got_ref[2 * inner : 2 * inner + 1], got_ref[2 * inner + 1 : 2 * inner + 2])
    far = back_far_ref[...] + dot_tn(wk_ref[...], d_kv[:inner, block:])
    far = far + dot_tn(wv_ref[...], d_kv[inner:, block:])
    give_ref[:width] = far.astype(BF)
    own = back_own_ref[...] + dot_tn(wk_ref[...], d_kv[:inner, :block])
    own = own + dot_tn(wv_ref[...], d_kv[inner:, :block])
    total_ref[...] = own
    gain = lane_sum(own * n0_ref[...].astype(F32) + far * n1_ref[...].astype(F32)) / gain_ref[...]
    small_ref[...] = jnp.zeros_like(small_ref)
    for first, row in ((2, gain), (8, gain_ffn_ref[...])):
        for at in range(0, width, block):
            size = min(block, width - at)
            line = first + at // block
            small_ref[line : line + 1, :size] = row[:, at : at + size]
    small_ref[1:2, : rel_ref.shape[1]] = rel_ref[...]
    small_ref[0:1] = col[:, block:]
    high, low = split(small_ref[...])
    give_ref[width : width + EXTRA] = high
    give_ref[width + EXTRA :] = low
    small_ref[...] = merge(high, low)
    small_ref[0:1] = col[:, :block]


def kv_back_kernel(dkv_ref, n0_ref, n1_ref, gk_ref, gv_ref):
    inner = gk_ref.shape[0]
    block = n0_ref.shape[1]
    for at, out in ((0, gk_ref), (inner, gv_ref)):
        d0 = dkv_ref[at : at + inner, :block]
        d1 = dkv_ref[at : at + inner, block:]
        out[...] = dot_nt(d0, n0_ref[...]) + dot_nt(d1, n1_ref[...])


def last_kernel(
    c_ref, own_ref, got_ref, small_ref, x_ref, inv_ref, gain_ref, dres_ref,
    keep_ref, give_ref, keep_small_ref, rows_ref,
):
    width = x_ref.shape[0]
    grad = own_ref[...] + got_ref[:width].astype(F32)
    small = small_ref[...] + merge(got_ref[width : width + EXTRA], got_ref[width + EXTRA :])
    x = x_ref[...].astype(F32)
    gain = column(gain_ref[...], x.shape[1])
    rows_ref[:width] = dres_ref[...] + rms_back(x, inv_ref[...], gain, grad)
    rows_ref[width:] = small
    rows = keep_ref.shape[1]
    mine = pl.ds(pl.multiple_of(c_ref[0] * rows, rows), rows)
    theirs = pl.ds(pl.multiple_of((1 - c_ref[0]) * rows, rows), rows)
    keep_ref[...] = rows_ref[:width, mine]
    give_ref[:width] = rows_ref[:width, theirs]
    keep_small_ref[:EXTRA] = small[:, :rows]
    keep_small_ref[EXTRA:] = small[:, rows:]
    give_ref[width:] = keep_small_ref[...]
    give_ref[width : width + 1] = rows_ref[width : width + 1, theirs]
    keep_small_ref[0:1] = rows_ref[width : width + 1, mine]


def out_rows_kernel(c_ref, res_ref, own_ref, ga_ref, gb_ref, gd_ref, keep_ref, give_ref, rows_ref):
    total = res_ref[...] + (
        own_ref[...]
        + ga_ref[...].astype(F32)
        + gb_ref[...].astype(F32)
        + gd_ref[...].astype(F32)
    )
    rows_ref[...] = total.astype(BF)
    rows = keep_ref.shape[1]
    keep_ref[...] = rows_ref[:, pl.ds(pl.multiple_of(c_ref[0] * rows, rows), rows)]
    give_ref[...] = rows_ref[:, pl.ds(pl.multiple_of((1 - c_ref[0]) * rows, rows), rows)]


def fold_core_kernel(c_ref, gq_ref, gk_ref, gv_ref, go_ref, got_ref, keep_ref, give_ref):
    out = go_ref[...] + got_ref[...].astype(F32)
    first = c_ref[0] == 0
    keep_ref[0] = jnp.where(first, gq_ref[...], gv_ref[...])
    keep_ref[1] = jnp.where(first, gk_ref[...], out)
    give_ref[0] = jnp.where(first, gv_ref[...], gq_ref[...]).astype(BF)
    give_ref[1] = jnp.where(first, out, gk_ref[...]).astype(BF)


def fold_x_kernel(x_ref, mine_ref, got_ref, keep_ref, give_ref):
    total = mine_ref[...] + got_ref[...].astype(F32)
    first = x_ref[0] == 0
    keep_ref[...] = jnp.where(first, total[0], total[1])
    give_ref[...] = jnp.where(first, total[1], total[0]).astype(BF)


def share_kernel(z_ref, mine_ref, got_ref, sum_ref, own_ref, *give_refs):
    sum_ref[...] = mine_ref[...] + got_ref[...].astype(F32)
    rows = own_ref.shape[0]
    n = len(give_refs) + 1
    for k, out in enumerate((own_ref, *give_refs)):
        at = lax.rem(z_ref[0] + k, n)
        out[...] = sum_ref[pl.ds(pl.multiple_of(at * rows, rows), rows), :].astype(out.dtype)


def lines(small, first, width):
    half = small.shape[0] // 2
    pieces = []
    for at in range(-(-width // (2 * LANES))):
        line = first + at
        pieces += [small[line : line + 1], small[half + line : half + line + 1]]
    return jnp.concatenate(pieces, axis=1)[:, :width]


def share_sum_kernel(own_ref, small_ref, small_got_ref, *refs):
    out_ref = refs[-1]
    rows, width = own_ref.shape
    total = own_ref[...]
    for ref in refs[:-1]:
        total = total + ref[...].astype(F32)
    out_ref[:rows] = total.astype(BF)
    small = small_ref[...] + small_got_ref[...]
    rel = small[1:2]
    rel = jnp.concatenate([rel, small[EXTRA + 1 : EXTRA + 2]], axis=1)
    rel = jnp.concatenate([rel, jnp.zeros((1, width - rel.shape[1]), F32)], axis=1)
    three = jnp.concatenate(
        [lines(small, 2, width), lines(small, 8, width), rel, jnp.zeros((5, width), F32)], axis=0
    )
    out_ref[rows:] = jnp.concatenate(split(three), axis=0)


def share_join_kernel(z_ref, *refs):
    shares, (out_ref, hold_ref) = refs[:-2], refs[-2:]
    n = len(shares)
    rows = shares[0].shape[0] - EXTRA
    for k, ref in enumerate(shares):
        at = lax.rem(z_ref[0] + n - k, n)
        out_ref[pl.ds(pl.multiple_of(at * rows, rows), rows), :] = ref[:rows]
        hold_ref[at] = merge(ref[rows : rows + 8], ref[rows + 8 :])
    total = hold_ref[0]
    for k in range(1, n):
        total = total + hold_ref[k]
    out_ref[n * rows :] = jnp.concatenate(split(total), axis=0)


def join_x_kernel(x_ref, own_ref, got_ref, out_ref, small_ref):
    inner = out_ref.shape[1]
    first = x_ref[0] == 0
    own = own_ref[:inner]
    got = got_ref[:inner]
    out_ref[0] = jnp.where(first, own, got)
    out_ref[1] = jnp.where(first, got, own)
    small_ref[...] = merge(own_ref[inner : inner + 8], own_ref[inner + 8 :]) + merge(
        got_ref[inner : inner + 8], got_ref[inner + 8 :]
    )


def join_core_kernel(c_ref, own_ref, got_ref, *outs):
    first = c_ref[0] == 0
    own = own_ref[...]
    got = got_ref[...]
    pair = (jnp.where(first, own, got), jnp.where(first, got, own))
    for at, out in enumerate(outs):
        out[...] = pair[at // 2][at % 2].astype(F32)


def place_kernel(c_ref, own_ref, got_ref, out_ref):
    out_ref[c_ref[0]] = own_ref[...]
    out_ref[1 - c_ref[0]] = got_ref[: own_ref.shape[0]]


def widen_kernel(src, *outs):
    for at, out in enumerate(outs):
        out[...] = src[0, at].astype(F32)


def widen(v):
    n, pieces, rows, width = v.shape
    outs = pl.pallas_call(
        widen_kernel,
        out_shape=[sds((n * rows, width), F32)] * pieces,
        grid=(n,),
        in_specs=[pl.BlockSpec((1, pieces, rows, width), lambda i: (i, 0, 0, 0))],
        out_specs=[pl.BlockSpec((rows, width), lambda i: (i, 0))] * pieces,
        compiler_params=pltpu.CompilerParams(vmem_limit_bytes=32 << 20),
        cost_estimate=cost(500),
        name="widen",
    )(Order.follow(v))
    return Order.done(outs)


def per_device(*args):
    Order.last = None
    return run(*args)


def run(
    inputs,
    lengths,
    delete_mask,
    buckets,
    gain_attn,
    w_query,
    w_key,
    w_value,
    w_out,
    rel_bias,
    gain_ffn,
    gate_weight,
    up_weight,
    down_weight,
    cotangent,
):
    seqs, row_count, width = inputs.shape
    dp_axis = lax.axis_size("dp")
    heads_axis = lax.axis_size("head")
    hid_axis = lax.axis_size("hid")
    assert seqs == 2 and heads_axis == 2 and hid_axis == 4
    z_at = lax.axis_index("dp")
    h_at = lax.axis_index("head")
    hid_at = lax.axis_index("hid")
    c_at = hid_at % 2
    x_at = hid_at // 2
    length = row_count * heads_axis * hid_axis
    block = 2 * row_count
    inner = w_query.shape[1]
    heads = inner // DH
    hidden = gate_weight.shape[1]
    bucket_count, total_heads = rel_bias.shape
    c_scalar = c_at.astype(jnp.int32).reshape(1)
    x_scalar = x_at.astype(jnp.int32).reshape(1)
    z_scalar = z_at.astype(jnp.int32).reshape(1)

    def core_swap(v, name):
        return move(v, "hid", [(i, i ^ 1) for i in range(hid_axis)], name)

    def x_swap(v, name):
        return move(v, "hid", [(i, i ^ 2) for i in range(hid_axis)], name)

    def y_swap(v, name):
        return move(v, "head", [(0, 1), (1, 0)], name)

    def grid_swap(v, relayed, name):
        pairs = []
        for h in range(heads_axis):
            for i in range(hid_axis):
                along_x = not relayed or i % 2 == 1
                along_y = not relayed or i % 2 == 0
                to = ((1 - h) if along_y else h) * hid_axis + ((i ^ 2) if along_x else i)
                pairs.append((h * hid_axis + i, to))
        return move(v, ("head", "hid"), pairs, name)

    def relay(from_x, from_y, name):
        picked = call(
            pick_kernel, sds(from_x.shape, BF), (from_x, from_y), "pick", scalars=(c_scalar,),
        )
        return grid_swap(picked, True, name)

    def stack(a, b):
        return jnp.concatenate([a, b], axis=0)

    def place(own, got):
        shape = sds((2, *own.shape), own.dtype)
        return call(place_kernel, shape, (own, got), "place", scalars=(c_scalar,), us=100)

    def after(v, *earlier):
        return lax.optimization_barrier((v, *earlier))[0]

    x_in = jnp.swapaxes(inputs, 1, 2)
    dy_in = jnp.swapaxes(cotangent, 1, 2)
    wq, wk, wv = w_query.T, w_key.T, w_value.T
    gate_w, up_w = gate_weight.T, up_weight.T
    gain_one = gain_attn.reshape(1, width)
    gain_two = gain_ffn.reshape(1, width)

    w_half = w_out.reshape(2, inner // 2, width)
    w_half = lax.dynamic_index_in_dim(w_half, c_at, 0, keepdims=False)
    x_rows, normed_one, inv_one = call(
        prep_kernel,
        (sds((width, block), BF), sds((width, block), BF), sds((1, block), F32)),
        (x_in, core_swap(x_in, "x_core"), gain_one),
        "prep",
        scalars=(c_scalar,),
    )
    normed_far_raw = y_swap(normed_one, "n1_y")

    dy_own = call(
        pair_kernel,
        sds((width, block), BF),
        (dy_in, core_swap(dy_in, "dy_core")),
        "pair",
        scalars=(c_scalar,),
    )

    gate_other = core_swap(gate_w, "gate_core")
    up_other = core_swap(up_w, "up_core")
    down_other = core_swap(down_weight, "down_core")
    ffn_weights = (gate_w, gate_other, up_w, up_other, down_weight, down_other)
    def project(n):
        return call(
            qkv_kernel,
            (sds((inner, block), BF), sds((2 * inner, block), BF)),
            (n, wq, wk, wv),
            "qkv",
        )

    q_own, kv_own = project(normed_one)
    base = jnp.stack(
        [(h * 2 + x) * block for x in (x_at, 1 - x_at) for h in (h_at, 1 - h_at)]
    ).astype(jnp.int32)
    starts = (length - block - (base[:, None] - base[None, :2])).reshape(-1).astype(jnp.int32)
    bucket_rev = jnp.concatenate([jnp.full((1,), -1, jnp.int32), buckets[::-1]])
    hot = bucket_rev[None, :] == jnp.arange(bucket_count, dtype=jnp.int32)[:, None]
    local_bias = lax.dynamic_slice_in_dim(rel_bias, h_at * heads, heads, 1)
    table = jnp.sum(jnp.where(hot[None], local_bias.T[:, :, None], 0.0), axis=1)
    table = jnp.concatenate([table, jnp.zeros((8 - heads, 2 * length), F32)], axis=0)
    seq_mask = lax.dynamic_index_in_dim(delete_mask, c_at, 0, keepdims=False)
    seq_len = lax.dynamic_index_in_dim(lengths, c_at, 0, keepdims=False)
    seq_mask = jnp.where(jnp.arange(length, dtype=jnp.int32) < seq_len, seq_mask, NEG)
    seq_mask = seq_mask.reshape(2, 2, block)
    seq_mask = jnp.where(h_at == 0, seq_mask, seq_mask[::-1])
    seq_mask = jnp.where(x_at == 0, seq_mask, seq_mask[:, ::-1])
    seq_mask = jnp.swapaxes(seq_mask, 0, 1).reshape(1, length)
    seq_mask = after(seq_mask, gate_other, up_other)
    bias = make_bias(starts, table, seq_mask, heads, block, 4, 2)

    kv_own_x = x_swap(kv_own, "kv_own_x")
    normed_far_raw = after(normed_far_raw, bias, kv_own)
    normed_far = after(normed_far_raw, down_other, kv_own_x)
    w_half = y_swap(after(w_half, normed_far_raw), "wout_y")
    dy_y = y_swap(after(dy_own, w_half), "dy_y")
    w_half_got = core_swap(w_half, "wout_core")
    q_far, kv_far = project(normed_far)
    kv_far_x = x_swap(kv_far, "kv_far_x")
    dy_x = x_swap(after(dy_own, kv_far_x), "dy_x")
    queries = jnp.concatenate([q_own, q_far], axis=1)
    kvs = (kv_own, kv_far, kv_own_x, kv_far_x)

    probs, mixed = attn_fwd(queries, kvs, bias, heads, block)
    mixed_far = y_swap(mixed[:, block:], "mixed_y")
    dy_d = relay(dy_x, dy_y, "dy_d")
    mixed_own = mixed[:, :block]
    residual, normed_two, inv_two = call(
        mid_kernel,
        (sds((width, block), F32), sds((width, block), BF), sds((1, block), F32)),
        (x_rows, mixed_own, mixed_far, w_out, w_half, w_half_got, gain_two),
        "mid",
        scalars=(c_scalar,),
    )

    n_x = x_swap(normed_two, "n2_x")
    n_y = y_swap(normed_two, "n2_y")
    act_o, dg_o, du_o, dn_o = ffn_chunk(normed_two, dy_own, ffn_weights, F32)
    n_d = relay(n_x, n_y, "n2_d")
    act_x, dg_x, du_x, dn_x = ffn_chunk(n_x, dy_x, ffn_weights, BF)
    got_x = x_swap(dn_x, "dn_x")
    act_y, dg_y, du_y, dn_y = ffn_chunk(n_y, dy_y, ffn_weights, BF)
    got_y = y_swap(dn_y, "dn_y")
    act_d, dg_d, du_d, dn_d = ffn_chunk(n_d, dy_d, ffn_weights, BF)
    got_d = grid_swap(dn_d, False, "dn_d")

    n_all = (normed_two, n_x, n_y, n_d)
    dy_all = (dy_own, dy_x, dy_y, dy_d)
    pieces = (
        ((act_o, act_x, act_y, act_d), dy_all),
        ((dg_o, dg_x, dg_y, dg_d), n_all),
        ((du_o, du_x, du_y, du_d), n_all),
    )
    out_o = ffn_out(act_o, down_weight, down_other, F32)
    mids, rows = pieces[0]
    pieces = (((after(mids[0], got_x, got_y), *mids[1:]), rows), *pieces[1:])
    given = core_swap(wgrad_give(pieces), "wgrad_core")
    part_x = ffn_out(act_x, down_weight, down_other, BF)
    part_y = ffn_out(act_y, down_weight, down_other, BF)
    part_d = ffn_out(act_d, down_weight, down_other, BF)
    shares = dp_axis if dp_axis <= 8 else 1
    ffn_grads = wgrad_sum(pieces, given, shares)
    if shares > 1:
        ffn_grads = lax.psum_scatter(ffn_grads, "dp", scatter_dimension=0, tiled=True)
    else:
        ffn_grads = lax.psum(ffn_grads, "dp")


    d_residual, d_branch, gain_ffn_part, d_mixed_own, d_mixed_give = call(
        mid_back_kernel,
        (
            sds((width, block), F32),
            sds((width, block), BF),
            sds((1, width), F32),
            sds((inner, block), BF),
            sds((inner, block), BF),
        ),
        (dn_o, got_x, got_y, got_d, dy_own, residual, inv_two, gain_two, w_out, w_half, w_half_got),
        "mid_back",
        scalars=(c_scalar,),
    )
    d_mixed = jnp.concatenate([d_mixed_own, y_swap(d_mixed_give, "dmixed_y")], axis=1)

    grad_out_own, grad_out_give = call(
        out_grad_kernel,
        (sds((inner, width), F32), sds((inner, width), BF)),
        (mixed_own, mixed_far, d_branch),
        "out_grad",
    )
    grad_out_got = y_swap(grad_out_give, "gout_y")

    dq, dkv_own, dkv_give, col, table_grad = attn_bwd(
        starts, probs, queries, d_mixed, kvs, heads, block
    )
    dkv_got = x_swap(dkv_give, "dkv_x")
    out_x = x_swap(after(part_x, got_d), "out_x")
    out_y = y_swap(after(part_y, got_d), "out_y")
    dq = after(dq, out_x, out_y)
    dkv_got = after(dkv_got, grad_out_got)
    grad_q, back_own, back_far = call(
        q_back_kernel,
        (sds((inner, width), F32), sds((width, block), F32), sds((width, block), F32)),
        (dq, normed_one, normed_far, wq),
        "q_back",
    )
    table_grad = sum(jnp.roll(table_grad[:, i], -i, axis=1) for i in range(8))
    grad_rel = jnp.sum(jnp.where(hot[None], table_grad[:, None, :], 0.0), axis=2).T
    grad_rel = lax.dynamic_update_slice_in_dim(
        jnp.zeros((bucket_count, total_heads), F32), grad_rel, h_at * heads, 1
    )
    d_kv, back_own, back_give, small = call(
        kv_sum_kernel,
        (
            sds((2 * inner, 2 * block), BF),
            sds((width, block), F32),
            sds((width + 2 * EXTRA, block), BF),
            sds((EXTRA, block), F32),
        ),
        (
            dkv_own, dkv_got, col, back_own, back_far, normed_one, normed_far, wk, wv,
            gain_one, gain_ffn_part, grad_rel.reshape(1, -1),
        ),
        "kv_sum",
    )
    back_got = y_swap(back_give, "back_y")
    grad_k, grad_v = call(
        kv_back_kernel,
        (sds((inner, width), F32), sds((inner, width), F32)),
        (d_kv, normed_one, normed_far),
        "kv_back",
    )

    pair_f32, pair_bf = sds((2, inner, width), F32), sds((2, inner, width), BF)
    one_f32, one_bf = sds((inner, width), F32), sds((inner, width), BF)
    keep, give = call(
        fold_core_kernel,
        (pair_f32, pair_bf),
        (grad_q, grad_k, grad_v, grad_out_own, grad_out_got),
        "fold_core",
        scalars=(c_scalar,),
    )
    keep, give = call(
        fold_x_kernel,
        (one_f32, one_bf),
        (keep, core_swap(give, "fold_core")),
        "fold_x",
        scalars=(x_scalar,),
    )
    got = x_swap(give, "fold_x")
    rows_keep, rows_give, small, _ = call(
        last_kernel,
        (
            sds((width, row_count), F32),
            sds((width + 2 * EXTRA, row_count), F32),
            sds((2 * EXTRA, row_count), F32),
            sds((width + EXTRA, block), F32),
        ),
        (back_own, after(back_got, got), small, x_rows, inv_one, gain_one, d_residual),
        "last",
        scalars=(c_scalar,),
    )
    rows_got = core_swap(rows_give, "grad_core")
    if shares > 1:
        ffn_grads = lax.all_gather(after(ffn_grads, grad_k), "dp", axis=0, tiled=True)
    small_got = rows_got[width:]

    folded, shared = z_sum(keep, got, small, small_got, dp_axis, z_scalar)
    part_d = after(part_d, shared)
    out_d = grid_swap(part_d, False, "out_d")
    out_keep, out_give, _ = call(
        out_rows_kernel,
        (
            sds((width, row_count), BF),
            sds((width, row_count), BF),
            sds((width, block), BF),
        ),
        (residual, out_o, out_x, out_y, out_d),
        "out_rows",
        scalars=(c_scalar,),
    )

    folded, sums = call(
        join_x_kernel,
        (pair_bf, sds((8, width), F32)),
        (folded, x_swap(folded, "join_x")),
        "join_x",
        scalars=(x_scalar,),
    )
    grad_w_query, grad_w_key, grad_w_value, grad_w_out = call(
        join_core_kernel,
        (one_f32,) * 4,
        (folded, core_swap(folded, "join_core")),
        "join_core",
        scalars=(c_scalar,),
    )

    output = place(out_keep, core_swap(out_give, "out_core"))

    grad_inputs = place(rows_keep, rows_got)
    mask_keep, mask_got = small[:1], small_got[:1]
    grad_mask = jnp.where(c_at == 0, stack(mask_keep, mask_got), stack(mask_got, mask_keep))
    grad_down, grad_gate, grad_up = widen(ffn_grads)
    return (
        jnp.swapaxes(output, 1, 2),
        jnp.swapaxes(grad_inputs, 1, 2),
        grad_mask,
        sums[0],
        grad_w_query.T,
        grad_w_key.T,
        grad_w_value.T,
        grad_w_out,
        sums[2, : bucket_count * total_heads].reshape(bucket_count, total_heads),
        sums[1],
        grad_gate.T,
        grad_up.T,
        grad_down,
    )


def z_sum(mine, got, small, small_got, n, z_scalar):
    rows, width = mine.shape
    if n > 8:
        total = lax.psum((mine + got.astype(F32)).astype(BF), "dp")
        small = lax.psum(small + small_got, "dp")
        half = small.shape[0] // 2

        def row(first):
            both = jnp.concatenate([small[first:half], small[half + first :]], axis=1)
            return both.reshape(1, -1)[:, :width]

        three = jnp.concatenate([row(2), row(8), row(1), jnp.zeros((5, width), F32)], axis=0)
        return jnp.concatenate([total, *split(three)], axis=0), mine
    share = rows // n

    def shift(v, k, name):
        return move(v, "dp", [(i, (i + k) % n) for i in range(n)], name)

    _, own, *give = call(
        share_kernel,
        (sds(mine.shape, F32), sds((share, width), F32), *[sds((share, width), BF)] * (n - 1)),
        (mine, got),
        "share",
        scalars=(z_scalar,),
    )
    gots = [shift(v, k + 1, "share_z") for k, v in enumerate(give)]
    total = call(
        share_sum_kernel,
        sds((share + EXTRA, width), BF),
        (own, small, small_got, *gots),
        "share_sum",
    )
    gots = [shift(total, k, "join_z") for k in range(1, n)]
    joined, _ = call(
        share_join_kernel,
        (sds((rows + EXTRA, width), BF), sds((n, 8, width), F32)),
        (total, *gots),
        "share_join",
        scalars=(z_scalar,),
    )
    return joined, own


def solution(mesh):
    rows = P("dp", ("head", "hid"), None)
    return jax.shard_map(
        per_device,
        mesh=mesh,
        in_specs=(
            rows,
            P("dp"),
            P("dp", None),
            P(),
            P(),
            P(None, "head"),
            P(None, "head"),
            P(None, "head"),
            P("head", None),
            P(),
            P(),
            P(None, ("head", "hid")),
            P(None, ("head", "hid")),
            P(("head", "hid"), None),
            rows,
        ),
        out_specs=(
            rows,
            rows,
            P("dp", ("head", "hid")),
            P(),
            P(None, "head"),
            P(None, "head"),
            P(None, "head"),
            P("head", None),
            P(),
            P(),
            P(None, ("head", "hid")),
            P(None, ("head", "hid")),
            P(("head", "hid"), None),
        ),
        check_vma=False,
    )
```

time: 578 us -> 363 us (0.63)
  the two profiles are of different devices: /device:TPU:0 before, /device:TPU:11 now
where the time goes in v2:
time: 363 us; the launch traced here: 358 us
  waiting for transfers between devices  163 us (45%)
  Pallas kernels  94.7 us (26%)
  local copies, waits for them, and re-layouts  46.6 us (13%)
  starting transfers between devices  36.3 us (10%)
  between operations  15.7 us (4%)
    ppermute x40, waiting for transfers between devices, move(): return lax.ppermute(v, axes, pairs)  159 us
    pallas_call x33, Pallas kernels, call(): pl.pallas_call(kernel, out_shape=out_shape, in_specs=in_specs, out_specs=...  65.3 us
    unnamed x191, local copies, waits for them, and re-layouts  39.2 us
    ppermute x40, starting transfers between devices, move(): return lax.ppermute(v, axes, pairs)  36.3 us
    pallas_call x1, Pallas kernels, attn_bwd(): pl.pallas_call(functools.partial(attn_bwd_kernel, inner=inner, heads=head...  10.9 us
    pallas_call x1, Pallas kernels, attn_fwd(): pl.pallas_call(functools.partial(attn_fwd_kernel, inner=inner), out_shape...  9.22 us
  transfers between devices with their start and end apart: 42, of which 24 were waited for; matrix products, arithmetic and copies ran while one was open for 3% of the time, Pallas kernels for 22%

profile of v2, /device:TPU:11, one launch (start us, length us, event | category | flops | bytes accessed | tf_op | source)
XLA Modules:
  0.0 358.3 jit_solution(9581666002730129367)
XLA Ops:
  11.1 1.7 dynamic-slice_bitcast_fusion
  15.9 1.7 prep.1
  22.5 5.9 %bias.1.bias_ref = f32[3,1024,512]{2,1,0:T(8,128)} custom-call(s32[8]{0:T(128)S(1)} %sub.40.start_ref, f32[8,2048]{1,0:T(8,128)S(1)} %concatenate.83.table_ref, f32[1,1024]{1,0:T(1,128)S(1)} %reshape.99.mask_ref), custom_call_target="tpu_custom_call" | custom-call | bytes 30000 | tf_op jit(solution)/shard_map/bias/pallas_call | solution.py:144
  28.3 7.8 %collective-permute-done.2.n_ref.n1_ref = bf16[1472,256]{1,0:T(8,128)(2,1)S(1)} collective-permute-done((bf16[1472,256]{1,0:T(8,128)(2,1)S(1)}, bf16[1472,256]{1,0:T(8,128)(2,1)S(1)}, u32[]{:S(2)}, u32[]{:S(2)}) %collective-permute-start.2) | collective-permute-done | bytes 753696 | tf_op jit(solution)/shard_map/n1_y/ppermute | solution.py:82
  38.4 5.0 %collective-permute-done.7.k3 = bf16[384,256]{1,0:T(8,128)(2,1)S(1)} collective-permute-done((bf16[384,256]{1,0:T(8,128)(2,1)S(1)}, bf16[384,256]{1,0:T(8,128)(2,1)S(1)}, u32[]{:S(2)}, u32[]{:S(2)}) %collective-permute-start.7) | collective-permute-done | bytes 196640 | tf_op jit(solution)/shard_map/kv_far_x/ppermute | solution.py:82
  45.1 9.2 %attn_fwd.1 = (f32[3,1024,512]{2,1,0:T(8,128)}, bf16[192,512]{1,0:T(8,128)(2,1)S(1)}) custom-call(bf16[192,512]{1,0:T(8,128)(2,1)S(1)} %constant_dynamic-update-slice_fusion.q_ref, bf16[384,256]{1,0:T(8,128)(2,1)S(1)} %get-tuple-element.141.k0, bf16[384,256]{1,0:T(8,128)(2,1)S(1)} %get-tuple-element.145.k1, bf16[384,256]{1,0:T(8,128)(2,1)S(1)} %collective-permute-done.6.k2, ...), custom_call_target="tpu_custom_call" | custom-call | bytes 30000 | tf_op jit(solution)/shard_map/attn_fwd/pallas_call | solution.py:186
  54.4 2.1 collective-permute-start.12
  57.2 2.4 collective-permute-done.8.first_ref.dy_ref.refs_5_
  60.1 2.0 collective-permute-done.11.m1_ref
  66.0 1.5 collective-permute-start.16
  67.5 6.5 %ffn.4 = (bf16[2,448,256]{2,1,0:T(8,128)(2,1)S(1)}, bf16[2,448,256]{2,1,0:T(8,128)(2,1)S(1)}, bf16[2,448,256]{2,1,0:T(8,128)(2,1)S(1)}, f32[1472,256]{1,0:T(8,128)S(1)}) custom-call(bf16[1472,256]{1,0:T(8,128)(2,1)S(1)} %get-tuple-element.157.n_ref.refs_12_.refs_20_, bf16[1472,256]{1,0:T(8,128)(2,1)S(1)} %pair.1.dy_ref.refs_4_, ...), custom_call_target="tpu_custom_call" | custom-call | bytes 30000 | tf_op jit(solution)/shard_map/ffn/pallas_call | solution.py:63
  75.1 4.5 %collective-permute-done.13.first_ref.n_ref.refs_13_.refs_21_ = bf16[1472,256]{1,0:T(8,128)(2,1)S(1)} collective-permute-done((bf16[1472,256]{1,0:T(8,128)(2,1)S(1)}, bf16[1472,256]{1,0:T(8,128)(2,1)S(1)}, u32[]{:S(2)}, u32[]{:S(2)}) %collective-permute-start.13) | collective-permute-done | bytes 753696 | tf_op jit(solution)/shard_map/n2_x/ppermute | solution.py:82
  81.3 6.5 %ffn.5 = (bf16[2,448,256]{2,1,0:T(8,128)(2,1)S(1)}, bf16[2,448,256]{2,1,0:T(8,128)(2,1)S(1)}, bf16[2,448,256]{2,1,0:T(8,128)(2,1)S(1)}, bf16[1472,256]{1,0:T(8,128)(2,1)S(1)}) custom-call(bf16[1472,256]{1,0:T(8,128)(2,1)S(1)} %collective-permute-done.13.first_ref.n_ref.refs_13_.refs_21_, ...), custom_call_target="tpu_custom_call" | custom-call | bytes 30000 | tf_op jit(solution)/shard_map/ffn/pallas_call | solution.py:63
  88.2 6.7 %ffn.6 = (bf16[2,448,256]{2,1,0:T(8,128)(2,1)S(1)}, bf16[2,448,256]{2,1,0:T(8,128)(2,1)S(1)}, bf16[2,448,256]{2,1,0:T(8,128)(2,1)S(1)}, bf16[1472,256]{1,0:T(8,128)(2,1)S(1)}) custom-call(bf16[1472,256]{1,0:T(8,128)(2,1)S(1)} %collective-permute-done.14.second_ref.n_ref.refs_14_.refs_22_, ...), custom_call_target="tpu_custom_call" | custom-call | bytes 30000 | tf_op jit(solution)/shard_map/ffn/pallas_call | solution.py:63
  94.9 1.7 collective-permute-start.18
  96.6 3.5 collective-permute-done.15.n_ref.refs_15_.refs_23_
  100.1 6.5 %ffn.7 = (bf16[2,448,256]{2,1,0:T(8,128)(2,1)S(1)}, bf16[2,448,256]{2,1,0:T(8,128)(2,1)S(1)}, bf16[2,448,256]{2,1,0:T(8,128)(2,1)S(1)}, bf16[1472,256]{1,0:T(8,128)(2,1)S(1)}) custom-call(bf16[1472,256]{1,0:T(8,128)(2,1)S(1)} %collective-permute-done.15.n_ref.refs_15_.refs_23_, bf16[1472,256]{1,0:T(8,128)(2,1)S(1)} %collective-permute-done.16.dy_ref.refs_7_, ...), custom_call_target="tpu_custom_call" | custom-call | bytes 30000 | tf_op jit(solution)/shard_map/ffn/pallas_call | solution.py:63
  106.6 9.0 %collective-permute-done.17.ga_ref = bf16[1472,256]{1,0:T(8,128)(2,1)S(1)} collective-permute-done((bf16[1472,256]{1,0:T(8,128)(2,1)S(1)}, bf16[1472,256]{1,0:T(8,128)(2,1)S(1)}, u32[]{:S(2)}, u32[]{:S(2)}) %collective-permute-start.17) | collective-permute-done | bytes 753696 | tf_op jit(solution)/shard_map/dn_x/ppermute | solution.py:82
  117.8 4.6 %wgrad_give.1 = bf16[3,448,1472]{2,1,0:T(8,128)(2,1)S(1)} custom-call(bf16[2,448,256]{2,1,0:T(8,128)(2,1)S(1)} %get-tuple-element.187.a_ref.refs_0_, bf16[2,448,256]{2,1,0:T(8,128)(2,1)S(1)} %get-tuple-element.179.refs_1_.a_ref, bf16[2,448,256]{2,1,0:T(8,128)(2,1)S(1)} %get-tuple-element.182.refs_2_.a_ref, ...), custom_call_target="tpu_custom_call" | custom-call | bytes 30000 | tf_op jit(solution)/shard_map/wgrad_give/pallas_call | solution.py:63
  130.4 4.6 %wgrad_sum.1 = bf16[4,3,112,1472]{3,2,1,0:T(8,128)(2,1)S(1)} custom-call(bf16[2,448,256]{2,1,0:T(8,128)(2,1)S(1)} %get-tuple-element.187.a_ref.refs_0_, bf16[2,448,256]{2,1,0:T(8,128)(2,1)S(1)} %get-tuple-element.179.refs_1_.a_ref, bf16[2,448,256]{2,1,0:T(8,128)(2,1)S(1)} %get-tuple-element.182.refs_2_.a_ref, ...), custom_call_target="tpu_custom_call" | custom-call | bytes 30000 | tf_op jit(solution)/shard_map/wgrad_sum/pallas_call | solution.py:63
  135.0 1.9 copy-done.5
  137.0 2.0 collective-permute-start.19
  139.1 17.2 %collective-permute-done.19.gd_ref = bf16[1472,256]{1,0:T(8,128)(2,1)S(1)} collective-permute-done((bf16[1472,256]{1,0:T(8,128)(2,1)}, bf16[1472,256]{1,0:T(8,128)(2,1)S(1)}, u32[]{:S(2)}, u32[]{:S(2)}) %collective-permute-start.19) | collective-permute-done | bytes 753696 | tf_op jit(solution)/shard_map/dn_d/ppermute | solution.py:82
  157.1 1.5 collective-permute-start.21
  162.2 1.6 mid_back.1
  169.0 7.4 %collective-permute-done.23 = bf16[192,256]{1,0:T(8,128)(2,1)S(1)} collective-permute-done((bf16[192,256]{1,0:T(8,128)(2,1)S(1)}, bf16[192,256]{1,0:T(8,128)(2,1)S(1)}, u32[]{:S(2)}, u32[]{:S(2)}) %collective-permute-start.23) | collective-permute-done | bytes 98336 | tf_op jit(solution)/shard_map/dmixed_y/ppermute | solution.py:82
  176.4 10.9 %attn_bwd.1 = (bf16[192,512]{1,0:T(8,128)(2,1)S(1)}, f32[384,512]{1,0:T(8,128)S(1)}, bf16[400,512]{1,0:T(8,128)(2,1)}, f32[1,512]{1,0:T(1,128)S(1)}, f32[3,8,2048]{2,1,0:T(8,128)S(1)}) custom-call(s32[8]{0:T(128)S(1)} %sub.40.start_ref, f32[3,1024,512]{2,1,0:T(8,128)} %get-tuple-element.185.p_ref, bf16[192,512]{1,0:T(8,128)(2,1)S(1)} %copy-done.37, ...), custom_call_target="tpu_custom_call" | custom-call | bytes 1500000000 | tf_op jit(solution)/shard_map/attn_bwd/pallas_call | solution.py:284
  194.0 5.3 %collective-permute-done.24.got_ref = bf16[400,512]{1,0:T(8,128)(2,1)} collective-permute-done((bf16[400,512]{1,0:T(8,128)(2,1)}, bf16[400,512]{1,0:T(8,128)(2,1)}, u32[]{:S(2)}, u32[]{:S(2)}) %collective-permute-start.24) | collective-permute-done | bytes 409632 | tf_op jit(solution)/shard_map/dkv_x/ppermute | solution.py:82
  202.1 2.5 kv_sum.1
  209.6 3.9 %reduce-scatter.2.cloned.1.call-done = bf16[1,3,112,1472]{3,2,1,0:T(8,128)(2,1)} async-done(((bf16[4,3,112,1472]{3,2,1,0:T(8,128)(2,1)}), bf16[1,3,112,1472]{3,2,1,0:T(8,128)(2,1)}) %reduce-scatter.2.cloned.1.call-update) | async-done | bytes 989200 | tf_op jit(solution)/shard_map/reduce_scatter | solution.py:844
  217.4 1.8 fold_core.1
  220.5 1.5 collective-permute-start.27
  224.1 15.2 %collective-permute-done.27.got_ref = bf16[1504,256]{1,0:T(8,128)(2,1)S(1)} collective-permute-done((bf16[1504,256]{1,0:T(8,128)(2,1)S(1)}, bf16[1504,256]{1,0:T(8,128)(2,1)S(1)}, u32[]{:S(2)}, u32[]{:S(2)}) %collective-permute-start.27) | collective-permute-done | bytes 770080 | tf_op jit(solution)/shard_map/back_y/ppermute | solution.py:82
  240.2 2.2 last.1
  248.7 1.5 collective-permute-start.33
  250.2 7.0 %collective-permute-done.31.refs_0_ = bf16[48,1472]{1,0:T(8,128)(2,1)S(1)} collective-permute-done((bf16[48,1472]{1,0:T(8,128)(2,1)S(1)}, bf16[48,1472]{1,0:T(8,128)(2,1)S(1)}, u32[]{:S(2)}, u32[]{:S(2)}) %collective-permute-start.31) | collective-permute-done | bytes 141344 | tf_op jit(solution)/shard_map/share_z/ppermute | solution.py:82
  257.1 19.8 %collective-permute-done.32.refs_1_ = bf16[48,1472]{1,0:T(8,128)(2,1)S(1)} collective-permute-done((bf16[48,1472]{1,0:T(8,128)(2,1)S(1)}, bf16[48,1472]{1,0:T(8,128)(2,1)S(1)}, u32[]{:S(2)}, u32[]{:S(2)}) %collective-permute-start.32) | collective-permute-done | bytes 141344 | tf_op jit(solution)/shard_map/share_z/ppermute | solution.py:82
  276.9 3.2 collective-permute-done.33.refs_2_
  283.5 10.7 %collective-permute-done.34.refs_1_ = bf16[64,1472]{1,0:T(8,128)(2,1)S(1)} collective-permute-done((bf16[64,1472]{1,0:T(8,128)(2,1)S(1)}, bf16[64,1472]{1,0:T(8,128)(2,1)S(1)}, u32[]{:S(2)}, u32[]{:S(2)}) %collective-permute-start.34) | collective-permute-done | bytes 188448 | tf_op jit(solution)/shard_map/join_z/ppermute | solution.py:82
  294.1 21.2 %collective-permute-done.35.refs_2_ = bf16[64,1472]{1,0:T(8,128)(2,1)S(1)} collective-permute-done((bf16[64,1472]{1,0:T(8,128)(2,1)S(1)}, bf16[64,1472]{1,0:T(8,128)(2,1)S(1)}, u32[]{:S(2)}, u32[]{:S(2)}) %collective-permute-start.35) | collective-permute-done | bytes 188448 | tf_op jit(solution)/shard_map/join_z/ppermute | solution.py:82
  315.4 2.9 collective-permute-done.36.refs_3_
  320.3 1.8 out_rows.1
  322.2 12.4 %collective-permute-done.37.got_ref = bf16[208,1472]{1,0:T(8,128)(2,1)S(1)} collective-permute-done((bf16[208,1472]{1,0:T(8,128)(2,1)S(1)}, bf16[208,1472]{1,0:T(8,128)(2,1)S(1)}, u32[]{:S(2)}, u32[]{:S(2)}) %collective-permute-start.37) | collective-permute-done | bytes 612384 | tf_op jit(solution)/shard_map/join_x/ppermute | solution.py:82
  338.6 1.5 slice_reduce_fusion
  340.1 2.4 join_core.1
  342.5 1.9 place.2
  345.6 2.2 copy-done.21
  347.8 3.4 widen.1
  (320 shorter events, 82.4 us)
Async XLA Ops:
  7.2 206.4 %reduce-scatter.2.cloned.1.call-start = ((), (), s32[]{:S(2)}) async-start(), calls=%async_computation.1 | async-start | bytes 5160960 | tf_op jit(solution)/shard_map/reduce_scatter | solution.py:844
  7.3 7.4 %collective-permute-start = (bf16[2,1472,128]{2,1,0:T(8,128)(2,1)}, bf16[2,1472,128]{2,1,0:T(8,128)(2,1)}, u32[]{:S(2)}, u32[]{:S(2)}) collective-permute-start(bf16[2,1472,128]{2,1,0:T(8,128)(2,1)} %bitcast.98), channel_id=1, source_target_pairs={{0,1},{1,0},{2,3},{3,2},{4,5},{5,4},{6,7},{7,6},{8,9},{9,8},{10,11... | collective-permute-start | bytes 2261000 | tf_op jit(solution)/shard_map/x_core/ppermute | solution.py:82
  8.0 11.1 %collective-permute-start.1 = (bf16[2,1472,128]{2,1,0:T(8,128)(2,1)}, bf16[2,1472,128]{2,1,0:T(8,128)(2,1)S(1)}, u32[]{:S(2)}, u32[]{:S(2)}) collective-permute-start(bf16[2,1472,128]{2,1,0:T(8,128)(2,1)} %bitcast.96), channel_id=1, source_target_pairs={{0,1},{1,0},{2,3},{3,2},{4,5},{5,4},{6,7},{7,6},{8,9},{9,8},{10,11... | collective-permute-start | bytes 2261000 | tf_op jit(solution)/shard_map/dy_core/ppermute | solution.py:82
  8.1 14.4 %collective-permute-start.3 = (bf16[448,1472]{1,0:T(8,128)(2,1)}, bf16[448,1472]{1,0:T(8,128)(2,1)S(1)}, u32[]{:S(2)}, u32[]{:S(2)}) collective-permute-start(bf16[448,1472]{1,0:T(8,128)(2,1)} %bitcast.76), channel_id=1, source_target_pairs={{0,1},{1,0},{2,3},{3,2},{4,5},{5,4},{6,7},{7,6},{8,9},{9,8},{10,11... | collective-permute-start | bytes 3956744 | tf_op jit(solution)/shard_map/gate_core/ppermute | solution.py:82
  8.5 14.0 %collective-permute-start.4 = (bf16[448,1472]{1,0:T(8,128)(2,1)}, bf16[448,1472]{1,0:T(8,128)(2,1)}, u32[]{:S(2)}, u32[]{:S(2)}) collective-permute-start(bf16[448,1472]{1,0:T(8,128)(2,1)} %bitcast.81), channel_id=1, source_target_pairs={{0,1},{1,0},{2,3},{3,2},{4,5},{5,4},{6,7},{7,6},{8,9},{9,8},{10,11... | collective-permute-start | bytes 3956744 | tf_op jit(solution)/shard_map/up_core/ppermute | solution.py:82
  8.6 28.8 %collective-permute-start.5 = (bf16[448,1472]{1,0:T(8,128)(2,1)}, bf16[448,1472]{1,0:T(8,128)(2,1)S(1)}, u32[]{:S(2)}, u32[]{:S(2)}) collective-permute-start(bf16[448,1472]{1,0:T(8,128)(2,1)} %d0.15), channel_id=1, source_target_pairs={{0,1},{1,0},{2,3},{3,2},{4,5},{5,4},{6,7},{7,6},{8,9},{9,8},{10,11... | collective-permute-start | bytes 3956744 | tf_op jit(solution)/shard_map/down_core/ppermute | solution.py:82
  17.6 44.5 %copy-start.24 = (bf16[1472,256]{1,0:T(8,128)(2,1)}, bf16[1472,256]{1,0:T(8,128)(2,1)S(1)}, u32[]{:S(2)}) copy-start(bf16[1472,256]{1,0:T(8,128)(2,1)S(1)} %get-tuple-element.153.x_ref) | copy-start | bytes 2260996
  17.7 18.5 %collective-permute-start.2 = (bf16[1472,256]{1,0:T(8,128)(2,1)S(1)}, bf16[1472,256]{1,0:T(8,128)(2,1)S(1)}, u32[]{:S(2)}, u32[]{:S(2)}) collective-permute-start(bf16[1472,256]{1,0:T(8,128)(2,1)S(1)} %get-tuple-element.138.n_ref.n0_ref), channel_id=1, source_target_pairs={{0,4},{4,0},{1,5},{5,1},{2,6},{6,2},{3,7},{7,3},{8,12},{12,8},{9,1... | collective-permute-start | bytes 2261000 | tf_op jit(solution)/shard_map/n1_y/ppermute | solution.py:82
  21.9 23.2 %copy-start.52 = (bf16[384,256]{1,0:T(8,128)(2,1)}, bf16[384,256]{1,0:T(8,128)(2,1)S(1)}, u32[]{:S(2)}) copy-start(bf16[384,256]{1,0:T(8,128)(2,1)S(1)} %get-tuple-element.141.k0) | copy-start | bytes 589828
  21.9 15.5 %collective-permute-start.6 = (bf16[384,256]{1,0:T(8,128)(2,1)S(1)}, bf16[384,256]{1,0:T(8,128)(2,1)S(1)}, u32[]{:S(2)}, u32[]{:S(2)}) collective-permute-start(bf16[384,256]{1,0:T(8,128)(2,1)S(1)} %get-tuple-element.141.k0), channel_id=1, source_target_pairs={{0,2},{1,3},{2,0},{3,1},{4,6},{5,7},{6,4},{7,5},{8,10},{9,11},{10,... | collective-permute-start | bytes 589832 | tf_op jit(solution)/shard_map/kv_own_x/ppermute | solution.py:82
  36.1 7.7 %collective-permute-start.9 = (bf16[96,1472]{1,0:T(8,128)(2,1)S(1)}, bf16[96,1472]{1,0:T(8,128)(2,1)S(1)}, u32[]{:S(2)}, u32[]{:S(2)}) collective-permute-start(bf16[96,1472]{1,0:T(8,128)(2,1)S(1)} %copy-done.90), channel_id=1, source_target_pairs={{0,4},{4,0},{1,5},{5,1},{2,6},{6,2},{3,7},{7,3},{8,12},{12,8},{9,1... | collective-permute-start | bytes 847880 | tf_op jit(solution)/shard_map/wout_y/ppermute | solution.py:82
  38.0 5.3 %collective-permute-start.7 = (bf16[384,256]{1,0:T(8,128)(2,1)S(1)}, bf16[384,256]{1,0:T(8,128)(2,1)S(1)}, u32[]{:S(2)}, u32[]{:S(2)}) collective-permute-start(bf16[384,256]{1,0:T(8,128)(2,1)S(1)} %get-tuple-element.145.k1), channel_id=1, source_target_pairs={{0,2},{1,3},{2,0},{3,1},{4,6},{5,7},{6,4},{7,5},{8,10},{9,11},{10,... | collective-permute-start | bytes 589832 | tf_op jit(solution)/shard_map/kv_far_x/ppermute | solution.py:82
  43.4 16.3 %collective-permute-start.8 = (bf16[1472,256]{1,0:T(8,128)(2,1)S(1)}, bf16[1472,256]{1,0:T(8,128)(2,1)S(1)}, u32[]{:S(2)}, u32[]{:S(2)}) collective-permute-start(bf16[1472,256]{1,0:T(8,128)(2,1)S(1)} %pair.1.dy_ref.refs_4_), channel_id=1, source_target_pairs={{0,2},{1,3},{2,0},{3,1},{4,6},{5,7},{6,4},{7,5},{8,10},{9,11},{10,... | collective-permute-start | bytes 2261000 | tf_op jit(solution)/shard_map/dy_x/ppermute | solution.py:82
  43.8 16.2 %collective-permute-start.10 = (bf16[1472,256]{1,0:T(8,128)(2,1)S(1)}, bf16[1472,256]{1,0:T(8,128)(2,1)S(1)}, u32[]{:S(2)}, u32[]{:S(2)}) collective-permute-start(bf16[1472,256]{1,0:T(8,128)(2,1)S(1)} %pair.1.dy_ref.refs_4_), channel_id=1, source_target_pairs={{0,4},{4,0},{1,5},{5,1},{2,6},{6,2},{3,7},{7,3},{8,12},{12,8},{9,1... | collective-permute-start | bytes 2261000 | tf_op jit(solution)/shard_map/dy_y/ppermute | solution.py:82
  54.4 7.7 %collective-permute-start.12 = (bf16[96,1472]{1,0:T(8,128)(2,1)S(1)}, bf16[96,1472]{1,0:T(8,128)(2,1)S(1)}, u32[]{:S(2)}, u32[]{:S(2)}) collective-permute-start(bf16[96,1472]{1,0:T(8,128)(2,1)S(1)} %collective-permute-done.9.w1_ref), channel_id=1, source_target_pairs={{0,1},{1,0},{2,3},{3,2},{4,5},{5,4},{6,7},{7,6},{8,9},{9,8},{10,11... | collective-permute-start | bytes 847880 | tf_op jit(solution)/shard_map/wout_core/ppermute | solution.py:82
  56.5 5.6 %collective-permute-start.11 = (bf16[192,256]{1,0:T(8,128)(2,1)S(1)}, bf16[192,256]{1,0:T(8,128)(2,1)S(1)}, u32[]{:S(2)}, u32[]{:S(2)}) collective-permute-start(bf16[192,256]{1,0:T(8,128)(2,1)S(1)} %get-tuple-element.312), channel_id=1, source_target_pairs={{0,4},{4,0},{1,5},{5,1},{2,6},{6,2},{3,7},{7,3},{8,12},{12,8},{9,1... | collective-permute-start | bytes 294920 | tf_op jit(solution)/shard_map/mixed_y/ppermute | solution.py:82
  64.4 15.2 %collective-permute-start.13 = (bf16[1472,256]{1,0:T(8,128)(2,1)S(1)}, bf16[1472,256]{1,0:T(8,128)(2,1)S(1)}, u32[]{:S(2)}, u32[]{:S(2)}) collective-permute-start(bf16[1472,256]{1,0:T(8,128)(2,1)S(1)} %get-tuple-element.157.n_ref.refs_12_.refs_20_), channel_id=1, source_target_pairs={{0,2},{1,3},{2,0},{3,1},{4,6},{5,7},{6,4},{7,5},{8,10},{9,11},{10,... | collective-permute-start | bytes 2261000 | tf_op jit(solution)/shard_map/n2_x/ppermute | solution.py:82
  65.2 14.8 %collective-permute-start.14 = (bf16[1472,256]{1,0:T(8,128)(2,1)S(1)}, bf16[1472,256]{1,0:T(8,128)(2,1)S(1)}, u32[]{:S(2)}, u32[]{:S(2)}) collective-permute-start(bf16[1472,256]{1,0:T(8,128)(2,1)S(1)} %get-tuple-element.157.n_ref.refs_12_.refs_20_), channel_id=1, source_target_pairs={{0,4},{4,0},{1,5},{5,1},{2,6},{6,2},{3,7},{7,3},{8,12},{12,8},{9,1... | collective-permute-start | bytes 2261000 | tf_op jit(solution)/shard_map/n2_y/ppermute | solution.py:82
  66.0 34.1 %collective-permute-start.16 = (bf16[1472,256]{1,0:T(8,128)(2,1)S(1)}, bf16[1472,256]{1,0:T(8,128)(2,1)S(1)}, u32[]{:S(2)}, u32[]{:S(2)}) collective-permute-start(bf16[1472,256]{1,0:T(8,128)(2,1)S(1)} %pick.2), channel_id=1, source_target_pairs={{0,4},{1,3},{2,6},{3,1},{4,0},{5,7},{6,2},{7,5},{8,12},{9,11},{10,... | collective-permute-start | bytes 2261000 | tf_op jit(solution)/shard_map/dy_d/ppermute | solution.py:82
  80.1 20.0 %collective-permute-start.15 = (bf16[1472,256]{1,0:T(8,128)(2,1)S(1)}, bf16[1472,256]{1,0:T(8,128)(2,1)S(1)}, u32[]{:S(2)}, u32[]{:S(2)}) collective-permute-start(bf16[1472,256]{1,0:T(8,128)(2,1)S(1)} %pick.3), channel_id=1, source_target_pairs={{0,4},{1,3},{2,6},{3,1},{4,0},{5,7},{6,2},{7,5},{8,12},{9,11},{10,... | collective-permute-start | bytes 2261000 | tf_op jit(solution)/shard_map/n2_d/ppermute | solution.py:82
  87.8 27.7 %collective-permute-start.17 = (bf16[1472,256]{1,0:T(8,128)(2,1)S(1)}, bf16[1472,256]{1,0:T(8,128)(2,1)S(1)}, u32[]{:S(2)}, u32[]{:S(2)}) collective-permute-start(bf16[1472,256]{1,0:T(8,128)(2,1)S(1)} %get-tuple-element.167), channel_id=1, source_target_pairs={{0,2},{1,3},{2,0},{3,1},{4,6},{5,7},{6,4},{7,5},{8,10},{9,11},{10,... | collective-permute-start | bytes 2261000 | tf_op jit(solution)/shard_map/dn_x/ppermute | solution.py:82
  94.9 20.7 %collective-permute-start.18 = (bf16[1472,256]{1,0:T(8,128)(2,1)S(1)}, bf16[1472,256]{1,0:T(8,128)(2,1)S(1)}, u32[]{:S(2)}, u32[]{:S(2)}) collective-permute-start(bf16[1472,256]{1,0:T(8,128)(2,1)S(1)} %get-tuple-element.168), channel_id=1, source_target_pairs={{0,4},{4,0},{1,5},{5,1},{2,6},{6,2},{3,7},{7,3},{8,12},{12,8},{9,1... | collective-permute-start | bytes 2261000 | tf_op jit(solution)/shard_map/dn_y/ppermute | solution.py:82
  122.4 8.0 %collective-permute-start.22 = (bf16[3,448,1472]{2,1,0:T(8,128)(2,1)S(1)}, bf16[3,448,1472]{2,1,0:T(8,128)(2,1)S(1)}, u32[]{:S(2)}, u32[]{:S(2)}) collective-permute-start(bf16[3,448,1472]{2,1,0:T(8,128)(2,1)S(1)} %wgrad_give.1), channel_id=1, source_target_pairs={{0,1},{1,0},{2,3},{3,2},{4,5},{5,4},{6,7},{7,6},{8,9},{9,8},{10,11... | collective-permute-start | bytes 11870216 | tf_op jit(solution)/shard_map/wgrad_core/ppermute | solution.py:82
  137.0 208.6 %all-gather.2.cloned.1.call-start = ((), (), s32[]{:S(2)}) async-start(), calls=%async_computation.2 | async-start | bytes 5160960 | tf_op jit(solution)/shard_map/all_gather | solution.py:944
  137.0 19.2 %collective-permute-start.19 = (bf16[1472,256]{1,0:T(8,128)(2,1)}, bf16[1472,256]{1,0:T(8,128)(2,1)S(1)}, u32[]{:S(2)}, u32[]{:S(2)}) collective-permute-start(bf16[1472,256]{1,0:T(8,128)(2,1)} %copy-done.87), channel_id=1, source_target_pairs={{0,6},{1,7},{2,4},{3,5},{4,2},{5,3},{6,0},{7,1},{8,14},{9,15},{10,... | collective-permute-start | bytes 2261000 | tf_op jit(solution)/shard_map/dn_d/ppermute | solution.py:82
  156.3 31.3 %collective-permute-start.20 = (bf16[1472,256]{1,0:T(8,128)(2,1)}, bf16[1472,256]{1,0:T(8,128)(2,1)S(1)}, u32[]{:S(2)}, u32[]{:S(2)}) collective-permute-start(bf16[1472,256]{1,0:T(8,128)(2,1)} %copy-done.69), channel_id=1, source_target_pairs={{0,2},{1,3},{2,0},{3,1},{4,6},{5,7},{6,4},{7,5},{8,10},{9,11},{10,... | collective-permute-start | bytes 2261000 | tf_op jit(solution)/shard_map/out_x/ppermute | solution.py:82
  157.1 30.5 %collective-permute-start.21 = (bf16[1472,256]{1,0:T(8,128)(2,1)}, bf16[1472,256]{1,0:T(8,128)(2,1)S(1)}, u32[]{:S(2)}, u32[]{:S(2)}) collective-permute-start(bf16[1472,256]{1,0:T(8,128)(2,1)} %copy-done.68), channel_id=1, source_target_pairs={{0,4},{4,0},{1,5},{5,1},{2,6},{6,2},{3,7},{7,3},{8,12},{12,8},{9,1... | collective-permute-start | bytes 2261000 | tf_op jit(solution)/shard_map/out_y/ppermute | solution.py:82
  165.0 11.4 %collective-permute-start.23 = (bf16[192,256]{1,0:T(8,128)(2,1)S(1)}, bf16[192,256]{1,0:T(8,128)(2,1)S(1)}, u32[]{:S(2)}, u32[]{:S(2)}) collective-permute-start(bf16[192,256]{1,0:T(8,128)(2,1)S(1)} %get-tuple-element.195), channel_id=1, source_target_pairs={{0,4},{4,0},{1,5},{5,1},{2,6},{6,2},{3,7},{7,3},{8,12},{12,8},{9,1... | collective-permute-start | bytes 294920 | tf_op jit(solution)/shard_map/dmixed_y/ppermute | solution.py:82
  167.5 31.8 %collective-permute-start.25 = (bf16[192,1472]{1,0:T(8,128)(2,1)}, bf16[192,1472]{1,0:T(8,128)(2,1)}, u32[]{:S(2)}, u32[]{:S(2)}) collective-permute-start(bf16[192,1472]{1,0:T(8,128)(2,1)} %get-tuple-element.204), channel_id=1, source_target_pairs={{0,4},{4,0},{1,5},{5,1},{2,6},{6,2},{3,7},{7,3},{8,12},{12,8},{9,1... | collective-permute-start | bytes 1695752 | tf_op jit(solution)/shard_map/gout_y/ppermute | solution.py:82
  191.9 7.4 %collective-permute-start.24 = (bf16[400,512]{1,0:T(8,128)(2,1)}, bf16[400,512]{1,0:T(8,128)(2,1)}, u32[]{:S(2)}, u32[]{:S(2)}) collective-permute-start(bf16[400,512]{1,0:T(8,128)(2,1)} %get-tuple-element.203), channel_id=1, source_target_pairs={{0,2},{1,3},{2,0},{3,1},{4,6},{5,7},{6,4},{7,5},{8,10},{9,11},{10,... | collective-permute-start | bytes 1228808 | tf_op jit(solution)/shard_map/dkv_x/ppermute | solution.py:82
  219.3 3.8 %collective-permute-start.26 = (bf16[2,192,1472]{2,1,0:T(8,128)(2,1)S(1)}, bf16[2,192,1472]{2,1,0:T(8,128)(2,1)S(1)}, u32[]{:S(2)}, u32[]{:S(2)}) collective-permute-start(bf16[2,192,1472]{2,1,0:T(8,128)(2,1)S(1)} %get-tuple-element.216), channel_id=1, source_target_pairs={{0,1},{1,0},{2,3},{3,2},{4,5},{5,4},{6,7},{7,6},{8,9},{9,8},{10,11... | collective-permute-start | bytes 3391496 | tf_op jit(solution)/shard_map/fold_core/ppermute | solution.py:82
  220.5 18.8 %collective-permute-start.27 = (bf16[1504,256]{1,0:T(8,128)(2,1)S(1)}, bf16[1504,256]{1,0:T(8,128)(2,1)S(1)}, u32[]{:S(2)}, u32[]{:S(2)}) collective-permute-start(bf16[1504,256]{1,0:T(8,128)(2,1)S(1)} %copy-done.86), channel_id=1, source_target_pairs={{0,4},{4,0},{1,5},{5,1},{2,6},{6,2},{3,7},{7,3},{8,12},{12,8},{9,1... | collective-permute-start | bytes 2310152 | tf_op jit(solution)/shard_map/back_y/ppermute | solution.py:82
  223.3 16.0 %collective-permute-start.28 = (bf16[192,1472]{1,0:T(8,128)(2,1)S(1)}, bf16[192,1472]{1,0:T(8,128)(2,1)S(1)}, u32[]{:S(2)}, u32[]{:S(2)}) collective-permute-start(bf16[192,1472]{1,0:T(8,128)(2,1)S(1)} %get-tuple-element.221), channel_id=1, source_target_pairs={{0,2},{1,3},{2,0},{3,1},{4,6},{5,7},{6,4},{7,5},{8,10},{9,11},{10,... | collective-permute-start | bytes 1695752 | tf_op jit(solution)/shard_map/fold_x/ppermute | solution.py:82
  240.1 42.1 %copy-start.67 = (bf16[1472,256]{1,0:T(8,128)(2,1)S(1)}, bf16[1472,256]{1,0:T(8,128)(2,1)}, u32[]{:S(2)}) copy-start(bf16[1472,256]{1,0:T(8,128)(2,1)} %copy-done.66) | copy-start | bytes 2260996
  240.1 79.1 %copy-start.71 = (bf16[1472,256]{1,0:T(8,128)(2,1)S(1)}, bf16[1472,256]{1,0:T(8,128)(2,1)}, u32[]{:S(2)}) copy-start(bf16[1472,256]{1,0:T(8,128)(2,1)} %copy-done.70) | copy-start | bytes 2260996
  243.2 6.9 %collective-permute-start.30 = (f32[1504,128]{1,0:T(8,128)}, f32[1504,128]{1,0:T(8,128)S(1)}, u32[]{:S(2)}, u32[]{:S(2)}) collective-permute-start(f32[1504,128]{1,0:T(8,128)} %get-tuple-element.230), channel_id=1, source_target_pairs={{0,1},{1,0},{2,3},{3,2},{4,5},{5,4},{6,7},{7,6},{8,9},{9,8},{10,11... | collective-permute-start | bytes 2310152 | tf_op jit(solution)/shard_map/grad_core/ppermute | solution.py:82
  245.2 74.1 %copy-start.12 = (f32[1472,256]{1,0:T(8,128)S(1)}, f32[1472,256]{1,0:T(8,128)}, u32[]{:S(2)}) copy-start(f32[1472,256]{1,0:T(8,128)} %copy-done.10) | copy-start | bytes 4521988
  245.2 74.1 %copy-start.14 = (f32[1472,256]{1,0:T(8,128)S(1)}, f32[1472,256]{1,0:T(8,128)}, u32[]{:S(2)}) copy-start(f32[1472,256]{1,0:T(8,128)} %copy-done.13) | copy-start | bytes 4521988
  246.4 10.8 %collective-permute-start.31 = (bf16[48,1472]{1,0:T(8,128)(2,1)S(1)}, bf16[48,1472]{1,0:T(8,128)(2,1)S(1)}, u32[]{:S(2)}, u32[]{:S(2)}) collective-permute-start(bf16[48,1472]{1,0:T(8,128)(2,1)S(1)} %get-tuple-element.231), channel_id=1, source_target_pairs={{0,8},{8,16},{16,24},{24,0},{1,9},{9,17},{17,25},{25,1},{2,10},{10... | collective-permute-start | bytes 423944 | tf_op jit(solution)/shard_map/share_z/ppermute | solution.py:82
  247.7 29.2 %collective-permute-start.32 = (bf16[48,1472]{1,0:T(8,128)(2,1)S(1)}, bf16[48,1472]{1,0:T(8,128)(2,1)S(1)}, u32[]{:S(2)}, u32[]{:S(2)}) collective-permute-start(bf16[48,1472]{1,0:T(8,128)(2,1)S(1)} %get-tuple-element.232), channel_id=1, source_target_pairs={{0,16},{8,24},{16,0},{24,8},{1,17},{9,25},{17,1},{25,9},{2,18},{10... | collective-permute-start | bytes 423944 | tf_op jit(solution)/shard_map/share_z/ppermute | solution.py:82
  248.7 31.4 %collective-permute-start.33 = (bf16[48,1472]{1,0:T(8,128)(2,1)S(1)}, bf16[48,1472]{1,0:T(8,128)(2,1)S(1)}, u32[]{:S(2)}, u32[]{:S(2)}) collective-permute-start(bf16[48,1472]{1,0:T(8,128)(2,1)S(1)} %get-tuple-element.233), channel_id=1, source_target_pairs={{0,24},{8,0},{16,8},{24,16},{1,25},{9,1},{17,9},{25,17},{2,26},{10... | collective-permute-start | bytes 423944 | tf_op jit(solution)/shard_map/share_z/ppermute | solution.py:82
  280.2 13.9 %collective-permute-start.34 = (bf16[64,1472]{1,0:T(8,128)(2,1)S(1)}, bf16[64,1472]{1,0:T(8,128)(2,1)S(1)}, u32[]{:S(2)}, u32[]{:S(2)}) collective-permute-start(bf16[64,1472]{1,0:T(8,128)(2,1)S(1)} %share_sum.1.refs_0_), channel_id=1, source_target_pairs={{0,8},{8,16},{16,24},{24,0},{1,9},{9,17},{17,25},{25,1},{2,10},{10... | collective-permute-start | bytes 565256 | tf_op jit(solution)/shard_map/join_z/ppermute | solution.py:82
  280.3 35.1 %collective-permute-start.35 = (bf16[64,1472]{1,0:T(8,128)(2,1)S(1)}, bf16[64,1472]{1,0:T(8,128)(2,1)S(1)}, u32[]{:S(2)}, u32[]{:S(2)}) collective-permute-start(bf16[64,1472]{1,0:T(8,128)(2,1)S(1)} %share_sum.1.refs_0_), channel_id=1, source_target_pairs={{0,16},{8,24},{16,0},{24,8},{1,17},{9,25},{17,1},{25,9},{2,18},{10... | collective-permute-start | bytes 565256 | tf_op jit(solution)/shard_map/join_z/ppermute | solution.py:82
  280.9 37.4 %collective-permute-start.36 = (bf16[64,1472]{1,0:T(8,128)(2,1)S(1)}, bf16[64,1472]{1,0:T(8,128)(2,1)S(1)}, u32[]{:S(2)}, u32[]{:S(2)}) collective-permute-start(bf16[64,1472]{1,0:T(8,128)(2,1)S(1)} %share_sum.1.refs_0_), channel_id=1, source_target_pairs={{0,24},{8,0},{16,8},{24,16},{1,25},{9,1},{17,9},{25,17},{2,26},{10... | collective-permute-start | bytes 565256 | tf_op jit(solution)/shard_map/join_z/ppermute | solution.py:82
  282.3 36.9 %collective-permute-start.29 = (bf16[1472,256]{1,0:T(8,128)(2,1)S(1)}, bf16[1472,256]{1,0:T(8,128)(2,1)S(1)}, u32[]{:S(2)}, u32[]{:S(2)}) collective-permute-start(bf16[1472,256]{1,0:T(8,128)(2,1)S(1)} %copy-done.67), channel_id=1, source_target_pairs={{0,6},{1,7},{2,4},{3,5},{4,2},{5,3},{6,0},{7,1},{8,14},{9,15},{10,... | collective-permute-start | bytes 2261000 | tf_op jit(solution)/shard_map/out_d/ppermute | solution.py:82
  319.0 15.6 %collective-permute-start.37 = (bf16[208,1472]{1,0:T(8,128)(2,1)S(1)}, bf16[208,1472]{1,0:T(8,128)(2,1)S(1)}, u32[]{:S(2)}, u32[]{:S(2)}) collective-permute-start(bf16[208,1472]{1,0:T(8,128)(2,1)S(1)} %get-tuple-element.236.own_ref), channel_id=1, source_target_pairs={{0,2},{1,3},{2,0},{3,1},{4,6},{5,7},{6,4},{7,5},{8,10},{9,11},{10,... | collective-permute-start | bytes 1837064 | tf_op jit(solution)/shard_map/join_x/ppermute | solution.py:82
  335.3 4.8 %collective-permute-start.38 = (bf16[2,192,1472]{2,1,0:T(8,128)(2,1)S(1)}, bf16[2,192,1472]{2,1,0:T(8,128)(2,1)S(1)}, u32[]{:S(2)}, u32[]{:S(2)}) collective-permute-start(bf16[2,192,1472]{2,1,0:T(8,128)(2,1)S(1)} %get-tuple-element.237.own_ref), channel_id=1, source_target_pairs={{0,1},{1,0},{2,3},{3,2},{4,5},{5,4},{6,7},{7,6},{8,9},{9,8},{10,11... | collective-permute-start | bytes 3391496 | tf_op jit(solution)/shard_map/join_core/ppermute | solution.py:82
  336.5 6.0 %collective-permute-start.39 = (bf16[1472,128]{1,0:T(8,128)(2,1)}, bf16[1472,128]{1,0:T(8,128)(2,1)}, u32[]{:S(2)}, u32[]{:S(2)}) collective-permute-start(bf16[1472,128]{1,0:T(8,128)(2,1)} %get-tuple-element.240), channel_id=1, source_target_pairs={{0,1},{1,0},{2,3},{3,2},{4,5},{5,4},{6,7},{7,6},{8,9},{9,8},{10,11... | collective-permute-start | bytes 1130504 | tf_op jit(solution)/shard_map/out_core/ppermute | solution.py:82
  (87 other events, 552.0 us)
Sparse Core Ops, SparseCore 0:
  137.1 76.4 reduce-scatter.1
  215.2 105.9 all-gather.1

commit v3 on v2

--- a/solution.py
+++ b/solution.py
@@ -71,6 +71,10 @@
         **kw,
     )(*scalars, *args)
     return Order.done(outs)
+
+
+def hbm(shape, dtype):
+    return pltpu.HBM(shape, dtype)
 
 
 def in_hbm(v):
@@ -287,8 +291,8 @@
         ),
         out_shape=(
             sds((inner, rows), BF),
-            sds((2 * inner, half), F32),
-            sds((2 * inner + EXTRA, half), BF),
+            hbm((2 * inner, half), F32),
+            hbm((2 * inner + EXTRA, half), BF),
             sds((1, half), F32),
             sds((heads, 8, 2 * length), F32),
         ),
@@ -343,7 +347,7 @@
     c_ref, own_ref, ga_ref, gb_ref, gd_ref, dy_ref, res_ref, inv_ref, gain_ref, w0_ref, w1_ref, w2_ref,
     dres_ref, branch_ref, gain_grad_ref, dm0_ref, dm1_ref,
 ):
-    grad = own_ref[...] + ga_ref[...].astype(F32) + gb_ref[...].astype(F32)
+    grad = own_ref[...].astype(F32) + ga_ref[...].astype(F32) + gb_ref[...].astype(F32)
     grad = grad + gd_ref[...].astype(F32)
     res = res_ref[...]
     inverse = inv_ref[...]
@@ -364,14 +368,19 @@
     far_ref[...] = dot_nt(m1_ref[...], branch).astype(BF)
 
 
-def ffn_kernel(n_ref, dy_ref, g0, g1, u0, u1, d0, d1, a_ref, dg_ref, du_ref, dn_ref):
+def d_act_kernel(dy_ref, d0, d1, out_ref):
+    dy = dy_ref[...]
+    for part, w_ref in enumerate((d0, d1)):
+        out_ref[part] = dot(w_ref[...], dy)
+
+
+def ffn_kernel(n_ref, da_ref, g0, g1, u0, u1, a_ref, dg_ref, du_ref, dn_ref):
     n = n_ref[...]
-    dy = dy_ref[...]
     total = None
-    for part, (g_w, u_w, d_w) in enumerate(((g0, u0, d0), (g1, u1, d1))):
+    for part, (g_w, u_w) in enumerate(((g0, u0), (g1, u1))):
         gate = dot(g_w[...], n)
         up = dot(u_w[...], n)
-        d_act = dot(d_w[...], dy)
+        d_act = da_ref[part]
         square = gate * gate
         t = jnp.tanh(gate * (GELU_C + (GELU_C * GELU_K) * square))
         half = 0.5 + 0.5 * t
@@ -387,16 +396,16 @@
     dn_ref[...] = total.astype(dn_ref.dtype)
 
 
-def ffn_chunk(n, dy, weights, out_dtype):
+def ffn_chunk(n, d_act, weights, out_dtype):
     width, rows = n.shape
     hidden = weights[0].shape[0]
     mid = sds((2, hidden, rows), BF)
     return call(
         ffn_kernel,
         (mid, mid, mid, sds((width, rows), out_dtype)),
-        (n, dy, *weights),
+        (n, d_act, *weights[:4]),
         "ffn",
-        vmem=16,
+        vmem=20,
     )
 
 
@@ -409,7 +418,7 @@
     _, hidden, rows = act.shape
     width = d0.shape[1]
     return call(
-        ffn_out_kernel, sds((width, rows), dtype), (act, d0, d1), "ffn_out",
+        ffn_out_kernel, hbm((width, rows), dtype), (act, d0, d1), "ffn_out", vmem=16,
     )
 
 
@@ -454,32 +463,24 @@
     shape = (shares, len(pieces), mids[0].shape[1] // shares, rows[0].shape[0])
     args = [v for mids, rows in pieces for v in (*mids, *rows)]
     return call(
-        wgrad_sum_kernel, sds(shape, BF), (*args, got), "wgrad_sum", vmem=20,
-    )
-
-
-def q_back_kernel(dq_ref, n0_ref, n1_ref, w_ref, gw_ref, own_ref, far_ref):
-    block = n0_ref.shape[1]
-    dq0 = dq_ref[:, :block]
-    dq1 = dq_ref[:, block:]
-    gw_ref[...] = (dot_nt(dq0, n0_ref[...]) + dot_nt(dq1, n1_ref[...])).astype(gw_ref.dtype)
-    own_ref[...] = dot_tn(w_ref[...], dq0)
-    far_ref[...] = dot_tn(w_ref[...], dq1)
+        wgrad_sum_kernel, hbm(shape, BF), (*args, got), "wgrad_sum", vmem=28,
+    )
 
 
 def kv_sum_kernel(
-    own_ref, got_ref, col_ref, back_own_ref, back_far_ref, n0_ref, n1_ref, wk_ref, wv_ref,
+    own_ref, got_ref, col_ref, dq_ref, n0_ref, n1_ref, wq_ref, wk_ref, wv_ref,
     gain_ref, gain_ffn_ref, rel_ref, dkv_ref, total_ref, give_ref, small_ref,
 ):
     inner = wk_ref.shape[0]
-    width, block = back_far_ref.shape
+    width, block = n0_ref.shape
+    dq = dq_ref[...]
     d_kv = (own_ref[...] + got_ref[: 2 * inner].astype(F32)).astype(BF)
     dkv_ref[...] = d_kv
     col = col_ref[...] + merge(got_ref[2 * inner : 2 * inner + 1], got_ref[2 * inner + 1 : 2 * inner + 2])
-    far = back_far_ref[...] + dot_tn(wk_ref[...], d_kv[:inner, block:])
+    far = dot_tn(wq_ref[...], dq[:, block:]) + dot_tn(wk_ref[...], d_kv[:inner, block:])
     far = far + dot_tn(wv_ref[...], d_kv[inner:, block:])
     give_ref[:width] = far.astype(BF)
-    own = back_own_ref[...] + dot_tn(wk_ref[...], d_kv[:inner, :block])
+    own = dot_tn(wq_ref[...], dq[:, :block]) + dot_tn(wk_ref[...], d_kv[:inner, :block])
     own = own + dot_tn(wv_ref[...], d_kv[inner:, :block])
     total_ref[...] = own
     gain = lane_sum(own * n0_ref[...].astype(F32) + far * n1_ref[...].astype(F32)) / gain_ref[...]
@@ -496,15 +497,6 @@
     give_ref[width + EXTRA :] = low
     small_ref[...] = merge(high, low)
     small_ref[0:1] = col[:, :block]
-
-
-def kv_back_kernel(dkv_ref, n0_ref, n1_ref, gk_ref, gv_ref):
-    inner = gk_ref.shape[0]
-    block = n0_ref.shape[1]
-    for at, out in ((0, gk_ref), (inner, gv_ref)):
-        d0 = dkv_ref[at : at + inner, :block]
-        d1 = dkv_ref[at : at + inner, block:]
-        out[...] = dot_nt(d0, n0_ref[...]) + dot_nt(d1, n1_ref[...])
 
 
 def last_kernel(
@@ -532,7 +524,7 @@
 
 def out_rows_kernel(c_ref, res_ref, own_ref, ga_ref, gb_ref, gd_ref, keep_ref, give_ref, rows_ref):
     total = res_ref[...] + (
-        own_ref[...]
+        own_ref[...].astype(F32)
         + ga_ref[...].astype(F32)
         + gb_ref[...].astype(F32)
         + gd_ref[...].astype(F32)
@@ -543,13 +535,26 @@
     give_ref[...] = rows_ref[:, pl.ds(pl.multiple_of((1 - c_ref[0]) * rows, rows), rows)]
 
 
-def fold_core_kernel(c_ref, gq_ref, gk_ref, gv_ref, go_ref, got_ref, keep_ref, give_ref):
-    out = go_ref[...] + got_ref[...].astype(F32)
+def fold_core_kernel(
+    c_ref, dq_ref, dkv_ref, n0_ref, n1_ref, go_ref, got_ref, keep_ref, give_ref
+):
+    inner = dq_ref.shape[0]
+    block = n0_ref.shape[1]
+    n0 = n0_ref[...]
+    n1 = n1_ref[...]
+
+    def gradient(rows):
+        return dot_nt(rows[:, :block], n0) + dot_nt(rows[:, block:], n1)
+
     first = c_ref[0] == 0
-    keep_ref[0] = jnp.where(first, gq_ref[...], gv_ref[...])
-    keep_ref[1] = jnp.where(first, gk_ref[...], out)
-    give_ref[0] = jnp.where(first, gv_ref[...], gq_ref[...]).astype(BF)
-    give_ref[1] = jnp.where(first, out, gk_ref[...]).astype(BF)
+    gq = gradient(dq_ref[...])
+    gv = gradient(dkv_ref[inner:])
+    keep_ref[0] = jnp.where(first, gq, gv)
+    give_ref[0] = jnp.where(first, gv, gq).astype(BF)
+    gk = gradient(dkv_ref[:inner])
+    go = go_ref[...] + got_ref[...].astype(F32)
+    keep_ref[1] = jnp.where(first, gk, go)
+    give_ref[1] = jnp.where(first, go, gk).astype(BF)
 
 
 def fold_x_kernel(x_ref, mine_ref, got_ref, keep_ref, give_ref):
@@ -559,13 +564,11 @@
     give_ref[...] = jnp.where(first, total[1], total[0]).astype(BF)
 
 
-def share_kernel(z_ref, mine_ref, got_ref, sum_ref, own_ref, *give_refs):
+def share_kernel(bit_ref, mine_ref, got_ref, own_ref, give_ref, sum_ref):
     sum_ref[...] = mine_ref[...] + got_ref[...].astype(F32)
-    rows = own_ref.shape[0]
-    n = len(give_refs) + 1
-    for k, out in enumerate((own_ref, *give_refs)):
-        at = lax.rem(z_ref[0] + k, n)
-        out[...] = sum_ref[pl.ds(pl.multiple_of(at * rows, rows), rows), :].astype(out.dtype)
+    keep, give = halves(bit_ref, own_ref.shape[0])
+    own_ref[...] = sum_ref[keep, :]
+    give_ref[...] = sum_ref[give, :].astype(BF)
 
 
 def lines(small, first, width):
@@ -577,13 +580,9 @@
     return jnp.concatenate(pieces, axis=1)[:, :width]
 
 
-def share_sum_kernel(own_ref, small_ref, small_got_ref, *refs):
-    out_ref = refs[-1]
-    rows, width = own_ref.shape
-    total = own_ref[...]
-    for ref in refs[:-1]:
-        total = total + ref[...].astype(F32)
-    out_ref[:rows] = total.astype(BF)
+def share_sum_kernel(mine_ref, got_ref, small_ref, small_got_ref, out_ref):
+    rows, width = mine_ref.shape
+    out_ref[:rows] = (mine_ref[...] + got_ref[...].astype(F32)).astype(BF)
     small = small_ref[...] + small_got_ref[...]
     rel = small[1:2]
     rel = jnp.concatenate([rel, small[EXTRA + 1 : EXTRA + 2]], axis=1)
@@ -600,7 +599,12 @@
     rows = shares[0].shape[0] - EXTRA
     for k, ref in enumerate(shares):
         at = lax.rem(z_ref[0] + n - k, n)
-        out_ref[pl.ds(pl.multiple_of(at * rows, rows), rows), :] = ref[:rows]
+        line, rest, size = 0, at, n
+        while size > 1:
+            size //= 2
+            line = line + lax.rem(rest, 2) * size
+            rest = rest // 2
+        out_ref[pl.ds(pl.multiple_of(line * rows, rows), rows), :] = ref[:rows]
         hold_ref[at] = merge(ref[rows : rows + 8], ref[rows + 8 :])
     total = hold_ref[0]
     for k in range(1, n):
@@ -650,7 +654,7 @@
         compiler_params=pltpu.CompilerParams(vmem_limit_bytes=32 << 20),
         cost_estimate=cost(500),
         name="widen",
-    )(Order.follow(v))
+    )(in_hbm(Order.follow(v)))
     return Order.done(outs)
 
 
@@ -743,8 +747,9 @@
     x_rows, normed_one, inv_one = call(
         prep_kernel,
         (sds((width, block), BF), sds((width, block), BF), sds((1, block), F32)),
-        (x_in, core_swap(x_in, "x_core"), gain_one),
+        (in_hbm(x_in), core_swap(x_in, "x_core"), gain_one),
         "prep",
+        vmem=20,
         scalars=(c_scalar,),
     )
     normed_far_raw = y_swap(normed_one, "n1_y")
@@ -752,8 +757,9 @@
     dy_own = call(
         pair_kernel,
         sds((width, block), BF),
-        (dy_in, core_swap(dy_in, "dy_core")),
+        (in_hbm(dy_in), in_hbm(core_swap(dy_in, "dy_core"))),
         "pair",
+        vmem=16,
         scalars=(c_scalar,),
     )
 
@@ -807,21 +813,29 @@
     mixed_own = mixed[:, :block]
     residual, normed_two, inv_two = call(
         mid_kernel,
-        (sds((width, block), F32), sds((width, block), BF), sds((1, block), F32)),
+        (hbm((width, block), F32), sds((width, block), BF), sds((1, block), F32)),
         (x_rows, mixed_own, mixed_far, w_out, w_half, w_half_got, gain_two),
         "mid",
+        vmem=20,
         scalars=(c_scalar,),
     )
 
     n_x = x_swap(normed_two, "n2_x")
     n_y = y_swap(normed_two, "n2_y")
-    act_o, dg_o, du_o, dn_o = ffn_chunk(normed_two, dy_own, ffn_weights, F32)
+    def d_act_of(dy):
+        shape = sds((2, hidden, block), F32)
+        return call(d_act_kernel, shape, (dy, down_weight, down_other), "d_act")
+
+    da_own = d_act_of(dy_own)
+    act_o, dg_o, du_o, dn_o = ffn_chunk(normed_two, da_own, ffn_weights, BF)
+    da_x = d_act_of(dy_x)
+    da_y = d_act_of(dy_y)
     n_d = relay(n_x, n_y, "n2_d")
-    act_x, dg_x, du_x, dn_x = ffn_chunk(n_x, dy_x, ffn_weights, BF)
+    act_x, dg_x, du_x, dn_x = ffn_chunk(n_x, da_x, ffn_weights, BF)
     got_x = x_swap(dn_x, "dn_x")
-    act_y, dg_y, du_y, dn_y = ffn_chunk(n_y, dy_y, ffn_weights, BF)
+    act_y, dg_y, du_y, dn_y = ffn_chunk(n_y, da_y, ffn_weights, BF)
     got_y = y_swap(dn_y, "dn_y")
-    act_d, dg_d, du_d, dn_d = ffn_chunk(n_d, dy_d, ffn_weights, BF)
+    act_d, dg_d, du_d, dn_d = ffn_chunk(n_d, d_act_of(dy_d), ffn_weights, BF)
     got_d = grid_swap(dn_d, False, "dn_d")
 
     n_all = (normed_two, n_x, n_y, n_d)
@@ -831,7 +845,7 @@
         ((dg_o, dg_x, dg_y, dg_d), n_all),
         ((du_o, du_x, du_y, du_d), n_all),
     )
-    out_o = ffn_out(act_o, down_weight, down_other, F32)
+    out_o = ffn_out(act_o, down_weight, down_other, BF)
     mids, rows = pieces[0]
     pieces = (((after(mids[0], got_x, got_y), *mids[1:]), rows), *pieces[1:])
     given = core_swap(wgrad_give(pieces), "wgrad_core")
@@ -849,40 +863,35 @@
     d_residual, d_branch, gain_ffn_part, d_mixed_own, d_mixed_give = call(
         mid_back_kernel,
         (
-            sds((width, block), F32),
+            hbm((width, block), F32),
             sds((width, block), BF),
             sds((1, width), F32),
             sds((inner, block), BF),
             sds((inner, block), BF),
         ),
-        (dn_o, got_x, got_y, got_d, dy_own, residual, inv_two, gain_two, w_out, w_half, w_half_got),
+        (*map(in_hbm, (dn_o, got_x, got_y, got_d, dy_own, residual)), inv_two, gain_two, w_out, w_half, w_half_got),
         "mid_back",
+        vmem=24,
         scalars=(c_scalar,),
     )
     d_mixed = jnp.concatenate([d_mixed_own, y_swap(d_mixed_give, "dmixed_y")], axis=1)
 
+    dq, dkv_own, dkv_give, col, table_grad = attn_bwd(
+        starts, probs, queries, d_mixed, kvs, heads, block
+    )
+    dkv_got = x_swap(dkv_give, "dkv_x")
+    out_x = in_hbm(x_swap(after(part_x, got_d), "out_x"))
+    out_y = in_hbm(y_swap(after(part_y, got_d), "out_y"))
+    d_branch = after(d_branch, dq)
     grad_out_own, grad_out_give = call(
         out_grad_kernel,
-        (sds((inner, width), F32), sds((inner, width), BF)),
+        (hbm((inner, width), F32), hbm((inner, width), BF)),
         (mixed_own, mixed_far, d_branch),
         "out_grad",
+        vmem=20,
     )
     grad_out_got = y_swap(grad_out_give, "gout_y")
-
-    dq, dkv_own, dkv_give, col, table_grad = attn_bwd(
-        starts, probs, queries, d_mixed, kvs, heads, block
-    )
-    dkv_got = x_swap(dkv_give, "dkv_x")
-    out_x = x_swap(after(part_x, got_d), "out_x")
-    out_y = y_swap(after(part_y, got_d), "out_y")
-    dq = after(dq, out_x, out_y)
-    dkv_got = after(dkv_got, grad_out_got)
-    grad_q, back_own, back_far = call(
-        q_back_kernel,
-        (sds((inner, width), F32), sds((width, block), F32), sds((width, block), F32)),
-        (dq, normed_one, normed_far, wq),
-        "q_back",
-    )
+    dkv_got = after(dkv_got, out_x, out_y)
     table_grad = sum(jnp.roll(table_grad[:, i], -i, axis=1) for i in range(8))
     grad_rel = jnp.sum(jnp.where(hot[None], table_grad[:, None, :], 0.0), axis=2).T
     grad_rel = lax.dynamic_update_slice_in_dim(
@@ -892,41 +901,43 @@
         kv_sum_kernel,
         (
             sds((2 * inner, 2 * block), BF),
-            sds((width, block), F32),
-            sds((width + 2 * EXTRA, block), BF),
+            hbm((width, block), F32),
+            hbm((width + 2 * EXTRA, block), BF),
             sds((EXTRA, block), F32),
         ),
         (
-            dkv_own, dkv_got, col, back_own, back_far, normed_one, normed_far, wk, wv,
+            *map(in_hbm, (dkv_own, dkv_got)), col,
+            dq, *map(in_hbm, (normed_one, normed_far)), wq, wk, wv,
             gain_one, gain_ffn_part, grad_rel.reshape(1, -1),
         ),
         "kv_sum",
+        vmem=24,
     )
     back_got = y_swap(back_give, "back_y")
-    grad_k, grad_v = call(
-        kv_back_kernel,
-        (sds((inner, width), F32), sds((inner, width), F32)),
-        (d_kv, normed_one, normed_far),
-        "kv_back",
-    )
 
     pair_f32, pair_bf = sds((2, inner, width), F32), sds((2, inner, width), BF)
     one_f32, one_bf = sds((inner, width), F32), sds((inner, width), BF)
     keep, give = call(
         fold_core_kernel,
-        (pair_f32, pair_bf),
-        (grad_q, grad_k, grad_v, grad_out_own, grad_out_got),
+        (hbm(pair_f32.shape, F32), hbm(pair_bf.shape, BF)),
+        (dq, d_kv, *map(in_hbm, (normed_one, normed_far, grad_out_own, grad_out_got))),
         "fold_core",
         scalars=(c_scalar,),
+        vmem=28,
     )
     keep, give = call(
         fold_x_kernel,
         (one_f32, one_bf),
-        (keep, core_swap(give, "fold_core")),
+        (in_hbm(keep), in_hbm(core_swap(give, "fold_core"))),
         "fold_x",
+        vmem=20,
         scalars=(x_scalar,),
     )
     got = x_swap(give, "fold_x")
+    steps = [1 << k for k in range(dp_axis.bit_length() - 1)]
+    short = shares > 1 and 1 << len(steps) == dp_axis
+    if short:
+        keep, got = z_share(keep, got, steps[0], dp_axis, z_at)
     rows_keep, rows_give, small, _ = call(
         last_kernel,
         (
@@ -935,17 +946,23 @@
             sds((2 * EXTRA, row_count), F32),
             sds((width + EXTRA, block), F32),
         ),
-        (back_own, after(back_got, got), small, x_rows, inv_one, gain_one, d_residual),
+        (in_hbm(back_own), in_hbm(back_got), small, in_hbm(x_rows), inv_one, gain_one, in_hbm(d_residual)),
         "last",
+        vmem=24,
         scalars=(c_scalar,),
     )
     rows_got = core_swap(rows_give, "grad_core")
+    small_got = rows_got[width:]
     if shares > 1:
-        ffn_grads = lax.all_gather(after(ffn_grads, grad_k), "dp", axis=0, tiled=True)
-    small_got = rows_got[width:]
-
-    folded, shared = z_sum(keep, got, small, small_got, dp_axis, z_scalar)
-    part_d = after(part_d, shared)
+        ffn_grads = lax.all_gather(after(ffn_grads, rows_keep), "dp", axis=0, tiled=True)
+    if short:
+        for step in steps[1:]:
+            keep, got = z_share(keep, got, step, dp_axis, z_at)
+        folded = z_join(keep, got, small, small_got, dp_axis, z_scalar)
+    else:
+        folded = z_psum(keep, got, small, small_got)
+
+    part_d = after(part_d, rows_keep)
     out_d = grid_swap(part_d, False, "out_d")
     out_keep, out_give, _ = call(
         out_rows_kernel,
@@ -954,29 +971,30 @@
             sds((width, row_count), BF),
             sds((width, block), BF),
         ),
-        (residual, out_o, out_x, out_y, out_d),
+        tuple(map(in_hbm, (residual, out_o, out_x, out_y, out_d))),
         "out_rows",
+        vmem=24,
         scalars=(c_scalar,),
     )
 
+    joined = x_swap(folded, "join_x")
+    grad_inputs = place(rows_keep, rows_got)
     folded, sums = call(
         join_x_kernel,
         (pair_bf, sds((8, width), F32)),
-        (folded, x_swap(folded, "join_x")),
+        (folded, joined),
         "join_x",
         scalars=(x_scalar,),
     )
+    joined = core_swap(folded, "join_core")
+    output = place(out_keep, core_swap(out_give, "out_core"))
     grad_w_query, grad_w_key, grad_w_value, grad_w_out = call(
         join_core_kernel,
         (one_f32,) * 4,
-        (folded, core_swap(folded, "join_core")),
+        (folded, joined),
         "join_core",
         scalars=(c_scalar,),
     )
-
-    output = place(out_keep, core_swap(out_give, "out_core"))
-
-    grad_inputs = place(rows_keep, rows_got)
     mask_keep, mask_got = small[:1], small_got[:1]
     grad_mask = jnp.where(c_at == 0, stack(mask_keep, mask_got), stack(mask_got, mask_keep))
     grad_down, grad_gate, grad_up = widen(ffn_grads)
@@ -997,47 +1015,57 @@
     )
 
 
-def z_sum(mine, got, small, small_got, n, z_scalar):
+def z_swap(v, step, n, name):
+    return move(v, "dp", [(i, i ^ step) for i in range(n)], name)
+
+
+def z_share(mine, got, step, n, z_at):
+    bit = ((z_at // step) % 2).astype(jnp.int32).reshape(1)
     rows, width = mine.shape
-    if n > 8:
-        total = lax.psum((mine + got.astype(F32)).astype(BF), "dp")
-        small = lax.psum(small + small_got, "dp")
-        half = small.shape[0] // 2
-
-        def row(first):
-            both = jnp.concatenate([small[first:half], small[half + first :]], axis=1)
-            return both.reshape(1, -1)[:, :width]
-
-        three = jnp.concatenate([row(2), row(8), row(1), jnp.zeros((5, width), F32)], axis=0)
-        return jnp.concatenate([total, *split(three)], axis=0), mine
-    share = rows // n
-
-    def shift(v, k, name):
-        return move(v, "dp", [(i, (i + k) % n) for i in range(n)], name)
-
-    _, own, *give = call(
+    half = (rows // 2, width)
+    mine, give, _ = call(
         share_kernel,
-        (sds(mine.shape, F32), sds((share, width), F32), *[sds((share, width), BF)] * (n - 1)),
+        (sds(half, F32), sds(half, BF), sds((rows, width), F32)),
         (mine, got),
         "share",
-        scalars=(z_scalar,),
-    )
-    gots = [shift(v, k + 1, "share_z") for k, v in enumerate(give)]
+        scalars=(bit,),
+    )
+    return mine, z_swap(give, step, n, "share_z")
+
+
+def z_join(mine, got, small, small_got, n, z_scalar):
+    rows, width = mine.shape
     total = call(
         share_sum_kernel,
-        sds((share + EXTRA, width), BF),
-        (own, small, small_got, *gots),
+        sds((rows + EXTRA, width), BF),
+        (mine, got, small, small_got),
         "share_sum",
     )
-    gots = [shift(total, k, "join_z") for k in range(1, n)]
+    gots = [
+        move(total, "dp", [(i, (i + k) % n) for i in range(n)], "join_z") for k in range(1, n)
+    ]
     joined, _ = call(
         share_join_kernel,
-        (sds((rows + EXTRA, width), BF), sds((n, 8, width), F32)),
+        (sds((n * rows + EXTRA, width), BF), sds((n, 8, width), F32)),
         (total, *gots),
         "share_join",
         scalars=(z_scalar,),
     )
-    return joined, own
+    return joined
+
+
+def z_psum(mine, got, small, small_got):
+    width = mine.shape[1]
+    total = lax.psum((mine + got.astype(F32)).astype(BF), "dp")
+    small = lax.psum(small + small_got, "dp")
+    half = small.shape[0] // 2
+
+    def row(first):
+        both = jnp.concatenate([small[first:half], small[half + first :]], axis=1)
+        return both.reshape(1, -1)[:, :width]
+
+    three = jnp.concatenate([row(2), row(8), row(1), jnp.zeros((5, width), F32)], axis=0)
+    return jnp.concatenate([total, *split(three)], axis=0)
 
 
 def solution(mesh):

time: 363 us -> 337 us (0.928)
  the two profiles are of different devices: /device:TPU:11 before, /device:TPU:0 now
where the time goes in v3:
time: 337 us; the launch traced here: 333 us
  waiting for transfers between devices  137 us (41%)
  Pallas kernels  121 us (36%)
  starting transfers between devices  41.2 us (12%)
  local copies, waits for them, and re-layouts  16.7 us (5%)
  between operations  15 us (4%)
    ppermute x39, waiting for transfers between devices, move(): return lax.ppermute(v, axes, pairs)  121 us
    pallas_call x36, Pallas kernels, call(): pl.pallas_call(kernel, out_shape=out_shape, in_specs=in_specs, out_specs=...  88.7 us
    ppermute x39, starting transfers between devices, move(): return lax.ppermute(v, axes, pairs)  41.1 us
    all_gather x1, waiting for transfers between devices, run(): lax.all_gather(after(ffn_grads, rows_keep), 'dp', axis=0, tiled=True)  16.1 us
    pallas_call x1, Pallas kernels, attn_bwd(): pl.pallas_call(functools.partial(attn_bwd_kernel, inner=inner, heads=head...  11.2 us
    unnamed x107, local copies, waits for them, and re-layouts  9.28 us
    pallas_call x1, Pallas kernels, attn_fwd(): pl.pallas_call(functools.partial(attn_fwd_kernel, inner=inner), out_shape...  9.14 us
  transfers between devices with their start and end apart: 41, of which 21 were waited for; matrix products, arithmetic and copies ran while one was open for 3% of the time, Pallas kernels for 32%

profile of v3, /device:TPU:0, one launch (start us, length us, event | category | flops | bytes accessed | tf_op | source)
XLA Modules:
  0.0 332.8 jit_solution(7312851523290711075)
XLA Ops:
  16.2 2.7 collective-permute-start.2
  23.0 6.0 %bias.1.bias_ref = f32[3,1024,512]{2,1,0:T(8,128)} custom-call(s32[8]{0:T(128)S(1)} %sub.44.start_ref, f32[8,2048]{1,0:T(8,128)S(1)} %concatenate.83.table_ref, f32[1,1024]{1,0:T(1,128)S(1)} %reshape.105.mask_ref), custom_call_target="tpu_custom_call" | custom-call | bytes 30000 | tf_op jit(solution)/shard_map/bias/pallas_call | solution.py:148
  29.0 7.3 %collective-permute-done.2.n_ref.n1_ref = bf16[1472,256]{1,0:T(8,128)(2,1)S(1)} collective-permute-done((bf16[1472,256]{1,0:T(8,128)(2,1)S(1)}, bf16[1472,256]{1,0:T(8,128)(2,1)S(1)}, u32[]{:S(2)}, u32[]{:S(2)}) %collective-permute-start.2) | collective-permute-done | bytes 753696 | tf_op jit(solution)/shard_map/n1_y/ppermute | solution.py:86
  36.3 1.8 collective-permute-start.9
  40.3 4.7 %collective-permute-done.7.k3 = bf16[384,256]{1,0:T(8,128)(2,1)S(1)} collective-permute-done((bf16[384,256]{1,0:T(8,128)(2,1)S(1)}, bf16[384,256]{1,0:T(8,128)(2,1)S(1)}, u32[]{:S(2)}, u32[]{:S(2)}) %collective-permute-start.7) | collective-permute-done | bytes 196640 | tf_op jit(solution)/shard_map/kv_far_x/ppermute | solution.py:86
  47.1 9.1 %attn_fwd.1 = (f32[3,1024,512]{2,1,0:T(8,128)}, bf16[192,512]{1,0:T(8,128)(2,1)S(1)}) custom-call(bf16[192,512]{1,0:T(8,128)(2,1)S(1)} %constant_dynamic-update-slice_fusion.q_ref, bf16[384,256]{1,0:T(8,128)(2,1)S(1)} %get-tuple-element.136.k0, bf16[384,256]{1,0:T(8,128)(2,1)S(1)} %get-tuple-element.140.k1, bf16[384,256]{1,0:T(8,128)(2,1)S(1)} %collective-permute-done.6.k2, ...), custom_call_target="tpu_custom_call" | custom-call | bytes 30000 | tf_op jit(solution)/shard_map/attn_fwd/pallas_call | solution.py:190
  58.0 4.2 %collective-permute-done.8.first_ref.dy_ref.refs_5_ = bf16[1472,256]{1,0:T(8,128)(2,1)S(1)} collective-permute-done((bf16[1472,256]{1,0:T(8,128)(2,1)S(1)}, bf16[1472,256]{1,0:T(8,128)(2,1)S(1)}, u32[]{:S(2)}, u32[]{:S(2)}) %collective-permute-start.8) | collective-permute-done | bytes 753696 | tf_op jit(solution)/shard_map/dy_x/ppermute | solution.py:86
  62.2 2.3 collective-permute-done.10.second_ref.dy_ref.refs_6_
  65.6 2.1 mid.1
  72.1 5.7 %ffn.4 = (bf16[2,448,256]{2,1,0:T(8,128)(2,1)S(1)}, bf16[2,448,256]{2,1,0:T(8,128)(2,1)S(1)}, bf16[2,448,256]{2,1,0:T(8,128)(2,1)S(1)}, bf16[1472,256]{1,0:T(8,128)(2,1)S(1)}) custom-call(bf16[1472,256]{1,0:T(8,128)(2,1)S(1)} %get-tuple-element.153.n_ref.refs_12_.refs_20_, f32[2,448,256]{2,1,0:T(8,128)S(1)} %d_act.4.da_ref, bf16[448,1472]{1,0:T(8,128)(2,1)S(1)} %bitcast.79, ...), custom_call_target="tpu_custom_call" | custom-call | bytes 30000 | tf_op jit(solution)/shard_map/ffn/pallas_call | solution.py:63
  79.6 7.8 %collective-permute-done.13.first_ref.n_ref.refs_13_.refs_21_ = bf16[1472,256]{1,0:T(8,128)(2,1)S(1)} collective-permute-done((bf16[1472,256]{1,0:T(8,128)(2,1)S(1)}, bf16[1472,256]{1,0:T(8,128)(2,1)S(1)}, u32[]{:S(2)}, u32[]{:S(2)}) %collective-permute-start.13) | collective-permute-done | bytes 753696 | tf_op jit(solution)/shard_map/n2_x/ppermute | solution.py:86
  88.3 5.7 %ffn.5 = (bf16[2,448,256]{2,1,0:T(8,128)(2,1)S(1)}, bf16[2,448,256]{2,1,0:T(8,128)(2,1)S(1)}, bf16[2,448,256]{2,1,0:T(8,128)(2,1)S(1)}, bf16[1472,256]{1,0:T(8,128)(2,1)S(1)}) custom-call(bf16[1472,256]{1,0:T(8,128)(2,1)S(1)} %collective-permute-done.13.first_ref.n_ref.refs_13_.refs_21_, f32[2,448,256]{2,1,0:T(8,128)S(1)} %d_act.5.da_ref, ...), custom_call_target="tpu_custom_call" | custom-call | bytes 30000 | tf_op jit(solution)/shard_map/ffn/pallas_call | solution.py:63
  95.6 5.9 %ffn.6 = (bf16[2,448,256]{2,1,0:T(8,128)(2,1)S(1)}, bf16[2,448,256]{2,1,0:T(8,128)(2,1)S(1)}, bf16[2,448,256]{2,1,0:T(8,128)(2,1)S(1)}, bf16[1472,256]{1,0:T(8,128)(2,1)S(1)}) custom-call(bf16[1472,256]{1,0:T(8,128)(2,1)S(1)} %collective-permute-done.14.second_ref.n_ref.refs_14_.refs_22_, f32[2,448,256]{2,1,0:T(8,128)S(1)} %d_act.6.da_ref, ...), custom_call_target="tpu_custom_call" | custom-call | bytes 30000 | tf_op jit(solution)/shard_map/ffn/pallas_call | solution.py:63
  104.0 6.6 %ffn.7 = (bf16[2,448,256]{2,1,0:T(8,128)(2,1)S(1)}, bf16[2,448,256]{2,1,0:T(8,128)(2,1)S(1)}, bf16[2,448,256]{2,1,0:T(8,128)(2,1)S(1)}, bf16[1472,256]{1,0:T(8,128)(2,1)}) custom-call(bf16[1472,256]{1,0:T(8,128)(2,1)S(1)} %collective-permute-done.15.n_ref.refs_15_.refs_23_, f32[2,448,256]{2,1,0:T(8,128)S(1)} %d_act.7.da_ref, bf16[448,1472]{1,0:T(8,128)(2,1)S(1)} %bitcast.82, ...), custom_call_target="tpu_custom_call" | custom-call | bytes 30000 | tf_op jit(solution)/shard_map/ffn/pallas_call | solution.py:63
  110.6 3.3 collective-permute-done.17.ga_ref
  113.9 2.9 collective-permute-done.18.gb_ref
  116.7 1.9 ffn_out.4.own_ref
  118.7 4.5 %wgrad_give.1 = bf16[3,448,1472]{2,1,0:T(8,128)(2,1)S(1)} custom-call(bf16[2,448,256]{2,1,0:T(8,128)(2,1)S(1)} %get-tuple-element.186.a_ref.refs_0_, bf16[2,448,256]{2,1,0:T(8,128)(2,1)S(1)} %get-tuple-element.178.refs_1_.a_ref, bf16[2,448,256]{2,1,0:T(8,128)(2,1)S(1)} %get-tuple-element.181.refs_2_.a_ref, ...), custom_call_target="tpu_custom_call" | custom-call | bytes 30000 | tf_op jit(solution)/shard_map/wgrad_give/pallas_call | solution.py:63
  124.8 1.9 ffn_out.5
  126.7 2.3 ffn_out.6
  129.1 2.0 ffn_out.7
  131.0 6.5 %wgrad_sum.1 = bf16[4,3,112,1472]{3,2,1,0:T(8,128)(2,1)} custom-call(bf16[2,448,256]{2,1,0:T(8,128)(2,1)S(1)} %get-tuple-element.186.a_ref.refs_0_, bf16[2,448,256]{2,1,0:T(8,128)(2,1)S(1)} %get-tuple-element.178.refs_1_.a_ref, bf16[2,448,256]{2,1,0:T(8,128)(2,1)S(1)} %get-tuple-element.181.refs_2_.a_ref, ...), custom_call_target="tpu_custom_call" | custom-call | bytes 30000 | tf_op jit(solution)/shard_map/wgrad_sum/pallas_call | solution.py:63
  137.6 6.0 %collective-permute-done.19.gd_ref = bf16[1472,256]{1,0:T(8,128)(2,1)S(1)} collective-permute-done((bf16[1472,256]{1,0:T(8,128)(2,1)}, bf16[1472,256]{1,0:T(8,128)(2,1)S(1)}, u32[]{:S(2)}, u32[]{:S(2)}) %collective-permute-start.19) | collective-permute-done | bytes 753696 | tf_op jit(solution)/shard_map/dn_d/ppermute | solution.py:86
  144.5 4.9 %mid_back.1 = (f32[1472,256]{1,0:T(8,128)}, bf16[1472,256]{1,0:T(8,128)(2,1)S(1)}, f32[1,1472]{1,0:T(1,128)S(1)}, bf16[192,256]{1,0:T(8,128)(2,1)S(1)}, bf16[192,256]{1,0:T(8,128)(2,1)S(1)}) custom-call(s32[1]{0:T(128)} %bitcast.c_ref, bf16[1472,256]{1,0:T(8,128)(2,1)} %copy-done.33, bf16[1472,256]{1,0:T(8,128)(2,1)} %copy-done.41, ...), custom_call_target="tpu_custom_call" | custom-call | bytes 30000 | tf_op jit(solution)/shard_map/mid_back/pallas_call | solution.py:63
  149.4 1.8 collective-permute-start.23
  154.4 11.2 %attn_bwd.1 = (bf16[192,512]{1,0:T(8,128)(2,1)S(1)}, f32[384,512]{1,0:T(8,128)}, bf16[400,512]{1,0:T(8,128)(2,1)}, f32[1,512]{1,0:T(1,128)S(1)}, f32[3,8,2048]{2,1,0:T(8,128)S(1)}) custom-call(s32[8]{0:T(128)S(1)} %sub.44.start_ref, f32[3,1024,512]{2,1,0:T(8,128)} %get-tuple-element.184.p_ref, bf16[192,512]{1,0:T(8,128)(2,1)S(1)} %copy-done.18, ...), custom_call_target="tpu_custom_call" | custom-call | bytes 1500000000 | tf_op jit(solution)/shard_map/attn_bwd/pallas_call | solution.py:288
  168.5 2.3 collective-permute-start.25
  173.1 5.5 %collective-permute-done.24.got_ref = bf16[400,512]{1,0:T(8,128)(2,1)S(1)} collective-permute-done((bf16[400,512]{1,0:T(8,128)(2,1)}, bf16[400,512]{1,0:T(8,128)(2,1)S(1)}, u32[]{:S(2)}, u32[]{:S(2)}) %collective-permute-start.24) | collective-permute-done | bytes 409632 | tf_op jit(solution)/shard_map/dkv_x/ppermute | solution.py:86
  179.3 4.6 %kv_sum.1 = (bf16[384,512]{1,0:T(8,128)(2,1)S(1)}, f32[1472,256]{1,0:T(8,128)}, bf16[1504,256]{1,0:T(8,128)(2,1)}, f32[16,256]{1,0:T(8,128)S(1)}) custom-call(f32[384,512]{1,0:T(8,128)} %get-tuple-element.199.own_ref, bf16[400,512]{1,0:T(8,128)(2,1)} %copy-done.47, f32[1,512]{1,0:T(1,128)S(1)} %get-tuple-element.193.col_ref, ...), custom_call_target="tpu_custom_call" | custom-call | bytes 30000 | tf_op jit(solution)/shard_map/kv_sum/pallas_call | solution.py:63
  184.0 5.2 %fold_core.1 = (f32[2,192,1472]{2,1,0:T(8,128)}, bf16[2,192,1472]{2,1,0:T(8,128)(2,1)}) custom-call(s32[1]{0:T(128)} %bitcast.c_ref, bf16[192,512]{1,0:T(8,128)(2,1)S(1)} %get-tuple-element.205.dq_ref, bf16[384,512]{1,0:T(8,128)(2,1)S(1)} %get-tuple-element.206.dkv_ref, bf16[1472,256]{1,0:T(8,128)(2,1)} %copy-done.6, bf16[1472,256]{1,0:T(8,128)(2,1)} %copy-done.7, ...), custom_call_target="tpu_custom_call" | custom-call | bytes 30000 | tf_op jit(solution)/shard_map/fold_core/pallas_call | solution.py:63
  190.3 1.9 collective-permute-done.26.got_ref
  193.2 2.3 fold_x.1
  196.3 14.6 %collective-permute-done.27.got_ref = bf16[192,1472]{1,0:T(8,128)(2,1)S(1)} collective-permute-done((bf16[192,1472]{1,0:T(8,128)(2,1)S(1)}, bf16[192,1472]{1,0:T(8,128)(2,1)S(1)}, u32[]{:S(2)}, u32[]{:S(2)}) %collective-permute-start.27) | collective-permute-done | bytes 565280 | tf_op jit(solution)/shard_map/fold_x/ppermute | solution.py:86
  213.0 4.3 %last.1 = (f32[1472,128]{1,0:T(8,128)S(1)}, f32[1504,128]{1,0:T(8,128)S(1)}, f32[32,128]{1,0:T(8,128)S(1)}, f32[1488,256]{1,0:T(8,128)}) custom-call(s32[1]{0:T(128)} %bitcast.c_ref, f32[1472,256]{1,0:T(8,128)} %get-tuple-element.213.own_ref, bf16[1504,256]{1,0:T(8,128)(2,1)} %copy-done.39, f32[16,256]{1,0:T(8,128)S(1)} %get-tuple-element.204.small_ref, ...), custom_call_target="tpu_custom_call" | custom-call | bytes 30000 | tf_op jit(solution)/shard_map/last/pallas_call | solution.py:63
  219.6 7.9 %collective-permute-done.30.got_ref = bf16[96,1472]{1,0:T(8,128)(2,1)S(1)} collective-permute-done((bf16[96,1472]{1,0:T(8,128)(2,1)S(1)}, bf16[96,1472]{1,0:T(8,128)(2,1)S(1)}, u32[]{:S(2)}, u32[]{:S(2)}) %collective-permute-start.30) | collective-permute-done | bytes 282656 | tf_op jit(solution)/shard_map/share_z/ppermute | solution.py:86
  228.4 2.5 collective-permute-start.31
  230.9 17.2 %collective-permute-done.31.got_ref = bf16[48,1472]{1,0:T(8,128)(2,1)S(1)} collective-permute-done((bf16[48,1472]{1,0:T(8,128)(2,1)S(1)}, bf16[48,1472]{1,0:T(8,128)(2,1)S(1)}, u32[]{:S(2)}, u32[]{:S(2)}) %collective-permute-start.31) | collective-permute-done | bytes 141344 | tf_op jit(solution)/shard_map/share_z/ppermute | solution.py:86
  248.2 3.2 collective-permute-start.34
  252.0 2.4 collective-permute-start.29
  254.4 7.5 %collective-permute-done.33.refs_1_ = bf16[64,1472]{1,0:T(8,128)(2,1)S(1)} collective-permute-done((bf16[64,1472]{1,0:T(8,128)(2,1)S(1)}, bf16[64,1472]{1,0:T(8,128)(2,1)S(1)}, u32[]{:S(2)}, u32[]{:S(2)}) %collective-permute-start.33) | collective-permute-done | bytes 188448 | tf_op jit(solution)/shard_map/join_z/ppermute | solution.py:86
  261.9 13.4 %collective-permute-done.34.refs_2_ = bf16[64,1472]{1,0:T(8,128)(2,1)S(1)} collective-permute-done((bf16[64,1472]{1,0:T(8,128)(2,1)S(1)}, bf16[64,1472]{1,0:T(8,128)(2,1)S(1)}, u32[]{:S(2)}, u32[]{:S(2)}) %collective-permute-start.34) | collective-permute-done | bytes 188448 | tf_op jit(solution)/shard_map/join_z/ppermute | solution.py:86
  278.4 4.2 %out_rows.1 = (bf16[1472,128]{1,0:T(8,128)(2,1)S(1)}, bf16[1472,128]{1,0:T(8,128)(2,1)}, bf16[1472,256]{1,0:T(8,128)(2,1)}) custom-call(s32[1]{0:T(128)} %bitcast.c_ref, f32[1472,256]{1,0:T(8,128)} %get-tuple-element.149.res_ref, bf16[1472,256]{1,0:T(8,128)(2,1)} %ffn_out.4.own_ref, bf16[1472,256]{1,0:T(8,128)(2,1)} %copy-done.40, ...), custom_call_target="tpu_custom_call" | custom-call | bytes 30000 | tf_op jit(solution)/shard_map/out_rows/pallas_call | solution.py:63
  283.8 8.8 %collective-permute-done.36.got_ref = bf16[208,1472]{1,0:T(8,128)(2,1)S(1)} collective-permute-done((bf16[208,1472]{1,0:T(8,128)(2,1)S(1)}, bf16[208,1472]{1,0:T(8,128)(2,1)S(1)}, u32[]{:S(2)}, u32[]{:S(2)}) %collective-permute-start.36) | collective-permute-done | bytes 612384 | tf_op jit(solution)/shard_map/join_x/ppermute | solution.py:86
  294.3 2.3 collective-permute-done.37.got_ref
  296.6 1.9 place.3
  301.5 2.4 join_core.1
  303.9 16.1 %all-gather.2.cloned.1.call-done.src = bf16[4,3,112,1472]{3,2,1,0:T(8,128)(2,1)} async-done(((bf16[1,3,112,1472]{3,2,1,0:T(8,128)(2,1)}), bf16[4,3,112,1472]{3,2,1,0:T(8,128)(2,1)}) %all-gather.2.cloned.1.call-update) | async-done | bytes 3956752 | tf_op jit(solution)/shard_map/all_gather | solution.py:957
  320.0 5.8 %widen.1 = (f32[448,1472]{1,0:T(8,128)}, f32[448,1472]{1,0:T(8,128)}, f32[448,1472]{1,0:T(8,128)}) custom-call(bf16[4,3,112,1472]{3,2,1,0:T(8,128)(2,1)} %all-gather.2.cloned.1.call-done.src), custom_call_target="tpu_custom_call" | custom-call | bytes 1500000000 | tf_op jit(solution)/shard_map/widen/pallas_call | solution.py:648
  (237 shorter events, 60.8 us)
Async XLA Ops:
  7.2 210.0 %reduce-scatter.2.cloned.1.call-start = ((), (), s32[]{:S(2)}) async-start(), calls=%async_computation.1 | async-start | bytes 5160960 | tf_op jit(solution)/shard_map/reduce_scatter | solution.py:858
  7.3 7.2 %collective-permute-start = (bf16[2,1472,128]{2,1,0:T(8,128)(2,1)}, bf16[2,1472,128]{2,1,0:T(8,128)(2,1)S(1)}, u32[]{:S(2)}, u32[]{:S(2)}) collective-permute-start(bf16[2,1472,128]{2,1,0:T(8,128)(2,1)} %bitcast.101), channel_id=1, source_target_pairs={{0,1},{1,0},{2,3},{3,2},{4,5},{5,4},{6,7},{7,6},{8,9},{9,8},{10,11... | collective-permute-start | bytes 2261000 | tf_op jit(solution)/shard_map/x_core/ppermute | solution.py:86
  7.8 11.3 %collective-permute-start.1 = (bf16[2,1472,128]{2,1,0:T(8,128)(2,1)}, bf16[2,1472,128]{2,1,0:T(8,128)(2,1)}, u32[]{:S(2)}, u32[]{:S(2)}) collective-permute-start(bf16[2,1472,128]{2,1,0:T(8,128)(2,1)} %bitcast.99), channel_id=1, source_target_pairs={{0,1},{1,0},{2,3},{3,2},{4,5},{5,4},{6,7},{7,6},{8,9},{9,8},{10,11... | collective-permute-start | bytes 2261000 | tf_op jit(solution)/shard_map/dy_core/ppermute | solution.py:86
  7.9 15.1 %collective-permute-start.3 = (bf16[448,1472]{1,0:T(8,128)(2,1)}, bf16[448,1472]{1,0:T(8,128)(2,1)S(1)}, u32[]{:S(2)}, u32[]{:S(2)}) collective-permute-start(bf16[448,1472]{1,0:T(8,128)(2,1)} %bitcast.78), channel_id=1, source_target_pairs={{0,1},{1,0},{2,3},{3,2},{4,5},{5,4},{6,7},{7,6},{8,9},{9,8},{10,11... | collective-permute-start | bytes 3956744 | tf_op jit(solution)/shard_map/gate_core/ppermute | solution.py:86
  8.3 14.7 %collective-permute-start.4 = (bf16[448,1472]{1,0:T(8,128)(2,1)}, bf16[448,1472]{1,0:T(8,128)(2,1)}, u32[]{:S(2)}, u32[]{:S(2)}) collective-permute-start(bf16[448,1472]{1,0:T(8,128)(2,1)} %bitcast.83), channel_id=1, source_target_pairs={{0,1},{1,0},{2,3},{3,2},{4,5},{5,4},{6,7},{7,6},{8,9},{9,8},{10,11... | collective-permute-start | bytes 3956744 | tf_op jit(solution)/shard_map/up_core/ppermute | solution.py:86
  8.4 29.7 %collective-permute-start.5 = (bf16[448,1472]{1,0:T(8,128)(2,1)}, bf16[448,1472]{1,0:T(8,128)(2,1)S(1)}, u32[]{:S(2)}, u32[]{:S(2)}) collective-permute-start(bf16[448,1472]{1,0:T(8,128)(2,1)} %d0.15), channel_id=1, source_target_pairs={{0,1},{1,0},{2,3},{3,2},{4,5},{5,4},{6,7},{7,6},{8,9},{9,8},{10,11... | collective-permute-start | bytes 3956744 | tf_op jit(solution)/shard_map/down_core/ppermute | solution.py:86
  16.2 49.3 %copy-start.16 = (bf16[1472,256]{1,0:T(8,128)(2,1)}, bf16[1472,256]{1,0:T(8,128)(2,1)S(1)}, u32[]{:S(2)}) copy-start(bf16[1472,256]{1,0:T(8,128)(2,1)S(1)} %get-tuple-element.148.x_ref) | copy-start | bytes 2260996
  16.2 20.1 %collective-permute-start.2 = (bf16[1472,256]{1,0:T(8,128)(2,1)S(1)}, bf16[1472,256]{1,0:T(8,128)(2,1)S(1)}, u32[]{:S(2)}, u32[]{:S(2)}) collective-permute-start(bf16[1472,256]{1,0:T(8,128)(2,1)S(1)} %get-tuple-element.133.n_ref.n0_ref), channel_id=1, source_target_pairs={{0,4},{4,0},{1,5},{5,1},{2,6},{6,2},{3,7},{7,3},{8,12},{12,8},{9,1... | collective-permute-start | bytes 2261000 | tf_op jit(solution)/shard_map/n1_y/ppermute | solution.py:86
  20.5 110.5 %copy-start.5 = (bf16[1472,256]{1,0:T(8,128)(2,1)}, bf16[1472,256]{1,0:T(8,128)(2,1)S(1)}, u32[]{:S(2)}) copy-start(bf16[1472,256]{1,0:T(8,128)(2,1)S(1)} %pair.1.dy_ref.refs_4_) | copy-start | bytes 2260996
  21.2 25.8 %copy-start.25 = (bf16[384,256]{1,0:T(8,128)(2,1)}, bf16[384,256]{1,0:T(8,128)(2,1)S(1)}, u32[]{:S(2)}) copy-start(bf16[384,256]{1,0:T(8,128)(2,1)S(1)} %get-tuple-element.136.k0) | copy-start | bytes 589828
  21.2 16.9 %collective-permute-start.6 = (bf16[384,256]{1,0:T(8,128)(2,1)S(1)}, bf16[384,256]{1,0:T(8,128)(2,1)S(1)}, u32[]{:S(2)}, u32[]{:S(2)}) collective-permute-start(bf16[384,256]{1,0:T(8,128)(2,1)S(1)} %get-tuple-element.136.k0), channel_id=1, source_target_pairs={{0,2},{1,3},{2,0},{3,1},{4,6},{5,7},{6,4},{7,5},{8,10},{9,11},{10,... | collective-permute-start | bytes 589832 | tf_op jit(solution)/shard_map/kv_own_x/ppermute | solution.py:86
  36.3 10.2 %collective-permute-start.9 = (bf16[96,1472]{1,0:T(8,128)(2,1)S(1)}, bf16[96,1472]{1,0:T(8,128)(2,1)S(1)}, u32[]{:S(2)}, u32[]{:S(2)}) collective-permute-start(bf16[96,1472]{1,0:T(8,128)(2,1)S(1)} %copy-done.48), channel_id=1, source_target_pairs={{0,4},{4,0},{1,5},{5,1},{2,6},{6,2},{3,7},{7,3},{8,12},{12,8},{9,1... | collective-permute-start | bytes 847880 | tf_op jit(solution)/shard_map/wout_y/ppermute | solution.py:86
  38.7 17.5 %copy-start.29 = (bf16[384,256]{1,0:T(8,128)(2,1)}, bf16[384,256]{1,0:T(8,128)(2,1)S(1)}, u32[]{:S(2)}) copy-start(bf16[384,256]{1,0:T(8,128)(2,1)S(1)} %get-tuple-element.140.k1) | copy-start | bytes 589828
  38.8 6.3 %collective-permute-start.7 = (bf16[384,256]{1,0:T(8,128)(2,1)S(1)}, bf16[384,256]{1,0:T(8,128)(2,1)S(1)}, u32[]{:S(2)}, u32[]{:S(2)}) collective-permute-start(bf16[384,256]{1,0:T(8,128)(2,1)S(1)} %get-tuple-element.140.k1), channel_id=1, source_target_pairs={{0,2},{1,3},{2,0},{3,1},{4,6},{5,7},{6,4},{7,5},{8,10},{9,11},{10,... | collective-permute-start | bytes 589832 | tf_op jit(solution)/shard_map/kv_far_x/ppermute | solution.py:86
  45.0 17.2 %collective-permute-start.8 = (bf16[1472,256]{1,0:T(8,128)(2,1)S(1)}, bf16[1472,256]{1,0:T(8,128)(2,1)S(1)}, u32[]{:S(2)}, u32[]{:S(2)}) collective-permute-start(bf16[1472,256]{1,0:T(8,128)(2,1)S(1)} %pair.1.dy_ref.refs_4_), channel_id=1, source_target_pairs={{0,2},{1,3},{2,0},{3,1},{4,6},{5,7},{6,4},{7,5},{8,10},{9,11},{10,... | collective-permute-start | bytes 2261000 | tf_op jit(solution)/shard_map/dy_x/ppermute | solution.py:86
  46.5 19.0 %copy-start.19 = (bf16[96,1472]{1,0:T(8,128)(2,1)}, bf16[96,1472]{1,0:T(8,128)(2,1)S(1)}, u32[]{:S(2)}) copy-start(bf16[96,1472]{1,0:T(8,128)(2,1)S(1)} %collective-permute-done.9.w1_ref) | copy-start | bytes 847876
  46.5 18.0 %collective-permute-start.10 = (bf16[1472,256]{1,0:T(8,128)(2,1)S(1)}, bf16[1472,256]{1,0:T(8,128)(2,1)S(1)}, u32[]{:S(2)}, u32[]{:S(2)}) collective-permute-start(bf16[1472,256]{1,0:T(8,128)(2,1)S(1)} %pair.1.dy_ref.refs_4_), channel_id=1, source_target_pairs={{0,4},{4,0},{1,5},{5,1},{2,6},{6,2},{3,7},{7,3},{8,12},{12,8},{9,1... | collective-permute-start | bytes 2261000 | tf_op jit(solution)/shard_map/dy_y/ppermute | solution.py:86
  56.3 9.3 %collective-permute-start.12 = (bf16[96,1472]{1,0:T(8,128)(2,1)S(1)}, bf16[96,1472]{1,0:T(8,128)(2,1)S(1)}, u32[]{:S(2)}, u32[]{:S(2)}) collective-permute-start(bf16[96,1472]{1,0:T(8,128)(2,1)S(1)} %collective-permute-done.9.w1_ref), channel_id=1, source_target_pairs={{0,1},{1,0},{2,3},{3,2},{4,5},{5,4},{6,7},{7,6},{8,9},{9,8},{10,11... | collective-permute-start | bytes 847880 | tf_op jit(solution)/shard_map/wout_core/ppermute | solution.py:86
  56.4 9.1 %collective-permute-start.11 = (bf16[192,256]{1,0:T(8,128)(2,1)S(1)}, bf16[192,256]{1,0:T(8,128)(2,1)S(1)}, u32[]{:S(2)}, u32[]{:S(2)}) collective-permute-start(bf16[192,256]{1,0:T(8,128)(2,1)S(1)} %get-tuple-element.303), channel_id=1, source_target_pairs={{0,4},{4,0},{1,5},{5,1},{2,6},{6,2},{3,7},{7,3},{8,12},{12,8},{9,1... | collective-permute-start | bytes 294920 | tf_op jit(solution)/shard_map/mixed_y/ppermute | solution.py:86
  67.6 19.8 %collective-permute-start.13 = (bf16[1472,256]{1,0:T(8,128)(2,1)S(1)}, bf16[1472,256]{1,0:T(8,128)(2,1)S(1)}, u32[]{:S(2)}, u32[]{:S(2)}) collective-permute-start(bf16[1472,256]{1,0:T(8,128)(2,1)S(1)} %get-tuple-element.153.n_ref.refs_12_.refs_20_), channel_id=1, source_target_pairs={{0,2},{1,3},{2,0},{3,1},{4,6},{5,7},{6,4},{7,5},{8,10},{9,11},{10,... | collective-permute-start | bytes 2261000 | tf_op jit(solution)/shard_map/n2_x/ppermute | solution.py:86
  68.3 19.1 %collective-permute-start.14 = (bf16[1472,256]{1,0:T(8,128)(2,1)S(1)}, bf16[1472,256]{1,0:T(8,128)(2,1)S(1)}, u32[]{:S(2)}, u32[]{:S(2)}) collective-permute-start(bf16[1472,256]{1,0:T(8,128)(2,1)S(1)} %get-tuple-element.153.n_ref.refs_12_.refs_20_), channel_id=1, source_target_pairs={{0,4},{4,0},{1,5},{5,1},{2,6},{6,2},{3,7},{7,3},{8,12},{12,8},{9,1... | collective-permute-start | bytes 2261000 | tf_op jit(solution)/shard_map/n2_y/ppermute | solution.py:86
  69.9 32.2 %collective-permute-start.16 = (bf16[1472,256]{1,0:T(8,128)(2,1)S(1)}, bf16[1472,256]{1,0:T(8,128)(2,1)S(1)}, u32[]{:S(2)}, u32[]{:S(2)}) collective-permute-start(bf16[1472,256]{1,0:T(8,128)(2,1)S(1)} %pick.2), channel_id=1, source_target_pairs={{0,4},{1,3},{2,6},{3,1},{4,0},{5,7},{6,2},{7,5},{8,12},{9,11},{10,... | collective-permute-start | bytes 2261000 | tf_op jit(solution)/shard_map/dy_d/ppermute | solution.py:86
  87.5 16.5 %collective-permute-start.15 = (bf16[1472,256]{1,0:T(8,128)(2,1)S(1)}, bf16[1472,256]{1,0:T(8,128)(2,1)S(1)}, u32[]{:S(2)}, u32[]{:S(2)}) collective-permute-start(bf16[1472,256]{1,0:T(8,128)(2,1)S(1)} %pick.3), channel_id=1, source_target_pairs={{0,4},{1,3},{2,6},{3,1},{4,0},{5,7},{6,2},{7,5},{8,12},{9,11},{10,... | collective-permute-start | bytes 2261000 | tf_op jit(solution)/shard_map/n2_d/ppermute | solution.py:86
  94.0 19.8 %collective-permute-start.17 = (bf16[1472,256]{1,0:T(8,128)(2,1)S(1)}, bf16[1472,256]{1,0:T(8,128)(2,1)S(1)}, u32[]{:S(2)}, u32[]{:S(2)}) collective-permute-start(bf16[1472,256]{1,0:T(8,128)(2,1)S(1)} %get-tuple-element.166), channel_id=1, source_target_pairs={{0,2},{1,3},{2,0},{3,1},{4,6},{5,7},{6,4},{7,5},{8,10},{9,11},{10,... | collective-permute-start | bytes 2261000 | tf_op jit(solution)/shard_map/dn_x/ppermute | solution.py:86
  101.5 15.2 %collective-permute-start.18 = (bf16[1472,256]{1,0:T(8,128)(2,1)S(1)}, bf16[1472,256]{1,0:T(8,128)(2,1)S(1)}, u32[]{:S(2)}, u32[]{:S(2)}) collective-permute-start(bf16[1472,256]{1,0:T(8,128)(2,1)S(1)} %get-tuple-element.167), channel_id=1, source_target_pairs={{0,4},{4,0},{1,5},{5,1},{2,6},{6,2},{3,7},{7,3},{8,12},{12,8},{9,1... | collective-permute-start | bytes 2261000 | tf_op jit(solution)/shard_map/dn_y/ppermute | solution.py:86
  123.1 7.9 %collective-permute-start.22 = (bf16[3,448,1472]{2,1,0:T(8,128)(2,1)S(1)}, bf16[3,448,1472]{2,1,0:T(8,128)(2,1)S(1)}, u32[]{:S(2)}, u32[]{:S(2)}) collective-permute-start(bf16[3,448,1472]{2,1,0:T(8,128)(2,1)S(1)} %wgrad_give.1), channel_id=1, source_target_pairs={{0,1},{1,0},{2,3},{3,2},{4,5},{5,4},{6,7},{7,6},{8,9},{9,8},{10,11... | collective-permute-start | bytes 11870216 | tf_op jit(solution)/shard_map/wgrad_core/ppermute | solution.py:86
  123.2 20.4 %collective-permute-start.19 = (bf16[1472,256]{1,0:T(8,128)(2,1)}, bf16[1472,256]{1,0:T(8,128)(2,1)S(1)}, u32[]{:S(2)}, u32[]{:S(2)}) collective-permute-start(bf16[1472,256]{1,0:T(8,128)(2,1)} %get-tuple-element.179), channel_id=1, source_target_pairs={{0,6},{1,7},{2,4},{3,5},{4,2},{5,3},{6,0},{7,1},{8,14},{9,15},{10,... | collective-permute-start | bytes 2261000 | tf_op jit(solution)/shard_map/dn_d/ppermute | solution.py:86
  137.6 182.4 %all-gather.2.cloned.1.call-start = ((), (), s32[]{:S(2)}) async-start(), calls=%async_computation.2 | async-start | bytes 5160960 | tf_op jit(solution)/shard_map/all_gather | solution.py:957
  149.4 4.9 %collective-permute-start.23 = (bf16[192,256]{1,0:T(8,128)(2,1)S(1)}, bf16[192,256]{1,0:T(8,128)(2,1)S(1)}, u32[]{:S(2)}, u32[]{:S(2)}) collective-permute-start(bf16[192,256]{1,0:T(8,128)(2,1)S(1)} %get-tuple-element.191), channel_id=1, source_target_pairs={{0,4},{4,0},{1,5},{5,1},{2,6},{6,2},{3,7},{7,3},{8,12},{12,8},{9,1... | collective-permute-start | bytes 294920 | tf_op jit(solution)/shard_map/dmixed_y/ppermute | solution.py:86
  151.2 21.0 %collective-permute-start.20 = (bf16[1472,256]{1,0:T(8,128)(2,1)}, bf16[1472,256]{1,0:T(8,128)(2,1)S(1)}, u32[]{:S(2)}, u32[]{:S(2)}) collective-permute-start(bf16[1472,256]{1,0:T(8,128)(2,1)} %ffn_out.5), channel_id=1, source_target_pairs={{0,2},{1,3},{2,0},{3,1},{4,6},{5,7},{6,4},{7,5},{8,10},{9,11},{10,... | collective-permute-start | bytes 2261000 | tf_op jit(solution)/shard_map/out_x/ppermute | solution.py:86
  152.1 20.2 %collective-permute-start.21 = (bf16[1472,256]{1,0:T(8,128)(2,1)}, bf16[1472,256]{1,0:T(8,128)(2,1)}, u32[]{:S(2)}, u32[]{:S(2)}) collective-permute-start(bf16[1472,256]{1,0:T(8,128)(2,1)} %ffn_out.6), channel_id=1, source_target_pairs={{0,4},{4,0},{1,5},{5,1},{2,6},{6,2},{3,7},{7,3},{8,12},{12,8},{9,1... | collective-permute-start | bytes 2261000 | tf_op jit(solution)/shard_map/out_y/ppermute | solution.py:86
  165.5 13.8 %copy-start.11 = (bf16[1472,192]{0,1:T(8,128)(2,1)S(1)}, bf16[1472,192]{0,1:T(8,128)(2,1)}, u32[]{:S(2)}) copy-start(bf16[1472,192]{0,1:T(8,128)(2,1)} %param.21) | copy-start | bytes 1695748
  165.5 13.8 %copy-start.13 = (bf16[1472,192]{0,1:T(8,128)(2,1)S(1)}, bf16[1472,192]{0,1:T(8,128)(2,1)}, u32[]{:S(2)}) copy-start(bf16[1472,192]{0,1:T(8,128)(2,1)} %param.22) | copy-start | bytes 1695748
  167.4 11.2 %collective-permute-start.24 = (bf16[400,512]{1,0:T(8,128)(2,1)}, bf16[400,512]{1,0:T(8,128)(2,1)S(1)}, u32[]{:S(2)}, u32[]{:S(2)}) collective-permute-start(bf16[400,512]{1,0:T(8,128)(2,1)} %get-tuple-element.200), channel_id=1, source_target_pairs={{0,2},{1,3},{2,0},{3,1},{4,6},{5,7},{6,4},{7,5},{8,10},{9,11},{10,... | collective-permute-start | bytes 1228808 | tf_op jit(solution)/shard_map/dkv_x/ppermute | solution.py:86
  168.5 15.4 %collective-permute-start.25 = (bf16[192,1472]{1,0:T(8,128)(2,1)}, bf16[192,1472]{1,0:T(8,128)(2,1)}, u32[]{:S(2)}, u32[]{:S(2)}) collective-permute-start(bf16[192,1472]{1,0:T(8,128)(2,1)} %get-tuple-element.207), channel_id=1, source_target_pairs={{0,4},{4,0},{1,5},{5,1},{2,6},{6,2},{3,7},{7,3},{8,12},{12,8},{9,1... | collective-permute-start | bytes 1695752 | tf_op jit(solution)/shard_map/gout_y/ppermute | solution.py:86
  189.1 3.1 collective-permute-start.26
  189.1 23.0 %collective-permute-start.28 = (bf16[1504,256]{1,0:T(8,128)(2,1)}, bf16[1504,256]{1,0:T(8,128)(2,1)S(1)}, u32[]{:S(2)}, u32[]{:S(2)}) collective-permute-start(bf16[1504,256]{1,0:T(8,128)(2,1)} %get-tuple-element.214), channel_id=1, source_target_pairs={{0,4},{4,0},{1,5},{5,1},{2,6},{6,2},{3,7},{7,3},{8,12},{12,8},{9,1... | collective-permute-start | bytes 2310152 | tf_op jit(solution)/shard_map/back_y/ppermute | solution.py:86
  195.5 15.4 %collective-permute-start.27 = (bf16[192,1472]{1,0:T(8,128)(2,1)S(1)}, bf16[192,1472]{1,0:T(8,128)(2,1)S(1)}, u32[]{:S(2)}, u32[]{:S(2)}) collective-permute-start(bf16[192,1472]{1,0:T(8,128)(2,1)S(1)} %get-tuple-element.211), channel_id=1, source_target_pairs={{0,2},{1,3},{2,0},{3,1},{4,6},{5,7},{6,4},{7,5},{8,10},{9,11},{10,... | collective-permute-start | bytes 1695752 | tf_op jit(solution)/shard_map/fold_x/ppermute | solution.py:86
  218.1 12.8 %collective-permute-start.32 = (f32[1504,128]{1,0:T(8,128)}, f32[1504,128]{1,0:T(8,128)S(1)}, u32[]{:S(2)}, u32[]{:S(2)}) collective-permute-start(f32[1504,128]{1,0:T(8,128)} %copy-done.37), channel_id=1, source_target_pairs={{0,1},{1,0},{2,3},{3,2},{4,5},{5,4},{6,7},{7,6},{8,9},{9,8},{10,11... | collective-permute-start | bytes 2310152 | tf_op jit(solution)/shard_map/grad_core/ppermute | solution.py:86
  218.1 9.4 %collective-permute-start.30 = (bf16[96,1472]{1,0:T(8,128)(2,1)S(1)}, bf16[96,1472]{1,0:T(8,128)(2,1)S(1)}, u32[]{:S(2)}, u32[]{:S(2)}) collective-permute-start(bf16[96,1472]{1,0:T(8,128)(2,1)S(1)} %get-tuple-element.221), channel_id=1, source_target_pairs={{0,8},{8,0},{16,24},{24,16},{1,9},{9,1},{17,25},{25,17},{2,10},{10... | collective-permute-start | bytes 847880 | tf_op jit(solution)/shard_map/share_z/ppermute | solution.py:86
  228.4 19.7 %collective-permute-start.31 = (bf16[48,1472]{1,0:T(8,128)(2,1)S(1)}, bf16[48,1472]{1,0:T(8,128)(2,1)S(1)}, u32[]{:S(2)}, u32[]{:S(2)}) collective-permute-start(bf16[48,1472]{1,0:T(8,128)(2,1)S(1)} %get-tuple-element.223), channel_id=1, source_target_pairs={{0,16},{8,24},{16,0},{24,8},{1,17},{9,25},{17,1},{25,9},{2,18},{10... | collective-permute-start | bytes 423944 | tf_op jit(solution)/shard_map/share_z/ppermute | solution.py:86
  248.2 13.8 %collective-permute-start.33 = (bf16[64,1472]{1,0:T(8,128)(2,1)S(1)}, bf16[64,1472]{1,0:T(8,128)(2,1)S(1)}, u32[]{:S(2)}, u32[]{:S(2)}) collective-permute-start(bf16[64,1472]{1,0:T(8,128)(2,1)S(1)} %share_sum.1.refs_0_), channel_id=1, source_target_pairs={{0,8},{8,16},{16,24},{24,0},{1,9},{9,17},{17,25},{25,1},{2,10},{10... | collective-permute-start | bytes 565256 | tf_op jit(solution)/shard_map/join_z/ppermute | solution.py:86
  248.2 27.1 %collective-permute-start.34 = (bf16[64,1472]{1,0:T(8,128)(2,1)S(1)}, bf16[64,1472]{1,0:T(8,128)(2,1)S(1)}, u32[]{:S(2)}, u32[]{:S(2)}) collective-permute-start(bf16[64,1472]{1,0:T(8,128)(2,1)S(1)} %share_sum.1.refs_0_), channel_id=1, source_target_pairs={{0,16},{8,24},{16,0},{24,8},{1,17},{9,25},{17,1},{25,9},{2,18},{10... | collective-permute-start | bytes 565256 | tf_op jit(solution)/shard_map/join_z/ppermute | solution.py:86
  251.4 23.9 %collective-permute-start.35 = (bf16[64,1472]{1,0:T(8,128)(2,1)S(1)}, bf16[64,1472]{1,0:T(8,128)(2,1)S(1)}, u32[]{:S(2)}, u32[]{:S(2)}) collective-permute-start(bf16[64,1472]{1,0:T(8,128)(2,1)S(1)} %share_sum.1.refs_0_), channel_id=1, source_target_pairs={{0,24},{8,0},{16,8},{24,16},{1,25},{9,1},{17,9},{25,17},{2,26},{10... | collective-permute-start | bytes 565256 | tf_op jit(solution)/shard_map/join_z/ppermute | solution.py:86
  252.0 25.5 %collective-permute-start.29 = (bf16[1472,256]{1,0:T(8,128)(2,1)}, bf16[1472,256]{1,0:T(8,128)(2,1)S(1)}, u32[]{:S(2)}, u32[]{:S(2)}) collective-permute-start(bf16[1472,256]{1,0:T(8,128)(2,1)} %ffn_out.7), channel_id=1, source_target_pairs={{0,6},{1,7},{2,4},{3,5},{4,2},{5,3},{6,0},{7,1},{8,14},{9,15},{10,... | collective-permute-start | bytes 2261000 | tf_op jit(solution)/shard_map/out_d/ppermute | solution.py:86
  276.0 16.5 %collective-permute-start.36 = (bf16[208,1472]{1,0:T(8,128)(2,1)S(1)}, bf16[208,1472]{1,0:T(8,128)(2,1)S(1)}, u32[]{:S(2)}, u32[]{:S(2)}) collective-permute-start(bf16[208,1472]{1,0:T(8,128)(2,1)S(1)} %get-tuple-element.228.own_ref), channel_id=1, source_target_pairs={{0,2},{1,3},{2,0},{3,1},{4,6},{5,7},{6,4},{7,5},{8,10},{9,11},{10,... | collective-permute-start | bytes 1837064 | tf_op jit(solution)/shard_map/join_x/ppermute | solution.py:86
  293.3 8.3 %collective-permute-start.38 = (bf16[2,192,1472]{2,1,0:T(8,128)(2,1)S(1)}, bf16[2,192,1472]{2,1,0:T(8,128)(2,1)S(1)}, u32[]{:S(2)}, u32[]{:S(2)}) collective-permute-start(bf16[2,192,1472]{2,1,0:T(8,128)(2,1)S(1)} %get-tuple-element.233.own_ref), channel_id=1, source_target_pairs={{0,1},{1,0},{2,3},{3,2},{4,5},{5,4},{6,7},{7,6},{8,9},{9,8},{10,11... | collective-permute-start | bytes 3391496 | tf_op jit(solution)/shard_map/join_core/ppermute | solution.py:86
  293.3 3.4 %collective-permute-start.37 = (bf16[1472,128]{1,0:T(8,128)(2,1)}, bf16[1472,128]{1,0:T(8,128)(2,1)}, u32[]{:S(2)}, u32[]{:S(2)}) collective-permute-start(bf16[1472,128]{1,0:T(8,128)(2,1)} %get-tuple-element.231), channel_id=1, source_target_pairs={{0,1},{1,0},{2,3},{3,2},{4,5},{5,4},{6,7},{7,6},{8,9},{9,8},{10,11... | collective-permute-start | bytes 1130504 | tf_op jit(solution)/shard_map/out_core/ppermute | solution.py:86
  (44 other events, 273.0 us)
Sparse Core Ops, SparseCore 0:
  137.7 76.2 reduce-scatter.1
  217.4 102.5 all-gather.1

commit v4 on v3

--- a/solution.py
+++ b/solution.py
@@ -422,19 +422,42 @@
     )
 
 
+def mids_shape(refs):
+    return refs[0].shape[1], refs[4].shape[0]
+
+
+def packing(rows, width):
+    full, rest = divmod(width, LANES)
+    assert 2 * rest == LANES and rows % 16 == 0
+    half = rows // 2
+    plan = []
+    for at in range(full):
+        lanes = slice(at * LANES, (at + 1) * LANES)
+        plan.append((lanes, (slice(at * rows, (at + 1) * rows), ((0, rows),))))
+    lanes = slice(full * LANES, width)
+    plan.append((lanes, (slice(full * rows, full * rows + half), ((0, half), (half, half)))))
+    return plan
+
+
 def wgrad_sum_kernel(*refs):
     out_ref = refs[-1]
-    n, pieces, rows, _ = out_ref.shape
-    got = refs[-2]
+    n, pieces = out_ref.shape[:2]
+    hidden, width = mids_shape(refs)
+    rows = hidden // n
+    gots = [(ref, at) for ref in refs[8 * pieces : -1] for at in range(ref.shape[0])]
     for at in range(pieces):
         mids, blocks = refs[8 * at : 8 * at + 4], refs[8 * at + 4 : 8 * at + 8]
         total = None
         for mid, block in zip(mids, blocks):
             more = dot_nt(mid[0], block[...])
             total = more if total is None else total + more
-        total = (total + got[at].astype(F32)).astype(BF)
+        got, line = gots[at]
+        total = total + got[line].astype(F32)
         for q in range(n):
-            out_ref[q, at] = total[q * rows : (q + 1) * rows]
+            share = total[q * rows : (q + 1) * rows]
+            for lanes, places in packing(rows, width):
+                piece = [share[first : first + size, lanes] for first, size in places[1]]
+                out_ref[q, at, places[0]] = jnp.concatenate(piece, axis=1).astype(BF)
 
 
 def wgrad_stack_kernel(part, *refs):
@@ -458,12 +481,13 @@
     )
 
 
-def wgrad_sum(pieces, got, shares):
+def wgrad_sum(pieces, gots, shares):
     mids, rows = pieces[0]
-    shape = (shares, len(pieces), mids[0].shape[1] // shares, rows[0].shape[0])
+    size = mids[0].shape[1] // shares * rows[0].shape[0]
+    shape = (shares, len(pieces), size // LANES, LANES)
     args = [v for mids, rows in pieces for v in (*mids, *rows)]
     return call(
-        wgrad_sum_kernel, hbm(shape, BF), (*args, got), "wgrad_sum", vmem=28,
+        wgrad_sum_kernel, hbm(shape, BF), (*args, *gots), "wgrad_sum", vmem=28,
     )
 
 
@@ -640,16 +664,22 @@
 
 def widen_kernel(src, *outs):
     for at, out in enumerate(outs):
-        out[...] = src[0, at].astype(F32)
-
-
-def widen(v):
-    n, pieces, rows, width = v.shape
+        for lanes, (lines, places) in packing(*out.shape):
+            piece = src[0, at, lines].astype(F32)
+            lane = 0
+            for first, size in places:
+                wide = lanes.stop - lanes.start
+                out[first : first + size, lanes] = piece[:, lane : lane + wide]
+                lane += wide
+
+
+def widen(v, rows, width):
+    n, pieces, lines, _ = v.shape
     outs = pl.pallas_call(
         widen_kernel,
         out_shape=[sds((n * rows, width), F32)] * pieces,
         grid=(n,),
-        in_specs=[pl.BlockSpec((1, pieces, rows, width), lambda i: (i, 0, 0, 0))],
+        in_specs=[pl.BlockSpec((1, pieces, lines, LANES), lambda i: (i, 0, 0, 0))],
         out_specs=[pl.BlockSpec((rows, width), lambda i: (i, 0))] * pieces,
         compiler_params=pltpu.CompilerParams(vmem_limit_bytes=32 << 20),
         cost_estimate=cost(500),
@@ -809,7 +839,7 @@
 
     probs, mixed = attn_fwd(queries, kvs, bias, heads, block)
     mixed_far = y_swap(mixed[:, block:], "mixed_y")
-    dy_d = relay(dy_x, dy_y, "dy_d")
+    mixed_far = after(mixed_far, dy_x, dy_y)
     mixed_own = mixed[:, :block]
     residual, normed_two, inv_two = call(
         mid_kernel,
@@ -822,6 +852,7 @@
 
     n_x = x_swap(normed_two, "n2_x")
     n_y = y_swap(normed_two, "n2_y")
+    dy_d = relay(dy_x, dy_y, "dy_d")
     def d_act_of(dy):
         shape = sds((2, hidden, block), F32)
         return call(d_act_kernel, shape, (dy, down_weight, down_other), "d_act")
@@ -845,15 +876,16 @@
         ((dg_o, dg_x, dg_y, dg_d), n_all),
         ((du_o, du_x, du_y, du_d), n_all),
     )
+    given_d = core_swap(wgrad_give(pieces[:1]), "wgrad_core")
     out_o = ffn_out(act_o, down_weight, down_other, BF)
-    mids, rows = pieces[0]
-    pieces = (((after(mids[0], got_x, got_y), *mids[1:]), rows), *pieces[1:])
-    given = core_swap(wgrad_give(pieces), "wgrad_core")
+    mids, rows = pieces[1]
+    gated = (((after(mids[0], got_x, got_y), *mids[1:]), rows), pieces[2])
+    given_gu = core_swap(wgrad_give(gated), "wgrad_core")
     part_x = ffn_out(act_x, down_weight, down_other, BF)
     part_y = ffn_out(act_y, down_weight, down_other, BF)
     part_d = ffn_out(act_d, down_weight, down_other, BF)
     shares = dp_axis if dp_axis <= 8 else 1
-    ffn_grads = wgrad_sum(pieces, given, shares)
+    ffn_grads = wgrad_sum(pieces, (given_d, given_gu), shares)
     if shares > 1:
         ffn_grads = lax.psum_scatter(ffn_grads, "dp", scatter_dimension=0, tiled=True)
     else:
@@ -997,7 +1029,7 @@
     )
     mask_keep, mask_got = small[:1], small_got[:1]
     grad_mask = jnp.where(c_at == 0, stack(mask_keep, mask_got), stack(mask_got, mask_keep))
-    grad_down, grad_gate, grad_up = widen(ffn_grads)
+    grad_down, grad_gate, grad_up = widen(ffn_grads, hidden // shares, width)
     return (
         jnp.swapaxes(output, 1, 2),
         jnp.swapaxes(grad_inputs, 1, 2),

time: 337 us -> 332 us (0.985)
    ppermute x39 -> x40, starting transfers between devices: 41.1 us -> 38.6 us  [move(): return lax.ppermute(v, axes, pairs)]
    unnamed x107 -> x105, local copies, waits for them, and re-layouts: 9.28 us -> 7.83 us
    pallas_call x36 -> x37, Pallas kernels: 88.7 us -> 89.5 us  [call(): pl.pallas_call(kernel, out_shape=out_shape, in_specs=in_specs, out_specs=...]
    ppermute x39 -> x40, waiting for transfers between devices: 121 us -> 120 us  [move(): return lax.ppermute(v, axes, pairs)]
  transfers between devices with their start and end apart: 41 -> 42, of which waited for: 21 -> 19; matrix products, arithmetic and copies ran while one was open for 3% -> 3% of each run, Pallas kernels for 32% -> 33%
where the time goes in v4:
time: 332 us; the launch traced here: 328 us
  waiting for transfers between devices  135 us (41%)
  Pallas kernels  122 us (37%)
  starting transfers between devices  38.6 us (12%)
  local copies, waits for them, and re-layouts  15.3 us (5%)
  between operations  15.1 us (5%)
    ppermute x40, waiting for transfers between devices, move(): return lax.ppermute(v, axes, pairs)  120 us
    pallas_call x37, Pallas kernels, call(): pl.pallas_call(kernel, out_shape=out_shape, in_specs=in_specs, out_specs=...  89.5 us
    ppermute x40, starting transfers between devices, move(): return lax.ppermute(v, axes, pairs)  38.6 us
    all_gather x1, waiting for transfers between devices, run(): lax.all_gather(after(ffn_grads, rows_keep), 'dp', axis=0, tiled=True)  14.6 us
    pallas_call x1, Pallas kernels, attn_bwd(): pl.pallas_call(functools.partial(attn_bwd_kernel, inner=inner, heads=head...  11.1 us
    pallas_call x1, Pallas kernels, attn_fwd(): pl.pallas_call(functools.partial(attn_fwd_kernel, inner=inner), out_shape...  9.18 us
    unnamed x105, local copies, waits for them, and re-layouts  7.83 us
  transfers between devices with their start and end apart: 42, of which 19 were waited for; matrix products, arithmetic and copies ran while one was open for 3% of the time, Pallas kernels for 33%

profile of v4, /device:TPU:0, one launch (start us, length us, event | category | flops | bytes accessed | tf_op | source)
XLA Modules:
  0.0 327.8 jit_solution(13727442491503786158)
XLA Ops:
  10.9 1.7 dynamic-slice_bitcast_fusion
  14.4 1.7 prep.1
  16.2 2.7 collective-permute-start.2
  23.0 6.0 %bias.1.bias_ref = f32[3,1024,512]{2,1,0:T(8,128)} custom-call(s32[8]{0:T(128)S(1)} %sub.44.start_ref, f32[8,2048]{1,0:T(8,128)S(1)} %concatenate.83.table_ref, f32[1,1024]{1,0:T(1,128)S(1)} %reshape.105.mask_ref), custom_call_target="tpu_custom_call" | custom-call | bytes 30000 | tf_op jit(solution)/shard_map/bias/pallas_call | solution.py:148
  29.0 7.3 %collective-permute-done.2.n_ref.n1_ref = bf16[1472,256]{1,0:T(8,128)(2,1)S(1)} collective-permute-done((bf16[1472,256]{1,0:T(8,128)(2,1)S(1)}, bf16[1472,256]{1,0:T(8,128)(2,1)S(1)}, u32[]{:S(2)}, u32[]{:S(2)}) %collective-permute-start.2) | collective-permute-done | bytes 753696 | tf_op jit(solution)/shard_map/n1_y/ppermute | solution.py:86
  36.3 1.8 collective-permute-start.10
  40.3 4.7 %collective-permute-done.7.k3 = bf16[384,256]{1,0:T(8,128)(2,1)S(1)} collective-permute-done((bf16[384,256]{1,0:T(8,128)(2,1)S(1)}, bf16[384,256]{1,0:T(8,128)(2,1)S(1)}, u32[]{:S(2)}, u32[]{:S(2)}) %collective-permute-start.7) | collective-permute-done | bytes 196640 | tf_op jit(solution)/shard_map/kv_far_x/ppermute | solution.py:86
  47.1 9.2 %attn_fwd.1 = (f32[3,1024,512]{2,1,0:T(8,128)}, bf16[192,512]{1,0:T(8,128)(2,1)S(1)}) custom-call(bf16[192,512]{1,0:T(8,128)(2,1)S(1)} %constant_dynamic-update-slice_fusion.q_ref, bf16[384,256]{1,0:T(8,128)(2,1)S(1)} %get-tuple-element.138.k0, bf16[384,256]{1,0:T(8,128)(2,1)S(1)} %get-tuple-element.144.k1, bf16[384,256]{1,0:T(8,128)(2,1)S(1)} %collective-permute-done.6.k2, ...), custom_call_target="tpu_custom_call" | custom-call | bytes 30000 | tf_op jit(solution)/shard_map/attn_fwd/pallas_call | solution.py:190
  58.0 7.5 %collective-permute-done.8.m1_ref = bf16[192,256]{1,0:T(8,128)(2,1)S(1)} collective-permute-done((bf16[192,256]{1,0:T(8,128)(2,1)S(1)}, bf16[192,256]{1,0:T(8,128)(2,1)S(1)}, u32[]{:S(2)}, u32[]{:S(2)}) %collective-permute-start.8) | collective-permute-done | bytes 98336 | tf_op jit(solution)/shard_map/mixed_y/ppermute | solution.py:86
  65.6 2.1 mid.1
  71.8 5.7 %ffn.4 = (bf16[2,448,256]{2,1,0:T(8,128)(2,1)S(1)}, bf16[2,448,256]{2,1,0:T(8,128)(2,1)S(1)}, bf16[2,448,256]{2,1,0:T(8,128)(2,1)S(1)}, bf16[1472,256]{1,0:T(8,128)(2,1)S(1)}) custom-call(bf16[1472,256]{1,0:T(8,128)(2,1)S(1)} %get-tuple-element.156.n_ref.refs_4_.refs_12_.refs_20_, f32[2,448,256]{2,1,0:T(8,128)S(1)} %d_act.4.da_ref, ...), custom_call_target="tpu_custom_call" | custom-call | bytes 30000 | tf_op jit(solution)/shard_map/ffn/pallas_call | solution.py:63
  79.2 8.2 %collective-permute-done.13.first_ref.n_ref.refs_5_.refs_13_.refs_21_ = bf16[1472,256]{1,0:T(8,128)(2,1)S(1)} collective-permute-done((bf16[1472,256]{1,0:T(8,128)(2,1)S(1)}, bf16[1472,256]{1,0:T(8,128)(2,1)S(1)}, u32[]{:S(2)}, u32[]{:S(2)}) %collective-permute-start.13) | collective-permute-done | bytes 753696 | tf_op jit(solution)/shard_map/n2_x/ppermute | solution.py:86
  88.3 5.7 %ffn.5 = (bf16[2,448,256]{2,1,0:T(8,128)(2,1)S(1)}, bf16[2,448,256]{2,1,0:T(8,128)(2,1)S(1)}, bf16[2,448,256]{2,1,0:T(8,128)(2,1)S(1)}, bf16[1472,256]{1,0:T(8,128)(2,1)S(1)}) custom-call(bf16[1472,256]{1,0:T(8,128)(2,1)S(1)} %collective-permute-done.13.first_ref.n_ref.refs_5_.refs_13_.refs_21_, f32[2,448,256]{2,1,0:T(8,128)S(1)} %d_act.5.da_ref, ...), custom_call_target="tpu_custom_call" | custom-call | bytes 30000 | tf_op jit(solution)/shard_map/ffn/pallas_call | solution.py:63
  95.6 5.9 %ffn.6 = (bf16[2,448,256]{2,1,0:T(8,128)(2,1)S(1)}, bf16[2,448,256]{2,1,0:T(8,128)(2,1)S(1)}, bf16[2,448,256]{2,1,0:T(8,128)(2,1)S(1)}, bf16[1472,256]{1,0:T(8,128)(2,1)S(1)}) custom-call(bf16[1472,256]{1,0:T(8,128)(2,1)S(1)} %collective-permute-done.14.second_ref.n_ref.refs_6_.refs_14_.refs_22_, f32[2,448,256]{2,1,0:T(8,128)S(1)} %d_act.6.da_ref, ...), custom_call_target="tpu_custom_call" | custom-call | bytes 30000 | tf_op jit(solution)/shard_map/ffn/pallas_call | solution.py:63
  104.1 6.6 %ffn.7 = (bf16[2,448,256]{2,1,0:T(8,128)(2,1)S(1)}, bf16[2,448,256]{2,1,0:T(8,128)(2,1)S(1)}, bf16[2,448,256]{2,1,0:T(8,128)(2,1)S(1)}, bf16[1472,256]{1,0:T(8,128)(2,1)}) custom-call(bf16[1472,256]{1,0:T(8,128)(2,1)S(1)} %collective-permute-done.15.n_ref.refs_7_.refs_15_.refs_23_, f32[2,448,256]{2,1,0:T(8,128)S(1)} %d_act.7.da_ref, ...), custom_call_target="tpu_custom_call" | custom-call | bytes 30000 | tf_op jit(solution)/shard_map/ffn/pallas_call | solution.py:63
  113.9 2.9 collective-permute-done.18.gb_ref
  116.8 1.9 ffn_out.4.own_ref
  118.7 3.0 wgrad_give.3
  123.8 2.4 ffn_out.5
  126.1 1.9 ffn_out.6
  128.1 2.0 ffn_out.7
  130.1 6.6 %wgrad_sum.1 = bf16[4,3,1288,128]{3,2,1,0:T(8,128)(2,1)} custom-call(bf16[2,448,256]{2,1,0:T(8,128)(2,1)S(1)} %get-tuple-element.190.refs_0_.a_ref, bf16[2,448,256]{2,1,0:T(8,128)(2,1)S(1)} %get-tuple-element.182.refs_1_.a_ref, bf16[2,448,256]{2,1,0:T(8,128)(2,1)S(1)} %get-tuple-element.185.refs_2_.a_ref, ...), custom_call_target="tpu_custom_call" | custom-call | bytes 30000 | tf_op jit(solution)/shard_map/wgrad_sum/pallas_call | solution.py:63
  136.7 5.6 %collective-permute-done.19.gd_ref = bf16[1472,256]{1,0:T(8,128)(2,1)} collective-permute-done((bf16[1472,256]{1,0:T(8,128)(2,1)}, bf16[1472,256]{1,0:T(8,128)(2,1)}, u32[]{:S(2)}, u32[]{:S(2)}) %collective-permute-start.19) | collective-permute-done | bytes 753696 | tf_op jit(solution)/shard_map/dn_d/ppermute | solution.py:86
  142.4 5.5 %mid_back.1 = (f32[1472,256]{1,0:T(8,128)}, bf16[1472,256]{1,0:T(8,128)(2,1)S(1)}, f32[1,1472]{1,0:T(1,128)S(1)}, bf16[192,256]{1,0:T(8,128)(2,1)S(1)}, bf16[192,256]{1,0:T(8,128)(2,1)S(1)}) custom-call(s32[1]{0:T(128)} %bitcast.c_ref, bf16[1472,256]{1,0:T(8,128)(2,1)} %copy-done.33, bf16[1472,256]{1,0:T(8,128)(2,1)} %copy-done.41, ...), custom_call_target="tpu_custom_call" | custom-call | bytes 30000 | tf_op jit(solution)/shard_map/mid_back/pallas_call | solution.py:63
  147.9 1.8 collective-permute-start.24
  150.8 2.8 collective-permute-done.24
  153.7 11.1 %attn_bwd.1 = (bf16[192,512]{1,0:T(8,128)(2,1)S(1)}, f32[384,512]{1,0:T(8,128)}, bf16[400,512]{1,0:T(8,128)(2,1)}, f32[1,512]{1,0:T(1,128)S(1)}, f32[3,8,2048]{2,1,0:T(8,128)S(1)}) custom-call(s32[8]{0:T(128)S(1)} %sub.44.start_ref, f32[3,1024,512]{2,1,0:T(8,128)} %get-tuple-element.188.p_ref, bf16[192,512]{1,0:T(8,128)(2,1)S(1)} %copy-done.18, ...), custom_call_target="tpu_custom_call" | custom-call | bytes 1500000000 | tf_op jit(solution)/shard_map/attn_bwd/pallas_call | solution.py:288
  170.9 5.3 %collective-permute-done.25.got_ref = bf16[400,512]{1,0:T(8,128)(2,1)S(1)} collective-permute-done((bf16[400,512]{1,0:T(8,128)(2,1)}, bf16[400,512]{1,0:T(8,128)(2,1)S(1)}, u32[]{:S(2)}, u32[]{:S(2)}) %collective-permute-start.25) | collective-permute-done | bytes 409632 | tf_op jit(solution)/shard_map/dkv_x/ppermute | solution.py:86
  176.9 4.6 %kv_sum.1 = (bf16[384,512]{1,0:T(8,128)(2,1)S(1)}, f32[1472,256]{1,0:T(8,128)}, bf16[1504,256]{1,0:T(8,128)(2,1)}, f32[16,256]{1,0:T(8,128)S(1)}) custom-call(f32[384,512]{1,0:T(8,128)} %get-tuple-element.203.own_ref, bf16[400,512]{1,0:T(8,128)(2,1)} %copy-done.46, f32[1,512]{1,0:T(1,128)S(1)} %get-tuple-element.197.col_ref, ...), custom_call_target="tpu_custom_call" | custom-call | bytes 30000 | tf_op jit(solution)/shard_map/kv_sum/pallas_call | solution.py:63
  181.6 5.2 %fold_core.1 = (f32[2,192,1472]{2,1,0:T(8,128)}, bf16[2,192,1472]{2,1,0:T(8,128)(2,1)}) custom-call(s32[1]{0:T(128)} %bitcast.c_ref, bf16[192,512]{1,0:T(8,128)(2,1)S(1)} %get-tuple-element.209.dq_ref, bf16[384,512]{1,0:T(8,128)(2,1)S(1)} %get-tuple-element.210.dkv_ref, bf16[1472,256]{1,0:T(8,128)(2,1)} %copy-done.6, bf16[1472,256]{1,0:T(8,128)(2,1)} %copy-done.7, ...), custom_call_target="tpu_custom_call" | custom-call | bytes 30000 | tf_op jit(solution)/shard_map/fold_core/pallas_call | solution.py:63
  187.8 1.9 collective-permute-done.27.got_ref
  190.8 2.3 fold_x.1
  193.9 14.6 %collective-permute-done.28.got_ref = bf16[192,1472]{1,0:T(8,128)(2,1)S(1)} collective-permute-done((bf16[192,1472]{1,0:T(8,128)(2,1)S(1)}, bf16[192,1472]{1,0:T(8,128)(2,1)S(1)}, u32[]{:S(2)}, u32[]{:S(2)}) %collective-permute-start.28) | collective-permute-done | bytes 565280 | tf_op jit(solution)/shard_map/fold_x/ppermute | solution.py:86
  210.6 4.2 %last.1 = (f32[1472,128]{1,0:T(8,128)S(1)}, f32[1504,128]{1,0:T(8,128)S(1)}, f32[32,128]{1,0:T(8,128)S(1)}, f32[1488,256]{1,0:T(8,128)}) custom-call(s32[1]{0:T(128)} %bitcast.c_ref, f32[1472,256]{1,0:T(8,128)} %get-tuple-element.217.own_ref, bf16[1504,256]{1,0:T(8,128)(2,1)} %copy-done.39, f32[16,256]{1,0:T(8,128)S(1)} %get-tuple-element.208.small_ref, ...), custom_call_target="tpu_custom_call" | custom-call | bytes 30000 | tf_op jit(solution)/shard_map/last/pallas_call | solution.py:63
  217.3 7.8 %collective-permute-done.31.got_ref = bf16[96,1472]{1,0:T(8,128)(2,1)S(1)} collective-permute-done((bf16[96,1472]{1,0:T(8,128)(2,1)S(1)}, bf16[96,1472]{1,0:T(8,128)(2,1)S(1)}, u32[]{:S(2)}, u32[]{:S(2)}) %collective-permute-start.31) | collective-permute-done | bytes 282656 | tf_op jit(solution)/shard_map/share_z/ppermute | solution.py:86
  225.9 2.7 collective-permute-start.32
  228.6 16.6 %collective-permute-done.32.got_ref = bf16[48,1472]{1,0:T(8,128)(2,1)S(1)} collective-permute-done((bf16[48,1472]{1,0:T(8,128)(2,1)S(1)}, bf16[48,1472]{1,0:T(8,128)(2,1)S(1)}, u32[]{:S(2)}, u32[]{:S(2)}) %collective-permute-start.32) | collective-permute-done | bytes 141344 | tf_op jit(solution)/shard_map/share_z/ppermute | solution.py:86
  245.3 2.8 collective-permute-start.34
  248.1 3.7 %collective-permute-start.35 = (bf16[64,1472]{1,0:T(8,128)(2,1)S(1)}, bf16[64,1472]{1,0:T(8,128)(2,1)S(1)}, u32[]{:S(2)}, u32[]{:S(2)}) collective-permute-start(bf16[64,1472]{1,0:T(8,128)(2,1)S(1)} %share_sum.1.refs_0_), channel_id=1, source_target_pairs={{0,16},{8,24},{16,0},{24,8},{1,17},{9,25},{17,1},{25,9},{2,18},{10... | collective-permute-start | bytes 565256 | tf_op jit(solution)/shard_map/join_z/ppermute | solution.py:86
  251.8 9.4 %collective-permute-done.34.refs_1_ = bf16[64,1472]{1,0:T(8,128)(2,1)S(1)} collective-permute-done((bf16[64,1472]{1,0:T(8,128)(2,1)S(1)}, bf16[64,1472]{1,0:T(8,128)(2,1)S(1)}, u32[]{:S(2)}, u32[]{:S(2)}) %collective-permute-start.34) | collective-permute-done | bytes 188448 | tf_op jit(solution)/shard_map/join_z/ppermute | solution.py:86
  261.1 13.0 %collective-permute-done.35.refs_2_ = bf16[64,1472]{1,0:T(8,128)(2,1)S(1)} collective-permute-done((bf16[64,1472]{1,0:T(8,128)(2,1)S(1)}, bf16[64,1472]{1,0:T(8,128)(2,1)S(1)}, u32[]{:S(2)}, u32[]{:S(2)}) %collective-permute-start.35) | collective-permute-done | bytes 188448 | tf_op jit(solution)/shard_map/join_z/ppermute | solution.py:86
  275.8 4.1 %out_rows.1 = (bf16[1472,128]{1,0:T(8,128)(2,1)S(1)}, bf16[1472,128]{1,0:T(8,128)(2,1)}, bf16[1472,256]{1,0:T(8,128)(2,1)}) custom-call(s32[1]{0:T(128)} %bitcast.c_ref, f32[1472,256]{1,0:T(8,128)} %get-tuple-element.151.res_ref, bf16[1472,256]{1,0:T(8,128)(2,1)} %ffn_out.4.own_ref, bf16[1472,256]{1,0:T(8,128)(2,1)} %copy-done.40, ...), custom_call_target="tpu_custom_call" | custom-call | bytes 30000 | tf_op jit(solution)/shard_map/out_rows/pallas_call | solution.py:63
  281.1 7.7 %collective-permute-done.37.got_ref = bf16[208,1472]{1,0:T(8,128)(2,1)S(1)} collective-permute-done((bf16[208,1472]{1,0:T(8,128)(2,1)S(1)}, bf16[208,1472]{1,0:T(8,128)(2,1)S(1)}, u32[]{:S(2)}, u32[]{:S(2)}) %collective-permute-start.37) | collective-permute-done | bytes 612384 | tf_op jit(solution)/shard_map/join_x/ppermute | solution.py:86
  290.6 2.3 collective-permute-done.38.got_ref
  292.9 1.9 place.3
  297.8 2.4 join_core.1
  300.2 14.6 %all-gather.2.cloned.1.call-done.src = bf16[4,3,1288,128]{3,2,1,0:T(8,128)(2,1)} async-done(((bf16[1,3,1288,128]{3,2,1,0:T(8,128)(2,1)}), bf16[4,3,1288,128]{3,2,1,0:T(8,128)(2,1)}) %all-gather.2.cloned.1.call-update) | async-done | bytes 3956752 | tf_op jit(solution)/shard_map/all_gather | solution.py:989
  314.7 6.0 %widen.1 = (f32[448,1472]{1,0:T(8,128)}, f32[448,1472]{1,0:T(8,128)}, f32[448,1472]{1,0:T(8,128)}) custom-call(bf16[4,3,1288,128]{3,2,1,0:T(8,128)(2,1)} %all-gather.2.cloned.1.call-done.src), custom_call_target="tpu_custom_call" | custom-call | bytes 1500000000 | tf_op jit(solution)/shard_map/widen/pallas_call | solution.py:678
  (238 shorter events, 55.4 us)
Async XLA Ops:
  7.2 207.5 %reduce-scatter.4.cloned.1.call-start = ((), (), s32[]{:S(2)}) async-start(), calls=%async_computation.2 | async-start | bytes 4945920
  7.3 7.2 %collective-permute-start = (bf16[2,1472,128]{2,1,0:T(8,128)(2,1)}, bf16[2,1472,128]{2,1,0:T(8,128)(2,1)S(1)}, u32[]{:S(2)}, u32[]{:S(2)}) collective-permute-start(bf16[2,1472,128]{2,1,0:T(8,128)(2,1)} %bitcast.102), channel_id=1, source_target_pairs={{0,1},{1,0},{2,3},{3,2},{4,5},{5,4},{6,7},{7,6},{8,9},{9,8},{10,11... | collective-permute-start | bytes 2261000 | tf_op jit(solution)/shard_map/x_core/ppermute | solution.py:86
  7.8 11.3 %collective-permute-start.1 = (bf16[2,1472,128]{2,1,0:T(8,128)(2,1)}, bf16[2,1472,128]{2,1,0:T(8,128)(2,1)}, u32[]{:S(2)}, u32[]{:S(2)}) collective-permute-start(bf16[2,1472,128]{2,1,0:T(8,128)(2,1)} %bitcast.100), channel_id=1, source_target_pairs={{0,1},{1,0},{2,3},{3,2},{4,5},{5,4},{6,7},{7,6},{8,9},{9,8},{10,11... | collective-permute-start | bytes 2261000 | tf_op jit(solution)/shard_map/dy_core/ppermute | solution.py:86
  7.9 15.1 %collective-permute-start.3 = (bf16[448,1472]{1,0:T(8,128)(2,1)}, bf16[448,1472]{1,0:T(8,128)(2,1)S(1)}, u32[]{:S(2)}, u32[]{:S(2)}) collective-permute-start(bf16[448,1472]{1,0:T(8,128)(2,1)} %bitcast.79), channel_id=1, source_target_pairs={{0,1},{1,0},{2,3},{3,2},{4,5},{5,4},{6,7},{7,6},{8,9},{9,8},{10,11... | collective-permute-start | bytes 3956744 | tf_op jit(solution)/shard_map/gate_core/ppermute | solution.py:86
  8.3 14.7 %collective-permute-start.4 = (bf16[448,1472]{1,0:T(8,128)(2,1)}, bf16[448,1472]{1,0:T(8,128)(2,1)}, u32[]{:S(2)}, u32[]{:S(2)}) collective-permute-start(bf16[448,1472]{1,0:T(8,128)(2,1)} %bitcast.84), channel_id=1, source_target_pairs={{0,1},{1,0},{2,3},{3,2},{4,5},{5,4},{6,7},{7,6},{8,9},{9,8},{10,11... | collective-permute-start | bytes 3956744 | tf_op jit(solution)/shard_map/up_core/ppermute | solution.py:86
  8.4 29.7 %collective-permute-start.5 = (bf16[448,1472]{1,0:T(8,128)(2,1)}, bf16[448,1472]{1,0:T(8,128)(2,1)S(1)}, u32[]{:S(2)}, u32[]{:S(2)}) collective-permute-start(bf16[448,1472]{1,0:T(8,128)(2,1)} %d0.15), channel_id=1, source_target_pairs={{0,1},{1,0},{2,3},{3,2},{4,5},{5,4},{6,7},{7,6},{8,9},{9,8},{10,11... | collective-permute-start | bytes 3956744 | tf_op jit(solution)/shard_map/down_core/ppermute | solution.py:86
  16.2 49.4 %copy-start.16 = (bf16[1472,256]{1,0:T(8,128)(2,1)}, bf16[1472,256]{1,0:T(8,128)(2,1)S(1)}, u32[]{:S(2)}) copy-start(bf16[1472,256]{1,0:T(8,128)(2,1)S(1)} %get-tuple-element.146.x_ref) | copy-start | bytes 2260996
  16.2 20.1 %collective-permute-start.2 = (bf16[1472,256]{1,0:T(8,128)(2,1)S(1)}, bf16[1472,256]{1,0:T(8,128)(2,1)S(1)}, u32[]{:S(2)}, u32[]{:S(2)}) collective-permute-start(bf16[1472,256]{1,0:T(8,128)(2,1)S(1)} %get-tuple-element.134.n_ref.n0_ref), channel_id=1, source_target_pairs={{0,4},{4,0},{1,5},{5,1},{2,6},{6,2},{3,7},{7,3},{8,12},{12,8},{9,1... | collective-permute-start | bytes 2261000 | tf_op jit(solution)/shard_map/n1_y/ppermute | solution.py:86
  20.5 109.6 %copy-start.5 = (bf16[1472,256]{1,0:T(8,128)(2,1)}, bf16[1472,256]{1,0:T(8,128)(2,1)S(1)}, u32[]{:S(2)}) copy-start(bf16[1472,256]{1,0:T(8,128)(2,1)S(1)} %pair.1.dy_ref.refs_4_) | copy-start | bytes 2260996
  21.2 25.8 %copy-start.25 = (bf16[384,256]{1,0:T(8,128)(2,1)}, bf16[384,256]{1,0:T(8,128)(2,1)S(1)}, u32[]{:S(2)}) copy-start(bf16[384,256]{1,0:T(8,128)(2,1)S(1)} %get-tuple-element.138.k0) | copy-start | bytes 589828
  21.2 16.9 %collective-permute-start.6 = (bf16[384,256]{1,0:T(8,128)(2,1)S(1)}, bf16[384,256]{1,0:T(8,128)(2,1)S(1)}, u32[]{:S(2)}, u32[]{:S(2)}) collective-permute-start(bf16[384,256]{1,0:T(8,128)(2,1)S(1)} %get-tuple-element.138.k0), channel_id=1, source_target_pairs={{0,2},{1,3},{2,0},{3,1},{4,6},{5,7},{6,4},{7,5},{8,10},{9,11},{10,... | collective-permute-start | bytes 589832 | tf_op jit(solution)/shard_map/kv_own_x/ppermute | solution.py:86
  36.3 10.2 %collective-permute-start.10 = (bf16[96,1472]{1,0:T(8,128)(2,1)S(1)}, bf16[96,1472]{1,0:T(8,128)(2,1)S(1)}, u32[]{:S(2)}, u32[]{:S(2)}) collective-permute-start(bf16[96,1472]{1,0:T(8,128)(2,1)S(1)} %copy-done.47), channel_id=1, source_target_pairs={{0,4},{4,0},{1,5},{5,1},{2,6},{6,2},{3,7},{7,3},{8,12},{12,8},{9,1... | collective-permute-start | bytes 847880 | tf_op jit(solution)/shard_map/wout_y/ppermute | solution.py:86
  38.7 17.5 %copy-start.29 = (bf16[384,256]{1,0:T(8,128)(2,1)}, bf16[384,256]{1,0:T(8,128)(2,1)S(1)}, u32[]{:S(2)}) copy-start(bf16[384,256]{1,0:T(8,128)(2,1)S(1)} %get-tuple-element.144.k1) | copy-start | bytes 589828
  38.8 6.3 %collective-permute-start.7 = (bf16[384,256]{1,0:T(8,128)(2,1)S(1)}, bf16[384,256]{1,0:T(8,128)(2,1)S(1)}, u32[]{:S(2)}, u32[]{:S(2)}) collective-permute-start(bf16[384,256]{1,0:T(8,128)(2,1)S(1)} %get-tuple-element.144.k1), channel_id=1, source_target_pairs={{0,2},{1,3},{2,0},{3,1},{4,6},{5,7},{6,4},{7,5},{8,10},{9,11},{10,... | collective-permute-start | bytes 589832 | tf_op jit(solution)/shard_map/kv_far_x/ppermute | solution.py:86
  45.0 20.5 %collective-permute-start.9 = (bf16[1472,256]{1,0:T(8,128)(2,1)S(1)}, bf16[1472,256]{1,0:T(8,128)(2,1)S(1)}, u32[]{:S(2)}, u32[]{:S(2)}) collective-permute-start(bf16[1472,256]{1,0:T(8,128)(2,1)S(1)} %pair.1.dy_ref.refs_4_), channel_id=1, source_target_pairs={{0,2},{1,3},{2,0},{3,1},{4,6},{5,7},{6,4},{7,5},{8,10},{9,11},{10,... | collective-permute-start | bytes 2261000 | tf_op jit(solution)/shard_map/dy_x/ppermute | solution.py:86
  46.5 19.1 %copy-start.19 = (bf16[96,1472]{1,0:T(8,128)(2,1)}, bf16[96,1472]{1,0:T(8,128)(2,1)S(1)}, u32[]{:S(2)}) copy-start(bf16[96,1472]{1,0:T(8,128)(2,1)S(1)} %collective-permute-done.10.w1_ref) | copy-start | bytes 847876
  46.5 19.0 %collective-permute-start.11 = (bf16[1472,256]{1,0:T(8,128)(2,1)S(1)}, bf16[1472,256]{1,0:T(8,128)(2,1)S(1)}, u32[]{:S(2)}, u32[]{:S(2)}) collective-permute-start(bf16[1472,256]{1,0:T(8,128)(2,1)S(1)} %pair.1.dy_ref.refs_4_), channel_id=1, source_target_pairs={{0,4},{4,0},{1,5},{5,1},{2,6},{6,2},{3,7},{7,3},{8,12},{12,8},{9,1... | collective-permute-start | bytes 2261000 | tf_op jit(solution)/shard_map/dy_y/ppermute | solution.py:86
  47.1 18.5 %copy-start.14 = (bf16[192,1472]{1,0:T(8,128)(2,1)S(1)}, bf16[192,1472]{1,0:T(8,128)(2,1)}, u32[]{:S(2)}) copy-start(bf16[192,1472]{1,0:T(8,128)(2,1)} %w0_ref.3) | copy-start | bytes 1695748
  56.3 9.2 %collective-permute-start.12 = (bf16[96,1472]{1,0:T(8,128)(2,1)S(1)}, bf16[96,1472]{1,0:T(8,128)(2,1)S(1)}, u32[]{:S(2)}, u32[]{:S(2)}) collective-permute-start(bf16[96,1472]{1,0:T(8,128)(2,1)S(1)} %collective-permute-done.10.w1_ref), channel_id=1, source_target_pairs={{0,1},{1,0},{2,3},{3,2},{4,5},{5,4},{6,7},{7,6},{8,9},{9,8},{10,11... | collective-permute-start | bytes 847880 | tf_op jit(solution)/shard_map/wout_core/ppermute | solution.py:86
  56.4 9.1 %collective-permute-start.8 = (bf16[192,256]{1,0:T(8,128)(2,1)S(1)}, bf16[192,256]{1,0:T(8,128)(2,1)S(1)}, u32[]{:S(2)}, u32[]{:S(2)}) collective-permute-start(bf16[192,256]{1,0:T(8,128)(2,1)S(1)} %get-tuple-element.307), channel_id=1, source_target_pairs={{0,4},{4,0},{1,5},{5,1},{2,6},{6,2},{3,7},{7,3},{8,12},{12,8},{9,1... | collective-permute-start | bytes 294920 | tf_op jit(solution)/shard_map/mixed_y/ppermute | solution.py:86
  67.6 19.8 %collective-permute-start.13 = (bf16[1472,256]{1,0:T(8,128)(2,1)S(1)}, bf16[1472,256]{1,0:T(8,128)(2,1)S(1)}, u32[]{:S(2)}, u32[]{:S(2)}) collective-permute-start(bf16[1472,256]{1,0:T(8,128)(2,1)S(1)} %get-tuple-element.156.n_ref.refs_4_.refs_12_.refs_20_), channel_id=1, source_target_pairs={{0,2},{1,3},{2,0},{3,1},{4,6},{5,7},{6,4},{7,5},{8,10},{9,11},{10,... | collective-permute-start | bytes 2261000 | tf_op jit(solution)/shard_map/n2_x/ppermute | solution.py:86
  68.4 19.1 %collective-permute-start.14 = (bf16[1472,256]{1,0:T(8,128)(2,1)S(1)}, bf16[1472,256]{1,0:T(8,128)(2,1)S(1)}, u32[]{:S(2)}, u32[]{:S(2)}) collective-permute-start(bf16[1472,256]{1,0:T(8,128)(2,1)S(1)} %get-tuple-element.156.n_ref.refs_4_.refs_12_.refs_20_), channel_id=1, source_target_pairs={{0,4},{4,0},{1,5},{5,1},{2,6},{6,2},{3,7},{7,3},{8,12},{12,8},{9,1... | collective-permute-start | bytes 2261000 | tf_op jit(solution)/shard_map/n2_y/ppermute | solution.py:86
  70.0 32.1 %collective-permute-start.16 = (bf16[1472,256]{1,0:T(8,128)(2,1)S(1)}, bf16[1472,256]{1,0:T(8,128)(2,1)S(1)}, u32[]{:S(2)}, u32[]{:S(2)}) collective-permute-start(bf16[1472,256]{1,0:T(8,128)(2,1)S(1)} %pick.2), channel_id=1, source_target_pairs={{0,4},{1,3},{2,6},{3,1},{4,0},{5,7},{6,2},{7,5},{8,12},{9,11},{10,... | collective-permute-start | bytes 2261000 | tf_op jit(solution)/shard_map/dy_d/ppermute | solution.py:86
  87.5 16.5 %collective-permute-start.15 = (bf16[1472,256]{1,0:T(8,128)(2,1)S(1)}, bf16[1472,256]{1,0:T(8,128)(2,1)S(1)}, u32[]{:S(2)}, u32[]{:S(2)}) collective-permute-start(bf16[1472,256]{1,0:T(8,128)(2,1)S(1)} %pick.3), channel_id=1, source_target_pairs={{0,4},{1,3},{2,6},{3,1},{4,0},{5,7},{6,2},{7,5},{8,12},{9,11},{10,... | collective-permute-start | bytes 2261000 | tf_op jit(solution)/shard_map/n2_d/ppermute | solution.py:86
  94.0 19.8 %collective-permute-start.17 = (bf16[1472,256]{1,0:T(8,128)(2,1)S(1)}, bf16[1472,256]{1,0:T(8,128)(2,1)S(1)}, u32[]{:S(2)}, u32[]{:S(2)}) collective-permute-start(bf16[1472,256]{1,0:T(8,128)(2,1)S(1)} %get-tuple-element.171), channel_id=1, source_target_pairs={{0,2},{1,3},{2,0},{3,1},{4,6},{5,7},{6,4},{7,5},{8,10},{9,11},{10,... | collective-permute-start | bytes 2261000 | tf_op jit(solution)/shard_map/dn_x/ppermute | solution.py:86
  101.5 15.2 %collective-permute-start.18 = (bf16[1472,256]{1,0:T(8,128)(2,1)S(1)}, bf16[1472,256]{1,0:T(8,128)(2,1)S(1)}, u32[]{:S(2)}, u32[]{:S(2)}) collective-permute-start(bf16[1472,256]{1,0:T(8,128)(2,1)S(1)} %get-tuple-element.172), channel_id=1, source_target_pairs={{0,4},{4,0},{1,5},{5,1},{2,6},{6,2},{3,7},{7,3},{8,12},{12,8},{9,1... | collective-permute-start | bytes 2261000 | tf_op jit(solution)/shard_map/dn_y/ppermute | solution.py:86
  121.7 8.3 %collective-permute-start.23 = (bf16[2,448,1472]{2,1,0:T(8,128)(2,1)S(1)}, bf16[2,448,1472]{2,1,0:T(8,128)(2,1)S(1)}, u32[]{:S(2)}, u32[]{:S(2)}) collective-permute-start(bf16[2,448,1472]{2,1,0:T(8,128)(2,1)S(1)} %wgrad_give.3), channel_id=1, source_target_pairs={{0,1},{1,0},{2,3},{3,2},{4,5},{5,4},{6,7},{7,6},{8,9},{9,8},{10,11... | collective-permute-start | bytes 7913480 | tf_op jit(solution)/shard_map/wgrad_core/ppermute | solution.py:86
  121.8 8.2 %collective-permute-start.22 = (bf16[1,448,1472]{2,1,0:T(8,128)(2,1)S(1)}, bf16[1,448,1472]{2,1,0:T(8,128)(2,1)S(1)}, u32[]{:S(2)}, u32[]{:S(2)}) collective-permute-start(bf16[1,448,1472]{2,1,0:T(8,128)(2,1)S(1)} %wgrad_give.2), channel_id=1, source_target_pairs={{0,1},{1,0},{2,3},{3,2},{4,5},{5,4},{6,7},{7,6},{8,9},{9,8},{10,11... | collective-permute-start | bytes 3956744 | tf_op jit(solution)/shard_map/wgrad_core/ppermute | solution.py:86
  122.3 20.0 %collective-permute-start.19 = (bf16[1472,256]{1,0:T(8,128)(2,1)}, bf16[1472,256]{1,0:T(8,128)(2,1)}, u32[]{:S(2)}, u32[]{:S(2)}) collective-permute-start(bf16[1472,256]{1,0:T(8,128)(2,1)} %get-tuple-element.183), channel_id=1, source_target_pairs={{0,6},{1,7},{2,4},{3,5},{4,2},{5,3},{6,0},{7,1},{8,14},{9,15},{10,... | collective-permute-start | bytes 2261000 | tf_op jit(solution)/shard_map/dn_d/ppermute | solution.py:86
  136.7 178.1 %all-gather.2.cloned.1.call-start = ((), (), s32[]{:S(2)}) async-start(), calls=%async_computation.1 | async-start | bytes 4945920 | tf_op jit(solution)/shard_map/all_gather | solution.py:989
  147.9 5.7 %collective-permute-start.24 = (bf16[192,256]{1,0:T(8,128)(2,1)S(1)}, bf16[192,256]{1,0:T(8,128)(2,1)S(1)}, u32[]{:S(2)}, u32[]{:S(2)}) collective-permute-start(bf16[192,256]{1,0:T(8,128)(2,1)S(1)} %get-tuple-element.195), channel_id=1, source_target_pairs={{0,4},{4,0},{1,5},{5,1},{2,6},{6,2},{3,7},{7,3},{8,12},{12,8},{9,1... | collective-permute-start | bytes 294920 | tf_op jit(solution)/shard_map/dmixed_y/ppermute | solution.py:86
  149.7 20.3 %collective-permute-start.20 = (bf16[1472,256]{1,0:T(8,128)(2,1)}, bf16[1472,256]{1,0:T(8,128)(2,1)S(1)}, u32[]{:S(2)}, u32[]{:S(2)}) collective-permute-start(bf16[1472,256]{1,0:T(8,128)(2,1)} %ffn_out.5), channel_id=1, source_target_pairs={{0,2},{1,3},{2,0},{3,1},{4,6},{5,7},{6,4},{7,5},{8,10},{9,11},{10,... | collective-permute-start | bytes 2261000 | tf_op jit(solution)/shard_map/out_x/ppermute | solution.py:86
  149.7 20.3 %collective-permute-start.21 = (bf16[1472,256]{1,0:T(8,128)(2,1)}, bf16[1472,256]{1,0:T(8,128)(2,1)}, u32[]{:S(2)}, u32[]{:S(2)}) collective-permute-start(bf16[1472,256]{1,0:T(8,128)(2,1)} %ffn_out.6), channel_id=1, source_target_pairs={{0,4},{4,0},{1,5},{5,1},{2,6},{6,2},{3,7},{7,3},{8,12},{12,8},{9,1... | collective-permute-start | bytes 2261000 | tf_op jit(solution)/shard_map/out_y/ppermute | solution.py:86
  166.7 9.5 %collective-permute-start.25 = (bf16[400,512]{1,0:T(8,128)(2,1)}, bf16[400,512]{1,0:T(8,128)(2,1)S(1)}, u32[]{:S(2)}, u32[]{:S(2)}) collective-permute-start(bf16[400,512]{1,0:T(8,128)(2,1)} %get-tuple-element.204), channel_id=1, source_target_pairs={{0,2},{1,3},{2,0},{3,1},{4,6},{5,7},{6,4},{7,5},{8,10},{9,11},{10,... | collective-permute-start | bytes 1228808 | tf_op jit(solution)/shard_map/dkv_x/ppermute | solution.py:86
  167.0 14.5 %collective-permute-start.26 = (bf16[192,1472]{1,0:T(8,128)(2,1)}, bf16[192,1472]{1,0:T(8,128)(2,1)}, u32[]{:S(2)}, u32[]{:S(2)}) collective-permute-start(bf16[192,1472]{1,0:T(8,128)(2,1)} %get-tuple-element.211), channel_id=1, source_target_pairs={{0,4},{4,0},{1,5},{5,1},{2,6},{6,2},{3,7},{7,3},{8,12},{12,8},{9,1... | collective-permute-start | bytes 1695752 | tf_op jit(solution)/shard_map/gout_y/ppermute | solution.py:86
  186.7 3.1 collective-permute-start.27
  186.7 23.0 %collective-permute-start.29 = (bf16[1504,256]{1,0:T(8,128)(2,1)}, bf16[1504,256]{1,0:T(8,128)(2,1)S(1)}, u32[]{:S(2)}, u32[]{:S(2)}) collective-permute-start(bf16[1504,256]{1,0:T(8,128)(2,1)} %get-tuple-element.218), channel_id=1, source_target_pairs={{0,4},{4,0},{1,5},{5,1},{2,6},{6,2},{3,7},{7,3},{8,12},{12,8},{9,1... | collective-permute-start | bytes 2310152 | tf_op jit(solution)/shard_map/back_y/ppermute | solution.py:86
  193.1 15.4 %collective-permute-start.28 = (bf16[192,1472]{1,0:T(8,128)(2,1)S(1)}, bf16[192,1472]{1,0:T(8,128)(2,1)S(1)}, u32[]{:S(2)}, u32[]{:S(2)}) collective-permute-start(bf16[192,1472]{1,0:T(8,128)(2,1)S(1)} %get-tuple-element.215), channel_id=1, source_target_pairs={{0,2},{1,3},{2,0},{3,1},{4,6},{5,7},{6,4},{7,5},{8,10},{9,11},{10,... | collective-permute-start | bytes 1695752 | tf_op jit(solution)/shard_map/fold_x/ppermute | solution.py:86
  215.6 13.0 %collective-permute-start.33 = (f32[1504,128]{1,0:T(8,128)}, f32[1504,128]{1,0:T(8,128)S(1)}, u32[]{:S(2)}, u32[]{:S(2)}) collective-permute-start(f32[1504,128]{1,0:T(8,128)} %copy-done.37), channel_id=1, source_target_pairs={{0,1},{1,0},{2,3},{3,2},{4,5},{5,4},{6,7},{7,6},{8,9},{9,8},{10,11... | collective-permute-start | bytes 2310152 | tf_op jit(solution)/shard_map/grad_core/ppermute | solution.py:86
  215.6 9.4 %collective-permute-start.31 = (bf16[96,1472]{1,0:T(8,128)(2,1)S(1)}, bf16[96,1472]{1,0:T(8,128)(2,1)S(1)}, u32[]{:S(2)}, u32[]{:S(2)}) collective-permute-start(bf16[96,1472]{1,0:T(8,128)(2,1)S(1)} %get-tuple-element.225), channel_id=1, source_target_pairs={{0,8},{8,0},{16,24},{24,16},{1,9},{9,1},{17,25},{25,17},{2,10},{10... | collective-permute-start | bytes 847880 | tf_op jit(solution)/shard_map/share_z/ppermute | solution.py:86
  225.9 19.3 %collective-permute-start.32 = (bf16[48,1472]{1,0:T(8,128)(2,1)S(1)}, bf16[48,1472]{1,0:T(8,128)(2,1)S(1)}, u32[]{:S(2)}, u32[]{:S(2)}) collective-permute-start(bf16[48,1472]{1,0:T(8,128)(2,1)S(1)} %get-tuple-element.227), channel_id=1, source_target_pairs={{0,16},{8,24},{16,0},{24,8},{1,17},{9,25},{17,1},{25,9},{2,18},{10... | collective-permute-start | bytes 423944 | tf_op jit(solution)/shard_map/share_z/ppermute | solution.py:86
  245.3 15.8 %collective-permute-start.34 = (bf16[64,1472]{1,0:T(8,128)(2,1)S(1)}, bf16[64,1472]{1,0:T(8,128)(2,1)S(1)}, u32[]{:S(2)}, u32[]{:S(2)}) collective-permute-start(bf16[64,1472]{1,0:T(8,128)(2,1)S(1)} %share_sum.1.refs_0_), channel_id=1, source_target_pairs={{0,8},{8,16},{16,24},{24,0},{1,9},{9,17},{17,25},{25,1},{2,10},{10... | collective-permute-start | bytes 565256 | tf_op jit(solution)/shard_map/join_z/ppermute | solution.py:86
  248.1 26.1 %collective-permute-start.35 = (bf16[64,1472]{1,0:T(8,128)(2,1)S(1)}, bf16[64,1472]{1,0:T(8,128)(2,1)S(1)}, u32[]{:S(2)}, u32[]{:S(2)}) collective-permute-start(bf16[64,1472]{1,0:T(8,128)(2,1)S(1)} %share_sum.1.refs_0_), channel_id=1, source_target_pairs={{0,16},{8,24},{16,0},{24,8},{1,17},{9,25},{17,1},{25,9},{2,18},{10... | collective-permute-start | bytes 565256 | tf_op jit(solution)/shard_map/join_z/ppermute | solution.py:86
  251.8 22.4 %collective-permute-start.36 = (bf16[64,1472]{1,0:T(8,128)(2,1)S(1)}, bf16[64,1472]{1,0:T(8,128)(2,1)S(1)}, u32[]{:S(2)}, u32[]{:S(2)}) collective-permute-start(bf16[64,1472]{1,0:T(8,128)(2,1)S(1)} %share_sum.1.refs_0_), channel_id=1, source_target_pairs={{0,24},{8,0},{16,8},{24,16},{1,25},{9,1},{17,9},{25,17},{2,26},{10... | collective-permute-start | bytes 565256 | tf_op jit(solution)/shard_map/join_z/ppermute | solution.py:86
  251.8 23.1 %collective-permute-start.30 = (bf16[1472,256]{1,0:T(8,128)(2,1)}, bf16[1472,256]{1,0:T(8,128)(2,1)S(1)}, u32[]{:S(2)}, u32[]{:S(2)}) collective-permute-start(bf16[1472,256]{1,0:T(8,128)(2,1)} %ffn_out.7), channel_id=1, source_target_pairs={{0,6},{1,7},{2,4},{3,5},{4,2},{5,3},{6,0},{7,1},{8,14},{9,15},{10,... | collective-permute-start | bytes 2261000 | tf_op jit(solution)/shard_map/out_d/ppermute | solution.py:86
  274.9 13.9 %collective-permute-start.37 = (bf16[208,1472]{1,0:T(8,128)(2,1)S(1)}, bf16[208,1472]{1,0:T(8,128)(2,1)S(1)}, u32[]{:S(2)}, u32[]{:S(2)}) collective-permute-start(bf16[208,1472]{1,0:T(8,128)(2,1)S(1)} %get-tuple-element.232.own_ref), channel_id=1, source_target_pairs={{0,2},{1,3},{2,0},{3,1},{4,6},{5,7},{6,4},{7,5},{8,10},{9,11},{10,... | collective-permute-start | bytes 1837064 | tf_op jit(solution)/shard_map/join_x/ppermute | solution.py:86
  289.5 8.3 %collective-permute-start.39 = (bf16[2,192,1472]{2,1,0:T(8,128)(2,1)S(1)}, bf16[2,192,1472]{2,1,0:T(8,128)(2,1)S(1)}, u32[]{:S(2)}, u32[]{:S(2)}) collective-permute-start(bf16[2,192,1472]{2,1,0:T(8,128)(2,1)S(1)} %get-tuple-element.237.own_ref), channel_id=1, source_target_pairs={{0,1},{1,0},{2,3},{3,2},{4,5},{5,4},{6,7},{7,6},{8,9},{9,8},{10,11... | collective-permute-start | bytes 3391496 | tf_op jit(solution)/shard_map/join_core/ppermute | solution.py:86
  289.5 3.4 %collective-permute-start.38 = (bf16[1472,128]{1,0:T(8,128)(2,1)}, bf16[1472,128]{1,0:T(8,128)(2,1)}, u32[]{:S(2)}, u32[]{:S(2)}) collective-permute-start(bf16[1472,128]{1,0:T(8,128)(2,1)} %get-tuple-element.235), channel_id=1, source_target_pairs={{0,1},{1,0},{2,3},{3,2},{4,5},{5,4},{6,7},{7,6},{8,9},{9,8},{10,11... | collective-permute-start | bytes 1130504 | tf_op jit(solution)/shard_map/out_core/ppermute | solution.py:86
  (44 other events, 284.6 us)
Sparse Core Ops, SparseCore 0:
  136.8 73.6 reduce-scatter.3
  214.9 99.8 all-gather.1

commit v5 on v4

--- a/solution.py
+++ b/solution.py
@@ -969,7 +969,9 @@
     steps = [1 << k for k in range(dp_axis.bit_length() - 1)]
     short = shares > 1 and 1 << len(steps) == dp_axis
     if short:
-        keep, got = z_share(keep, got, steps[0], dp_axis, z_at)
+        keep, got = z_share(after(keep, back_got), got, steps[0], dp_axis, z_at)
+    if shares > 1:
+        ffn_grads = lax.all_gather(after(ffn_grads, keep), "dp", axis=0, tiled=True)
     rows_keep, rows_give, small, _ = call(
         last_kernel,
         (
@@ -985,8 +987,6 @@
     )
     rows_got = core_swap(rows_give, "grad_core")
     small_got = rows_got[width:]
-    if shares > 1:
-        ffn_grads = lax.all_gather(after(ffn_grads, rows_keep), "dp", axis=0, tiled=True)
     if short:
         for step in steps[1:]:
             keep, got = z_share(keep, got, step, dp_axis, z_at)
@@ -1011,6 +1011,7 @@
 
     joined = x_swap(folded, "join_x")
     grad_inputs = place(rows_keep, rows_got)
+    output = place(out_keep, core_swap(out_give, "out_core"))
     folded, sums = call(
         join_x_kernel,
         (pair_bf, sds((8, width), F32)),
@@ -1019,7 +1020,6 @@
         scalars=(x_scalar,),
     )
     joined = core_swap(folded, "join_core")
-    output = place(out_keep, core_swap(out_give, "out_core"))
     grad_w_query, grad_w_key, grad_w_value, grad_w_out = call(
         join_core_kernel,
         (one_f32,) * 4,

time: 332 us -> 330 us (level)
  local copies, waits for them, and re-layouts: 15.3 us -> 10.5 us
    unnamed x105 -> x99, local copies, waits for them, and re-layouts: 7.83 us -> 4.63 us
  transfers between devices with their start and end apart: 42 -> 42, of which waited for: 19 -> 22; matrix products, arithmetic and copies ran while one was open for 3% -> 3% of each run, Pallas kernels for 33% -> 33%
where the time goes in v5:
time: 330 us; the launch traced here: 325 us
  waiting for transfers between devices  138 us (42%)
  Pallas kernels  121 us (37%)
  starting transfers between devices  38.5 us (12%)
  between operations  15.1 us (5%)
  local copies, waits for them, and re-layouts  10.5 us (3%)
    ppermute x40, waiting for transfers between devices, move(): return lax.ppermute(v, axes, pairs)  123 us
    pallas_call x37, Pallas kernels, call(): pl.pallas_call(kernel, out_shape=out_shape, in_specs=in_specs, out_specs=...  88.7 us
    ppermute x40, starting transfers between devices, move(): return lax.ppermute(v, axes, pairs)  38.4 us
    all_gather x1, waiting for transfers between devices, run(): ffn_grads = lax.all_gather(after(ffn_grads, keep), 'dp', axis=0, tiled=True)  14.1 us
    pallas_call x1, Pallas kernels, attn_bwd(): pl.pallas_call(functools.partial(attn_bwd_kernel, inner=inner, heads=head...  11.2 us
    pallas_call x1, Pallas kernels, attn_fwd(): pl.pallas_call(functools.partial(attn_fwd_kernel, inner=inner), out_shape...  9.2 us
  transfers between devices with their start and end apart: 42, of which 22 were waited for; matrix products, arithmetic and copies ran while one was open for 3% of the time, Pallas kernels for 33%

profile of v5, /device:TPU:0, one launch (start us, length us, event | category | flops | bytes accessed | tf_op | source)
XLA Modules:
  0.0 325.2 jit_solution(15290422125826215694)
XLA Ops:
  10.9 1.7 dynamic-slice_bitcast_fusion
  14.4 1.7 prep.1
  16.2 2.7 collective-permute-start.2
  23.0 6.0 %bias.1.bias_ref = f32[3,1024,512]{2,1,0:T(8,128)} custom-call(s32[8]{0:T(128)S(1)} %sub.44.start_ref, f32[8,2048]{1,0:T(8,128)S(1)} %concatenate.83.table_ref, f32[1,1024]{1,0:T(1,128)S(1)} %reshape.105.mask_ref), custom_call_target="tpu_custom_call" | custom-call | bytes 30000 | tf_op jit(solution)/shard_map/bias/pallas_call | solution.py:148
  29.0 7.3 %collective-permute-done.2.n_ref.n1_ref = bf16[1472,256]{1,0:T(8,128)(2,1)S(1)} collective-permute-done((bf16[1472,256]{1,0:T(8,128)(2,1)S(1)}, bf16[1472,256]{1,0:T(8,128)(2,1)S(1)}, u32[]{:S(2)}, u32[]{:S(2)}) %collective-permute-start.2) | collective-permute-done | bytes 753696 | tf_op jit(solution)/shard_map/n1_y/ppermute | solution.py:86
  36.3 1.8 collective-permute-start.10
  40.3 4.7 %collective-permute-done.7.k3 = bf16[384,256]{1,0:T(8,128)(2,1)S(1)} collective-permute-done((bf16[384,256]{1,0:T(8,128)(2,1)S(1)}, bf16[384,256]{1,0:T(8,128)(2,1)S(1)}, u32[]{:S(2)}, u32[]{:S(2)}) %collective-permute-start.7) | collective-permute-done | bytes 196640 | tf_op jit(solution)/shard_map/kv_far_x/ppermute | solution.py:86
  47.1 9.2 %attn_fwd.1 = (f32[3,1024,512]{2,1,0:T(8,128)}, bf16[192,512]{1,0:T(8,128)(2,1)S(1)}) custom-call(bf16[192,512]{1,0:T(8,128)(2,1)S(1)} %constant_dynamic-update-slice_fusion.q_ref, bf16[384,256]{1,0:T(8,128)(2,1)S(1)} %get-tuple-element.140.k0, bf16[384,256]{1,0:T(8,128)(2,1)S(1)} %get-tuple-element.146.k1, bf16[384,256]{1,0:T(8,128)(2,1)S(1)} %collective-permute-done.6.k2, ...), custom_call_target="tpu_custom_call" | custom-call | bytes 30000 | tf_op jit(solution)/shard_map/attn_fwd/pallas_call | solution.py:190
  58.0 7.5 %collective-permute-done.8.m1_ref = bf16[192,256]{1,0:T(8,128)(2,1)S(1)} collective-permute-done((bf16[192,256]{1,0:T(8,128)(2,1)S(1)}, bf16[192,256]{1,0:T(8,128)(2,1)S(1)}, u32[]{:S(2)}, u32[]{:S(2)}) %collective-permute-start.8) | collective-permute-done | bytes 98336 | tf_op jit(solution)/shard_map/mixed_y/ppermute | solution.py:86
  65.6 2.1 mid.1
  71.8 5.7 %ffn.4 = (bf16[2,448,256]{2,1,0:T(8,128)(2,1)S(1)}, bf16[2,448,256]{2,1,0:T(8,128)(2,1)S(1)}, bf16[2,448,256]{2,1,0:T(8,128)(2,1)S(1)}, bf16[1472,256]{1,0:T(8,128)(2,1)S(1)}) custom-call(bf16[1472,256]{1,0:T(8,128)(2,1)S(1)} %get-tuple-element.158.n_ref.refs_4_.refs_12_.refs_20_, f32[2,448,256]{2,1,0:T(8,128)S(1)} %d_act.4.da_ref, ...), custom_call_target="tpu_custom_call" | custom-call | bytes 30000 | tf_op jit(solution)/shard_map/ffn/pallas_call | solution.py:63
  79.2 8.2 %collective-permute-done.13.first_ref.n_ref.refs_5_.refs_13_.refs_21_ = bf16[1472,256]{1,0:T(8,128)(2,1)S(1)} collective-permute-done((bf16[1472,256]{1,0:T(8,128)(2,1)S(1)}, bf16[1472,256]{1,0:T(8,128)(2,1)S(1)}, u32[]{:S(2)}, u32[]{:S(2)}) %collective-permute-start.13) | collective-permute-done | bytes 753696 | tf_op jit(solution)/shard_map/n2_x/ppermute | solution.py:86
  88.3 5.7 %ffn.5 = (bf16[2,448,256]{2,1,0:T(8,128)(2,1)S(1)}, bf16[2,448,256]{2,1,0:T(8,128)(2,1)S(1)}, bf16[2,448,256]{2,1,0:T(8,128)(2,1)S(1)}, bf16[1472,256]{1,0:T(8,128)(2,1)S(1)}) custom-call(bf16[1472,256]{1,0:T(8,128)(2,1)S(1)} %collective-permute-done.13.first_ref.n_ref.refs_5_.refs_13_.refs_21_, f32[2,448,256]{2,1,0:T(8,128)S(1)} %d_act.5.da_ref, ...), custom_call_target="tpu_custom_call" | custom-call | bytes 30000 | tf_op jit(solution)/shard_map/ffn/pallas_call | solution.py:63
  95.6 5.9 %ffn.6 = (bf16[2,448,256]{2,1,0:T(8,128)(2,1)S(1)}, bf16[2,448,256]{2,1,0:T(8,128)(2,1)S(1)}, bf16[2,448,256]{2,1,0:T(8,128)(2,1)S(1)}, bf16[1472,256]{1,0:T(8,128)(2,1)S(1)}) custom-call(bf16[1472,256]{1,0:T(8,128)(2,1)S(1)} %collective-permute-done.14.second_ref.n_ref.refs_6_.refs_14_.refs_22_, f32[2,448,256]{2,1,0:T(8,128)S(1)} %d_act.6.da_ref, ...), custom_call_target="tpu_custom_call" | custom-call | bytes 30000 | tf_op jit(solution)/shard_map/ffn/pallas_call | solution.py:63
  104.1 6.6 %ffn.7 = (bf16[2,448,256]{2,1,0:T(8,128)(2,1)S(1)}, bf16[2,448,256]{2,1,0:T(8,128)(2,1)S(1)}, bf16[2,448,256]{2,1,0:T(8,128)(2,1)S(1)}, bf16[1472,256]{1,0:T(8,128)(2,1)}) custom-call(bf16[1472,256]{1,0:T(8,128)(2,1)S(1)} %collective-permute-done.15.n_ref.refs_7_.refs_15_.refs_23_, f32[2,448,256]{2,1,0:T(8,128)S(1)} %d_act.7.da_ref, ...), custom_call_target="tpu_custom_call" | custom-call | bytes 30000 | tf_op jit(solution)/shard_map/ffn/pallas_call | solution.py:63
  113.9 2.9 collective-permute-done.18.gb_ref
  116.8 1.9 ffn_out.4.own_ref
  118.7 3.0 wgrad_give.3
  123.8 2.4 ffn_out.5
  126.1 1.9 ffn_out.6
  128.1 2.0 ffn_out.7
  130.1 6.6 %wgrad_sum.1 = bf16[4,3,1288,128]{3,2,1,0:T(8,128)(2,1)} custom-call(bf16[2,448,256]{2,1,0:T(8,128)(2,1)S(1)} %get-tuple-element.192.refs_0_.a_ref, bf16[2,448,256]{2,1,0:T(8,128)(2,1)S(1)} %get-tuple-element.184.refs_1_.a_ref, bf16[2,448,256]{2,1,0:T(8,128)(2,1)S(1)} %get-tuple-element.187.refs_2_.a_ref, ...), custom_call_target="tpu_custom_call" | custom-call | bytes 30000 | tf_op jit(solution)/shard_map/wgrad_sum/pallas_call | solution.py:63
  136.7 5.6 %collective-permute-done.19.gd_ref = bf16[1472,256]{1,0:T(8,128)(2,1)} collective-permute-done((bf16[1472,256]{1,0:T(8,128)(2,1)}, bf16[1472,256]{1,0:T(8,128)(2,1)}, u32[]{:S(2)}, u32[]{:S(2)}) %collective-permute-start.19) | collective-permute-done | bytes 753696 | tf_op jit(solution)/shard_map/dn_d/ppermute | solution.py:86
  142.4 5.5 %mid_back.1 = (f32[1472,256]{1,0:T(8,128)}, bf16[1472,256]{1,0:T(8,128)(2,1)S(1)}, f32[1,1472]{1,0:T(1,128)S(1)}, bf16[192,256]{1,0:T(8,128)(2,1)S(1)}, bf16[192,256]{1,0:T(8,128)(2,1)S(1)}) custom-call(s32[1]{0:T(128)} %bitcast.c_ref, bf16[1472,256]{1,0:T(8,128)(2,1)} %copy-done.33, bf16[1472,256]{1,0:T(8,128)(2,1)} %copy-done.39, ...), custom_call_target="tpu_custom_call" | custom-call | bytes 30000 | tf_op jit(solution)/shard_map/mid_back/pallas_call | solution.py:63
  147.9 1.8 collective-permute-start.24
  150.8 2.8 collective-permute-done.24
  153.7 11.2 %attn_bwd.1 = (bf16[192,512]{1,0:T(8,128)(2,1)S(1)}, f32[384,512]{1,0:T(8,128)}, bf16[400,512]{1,0:T(8,128)(2,1)}, f32[1,512]{1,0:T(1,128)S(1)}, f32[3,8,2048]{2,1,0:T(8,128)S(1)}) custom-call(s32[8]{0:T(128)S(1)} %sub.44.start_ref, f32[3,1024,512]{2,1,0:T(8,128)} %get-tuple-element.190.p_ref, bf16[192,512]{1,0:T(8,128)(2,1)S(1)} %copy-done.18, ...), custom_call_target="tpu_custom_call" | custom-call | bytes 1500000000 | tf_op jit(solution)/shard_map/attn_bwd/pallas_call | solution.py:288
  165.0 1.7 out_grad.1
  170.9 5.3 %collective-permute-done.25.got_ref = bf16[400,512]{1,0:T(8,128)(2,1)S(1)} collective-permute-done((bf16[400,512]{1,0:T(8,128)(2,1)}, bf16[400,512]{1,0:T(8,128)(2,1)S(1)}, u32[]{:S(2)}, u32[]{:S(2)}) %collective-permute-start.25) | collective-permute-done | bytes 409632 | tf_op jit(solution)/shard_map/dkv_x/ppermute | solution.py:86
  176.9 4.6 %kv_sum.1 = (bf16[384,512]{1,0:T(8,128)(2,1)S(1)}, f32[1472,256]{1,0:T(8,128)}, bf16[1504,256]{1,0:T(8,128)(2,1)}, f32[16,256]{1,0:T(8,128)S(1)}) custom-call(f32[384,512]{1,0:T(8,128)} %get-tuple-element.205.own_ref, bf16[400,512]{1,0:T(8,128)(2,1)} %copy-done.43, f32[1,512]{1,0:T(1,128)S(1)} %get-tuple-element.199.col_ref, ...), custom_call_target="tpu_custom_call" | custom-call | bytes 30000 | tf_op jit(solution)/shard_map/kv_sum/pallas_call | solution.py:63
  181.6 5.1 %fold_core.1 = (f32[2,192,1472]{2,1,0:T(8,128)}, bf16[2,192,1472]{2,1,0:T(8,128)(2,1)}) custom-call(s32[1]{0:T(128)} %bitcast.c_ref, bf16[192,512]{1,0:T(8,128)(2,1)S(1)} %get-tuple-element.211.dq_ref, bf16[384,512]{1,0:T(8,128)(2,1)S(1)} %get-tuple-element.212.dkv_ref, bf16[1472,256]{1,0:T(8,128)(2,1)} %copy-done.6, bf16[1472,256]{1,0:T(8,128)(2,1)} %copy-done.7, ...), custom_call_target="tpu_custom_call" | custom-call | bytes 30000 | tf_op jit(solution)/shard_map/fold_core/pallas_call | solution.py:63
  187.8 1.9 collective-permute-done.27.got_ref
  190.8 2.3 fold_x.1
  193.9 12.6 %collective-permute-done.28.got_ref = bf16[1504,256]{1,0:T(8,128)(2,1)S(1)} collective-permute-done((bf16[1504,256]{1,0:T(8,128)(2,1)}, bf16[1504,256]{1,0:T(8,128)(2,1)S(1)}, u32[]{:S(2)}, u32[]{:S(2)}) %collective-permute-start.28) | collective-permute-done | bytes 770080 | tf_op jit(solution)/shard_map/back_y/ppermute | solution.py:86
  206.5 2.0 collective-permute-done.29.got_ref
  210.5 4.4 %last.1 = (f32[1472,128]{1,0:T(8,128)S(1)}, f32[1504,128]{1,0:T(8,128)}, f32[32,128]{1,0:T(8,128)S(1)}, f32[1488,256]{1,0:T(8,128)}) custom-call(s32[1]{0:T(128)} %bitcast.c_ref, f32[1472,256]{1,0:T(8,128)} %get-tuple-element.222.own_ref, bf16[1504,256]{1,0:T(8,128)(2,1)} %copy-done.37, f32[16,256]{1,0:T(8,128)S(1)} %get-tuple-element.210.small_ref, ...), custom_call_target="tpu_custom_call" | custom-call | bytes 30000 | tf_op jit(solution)/shard_map/last/pallas_call | solution.py:63
  216.4 2.4 collective-permute-start.30
  218.8 7.9 %collective-permute-done.33.got_ref = bf16[96,1472]{1,0:T(8,128)(2,1)S(1)} collective-permute-done((bf16[96,1472]{1,0:T(8,128)(2,1)S(1)}, bf16[96,1472]{1,0:T(8,128)(2,1)S(1)}, u32[]{:S(2)}, u32[]{:S(2)}) %collective-permute-start.33) | collective-permute-done | bytes 282656 | tf_op jit(solution)/shard_map/share_z/ppermute | solution.py:86
  227.6 2.3 collective-permute-start.34
  230.0 18.7 %collective-permute-done.34.got_ref = bf16[48,1472]{1,0:T(8,128)(2,1)S(1)} collective-permute-done((bf16[48,1472]{1,0:T(8,128)(2,1)S(1)}, bf16[48,1472]{1,0:T(8,128)(2,1)S(1)}, u32[]{:S(2)}, u32[]{:S(2)}) %collective-permute-start.34) | collective-permute-done | bytes 141344 | tf_op jit(solution)/shard_map/share_z/ppermute | solution.py:86
  248.8 3.1 collective-permute-start.36
  252.6 9.9 %collective-permute-done.35.refs_1_ = bf16[64,1472]{1,0:T(8,128)(2,1)S(1)} collective-permute-done((bf16[64,1472]{1,0:T(8,128)(2,1)S(1)}, bf16[64,1472]{1,0:T(8,128)(2,1)S(1)}, u32[]{:S(2)}, u32[]{:S(2)}) %collective-permute-start.35) | collective-permute-done | bytes 188448 | tf_op jit(solution)/shard_map/join_z/ppermute | solution.py:86
  262.5 12.9 %collective-permute-done.36.refs_2_ = bf16[64,1472]{1,0:T(8,128)(2,1)S(1)} collective-permute-done((bf16[64,1472]{1,0:T(8,128)(2,1)S(1)}, bf16[64,1472]{1,0:T(8,128)(2,1)S(1)}, u32[]{:S(2)}, u32[]{:S(2)}) %collective-permute-start.36) | collective-permute-done | bytes 188448 | tf_op jit(solution)/shard_map/join_z/ppermute | solution.py:86
  277.2 4.0 %out_rows.1 = (bf16[1472,128]{1,0:T(8,128)(2,1)S(1)}, bf16[1472,128]{1,0:T(8,128)(2,1)S(1)}, bf16[1472,256]{1,0:T(8,128)(2,1)}) custom-call(s32[1]{0:T(128)} %bitcast.c_ref, f32[1472,256]{1,0:T(8,128)} %get-tuple-element.153.res_ref, bf16[1472,256]{1,0:T(8,128)(2,1)} %ffn_out.4.own_ref, bf16[1472,256]{1,0:T(8,128)(2,1)} %copy-done.38, ...), custom_call_target="tpu_custom_call" | custom-call | bytes 30000 | tf_op jit(solution)/shard_map/out_rows/pallas_call | solution.py:63
  283.8 8.8 %collective-permute-done.38.got_ref = bf16[208,1472]{1,0:T(8,128)(2,1)S(1)} collective-permute-done((bf16[208,1472]{1,0:T(8,128)(2,1)S(1)}, bf16[208,1472]{1,0:T(8,128)(2,1)S(1)}, u32[]{:S(2)}, u32[]{:S(2)}) %collective-permute-start.38) | collective-permute-done | bytes 612384 | tf_op jit(solution)/shard_map/join_x/ppermute | solution.py:86
  295.7 2.4 join_core.1
  298.1 14.1 %all-gather.2.cloned.1.call-done.src = bf16[4,3,1288,128]{3,2,1,0:T(8,128)(2,1)} async-done(((bf16[1,3,1288,128]{3,2,1,0:T(8,128)(2,1)}), bf16[4,3,1288,128]{3,2,1,0:T(8,128)(2,1)}) %all-gather.2.cloned.1.call-update) | async-done | bytes 3956752 | tf_op jit(solution)/shard_map/all_gather | solution.py:974
  312.1 6.0 %widen.1 = (f32[448,1472]{1,0:T(8,128)}, f32[448,1472]{1,0:T(8,128)}, f32[448,1472]{1,0:T(8,128)}) custom-call(bf16[4,3,1288,128]{3,2,1,0:T(8,128)(2,1)} %all-gather.2.cloned.1.call-done.src), custom_call_target="tpu_custom_call" | custom-call | bytes 1500000000 | tf_op jit(solution)/shard_map/widen/pallas_call | solution.py:678
  (232 shorter events, 53.1 us)
Async XLA Ops:
  7.2 203.2 %reduce-scatter.4.cloned.1.call-start = ((), (), s32[]{:S(2)}) async-start(), calls=%async_computation.2 | async-start | bytes 4945920
  7.3 7.2 %collective-permute-start = (bf16[2,1472,128]{2,1,0:T(8,128)(2,1)}, bf16[2,1472,128]{2,1,0:T(8,128)(2,1)S(1)}, u32[]{:S(2)}, u32[]{:S(2)}) collective-permute-start(bf16[2,1472,128]{2,1,0:T(8,128)(2,1)} %bitcast.102), channel_id=1, source_target_pairs={{0,1},{1,0},{2,3},{3,2},{4,5},{5,4},{6,7},{7,6},{8,9},{9,8},{10,11... | collective-permute-start | bytes 2261000 | tf_op jit(solution)/shard_map/x_core/ppermute | solution.py:86
  7.8 11.3 %collective-permute-start.1 = (bf16[2,1472,128]{2,1,0:T(8,128)(2,1)}, bf16[2,1472,128]{2,1,0:T(8,128)(2,1)}, u32[]{:S(2)}, u32[]{:S(2)}) collective-permute-start(bf16[2,1472,128]{2,1,0:T(8,128)(2,1)} %bitcast.100), channel_id=1, source_target_pairs={{0,1},{1,0},{2,3},{3,2},{4,5},{5,4},{6,7},{7,6},{8,9},{9,8},{10,11... | collective-permute-start | bytes 2261000 | tf_op jit(solution)/shard_map/dy_core/ppermute | solution.py:86
  7.9 15.1 %collective-permute-start.3 = (bf16[448,1472]{1,0:T(8,128)(2,1)}, bf16[448,1472]{1,0:T(8,128)(2,1)S(1)}, u32[]{:S(2)}, u32[]{:S(2)}) collective-permute-start(bf16[448,1472]{1,0:T(8,128)(2,1)} %bitcast.79), channel_id=1, source_target_pairs={{0,1},{1,0},{2,3},{3,2},{4,5},{5,4},{6,7},{7,6},{8,9},{9,8},{10,11... | collective-permute-start | bytes 3956744 | tf_op jit(solution)/shard_map/gate_core/ppermute | solution.py:86
  8.3 14.7 %collective-permute-start.4 = (bf16[448,1472]{1,0:T(8,128)(2,1)}, bf16[448,1472]{1,0:T(8,128)(2,1)}, u32[]{:S(2)}, u32[]{:S(2)}) collective-permute-start(bf16[448,1472]{1,0:T(8,128)(2,1)} %bitcast.84), channel_id=1, source_target_pairs={{0,1},{1,0},{2,3},{3,2},{4,5},{5,4},{6,7},{7,6},{8,9},{9,8},{10,11... | collective-permute-start | bytes 3956744 | tf_op jit(solution)/shard_map/up_core/ppermute | solution.py:86
  8.4 29.7 %collective-permute-start.5 = (bf16[448,1472]{1,0:T(8,128)(2,1)}, bf16[448,1472]{1,0:T(8,128)(2,1)S(1)}, u32[]{:S(2)}, u32[]{:S(2)}) collective-permute-start(bf16[448,1472]{1,0:T(8,128)(2,1)} %d0.15), channel_id=1, source_target_pairs={{0,1},{1,0},{2,3},{3,2},{4,5},{5,4},{6,7},{7,6},{8,9},{9,8},{10,11... | collective-permute-start | bytes 3956744 | tf_op jit(solution)/shard_map/down_core/ppermute | solution.py:86
  16.2 49.4 %copy-start.16 = (bf16[1472,256]{1,0:T(8,128)(2,1)}, bf16[1472,256]{1,0:T(8,128)(2,1)S(1)}, u32[]{:S(2)}) copy-start(bf16[1472,256]{1,0:T(8,128)(2,1)S(1)} %get-tuple-element.148.x_ref) | copy-start | bytes 2260996
  16.2 20.1 %collective-permute-start.2 = (bf16[1472,256]{1,0:T(8,128)(2,1)S(1)}, bf16[1472,256]{1,0:T(8,128)(2,1)S(1)}, u32[]{:S(2)}, u32[]{:S(2)}) collective-permute-start(bf16[1472,256]{1,0:T(8,128)(2,1)S(1)} %get-tuple-element.136.n_ref.n0_ref), channel_id=1, source_target_pairs={{0,4},{4,0},{1,5},{5,1},{2,6},{6,2},{3,7},{7,3},{8,12},{12,8},{9,1... | collective-permute-start | bytes 2261000 | tf_op jit(solution)/shard_map/n1_y/ppermute | solution.py:86
  20.5 109.6 %copy-start.5 = (bf16[1472,256]{1,0:T(8,128)(2,1)}, bf16[1472,256]{1,0:T(8,128)(2,1)S(1)}, u32[]{:S(2)}) copy-start(bf16[1472,256]{1,0:T(8,128)(2,1)S(1)} %pair.1.dy_ref.refs_4_) | copy-start | bytes 2260996
  21.2 25.8 %copy-start.25 = (bf16[384,256]{1,0:T(8,128)(2,1)}, bf16[384,256]{1,0:T(8,128)(2,1)S(1)}, u32[]{:S(2)}) copy-start(bf16[384,256]{1,0:T(8,128)(2,1)S(1)} %get-tuple-element.140.k0) | copy-start | bytes 589828
  21.2 16.9 %collective-permute-start.6 = (bf16[384,256]{1,0:T(8,128)(2,1)S(1)}, bf16[384,256]{1,0:T(8,128)(2,1)S(1)}, u32[]{:S(2)}, u32[]{:S(2)}) collective-permute-start(bf16[384,256]{1,0:T(8,128)(2,1)S(1)} %get-tuple-element.140.k0), channel_id=1, source_target_pairs={{0,2},{1,3},{2,0},{3,1},{4,6},{5,7},{6,4},{7,5},{8,10},{9,11},{10,... | collective-permute-start | bytes 589832 | tf_op jit(solution)/shard_map/kv_own_x/ppermute | solution.py:86
  36.3 10.2 %collective-permute-start.10 = (bf16[96,1472]{1,0:T(8,128)(2,1)S(1)}, bf16[96,1472]{1,0:T(8,128)(2,1)S(1)}, u32[]{:S(2)}, u32[]{:S(2)}) collective-permute-start(bf16[96,1472]{1,0:T(8,128)(2,1)S(1)} %copy-done.44), channel_id=1, source_target_pairs={{0,4},{4,0},{1,5},{5,1},{2,6},{6,2},{3,7},{7,3},{8,12},{12,8},{9,1... | collective-permute-start | bytes 847880 | tf_op jit(solution)/shard_map/wout_y/ppermute | solution.py:86
  38.7 17.6 %copy-start.29 = (bf16[384,256]{1,0:T(8,128)(2,1)}, bf16[384,256]{1,0:T(8,128)(2,1)S(1)}, u32[]{:S(2)}) copy-start(bf16[384,256]{1,0:T(8,128)(2,1)S(1)} %get-tuple-element.146.k1) | copy-start | bytes 589828
  38.8 6.3 %collective-permute-start.7 = (bf16[384,256]{1,0:T(8,128)(2,1)S(1)}, bf16[384,256]{1,0:T(8,128)(2,1)S(1)}, u32[]{:S(2)}, u32[]{:S(2)}) collective-permute-start(bf16[384,256]{1,0:T(8,128)(2,1)S(1)} %get-tuple-element.146.k1), channel_id=1, source_target_pairs={{0,2},{1,3},{2,0},{3,1},{4,6},{5,7},{6,4},{7,5},{8,10},{9,11},{10,... | collective-permute-start | bytes 589832 | tf_op jit(solution)/shard_map/kv_far_x/ppermute | solution.py:86
  45.0 20.5 %collective-permute-start.9 = (bf16[1472,256]{1,0:T(8,128)(2,1)S(1)}, bf16[1472,256]{1,0:T(8,128)(2,1)S(1)}, u32[]{:S(2)}, u32[]{:S(2)}) collective-permute-start(bf16[1472,256]{1,0:T(8,128)(2,1)S(1)} %pair.1.dy_ref.refs_4_), channel_id=1, source_target_pairs={{0,2},{1,3},{2,0},{3,1},{4,6},{5,7},{6,4},{7,5},{8,10},{9,11},{10,... | collective-permute-start | bytes 2261000 | tf_op jit(solution)/shard_map/dy_x/ppermute | solution.py:86
  46.5 19.1 %copy-start.19 = (bf16[96,1472]{1,0:T(8,128)(2,1)}, bf16[96,1472]{1,0:T(8,128)(2,1)S(1)}, u32[]{:S(2)}) copy-start(bf16[96,1472]{1,0:T(8,128)(2,1)S(1)} %collective-permute-done.10.w1_ref) | copy-start | bytes 847876
  46.5 19.0 %collective-permute-start.11 = (bf16[1472,256]{1,0:T(8,128)(2,1)S(1)}, bf16[1472,256]{1,0:T(8,128)(2,1)S(1)}, u32[]{:S(2)}, u32[]{:S(2)}) collective-permute-start(bf16[1472,256]{1,0:T(8,128)(2,1)S(1)} %pair.1.dy_ref.refs_4_), channel_id=1, source_target_pairs={{0,4},{4,0},{1,5},{5,1},{2,6},{6,2},{3,7},{7,3},{8,12},{12,8},{9,1... | collective-permute-start | bytes 2261000 | tf_op jit(solution)/shard_map/dy_y/ppermute | solution.py:86
  47.1 18.5 %copy-start.14 = (bf16[192,1472]{1,0:T(8,128)(2,1)S(1)}, bf16[192,1472]{1,0:T(8,128)(2,1)}, u32[]{:S(2)}) copy-start(bf16[192,1472]{1,0:T(8,128)(2,1)} %w0_ref.3) | copy-start | bytes 1695748
  56.3 9.2 %collective-permute-start.12 = (bf16[96,1472]{1,0:T(8,128)(2,1)S(1)}, bf16[96,1472]{1,0:T(8,128)(2,1)S(1)}, u32[]{:S(2)}, u32[]{:S(2)}) collective-permute-start(bf16[96,1472]{1,0:T(8,128)(2,1)S(1)} %collective-permute-done.10.w1_ref), channel_id=1, source_target_pairs={{0,1},{1,0},{2,3},{3,2},{4,5},{5,4},{6,7},{7,6},{8,9},{9,8},{10,11... | collective-permute-start | bytes 847880 | tf_op jit(solution)/shard_map/wout_core/ppermute | solution.py:86
  56.4 9.1 %collective-permute-start.8 = (bf16[192,256]{1,0:T(8,128)(2,1)S(1)}, bf16[192,256]{1,0:T(8,128)(2,1)S(1)}, u32[]{:S(2)}, u32[]{:S(2)}) collective-permute-start(bf16[192,256]{1,0:T(8,128)(2,1)S(1)} %get-tuple-element.310), channel_id=1, source_target_pairs={{0,4},{4,0},{1,5},{5,1},{2,6},{6,2},{3,7},{7,3},{8,12},{12,8},{9,1... | collective-permute-start | bytes 294920 | tf_op jit(solution)/shard_map/mixed_y/ppermute | solution.py:86
  67.6 19.8 %collective-permute-start.13 = (bf16[1472,256]{1,0:T(8,128)(2,1)S(1)}, bf16[1472,256]{1,0:T(8,128)(2,1)S(1)}, u32[]{:S(2)}, u32[]{:S(2)}) collective-permute-start(bf16[1472,256]{1,0:T(8,128)(2,1)S(1)} %get-tuple-element.158.n_ref.refs_4_.refs_12_.refs_20_), channel_id=1, source_target_pairs={{0,2},{1,3},{2,0},{3,1},{4,6},{5,7},{6,4},{7,5},{8,10},{9,11},{10,... | collective-permute-start | bytes 2261000 | tf_op jit(solution)/shard_map/n2_x/ppermute | solution.py:86
  68.4 19.1 %collective-permute-start.14 = (bf16[1472,256]{1,0:T(8,128)(2,1)S(1)}, bf16[1472,256]{1,0:T(8,128)(2,1)S(1)}, u32[]{:S(2)}, u32[]{:S(2)}) collective-permute-start(bf16[1472,256]{1,0:T(8,128)(2,1)S(1)} %get-tuple-element.158.n_ref.refs_4_.refs_12_.refs_20_), channel_id=1, source_target_pairs={{0,4},{4,0},{1,5},{5,1},{2,6},{6,2},{3,7},{7,3},{8,12},{12,8},{9,1... | collective-permute-start | bytes 2261000 | tf_op jit(solution)/shard_map/n2_y/ppermute | solution.py:86
  70.0 32.1 %collective-permute-start.16 = (bf16[1472,256]{1,0:T(8,128)(2,1)S(1)}, bf16[1472,256]{1,0:T(8,128)(2,1)S(1)}, u32[]{:S(2)}, u32[]{:S(2)}) collective-permute-start(bf16[1472,256]{1,0:T(8,128)(2,1)S(1)} %pick.2), channel_id=1, source_target_pairs={{0,4},{1,3},{2,6},{3,1},{4,0},{5,7},{6,2},{7,5},{8,12},{9,11},{10,... | collective-permute-start | bytes 2261000 | tf_op jit(solution)/shard_map/dy_d/ppermute | solution.py:86
  87.5 16.5 %collective-permute-start.15 = (bf16[1472,256]{1,0:T(8,128)(2,1)S(1)}, bf16[1472,256]{1,0:T(8,128)(2,1)S(1)}, u32[]{:S(2)}, u32[]{:S(2)}) collective-permute-start(bf16[1472,256]{1,0:T(8,128)(2,1)S(1)} %pick.3), channel_id=1, source_target_pairs={{0,4},{1,3},{2,6},{3,1},{4,0},{5,7},{6,2},{7,5},{8,12},{9,11},{10,... | collective-permute-start | bytes 2261000 | tf_op jit(solution)/shard_map/n2_d/ppermute | solution.py:86
  94.0 19.8 %collective-permute-start.17 = (bf16[1472,256]{1,0:T(8,128)(2,1)S(1)}, bf16[1472,256]{1,0:T(8,128)(2,1)S(1)}, u32[]{:S(2)}, u32[]{:S(2)}) collective-permute-start(bf16[1472,256]{1,0:T(8,128)(2,1)S(1)} %get-tuple-element.173), channel_id=1, source_target_pairs={{0,2},{1,3},{2,0},{3,1},{4,6},{5,7},{6,4},{7,5},{8,10},{9,11},{10,... | collective-permute-start | bytes 2261000 | tf_op jit(solution)/shard_map/dn_x/ppermute | solution.py:86
  101.5 15.2 %collective-permute-start.18 = (bf16[1472,256]{1,0:T(8,128)(2,1)S(1)}, bf16[1472,256]{1,0:T(8,128)(2,1)S(1)}, u32[]{:S(2)}, u32[]{:S(2)}) collective-permute-start(bf16[1472,256]{1,0:T(8,128)(2,1)S(1)} %get-tuple-element.174), channel_id=1, source_target_pairs={{0,4},{4,0},{1,5},{5,1},{2,6},{6,2},{3,7},{7,3},{8,12},{12,8},{9,1... | collective-permute-start | bytes 2261000 | tf_op jit(solution)/shard_map/dn_y/ppermute | solution.py:86
  121.7 8.3 %collective-permute-start.23 = (bf16[2,448,1472]{2,1,0:T(8,128)(2,1)S(1)}, bf16[2,448,1472]{2,1,0:T(8,128)(2,1)S(1)}, u32[]{:S(2)}, u32[]{:S(2)}) collective-permute-start(bf16[2,448,1472]{2,1,0:T(8,128)(2,1)S(1)} %wgrad_give.3), channel_id=1, source_target_pairs={{0,1},{1,0},{2,3},{3,2},{4,5},{5,4},{6,7},{7,6},{8,9},{9,8},{10,11... | collective-permute-start | bytes 7913480 | tf_op jit(solution)/shard_map/wgrad_core/ppermute | solution.py:86
  121.8 8.2 %collective-permute-start.22 = (bf16[1,448,1472]{2,1,0:T(8,128)(2,1)S(1)}, bf16[1,448,1472]{2,1,0:T(8,128)(2,1)S(1)}, u32[]{:S(2)}, u32[]{:S(2)}) collective-permute-start(bf16[1,448,1472]{2,1,0:T(8,128)(2,1)S(1)} %wgrad_give.2), channel_id=1, source_target_pairs={{0,1},{1,0},{2,3},{3,2},{4,5},{5,4},{6,7},{7,6},{8,9},{9,8},{10,11... | collective-permute-start | bytes 3956744 | tf_op jit(solution)/shard_map/wgrad_core/ppermute | solution.py:86
  122.3 20.0 %collective-permute-start.19 = (bf16[1472,256]{1,0:T(8,128)(2,1)}, bf16[1472,256]{1,0:T(8,128)(2,1)}, u32[]{:S(2)}, u32[]{:S(2)}) collective-permute-start(bf16[1472,256]{1,0:T(8,128)(2,1)} %get-tuple-element.185), channel_id=1, source_target_pairs={{0,6},{1,7},{2,4},{3,5},{4,2},{5,3},{6,0},{7,1},{8,14},{9,15},{10,... | collective-permute-start | bytes 2261000 | tf_op jit(solution)/shard_map/dn_d/ppermute | solution.py:86
  136.7 175.5 %all-gather.2.cloned.1.call-start = ((), (), s32[]{:S(2)}) async-start(), calls=%async_computation.1 | async-start | bytes 4945920 | tf_op jit(solution)/shard_map/all_gather | solution.py:974
  147.9 5.7 %collective-permute-start.24 = (bf16[192,256]{1,0:T(8,128)(2,1)S(1)}, bf16[192,256]{1,0:T(8,128)(2,1)S(1)}, u32[]{:S(2)}, u32[]{:S(2)}) collective-permute-start(bf16[192,256]{1,0:T(8,128)(2,1)S(1)} %get-tuple-element.197), channel_id=1, source_target_pairs={{0,4},{4,0},{1,5},{5,1},{2,6},{6,2},{3,7},{7,3},{8,12},{12,8},{9,1... | collective-permute-start | bytes 294920 | tf_op jit(solution)/shard_map/dmixed_y/ppermute | solution.py:86
  149.7 20.3 %collective-permute-start.20 = (bf16[1472,256]{1,0:T(8,128)(2,1)}, bf16[1472,256]{1,0:T(8,128)(2,1)S(1)}, u32[]{:S(2)}, u32[]{:S(2)}) collective-permute-start(bf16[1472,256]{1,0:T(8,128)(2,1)} %ffn_out.5), channel_id=1, source_target_pairs={{0,2},{1,3},{2,0},{3,1},{4,6},{5,7},{6,4},{7,5},{8,10},{9,11},{10,... | collective-permute-start | bytes 2261000 | tf_op jit(solution)/shard_map/out_x/ppermute | solution.py:86
  149.7 20.4 %collective-permute-start.21 = (bf16[1472,256]{1,0:T(8,128)(2,1)}, bf16[1472,256]{1,0:T(8,128)(2,1)}, u32[]{:S(2)}, u32[]{:S(2)}) collective-permute-start(bf16[1472,256]{1,0:T(8,128)(2,1)} %ffn_out.6), channel_id=1, source_target_pairs={{0,4},{4,0},{1,5},{5,1},{2,6},{6,2},{3,7},{7,3},{8,12},{12,8},{9,1... | collective-permute-start | bytes 2261000 | tf_op jit(solution)/shard_map/out_y/ppermute | solution.py:86
  166.7 9.5 %collective-permute-start.25 = (bf16[400,512]{1,0:T(8,128)(2,1)}, bf16[400,512]{1,0:T(8,128)(2,1)S(1)}, u32[]{:S(2)}, u32[]{:S(2)}) collective-permute-start(bf16[400,512]{1,0:T(8,128)(2,1)} %get-tuple-element.206), channel_id=1, source_target_pairs={{0,2},{1,3},{2,0},{3,1},{4,6},{5,7},{6,4},{7,5},{8,10},{9,11},{10,... | collective-permute-start | bytes 1228808 | tf_op jit(solution)/shard_map/dkv_x/ppermute | solution.py:86
  167.0 14.5 %collective-permute-start.26 = (bf16[192,1472]{1,0:T(8,128)(2,1)}, bf16[192,1472]{1,0:T(8,128)(2,1)}, u32[]{:S(2)}, u32[]{:S(2)}) collective-permute-start(bf16[192,1472]{1,0:T(8,128)(2,1)} %get-tuple-element.213), channel_id=1, source_target_pairs={{0,4},{4,0},{1,5},{5,1},{2,6},{6,2},{3,7},{7,3},{8,12},{12,8},{9,1... | collective-permute-start | bytes 1695752 | tf_op jit(solution)/shard_map/gout_y/ppermute | solution.py:86
  186.7 3.1 collective-permute-start.27
  186.7 19.8 %collective-permute-start.28 = (bf16[1504,256]{1,0:T(8,128)(2,1)}, bf16[1504,256]{1,0:T(8,128)(2,1)S(1)}, u32[]{:S(2)}, u32[]{:S(2)}) collective-permute-start(bf16[1504,256]{1,0:T(8,128)(2,1)} %get-tuple-element.217), channel_id=1, source_target_pairs={{0,4},{4,0},{1,5},{5,1},{2,6},{6,2},{3,7},{7,3},{8,12},{12,8},{9,1... | collective-permute-start | bytes 2310152 | tf_op jit(solution)/shard_map/back_y/ppermute | solution.py:86
  193.1 15.4 %collective-permute-start.29 = (bf16[192,1472]{1,0:T(8,128)(2,1)S(1)}, bf16[192,1472]{1,0:T(8,128)(2,1)S(1)}, u32[]{:S(2)}, u32[]{:S(2)}) collective-permute-start(bf16[192,1472]{1,0:T(8,128)(2,1)S(1)} %get-tuple-element.220), channel_id=1, source_target_pairs={{0,2},{1,3},{2,0},{3,1},{4,6},{5,7},{6,4},{7,5},{8,10},{9,11},{10,... | collective-permute-start | bytes 1695752 | tf_op jit(solution)/shard_map/fold_x/ppermute | solution.py:86
  214.9 15.0 %collective-permute-start.31 = (f32[1504,128]{1,0:T(8,128)}, f32[1504,128]{1,0:T(8,128)S(1)}, u32[]{:S(2)}, u32[]{:S(2)}) collective-permute-start(f32[1504,128]{1,0:T(8,128)} %get-tuple-element.228), channel_id=1, source_target_pairs={{0,1},{1,0},{2,3},{3,2},{4,5},{5,4},{6,7},{7,6},{8,9},{9,8},{10,11... | collective-permute-start | bytes 2310152 | tf_op jit(solution)/shard_map/grad_core/ppermute | solution.py:86
  214.9 11.8 %collective-permute-start.33 = (bf16[96,1472]{1,0:T(8,128)(2,1)S(1)}, bf16[96,1472]{1,0:T(8,128)(2,1)S(1)}, u32[]{:S(2)}, u32[]{:S(2)}) collective-permute-start(bf16[96,1472]{1,0:T(8,128)(2,1)S(1)} %get-tuple-element.233), channel_id=1, source_target_pairs={{0,8},{8,0},{16,24},{24,16},{1,9},{9,1},{17,25},{25,17},{2,10},{10... | collective-permute-start | bytes 847880 | tf_op jit(solution)/shard_map/share_z/ppermute | solution.py:86
  216.4 60.8 %collective-permute-start.30 = (bf16[1472,256]{1,0:T(8,128)(2,1)}, bf16[1472,256]{1,0:T(8,128)(2,1)}, u32[]{:S(2)}, u32[]{:S(2)}) collective-permute-start(bf16[1472,256]{1,0:T(8,128)(2,1)} %ffn_out.7), channel_id=1, source_target_pairs={{0,6},{1,7},{2,4},{3,5},{4,2},{5,3},{6,0},{7,1},{8,14},{9,15},{10,... | collective-permute-start | bytes 2261000 | tf_op jit(solution)/shard_map/out_d/ppermute | solution.py:86
  227.6 21.0 %collective-permute-start.34 = (bf16[48,1472]{1,0:T(8,128)(2,1)S(1)}, bf16[48,1472]{1,0:T(8,128)(2,1)S(1)}, u32[]{:S(2)}, u32[]{:S(2)}) collective-permute-start(bf16[48,1472]{1,0:T(8,128)(2,1)S(1)} %get-tuple-element.235), channel_id=1, source_target_pairs={{0,16},{8,24},{16,0},{24,8},{1,17},{9,25},{17,1},{25,9},{2,18},{10... | collective-permute-start | bytes 423944 | tf_op jit(solution)/shard_map/share_z/ppermute | solution.py:86
  248.7 13.8 %collective-permute-start.35 = (bf16[64,1472]{1,0:T(8,128)(2,1)S(1)}, bf16[64,1472]{1,0:T(8,128)(2,1)S(1)}, u32[]{:S(2)}, u32[]{:S(2)}) collective-permute-start(bf16[64,1472]{1,0:T(8,128)(2,1)S(1)} %share_sum.1.refs_0_), channel_id=1, source_target_pairs={{0,8},{8,16},{16,24},{24,0},{1,9},{9,17},{17,25},{25,1},{2,10},{10... | collective-permute-start | bytes 565256 | tf_op jit(solution)/shard_map/join_z/ppermute | solution.py:86
  248.8 26.7 %collective-permute-start.36 = (bf16[64,1472]{1,0:T(8,128)(2,1)S(1)}, bf16[64,1472]{1,0:T(8,128)(2,1)S(1)}, u32[]{:S(2)}, u32[]{:S(2)}) collective-permute-start(bf16[64,1472]{1,0:T(8,128)(2,1)S(1)} %share_sum.1.refs_0_), channel_id=1, source_target_pairs={{0,16},{8,24},{16,0},{24,8},{1,17},{9,25},{17,1},{25,9},{2,18},{10... | collective-permute-start | bytes 565256 | tf_op jit(solution)/shard_map/join_z/ppermute | solution.py:86
  251.9 23.6 %collective-permute-start.37 = (bf16[64,1472]{1,0:T(8,128)(2,1)S(1)}, bf16[64,1472]{1,0:T(8,128)(2,1)S(1)}, u32[]{:S(2)}, u32[]{:S(2)}) collective-permute-start(bf16[64,1472]{1,0:T(8,128)(2,1)S(1)} %share_sum.1.refs_0_), channel_id=1, source_target_pairs={{0,24},{8,0},{16,8},{24,16},{1,25},{9,1},{17,9},{25,17},{2,26},{10... | collective-permute-start | bytes 565256 | tf_op jit(solution)/shard_map/join_z/ppermute | solution.py:86
  276.2 16.5 %collective-permute-start.38 = (bf16[208,1472]{1,0:T(8,128)(2,1)S(1)}, bf16[208,1472]{1,0:T(8,128)(2,1)S(1)}, u32[]{:S(2)}, u32[]{:S(2)}) collective-permute-start(bf16[208,1472]{1,0:T(8,128)(2,1)S(1)} %get-tuple-element.238.own_ref), channel_id=1, source_target_pairs={{0,2},{1,3},{2,0},{3,1},{4,6},{5,7},{6,4},{7,5},{8,10},{9,11},{10,... | collective-permute-start | bytes 1837064 | tf_op jit(solution)/shard_map/join_x/ppermute | solution.py:86
  281.2 1.7 collective-permute-start.32
  292.8 2.9 collective-permute-start.39
  (41 other events, 285.4 us)
Sparse Core Ops, SparseCore 0:
  136.8 73.6 reduce-scatter.3
  212.0 100.0 all-gather.1

commit v6 on v5

--- a/solution.py
+++ b/solution.py
@@ -772,12 +772,11 @@
     gain_one = gain_attn.reshape(1, width)
     gain_two = gain_ffn.reshape(1, width)
 
-    w_half = w_out.reshape(2, inner // 2, width)
-    w_half = lax.dynamic_index_in_dim(w_half, c_at, 0, keepdims=False)
+    x_got = core_swap(x_in, "x_core")
     x_rows, normed_one, inv_one = call(
         prep_kernel,
         (sds((width, block), BF), sds((width, block), BF), sds((1, block), F32)),
-        (in_hbm(x_in), core_swap(x_in, "x_core"), gain_one),
+        (in_hbm(x_in), x_got, gain_one),
         "prep",
         vmem=20,
         scalars=(c_scalar,),
@@ -793,9 +792,9 @@
         scalars=(c_scalar,),
     )
 
-    gate_other = core_swap(gate_w, "gate_core")
-    up_other = core_swap(up_w, "up_core")
-    down_other = core_swap(down_weight, "down_core")
+    gate_other = core_swap(after(gate_w, x_got), "gate_core")
+    up_other = core_swap(after(up_w, x_got), "up_core")
+    down_other = core_swap(after(down_weight, x_got), "down_core")
     ffn_weights = (gate_w, gate_other, up_w, up_other, down_weight, down_other)
     def project(n):
         return call(
@@ -828,6 +827,8 @@
     kv_own_x = x_swap(kv_own, "kv_own_x")
     normed_far_raw = after(normed_far_raw, bias, kv_own)
     normed_far = after(normed_far_raw, down_other, kv_own_x)
+    w_half = after(w_out, kv_own).reshape(2, inner // 2, width)
+    w_half = lax.dynamic_index_in_dim(w_half, c_at, 0, keepdims=False)
     w_half = y_swap(after(w_half, normed_far_raw), "wout_y")
     dy_y = y_swap(after(dy_own, w_half), "dy_y")
     w_half_got = core_swap(w_half, "wout_core")

time: 330 us -> 329 us (level)
  transfers between devices with their start and end apart: 42 -> 42, of which waited for: 22 -> 23; matrix products, arithmetic and copies ran while one was open for 3% -> 3% of each run, Pallas kernels for 33% -> 33%
where the time goes in v6:
time: 329 us; the launch traced here: 324 us
  waiting for transfers between devices  138 us (42%)
  Pallas kernels  121 us (37%)
  starting transfers between devices  38.5 us (12%)
  between operations  15.1 us (5%)
  local copies, waits for them, and re-layouts  9.91 us (3%)
    ppermute x40, waiting for transfers between devices, move(): return lax.ppermute(v, axes, pairs)  123 us
    pallas_call x37, Pallas kernels, call(): pl.pallas_call(kernel, out_shape=out_shape, in_specs=in_specs, out_specs=...  88.6 us
    ppermute x40, starting transfers between devices, move(): return lax.ppermute(v, axes, pairs)  38.4 us
    all_gather x1, waiting for transfers between devices, run(): ffn_grads = lax.all_gather(after(ffn_grads, keep), 'dp', axis=0, tiled=True)  14.1 us
    pallas_call x1, Pallas kernels, attn_bwd(): pl.pallas_call(functools.partial(attn_bwd_kernel, inner=inner, heads=head...  11.2 us
    pallas_call x1, Pallas kernels, attn_fwd(): pl.pallas_call(functools.partial(attn_fwd_kernel, inner=inner), out_shape...  9.16 us
  transfers between devices with their start and end apart: 42, of which 23 were waited for; matrix products, arithmetic and copies ran while one was open for 3% of the time, Pallas kernels for 33%

profile of v6, /device:TPU:0, one launch (start us, length us, event | category | flops | bytes accessed | tf_op | source)
XLA Modules:
  0.0 324.3 jit_solution(7132604659548674253)
XLA Ops:
  13.7 1.7 prep.1
  15.5 2.7 collective-permute-start.2
  22.6 6.0 %bias.1.bias_ref = f32[3,1024,512]{2,1,0:T(8,128)} custom-call(s32[8]{0:T(128)S(1)} %sub.44.start_ref, f32[8,2048]{1,0:T(8,128)S(1)} %concatenate.83.table_ref, f32[1,1024]{1,0:T(1,128)S(1)} %reshape.105.mask_ref), custom_call_target="tpu_custom_call" | custom-call | bytes 30000 | tf_op jit(solution)/shard_map/bias/pallas_call | solution.py:148
  28.5 7.0 %collective-permute-done.2.n_ref.n1_ref = bf16[1472,256]{1,0:T(8,128)(2,1)S(1)} collective-permute-done((bf16[1472,256]{1,0:T(8,128)(2,1)S(1)}, bf16[1472,256]{1,0:T(8,128)(2,1)S(1)}, u32[]{:S(2)}, u32[]{:S(2)}) %collective-permute-start.2) | collective-permute-done | bytes 753696 | tf_op jit(solution)/shard_map/n1_y/ppermute | solution.py:86
  35.6 1.8 collective-permute-start.10
  39.5 4.7 %collective-permute-done.7.k3 = bf16[384,256]{1,0:T(8,128)(2,1)S(1)} collective-permute-done((bf16[384,256]{1,0:T(8,128)(2,1)S(1)}, bf16[384,256]{1,0:T(8,128)(2,1)S(1)}, u32[]{:S(2)}, u32[]{:S(2)}) %collective-permute-start.7) | collective-permute-done | bytes 196640 | tf_op jit(solution)/shard_map/kv_far_x/ppermute | solution.py:86
  46.3 9.2 %attn_fwd.1 = (f32[3,1024,512]{2,1,0:T(8,128)}, bf16[192,512]{1,0:T(8,128)(2,1)S(1)}) custom-call(bf16[192,512]{1,0:T(8,128)(2,1)S(1)} %constant_dynamic-update-slice_fusion.q_ref, bf16[384,256]{1,0:T(8,128)(2,1)S(1)} %get-tuple-element.146.k0, bf16[384,256]{1,0:T(8,128)(2,1)S(1)} %get-tuple-element.153.k1, bf16[384,256]{1,0:T(8,128)(2,1)S(1)} %collective-permute-done.6.k2, ...), custom_call_target="tpu_custom_call" | custom-call | bytes 30000 | tf_op jit(solution)/shard_map/attn_fwd/pallas_call | solution.py:190
  57.2 7.5 %collective-permute-done.8.m1_ref = bf16[192,256]{1,0:T(8,128)(2,1)S(1)} collective-permute-done((bf16[192,256]{1,0:T(8,128)(2,1)S(1)}, bf16[192,256]{1,0:T(8,128)(2,1)S(1)}, u32[]{:S(2)}, u32[]{:S(2)}) %collective-permute-start.8) | collective-permute-done | bytes 98336 | tf_op jit(solution)/shard_map/mixed_y/ppermute | solution.py:86
  64.8 2.1 mid.1
  70.9 5.7 %ffn.4 = (bf16[2,448,256]{2,1,0:T(8,128)(2,1)S(1)}, bf16[2,448,256]{2,1,0:T(8,128)(2,1)S(1)}, bf16[2,448,256]{2,1,0:T(8,128)(2,1)S(1)}, bf16[1472,256]{1,0:T(8,128)(2,1)S(1)}) custom-call(bf16[1472,256]{1,0:T(8,128)(2,1)S(1)} %get-tuple-element.166.n_ref.refs_4_.refs_12_.refs_20_, f32[2,448,256]{2,1,0:T(8,128)S(1)} %d_act.4.da_ref, ...), custom_call_target="tpu_custom_call" | custom-call | bytes 30000 | tf_op jit(solution)/shard_map/ffn/pallas_call | solution.py:63
  78.4 8.2 %collective-permute-done.13.first_ref.n_ref.refs_5_.refs_13_.refs_21_ = bf16[1472,256]{1,0:T(8,128)(2,1)S(1)} collective-permute-done((bf16[1472,256]{1,0:T(8,128)(2,1)S(1)}, bf16[1472,256]{1,0:T(8,128)(2,1)S(1)}, u32[]{:S(2)}, u32[]{:S(2)}) %collective-permute-start.13) | collective-permute-done | bytes 753696 | tf_op jit(solution)/shard_map/n2_x/ppermute | solution.py:86
  87.5 5.7 %ffn.5 = (bf16[2,448,256]{2,1,0:T(8,128)(2,1)S(1)}, bf16[2,448,256]{2,1,0:T(8,128)(2,1)S(1)}, bf16[2,448,256]{2,1,0:T(8,128)(2,1)S(1)}, bf16[1472,256]{1,0:T(8,128)(2,1)S(1)}) custom-call(bf16[1472,256]{1,0:T(8,128)(2,1)S(1)} %collective-permute-done.13.first_ref.n_ref.refs_5_.refs_13_.refs_21_, f32[2,448,256]{2,1,0:T(8,128)S(1)} %d_act.5.da_ref, ...), custom_call_target="tpu_custom_call" | custom-call | bytes 30000 | tf_op jit(solution)/shard_map/ffn/pallas_call | solution.py:63
  94.8 5.9 %ffn.6 = (bf16[2,448,256]{2,1,0:T(8,128)(2,1)S(1)}, bf16[2,448,256]{2,1,0:T(8,128)(2,1)S(1)}, bf16[2,448,256]{2,1,0:T(8,128)(2,1)S(1)}, bf16[1472,256]{1,0:T(8,128)(2,1)S(1)}) custom-call(bf16[1472,256]{1,0:T(8,128)(2,1)S(1)} %collective-permute-done.14.second_ref.n_ref.refs_6_.refs_14_.refs_22_, f32[2,448,256]{2,1,0:T(8,128)S(1)} %d_act.6.da_ref, ...), custom_call_target="tpu_custom_call" | custom-call | bytes 30000 | tf_op jit(solution)/shard_map/ffn/pallas_call | solution.py:63
  103.2 6.6 %ffn.7 = (bf16[2,448,256]{2,1,0:T(8,128)(2,1)S(1)}, bf16[2,448,256]{2,1,0:T(8,128)(2,1)S(1)}, bf16[2,448,256]{2,1,0:T(8,128)(2,1)S(1)}, bf16[1472,256]{1,0:T(8,128)(2,1)}) custom-call(bf16[1472,256]{1,0:T(8,128)(2,1)S(1)} %collective-permute-done.15.n_ref.refs_7_.refs_15_.refs_23_, f32[2,448,256]{2,1,0:T(8,128)S(1)} %d_act.7.da_ref, ...), custom_call_target="tpu_custom_call" | custom-call | bytes 30000 | tf_op jit(solution)/shard_map/ffn/pallas_call | solution.py:63
  111.4 1.6 collective-permute-done.17.ga_ref
  113.1 2.8 collective-permute-done.18.gb_ref
  115.9 1.9 ffn_out.4.own_ref
  117.8 3.0 wgrad_give.3
  122.9 2.3 ffn_out.5
  125.3 1.9 ffn_out.6
  127.2 2.0 ffn_out.7
  129.2 6.6 %wgrad_sum.1 = bf16[4,3,1288,128]{3,2,1,0:T(8,128)(2,1)} custom-call(bf16[2,448,256]{2,1,0:T(8,128)(2,1)S(1)} %get-tuple-element.200.refs_0_.a_ref, bf16[2,448,256]{2,1,0:T(8,128)(2,1)S(1)} %get-tuple-element.192.refs_1_.a_ref, bf16[2,448,256]{2,1,0:T(8,128)(2,1)S(1)} %get-tuple-element.195.refs_2_.a_ref, ...), custom_call_target="tpu_custom_call" | custom-call | bytes 30000 | tf_op jit(solution)/shard_map/wgrad_sum/pallas_call | solution.py:63
  135.8 5.7 %collective-permute-done.19.gd_ref = bf16[1472,256]{1,0:T(8,128)(2,1)} collective-permute-done((bf16[1472,256]{1,0:T(8,128)(2,1)}, bf16[1472,256]{1,0:T(8,128)(2,1)}, u32[]{:S(2)}, u32[]{:S(2)}) %collective-permute-start.19) | collective-permute-done | bytes 753696 | tf_op jit(solution)/shard_map/dn_d/ppermute | solution.py:86
  141.6 5.5 %mid_back.1 = (f32[1472,256]{1,0:T(8,128)}, bf16[1472,256]{1,0:T(8,128)(2,1)S(1)}, f32[1,1472]{1,0:T(1,128)S(1)}, bf16[192,256]{1,0:T(8,128)(2,1)S(1)}, bf16[192,256]{1,0:T(8,128)(2,1)S(1)}) custom-call(s32[1]{0:T(128)} %bitcast.c_ref, bf16[1472,256]{1,0:T(8,128)(2,1)} %copy-done.33, bf16[1472,256]{1,0:T(8,128)(2,1)} %copy-done.39, ...), custom_call_target="tpu_custom_call" | custom-call | bytes 30000 | tf_op jit(solution)/shard_map/mid_back/pallas_call | solution.py:63
  147.1 1.8 collective-permute-start.24
  150.0 2.8 collective-permute-done.24
  152.8 11.2 %attn_bwd.1 = (bf16[192,512]{1,0:T(8,128)(2,1)S(1)}, f32[384,512]{1,0:T(8,128)}, bf16[400,512]{1,0:T(8,128)(2,1)}, f32[1,512]{1,0:T(1,128)S(1)}, f32[3,8,2048]{2,1,0:T(8,128)S(1)}) custom-call(s32[8]{0:T(128)S(1)} %sub.44.start_ref, f32[3,1024,512]{2,1,0:T(8,128)} %get-tuple-element.198.p_ref, bf16[192,512]{1,0:T(8,128)(2,1)S(1)} %copy-done.18, ...), custom_call_target="tpu_custom_call" | custom-call | bytes 1500000000 | tf_op jit(solution)/shard_map/attn_bwd/pallas_call | solution.py:288
  164.2 1.7 out_grad.1
  170.0 5.3 %collective-permute-done.25.got_ref = bf16[400,512]{1,0:T(8,128)(2,1)S(1)} collective-permute-done((bf16[400,512]{1,0:T(8,128)(2,1)}, bf16[400,512]{1,0:T(8,128)(2,1)S(1)}, u32[]{:S(2)}, u32[]{:S(2)}) %collective-permute-start.25) | collective-permute-done | bytes 409632 | tf_op jit(solution)/shard_map/dkv_x/ppermute | solution.py:86
  176.1 4.6 %kv_sum.1 = (bf16[384,512]{1,0:T(8,128)(2,1)S(1)}, f32[1472,256]{1,0:T(8,128)}, bf16[1504,256]{1,0:T(8,128)(2,1)}, f32[16,256]{1,0:T(8,128)S(1)}) custom-call(f32[384,512]{1,0:T(8,128)} %get-tuple-element.213.own_ref, bf16[400,512]{1,0:T(8,128)(2,1)} %copy-done.43, f32[1,512]{1,0:T(1,128)S(1)} %get-tuple-element.207.col_ref, ...), custom_call_target="tpu_custom_call" | custom-call | bytes 30000 | tf_op jit(solution)/shard_map/kv_sum/pallas_call | solution.py:63
  180.7 5.2 %fold_core.1 = (f32[2,192,1472]{2,1,0:T(8,128)}, bf16[2,192,1472]{2,1,0:T(8,128)(2,1)}) custom-call(s32[1]{0:T(128)} %bitcast.c_ref, bf16[192,512]{1,0:T(8,128)(2,1)S(1)} %get-tuple-element.219.dq_ref, bf16[384,512]{1,0:T(8,128)(2,1)S(1)} %get-tuple-element.220.dkv_ref, bf16[1472,256]{1,0:T(8,128)(2,1)} %copy-done.6, bf16[1472,256]{1,0:T(8,128)(2,1)} %copy-done.7, ...), custom_call_target="tpu_custom_call" | custom-call | bytes 30000 | tf_op jit(solution)/shard_map/fold_core/pallas_call | solution.py:63
  187.0 1.9 collective-permute-done.27.got_ref
  190.0 2.3 fold_x.1
  193.1 12.6 %collective-permute-done.28.got_ref = bf16[1504,256]{1,0:T(8,128)(2,1)S(1)} collective-permute-done((bf16[1504,256]{1,0:T(8,128)(2,1)}, bf16[1504,256]{1,0:T(8,128)(2,1)S(1)}, u32[]{:S(2)}, u32[]{:S(2)}) %collective-permute-start.28) | collective-permute-done | bytes 770080 | tf_op jit(solution)/shard_map/back_y/ppermute | solution.py:86
  205.7 2.0 collective-permute-done.29.got_ref
  209.6 4.4 %last.1 = (f32[1472,128]{1,0:T(8,128)S(1)}, f32[1504,128]{1,0:T(8,128)}, f32[32,128]{1,0:T(8,128)S(1)}, f32[1488,256]{1,0:T(8,128)}) custom-call(s32[1]{0:T(128)} %bitcast.c_ref, f32[1472,256]{1,0:T(8,128)} %get-tuple-element.230.own_ref, bf16[1504,256]{1,0:T(8,128)(2,1)} %copy-done.37, f32[16,256]{1,0:T(8,128)S(1)} %get-tuple-element.218.small_ref, ...), custom_call_target="tpu_custom_call" | custom-call | bytes 30000 | tf_op jit(solution)/shard_map/last/pallas_call | solution.py:63
  215.5 2.4 collective-permute-start.30
  217.9 7.9 %collective-permute-done.33.got_ref = bf16[96,1472]{1,0:T(8,128)(2,1)S(1)} collective-permute-done((bf16[96,1472]{1,0:T(8,128)(2,1)S(1)}, bf16[96,1472]{1,0:T(8,128)(2,1)S(1)}, u32[]{:S(2)}, u32[]{:S(2)}) %collective-permute-start.33) | collective-permute-done | bytes 282656 | tf_op jit(solution)/shard_map/share_z/ppermute | solution.py:86
  226.7 2.3 collective-permute-start.34
  229.0 18.7 %collective-permute-done.34.got_ref = bf16[48,1472]{1,0:T(8,128)(2,1)S(1)} collective-permute-done((bf16[48,1472]{1,0:T(8,128)(2,1)S(1)}, bf16[48,1472]{1,0:T(8,128)(2,1)S(1)}, u32[]{:S(2)}, u32[]{:S(2)}) %collective-permute-start.34) | collective-permute-done | bytes 141344 | tf_op jit(solution)/shard_map/share_z/ppermute | solution.py:86
  247.9 3.1 collective-permute-start.36
  251.7 9.9 %collective-permute-done.35.refs_1_ = bf16[64,1472]{1,0:T(8,128)(2,1)S(1)} collective-permute-done((bf16[64,1472]{1,0:T(8,128)(2,1)S(1)}, bf16[64,1472]{1,0:T(8,128)(2,1)S(1)}, u32[]{:S(2)}, u32[]{:S(2)}) %collective-permute-start.35) | collective-permute-done | bytes 188448 | tf_op jit(solution)/shard_map/join_z/ppermute | solution.py:86
  261.6 12.9 %collective-permute-done.36.refs_2_ = bf16[64,1472]{1,0:T(8,128)(2,1)S(1)} collective-permute-done((bf16[64,1472]{1,0:T(8,128)(2,1)S(1)}, bf16[64,1472]{1,0:T(8,128)(2,1)S(1)}, u32[]{:S(2)}, u32[]{:S(2)}) %collective-permute-start.36) | collective-permute-done | bytes 188448 | tf_op jit(solution)/shard_map/join_z/ppermute | solution.py:86
  276.3 4.0 %out_rows.1 = (bf16[1472,128]{1,0:T(8,128)(2,1)S(1)}, bf16[1472,128]{1,0:T(8,128)(2,1)S(1)}, bf16[1472,256]{1,0:T(8,128)(2,1)}) custom-call(s32[1]{0:T(128)} %bitcast.c_ref, f32[1472,256]{1,0:T(8,128)} %get-tuple-element.161.res_ref, bf16[1472,256]{1,0:T(8,128)(2,1)} %ffn_out.4.own_ref, bf16[1472,256]{1,0:T(8,128)(2,1)} %copy-done.38, ...), custom_call_target="tpu_custom_call" | custom-call | bytes 30000 | tf_op jit(solution)/shard_map/out_rows/pallas_call | solution.py:63
  283.0 8.8 %collective-permute-done.38.got_ref = bf16[208,1472]{1,0:T(8,128)(2,1)S(1)} collective-permute-done((bf16[208,1472]{1,0:T(8,128)(2,1)S(1)}, bf16[208,1472]{1,0:T(8,128)(2,1)S(1)}, u32[]{:S(2)}, u32[]{:S(2)}) %collective-permute-start.38) | collective-permute-done | bytes 612384 | tf_op jit(solution)/shard_map/join_x/ppermute | solution.py:86
  294.8 2.4 join_core.1
  297.2 14.1 %all-gather.2.cloned.1.call-done.src = bf16[4,3,1288,128]{3,2,1,0:T(8,128)(2,1)} async-done(((bf16[1,3,1288,128]{3,2,1,0:T(8,128)(2,1)}), bf16[4,3,1288,128]{3,2,1,0:T(8,128)(2,1)}) %all-gather.2.cloned.1.call-update) | async-done | bytes 3956752 | tf_op jit(solution)/shard_map/all_gather | solution.py:975
  311.3 6.0 %widen.1 = (f32[448,1472]{1,0:T(8,128)}, f32[448,1472]{1,0:T(8,128)}, f32[448,1472]{1,0:T(8,128)}) custom-call(bf16[4,3,1288,128]{3,2,1,0:T(8,128)(2,1)} %all-gather.2.cloned.1.call-done.src), custom_call_target="tpu_custom_call" | custom-call | bytes 1500000000 | tf_op jit(solution)/shard_map/widen/pallas_call | solution.py:678
  (228 shorter events, 52.7 us)
Async XLA Ops:
  7.2 202.4 %reduce-scatter.4.cloned.1.call-start = ((), (), s32[]{:S(2)}) async-start(), calls=%async_computation.2 | async-start | bytes 4945920
  7.2 2.9 collective-permute-start
  7.8 11.0 %collective-permute-start.1 = (bf16[2,1472,128]{2,1,0:T(8,128)(2,1)}, bf16[2,1472,128]{2,1,0:T(8,128)(2,1)}, u32[]{:S(2)}, u32[]{:S(2)}) collective-permute-start(bf16[2,1472,128]{2,1,0:T(8,128)(2,1)} %bitcast.100), channel_id=1, source_target_pairs={{0,1},{1,0},{2,3},{3,2},{4,5},{5,4},{6,7},{7,6},{8,9},{9,8},{10,11... | collective-permute-start | bytes 2261000 | tf_op jit(solution)/shard_map/dy_core/ppermute | solution.py:86
  10.1 12.4 %collective-permute-start.3 = (bf16[448,1472]{1,0:T(8,128)(2,1)}, bf16[448,1472]{1,0:T(8,128)(2,1)S(1)}, u32[]{:S(2)}, u32[]{:S(2)}) collective-permute-start(bf16[448,1472]{1,0:T(8,128)(2,1)} %bitcast.79), channel_id=1, source_target_pairs={{0,1},{1,0},{2,3},{3,2},{4,5},{5,4},{6,7},{7,6},{8,9},{9,8},{10,11... | collective-permute-start | bytes 3956744 | tf_op jit(solution)/shard_map/gate_core/ppermute | solution.py:86
  10.5 12.0 %collective-permute-start.4 = (bf16[448,1472]{1,0:T(8,128)(2,1)}, bf16[448,1472]{1,0:T(8,128)(2,1)}, u32[]{:S(2)}, u32[]{:S(2)}) collective-permute-start(bf16[448,1472]{1,0:T(8,128)(2,1)} %bitcast.84), channel_id=1, source_target_pairs={{0,1},{1,0},{2,3},{3,2},{4,5},{5,4},{6,7},{7,6},{8,9},{9,8},{10,11... | collective-permute-start | bytes 3956744 | tf_op jit(solution)/shard_map/up_core/ppermute | solution.py:86
  12.4 24.9 %collective-permute-start.5 = (bf16[448,1472]{1,0:T(8,128)(2,1)}, bf16[448,1472]{1,0:T(8,128)(2,1)S(1)}, u32[]{:S(2)}, u32[]{:S(2)}) collective-permute-start(bf16[448,1472]{1,0:T(8,128)(2,1)} %d0.15), channel_id=1, source_target_pairs={{0,1},{1,0},{2,3},{3,2},{4,5},{5,4},{6,7},{7,6},{8,9},{9,8},{10,11... | collective-permute-start | bytes 3956744 | tf_op jit(solution)/shard_map/down_core/ppermute | solution.py:86
  15.4 49.3 %copy-start.16 = (bf16[1472,256]{1,0:T(8,128)(2,1)}, bf16[1472,256]{1,0:T(8,128)(2,1)S(1)}, u32[]{:S(2)}) copy-start(bf16[1472,256]{1,0:T(8,128)(2,1)S(1)} %get-tuple-element.155.x_ref) | copy-start | bytes 2260996
  15.5 20.1 %collective-permute-start.2 = (bf16[1472,256]{1,0:T(8,128)(2,1)S(1)}, bf16[1472,256]{1,0:T(8,128)(2,1)S(1)}, u32[]{:S(2)}, u32[]{:S(2)}) collective-permute-start(bf16[1472,256]{1,0:T(8,128)(2,1)S(1)} %get-tuple-element.140.n_ref.n0_ref), channel_id=1, source_target_pairs={{0,4},{4,0},{1,5},{5,1},{2,6},{6,2},{3,7},{7,3},{8,12},{12,8},{9,1... | collective-permute-start | bytes 2261000 | tf_op jit(solution)/shard_map/n1_y/ppermute | solution.py:86
  20.2 108.9 %copy-start.5 = (bf16[1472,256]{1,0:T(8,128)(2,1)}, bf16[1472,256]{1,0:T(8,128)(2,1)S(1)}, u32[]{:S(2)}) copy-start(bf16[1472,256]{1,0:T(8,128)(2,1)S(1)} %pair.1.dy_ref.refs_4_) | copy-start | bytes 2260996
  20.9 25.3 %copy-start.25 = (bf16[384,256]{1,0:T(8,128)(2,1)}, bf16[384,256]{1,0:T(8,128)(2,1)S(1)}, u32[]{:S(2)}) copy-start(bf16[384,256]{1,0:T(8,128)(2,1)S(1)} %get-tuple-element.146.k0) | copy-start | bytes 589828
  21.0 16.4 %collective-permute-start.6 = (bf16[384,256]{1,0:T(8,128)(2,1)S(1)}, bf16[384,256]{1,0:T(8,128)(2,1)S(1)}, u32[]{:S(2)}, u32[]{:S(2)}) collective-permute-start(bf16[384,256]{1,0:T(8,128)(2,1)S(1)} %get-tuple-element.146.k0), channel_id=1, source_target_pairs={{0,2},{1,3},{2,0},{3,1},{4,6},{5,7},{6,4},{7,5},{8,10},{9,11},{10,... | collective-permute-start | bytes 589832 | tf_op jit(solution)/shard_map/kv_own_x/ppermute | solution.py:86
  35.6 10.1 %collective-permute-start.10 = (bf16[96,1472]{1,0:T(8,128)(2,1)S(1)}, bf16[96,1472]{1,0:T(8,128)(2,1)S(1)}, u32[]{:S(2)}, u32[]{:S(2)}) collective-permute-start(bf16[96,1472]{1,0:T(8,128)(2,1)S(1)} %dynamic-slice_bitcast_fusion), channel_id=1, source_target_pairs={{0,4},{4,0},{1,5},{5,1},{2,6},{6,2},{3,7},{7,3},{8,12},{12,8},{9,1... | collective-permute-start | bytes 847880 | tf_op jit(solution)/shard_map/wout_y/ppermute | solution.py:86
  38.0 17.5 %copy-start.29 = (bf16[384,256]{1,0:T(8,128)(2,1)}, bf16[384,256]{1,0:T(8,128)(2,1)S(1)}, u32[]{:S(2)}) copy-start(bf16[384,256]{1,0:T(8,128)(2,1)S(1)} %get-tuple-element.153.k1) | copy-start | bytes 589828
  38.0 6.2 %collective-permute-start.7 = (bf16[384,256]{1,0:T(8,128)(2,1)S(1)}, bf16[384,256]{1,0:T(8,128)(2,1)S(1)}, u32[]{:S(2)}, u32[]{:S(2)}) collective-permute-start(bf16[384,256]{1,0:T(8,128)(2,1)S(1)} %get-tuple-element.153.k1), channel_id=1, source_target_pairs={{0,2},{1,3},{2,0},{3,1},{4,6},{5,7},{6,4},{7,5},{8,10},{9,11},{10,... | collective-permute-start | bytes 589832 | tf_op jit(solution)/shard_map/kv_far_x/ppermute | solution.py:86
  44.2 20.5 %collective-permute-start.9 = (bf16[1472,256]{1,0:T(8,128)(2,1)S(1)}, bf16[1472,256]{1,0:T(8,128)(2,1)S(1)}, u32[]{:S(2)}, u32[]{:S(2)}) collective-permute-start(bf16[1472,256]{1,0:T(8,128)(2,1)S(1)} %pair.1.dy_ref.refs_4_), channel_id=1, source_target_pairs={{0,2},{1,3},{2,0},{3,1},{4,6},{5,7},{6,4},{7,5},{8,10},{9,11},{10,... | collective-permute-start | bytes 2261000 | tf_op jit(solution)/shard_map/dy_x/ppermute | solution.py:86
  45.7 19.1 %copy-start.19 = (bf16[96,1472]{1,0:T(8,128)(2,1)}, bf16[96,1472]{1,0:T(8,128)(2,1)S(1)}, u32[]{:S(2)}) copy-start(bf16[96,1472]{1,0:T(8,128)(2,1)S(1)} %collective-permute-done.10.w1_ref) | copy-start | bytes 847876
  45.7 19.0 %collective-permute-start.11 = (bf16[1472,256]{1,0:T(8,128)(2,1)S(1)}, bf16[1472,256]{1,0:T(8,128)(2,1)S(1)}, u32[]{:S(2)}, u32[]{:S(2)}) collective-permute-start(bf16[1472,256]{1,0:T(8,128)(2,1)S(1)} %pair.1.dy_ref.refs_4_), channel_id=1, source_target_pairs={{0,4},{4,0},{1,5},{5,1},{2,6},{6,2},{3,7},{7,3},{8,12},{12,8},{9,1... | collective-permute-start | bytes 2261000 | tf_op jit(solution)/shard_map/dy_y/ppermute | solution.py:86
  55.5 9.2 %collective-permute-start.12 = (bf16[96,1472]{1,0:T(8,128)(2,1)S(1)}, bf16[96,1472]{1,0:T(8,128)(2,1)S(1)}, u32[]{:S(2)}, u32[]{:S(2)}) collective-permute-start(bf16[96,1472]{1,0:T(8,128)(2,1)S(1)} %collective-permute-done.10.w1_ref), channel_id=1, source_target_pairs={{0,1},{1,0},{2,3},{3,2},{4,5},{5,4},{6,7},{7,6},{8,9},{9,8},{10,11... | collective-permute-start | bytes 847880 | tf_op jit(solution)/shard_map/wout_core/ppermute | solution.py:86
  55.6 13.6 %copy-start.23 = (bf16[192,256]{1,0:T(8,128)(2,1)}, bf16[192,256]{1,0:T(8,128)(2,1)S(1)}, u32[]{:S(2)}) copy-start(bf16[192,256]{1,0:T(8,128)(2,1)S(1)} %get-tuple-element.208.m0_ref) | copy-start | bytes 294916
  55.6 9.1 %collective-permute-start.8 = (bf16[192,256]{1,0:T(8,128)(2,1)S(1)}, bf16[192,256]{1,0:T(8,128)(2,1)S(1)}, u32[]{:S(2)}, u32[]{:S(2)}) collective-permute-start(bf16[192,256]{1,0:T(8,128)(2,1)S(1)} %get-tuple-element.318), channel_id=1, source_target_pairs={{0,4},{4,0},{1,5},{5,1},{2,6},{6,2},{3,7},{7,3},{8,12},{12,8},{9,1... | collective-permute-start | bytes 294920 | tf_op jit(solution)/shard_map/mixed_y/ppermute | solution.py:86
  66.8 19.8 %collective-permute-start.13 = (bf16[1472,256]{1,0:T(8,128)(2,1)S(1)}, bf16[1472,256]{1,0:T(8,128)(2,1)S(1)}, u32[]{:S(2)}, u32[]{:S(2)}) collective-permute-start(bf16[1472,256]{1,0:T(8,128)(2,1)S(1)} %get-tuple-element.166.n_ref.refs_4_.refs_12_.refs_20_), channel_id=1, source_target_pairs={{0,2},{1,3},{2,0},{3,1},{4,6},{5,7},{6,4},{7,5},{8,10},{9,11},{10,... | collective-permute-start | bytes 2261000 | tf_op jit(solution)/shard_map/n2_x/ppermute | solution.py:86
  67.5 19.1 %collective-permute-start.14 = (bf16[1472,256]{1,0:T(8,128)(2,1)S(1)}, bf16[1472,256]{1,0:T(8,128)(2,1)S(1)}, u32[]{:S(2)}, u32[]{:S(2)}) collective-permute-start(bf16[1472,256]{1,0:T(8,128)(2,1)S(1)} %get-tuple-element.166.n_ref.refs_4_.refs_12_.refs_20_), channel_id=1, source_target_pairs={{0,4},{4,0},{1,5},{5,1},{2,6},{6,2},{3,7},{7,3},{8,12},{12,8},{9,1... | collective-permute-start | bytes 2261000 | tf_op jit(solution)/shard_map/n2_y/ppermute | solution.py:86
  69.2 32.1 %collective-permute-start.16 = (bf16[1472,256]{1,0:T(8,128)(2,1)S(1)}, bf16[1472,256]{1,0:T(8,128)(2,1)S(1)}, u32[]{:S(2)}, u32[]{:S(2)}) collective-permute-start(bf16[1472,256]{1,0:T(8,128)(2,1)S(1)} %pick.2), channel_id=1, source_target_pairs={{0,4},{1,3},{2,6},{3,1},{4,0},{5,7},{6,2},{7,5},{8,12},{9,11},{10,... | collective-permute-start | bytes 2261000 | tf_op jit(solution)/shard_map/dy_d/ppermute | solution.py:86
  86.7 16.5 %collective-permute-start.15 = (bf16[1472,256]{1,0:T(8,128)(2,1)S(1)}, bf16[1472,256]{1,0:T(8,128)(2,1)S(1)}, u32[]{:S(2)}, u32[]{:S(2)}) collective-permute-start(bf16[1472,256]{1,0:T(8,128)(2,1)S(1)} %pick.3), channel_id=1, source_target_pairs={{0,4},{1,3},{2,6},{3,1},{4,0},{5,7},{6,2},{7,5},{8,12},{9,11},{10,... | collective-permute-start | bytes 2261000 | tf_op jit(solution)/shard_map/n2_d/ppermute | solution.py:86
  93.2 19.8 %collective-permute-start.17 = (bf16[1472,256]{1,0:T(8,128)(2,1)S(1)}, bf16[1472,256]{1,0:T(8,128)(2,1)S(1)}, u32[]{:S(2)}, u32[]{:S(2)}) collective-permute-start(bf16[1472,256]{1,0:T(8,128)(2,1)S(1)} %get-tuple-element.181), channel_id=1, source_target_pairs={{0,2},{1,3},{2,0},{3,1},{4,6},{5,7},{6,4},{7,5},{8,10},{9,11},{10,... | collective-permute-start | bytes 2261000 | tf_op jit(solution)/shard_map/dn_x/ppermute | solution.py:86
  100.7 15.2 %collective-permute-start.18 = (bf16[1472,256]{1,0:T(8,128)(2,1)S(1)}, bf16[1472,256]{1,0:T(8,128)(2,1)S(1)}, u32[]{:S(2)}, u32[]{:S(2)}) collective-permute-start(bf16[1472,256]{1,0:T(8,128)(2,1)S(1)} %get-tuple-element.182), channel_id=1, source_target_pairs={{0,4},{4,0},{1,5},{5,1},{2,6},{6,2},{3,7},{7,3},{8,12},{12,8},{9,1... | collective-permute-start | bytes 2261000 | tf_op jit(solution)/shard_map/dn_y/ppermute | solution.py:86
  120.9 8.3 %collective-permute-start.23 = (bf16[2,448,1472]{2,1,0:T(8,128)(2,1)S(1)}, bf16[2,448,1472]{2,1,0:T(8,128)(2,1)S(1)}, u32[]{:S(2)}, u32[]{:S(2)}) collective-permute-start(bf16[2,448,1472]{2,1,0:T(8,128)(2,1)S(1)} %wgrad_give.3), channel_id=1, source_target_pairs={{0,1},{1,0},{2,3},{3,2},{4,5},{5,4},{6,7},{7,6},{8,9},{9,8},{10,11... | collective-permute-start | bytes 7913480 | tf_op jit(solution)/shard_map/wgrad_core/ppermute | solution.py:86
  121.0 8.2 %collective-permute-start.22 = (bf16[1,448,1472]{2,1,0:T(8,128)(2,1)S(1)}, bf16[1,448,1472]{2,1,0:T(8,128)(2,1)S(1)}, u32[]{:S(2)}, u32[]{:S(2)}) collective-permute-start(bf16[1,448,1472]{2,1,0:T(8,128)(2,1)S(1)} %wgrad_give.2), channel_id=1, source_target_pairs={{0,1},{1,0},{2,3},{3,2},{4,5},{5,4},{6,7},{7,6},{8,9},{9,8},{10,11... | collective-permute-start | bytes 3956744 | tf_op jit(solution)/shard_map/wgrad_core/ppermute | solution.py:86
  121.5 20.0 %collective-permute-start.19 = (bf16[1472,256]{1,0:T(8,128)(2,1)}, bf16[1472,256]{1,0:T(8,128)(2,1)}, u32[]{:S(2)}, u32[]{:S(2)}) collective-permute-start(bf16[1472,256]{1,0:T(8,128)(2,1)} %get-tuple-element.193), channel_id=1, source_target_pairs={{0,6},{1,7},{2,4},{3,5},{4,2},{5,3},{6,0},{7,1},{8,14},{9,15},{10,... | collective-permute-start | bytes 2261000 | tf_op jit(solution)/shard_map/dn_d/ppermute | solution.py:86
  135.8 175.5 %all-gather.2.cloned.1.call-start = ((), (), s32[]{:S(2)}) async-start(), calls=%async_computation.1 | async-start | bytes 4945920 | tf_op jit(solution)/shard_map/all_gather | solution.py:975
  147.1 5.7 %collective-permute-start.24 = (bf16[192,256]{1,0:T(8,128)(2,1)S(1)}, bf16[192,256]{1,0:T(8,128)(2,1)S(1)}, u32[]{:S(2)}, u32[]{:S(2)}) collective-permute-start(bf16[192,256]{1,0:T(8,128)(2,1)S(1)} %get-tuple-element.205), channel_id=1, source_target_pairs={{0,4},{4,0},{1,5},{5,1},{2,6},{6,2},{3,7},{7,3},{8,12},{12,8},{9,1... | collective-permute-start | bytes 294920 | tf_op jit(solution)/shard_map/dmixed_y/ppermute | solution.py:86
  148.8 20.3 %collective-permute-start.20 = (bf16[1472,256]{1,0:T(8,128)(2,1)}, bf16[1472,256]{1,0:T(8,128)(2,1)S(1)}, u32[]{:S(2)}, u32[]{:S(2)}) collective-permute-start(bf16[1472,256]{1,0:T(8,128)(2,1)} %ffn_out.5), channel_id=1, source_target_pairs={{0,2},{1,3},{2,0},{3,1},{4,6},{5,7},{6,4},{7,5},{8,10},{9,11},{10,... | collective-permute-start | bytes 2261000 | tf_op jit(solution)/shard_map/out_x/ppermute | solution.py:86
  148.8 20.3 %collective-permute-start.21 = (bf16[1472,256]{1,0:T(8,128)(2,1)}, bf16[1472,256]{1,0:T(8,128)(2,1)}, u32[]{:S(2)}, u32[]{:S(2)}) collective-permute-start(bf16[1472,256]{1,0:T(8,128)(2,1)} %ffn_out.6), channel_id=1, source_target_pairs={{0,4},{4,0},{1,5},{5,1},{2,6},{6,2},{3,7},{7,3},{8,12},{12,8},{9,1... | collective-permute-start | bytes 2261000 | tf_op jit(solution)/shard_map/out_y/ppermute | solution.py:86
  165.8 9.5 %collective-permute-start.25 = (bf16[400,512]{1,0:T(8,128)(2,1)}, bf16[400,512]{1,0:T(8,128)(2,1)S(1)}, u32[]{:S(2)}, u32[]{:S(2)}) collective-permute-start(bf16[400,512]{1,0:T(8,128)(2,1)} %get-tuple-element.214), channel_id=1, source_target_pairs={{0,2},{1,3},{2,0},{3,1},{4,6},{5,7},{6,4},{7,5},{8,10},{9,11},{10,... | collective-permute-start | bytes 1228808 | tf_op jit(solution)/shard_map/dkv_x/ppermute | solution.py:86
  166.2 14.5 %collective-permute-start.26 = (bf16[192,1472]{1,0:T(8,128)(2,1)}, bf16[192,1472]{1,0:T(8,128)(2,1)}, u32[]{:S(2)}, u32[]{:S(2)}) collective-permute-start(bf16[192,1472]{1,0:T(8,128)(2,1)} %get-tuple-element.221), channel_id=1, source_target_pairs={{0,4},{4,0},{1,5},{5,1},{2,6},{6,2},{3,7},{7,3},{8,12},{12,8},{9,1... | collective-permute-start | bytes 1695752 | tf_op jit(solution)/shard_map/gout_y/ppermute | solution.py:86
  185.9 3.1 collective-permute-start.27
  185.9 19.8 %collective-permute-start.28 = (bf16[1504,256]{1,0:T(8,128)(2,1)}, bf16[1504,256]{1,0:T(8,128)(2,1)S(1)}, u32[]{:S(2)}, u32[]{:S(2)}) collective-permute-start(bf16[1504,256]{1,0:T(8,128)(2,1)} %get-tuple-element.225), channel_id=1, source_target_pairs={{0,4},{4,0},{1,5},{5,1},{2,6},{6,2},{3,7},{7,3},{8,12},{12,8},{9,1... | collective-permute-start | bytes 2310152 | tf_op jit(solution)/shard_map/back_y/ppermute | solution.py:86
  192.3 15.4 %collective-permute-start.29 = (bf16[192,1472]{1,0:T(8,128)(2,1)S(1)}, bf16[192,1472]{1,0:T(8,128)(2,1)S(1)}, u32[]{:S(2)}, u32[]{:S(2)}) collective-permute-start(bf16[192,1472]{1,0:T(8,128)(2,1)S(1)} %get-tuple-element.228), channel_id=1, source_target_pairs={{0,2},{1,3},{2,0},{3,1},{4,6},{5,7},{6,4},{7,5},{8,10},{9,11},{10,... | collective-permute-start | bytes 1695752 | tf_op jit(solution)/shard_map/fold_x/ppermute | solution.py:86
  214.1 15.0 %collective-permute-start.31 = (f32[1504,128]{1,0:T(8,128)}, f32[1504,128]{1,0:T(8,128)S(1)}, u32[]{:S(2)}, u32[]{:S(2)}) collective-permute-start(f32[1504,128]{1,0:T(8,128)} %get-tuple-element.236), channel_id=1, source_target_pairs={{0,1},{1,0},{2,3},{3,2},{4,5},{5,4},{6,7},{7,6},{8,9},{9,8},{10,11... | collective-permute-start | bytes 2310152 | tf_op jit(solution)/shard_map/grad_core/ppermute | solution.py:86
  214.1 11.8 %collective-permute-start.33 = (bf16[96,1472]{1,0:T(8,128)(2,1)S(1)}, bf16[96,1472]{1,0:T(8,128)(2,1)S(1)}, u32[]{:S(2)}, u32[]{:S(2)}) collective-permute-start(bf16[96,1472]{1,0:T(8,128)(2,1)S(1)} %get-tuple-element.241), channel_id=1, source_target_pairs={{0,8},{8,0},{16,24},{24,16},{1,9},{9,1},{17,25},{25,17},{2,10},{10... | collective-permute-start | bytes 847880 | tf_op jit(solution)/shard_map/share_z/ppermute | solution.py:86
  215.5 60.8 %collective-permute-start.30 = (bf16[1472,256]{1,0:T(8,128)(2,1)}, bf16[1472,256]{1,0:T(8,128)(2,1)}, u32[]{:S(2)}, u32[]{:S(2)}) collective-permute-start(bf16[1472,256]{1,0:T(8,128)(2,1)} %ffn_out.7), channel_id=1, source_target_pairs={{0,6},{1,7},{2,4},{3,5},{4,2},{5,3},{6,0},{7,1},{8,14},{9,15},{10,... | collective-permute-start | bytes 2261000 | tf_op jit(solution)/shard_map/out_d/ppermute | solution.py:86
  226.7 21.0 %collective-permute-start.34 = (bf16[48,1472]{1,0:T(8,128)(2,1)S(1)}, bf16[48,1472]{1,0:T(8,128)(2,1)S(1)}, u32[]{:S(2)}, u32[]{:S(2)}) collective-permute-start(bf16[48,1472]{1,0:T(8,128)(2,1)S(1)} %get-tuple-element.243), channel_id=1, source_target_pairs={{0,16},{8,24},{16,0},{24,8},{1,17},{9,25},{17,1},{25,9},{2,18},{10... | collective-permute-start | bytes 423944 | tf_op jit(solution)/shard_map/share_z/ppermute | solution.py:86
  247.8 13.8 %collective-permute-start.35 = (bf16[64,1472]{1,0:T(8,128)(2,1)S(1)}, bf16[64,1472]{1,0:T(8,128)(2,1)S(1)}, u32[]{:S(2)}, u32[]{:S(2)}) collective-permute-start(bf16[64,1472]{1,0:T(8,128)(2,1)S(1)} %share_sum.1.refs_0_), channel_id=1, source_target_pairs={{0,8},{8,16},{16,24},{24,0},{1,9},{9,17},{17,25},{25,1},{2,10},{10... | collective-permute-start | bytes 565256 | tf_op jit(solution)/shard_map/join_z/ppermute | solution.py:86
  247.9 26.7 %collective-permute-start.36 = (bf16[64,1472]{1,0:T(8,128)(2,1)S(1)}, bf16[64,1472]{1,0:T(8,128)(2,1)S(1)}, u32[]{:S(2)}, u32[]{:S(2)}) collective-permute-start(bf16[64,1472]{1,0:T(8,128)(2,1)S(1)} %share_sum.1.refs_0_), channel_id=1, source_target_pairs={{0,16},{8,24},{16,0},{24,8},{1,17},{9,25},{17,1},{25,9},{2,18},{10... | collective-permute-start | bytes 565256 | tf_op jit(solution)/shard_map/join_z/ppermute | solution.py:86
  251.0 23.6 %collective-permute-start.37 = (bf16[64,1472]{1,0:T(8,128)(2,1)S(1)}, bf16[64,1472]{1,0:T(8,128)(2,1)S(1)}, u32[]{:S(2)}, u32[]{:S(2)}) collective-permute-start(bf16[64,1472]{1,0:T(8,128)(2,1)S(1)} %share_sum.1.refs_0_), channel_id=1, source_target_pairs={{0,24},{8,0},{16,8},{24,16},{1,25},{9,1},{17,9},{25,17},{2,26},{10... | collective-permute-start | bytes 565256 | tf_op jit(solution)/shard_map/join_z/ppermute | solution.py:86
  275.3 16.5 %collective-permute-start.38 = (bf16[208,1472]{1,0:T(8,128)(2,1)S(1)}, bf16[208,1472]{1,0:T(8,128)(2,1)S(1)}, u32[]{:S(2)}, u32[]{:S(2)}) collective-permute-start(bf16[208,1472]{1,0:T(8,128)(2,1)S(1)} %get-tuple-element.246.own_ref), channel_id=1, source_target_pairs={{0,2},{1,3},{2,0},{3,1},{4,6},{5,7},{6,4},{7,5},{8,10},{9,11},{10,... | collective-permute-start | bytes 1837064 | tf_op jit(solution)/shard_map/join_x/ppermute | solution.py:86
  280.4 1.7 collective-permute-start.32
  291.9 2.9 collective-permute-start.39
  (39 other events, 247.0 us)
Sparse Core Ops, SparseCore 0:
  135.9 73.6 reduce-scatter.3
  211.2 100.0 all-gather.1
